TPU v7x, 32 devices: a whole 2x2x4 slice. The times are simulated.
32 devices in a mesh: fsdp: 16 (over z, x, core), tensor: 2 (over y).
Axes of the slice: x: 2, y: 2, z: 4, core: 2. Of those that a mesh axis runs over, the one named last changes fastest.
Arguments:
- tokens: bfloat16 [2, 1024, 16, 1024], P(None, 'tensor', 'fsdp'), may hold values from -6 to 6
- piece_starts: int32 [2, 16, 3], P(None, 'fsdp'), may hold values from 0 to 1024, as said below
- gain_attn: float32 [1024], P(('fsdp', 'tensor')), may hold values from 0.25 to 1.75
- w_qkv: bfloat16 [3, 1024, 1024], P(None, 'fsdp', 'tensor'), may hold values from -0.1875 to 0.1875
- w_out: bfloat16 [1024, 1024], P('tensor', 'fsdp'), may hold values from -1.5 to 1.5
- gain_mlp: float32 [1024], P(('fsdp', 'tensor')), may hold values from 0.25 to 1.75
- w_gate_up: bfloat16 [2, 1024, 4096], P(None, 'fsdp', 'tensor'), may hold values from -0.1875 to 0.1875
- w_down: bfloat16 [4096, 1024], P('tensor', 'fsdp'), may hold values from -0.09375 to 0.09375
- out_grad: bfloat16 [2, 1024, 16, 1024], P(None, 'tensor', 'fsdp'), may hold values from -6 to 6
Outputs:
- layer_out: bfloat16 [2, 1024, 16, 1024], P(None, 'tensor', 'fsdp')
- input_grad: float32 [2, 1024, 16, 1024], P(None, 'tensor', 'fsdp')
- grad_gain_attn: float32 [1024], P(('fsdp', 'tensor'))
- grad_qkv: float32 [3, 1024, 1024], P(None, 'fsdp', 'tensor')
- grad_out: float32 [1024, 1024], P('tensor', 'fsdp')
- feedforward_gain_gradient: float32 [1024], P(('fsdp', 'tensor'))
- grad_gate_up: float32 [2, 1024, 4096], P(None, 'fsdp', 'tensor')
- grad_down: float32 [4096, 1024], P('tensor', 'fsdp')
Inputs may be any that keep to these rules, and one draw needn't show every extreme that they name: `piece_starts`: entry p of a row is the first position of picture piece p of that sequence; each piece covers 256 positions inside the sequence, pieces do not intersect and come in rising order; an entry equal to 1024 marks an unused slot, and unused slots follow the used ones.
All inputs are finite; a program needn't handle non-finite values.
Results may differ from a plain program's by a relative error of at most 0.022.
Values may be sent and summed in bfloat16 or wider, within the bound.
No kernel may reach another device: no remote copies, remote signals or barrier semaphores. Data moves between devices by JAX's collectives and lax.ppermute only.
A program may use at most 384 MiB of HBM per device.

v0:
```python
import jax
import jax.numpy as jnp
from jax import lax
from jax.sharding import PartitionSpec as P

D = 1024
HEAD_DIM = 64
QBLOCK = 512
PIECE = 256


norm_eps = 1e-05
masked_score = -1e30


def rms_scale(values_float_rows):
    return lax.rsqrt(
        jnp.mean(values_float_rows * values_float_rows, axis=-1, keepdims=True) + norm_eps
    )


def norm_backward_pass(d_normed, normed_pre, scale_rows, gain_vector_row):
    d_scaled = d_normed * gain_vector_row
    return scale_rows * (
        d_scaled - normed_pre * jnp.mean(d_scaled * normed_pre, axis=-1, keepdims=True)
    )


def piece_index_labels(starts_row, length):
    positions = jnp.arange(length, dtype=jnp.int32)[:, None]
    inside = (positions >= starts_row[None, :]) & (positions < starts_row[None, :] + PIECE)
    numbers = jnp.arange(1, starts_row.shape[0] + 1, dtype=jnp.int32)
    return jnp.sum(jnp.where(inside, numbers[None, :], 0), axis=1)


def allowed_block(labels, first_row, key_count):
    row_ids = first_row + jnp.arange(QBLOCK, dtype=jnp.int32)
    col_ids = jnp.arange(key_count, dtype=jnp.int32)
    row_labels = labels[first_row : first_row + QBLOCK]
    causal = col_ids[None, :] <= row_ids[:, None]
    same_piece = (row_labels[:, None] == labels[None, :]) & (row_labels[:, None] > 0)
    return causal | same_piece


def attend_forward(queries, keys_all, values_all, labels, key_spans):
    score_scale = HEAD_DIM ** (-0.5)
    outputs = []
    totals = []
    for first_row, key_count in key_spans:
        block_q = queries[first_row : first_row + QBLOCK]
        scores = (
            jnp.einsum("qhd,khd->hqk", block_q, keys_all, preferred_element_type=jnp.float32)
            * score_scale
        )
        scores = jnp.where(allowed_block(labels, first_row, key_count)[None], scores, masked_score)
        row_max = jnp.max(scores, axis=-1, keepdims=True)
        exp_scores = jnp.exp(scores - row_max)
        row_total = jnp.sum(exp_scores, axis=-1, keepdims=True)
        attn_probs = (exp_scores / row_total).astype(jnp.bfloat16)
        block_out = jnp.einsum(
            "hqk,khd->qhd", attn_probs, values_all, preferred_element_type=jnp.float32
        )
        outputs.append(block_out.astype(jnp.bfloat16))
        totals.append((row_max + jnp.log(row_total))[..., 0])
    return (jnp.concatenate(outputs, 0), jnp.concatenate(totals, 1))


def attend_backward(queries, keys_all, values_all, labels, log_total, d_heads, key_spans):
    score_scale = HEAD_DIM ** (-0.5)
    query_parts = []
    d_keys = jnp.zeros(keys_all.shape, jnp.float32)
    d_values = jnp.zeros(values_all.shape, jnp.float32)
    for first_row, key_count in key_spans:
        block_q = queries[first_row : first_row + QBLOCK]
        block_d = d_heads[first_row : first_row + QBLOCK]
        scores = (
            jnp.einsum("qhd,khd->hqk", block_q, keys_all, preferred_element_type=jnp.float32)
            * score_scale
        )
        mask_now = allowed_block(labels, first_row, key_count)[None]
        attn_probs = jnp.where(
            mask_now, jnp.exp(scores - log_total[:, first_row : first_row + QBLOCK, None]), 0.0
        )
        probs_low = attn_probs.astype(jnp.bfloat16)
        d_probs = jnp.einsum(
            "qhd,khd->hqk", block_d, values_all, preferred_element_type=jnp.float32
        )
        row_dot = jnp.sum(attn_probs * d_probs, axis=-1, keepdims=True)
        d_scores = (attn_probs * (d_probs - row_dot)).astype(jnp.bfloat16)
        query_parts.append(
            jnp.einsum("hqk,khd->qhd", d_scores, keys_all, preferred_element_type=jnp.float32)
            * score_scale
        )
        d_keys = d_keys.at[:key_count].add(
            jnp.einsum("hqk,qhd->khd", d_scores, block_q, preferred_element_type=jnp.float32)
            * score_scale
        )
        d_values = d_values.at[:key_count].add(
            jnp.einsum("hqk,qhd->khd", probs_low, block_d, preferred_element_type=jnp.float32)
        )
    return (jnp.concatenate(query_parts, 0), d_keys, d_values)


def attention_forward(qkv_low, labels_all, key_spans):
    length, seq_count, width = (qkv_low.shape[0], qkv_low.shape[1], qkv_low.shape[3])
    per_seq = jnp.moveaxis(qkv_low, 1, 0).reshape(seq_count, length, 3, width // HEAD_DIM, HEAD_DIM)

    def one_seq(seq_items):
        seq_qkv, labels = seq_items
        return attend_forward(seq_qkv[:, 0], seq_qkv[:, 1], seq_qkv[:, 2], labels, key_spans)

    seq_outs, totals = lax.map(one_seq, (per_seq, labels_all))
    return (jnp.moveaxis(seq_outs.reshape(seq_count, length, width), 0, 1), totals)


def attention_backward(qkv_low, labels_all, totals, d_attended, key_spans):
    length, seq_count, width = (qkv_low.shape[0], qkv_low.shape[1], qkv_low.shape[3])
    per_seq = jnp.moveaxis(qkv_low, 1, 0).reshape(seq_count, length, 3, width // HEAD_DIM, HEAD_DIM)
    d_seq = jnp.moveaxis(d_attended, 1, 0).reshape(seq_count, length, width // HEAD_DIM, HEAD_DIM)

    def one_seq(seq_items):
        seq_qkv, labels, log_total, seq_d = seq_items
        d_query, d_keys, d_values = attend_backward(
            seq_qkv[:, 0], seq_qkv[:, 1], seq_qkv[:, 2], labels, log_total, seq_d, key_spans
        )
        return jnp.stack([d_query, d_keys, d_values], 1).astype(jnp.bfloat16)

    seq_grads = lax.map(one_seq, (per_seq, labels_all, totals, d_seq))
    return jnp.moveaxis(seq_grads, 0, 1).reshape(length, seq_count, 3, width)


def fetch_weights(w_qkv, w_out, w_gate_up, w_down):
    qkv_all, out_all, gate_up_all, down_weight_full = (
        lax.all_gather(w_qkv, "fsdp", axis=1, tiled=True),
        lax.all_gather(w_out, "fsdp", axis=1, tiled=True),
        lax.all_gather(w_gate_up, "fsdp", axis=1, tiled=True),
        lax.all_gather(w_down, "fsdp", axis=1, tiled=True),
    )
    return (qkv_all, out_all, gate_up_all, down_weight_full)


def local(tokens, piece_starts, gain_attn, w_qkv, w_out, gain_mlp, w_gate_up, w_down, out_grad):
    both_gains = lax.all_gather(
        jnp.stack([gain_attn, gain_mlp]), ("fsdp", "tensor"), axis=1, tiled=True
    )
    local_rows = tokens.shape[1]
    length = local_rows * lax.axis_size("tensor")
    key_spans = [(first_row, length) for first_row in range(0, length, QBLOCK)]

    def label_row(starts_row):
        return piece_index_labels(starts_row, length)

    labels_every = jax.vmap(jax.vmap(label_row))(piece_starts)
    ff_cols = w_gate_up.shape[2]
    acc_gain = jnp.zeros((2, D), jnp.float32)
    acc_qkv = jnp.zeros((3, D, w_qkv.shape[2]), jnp.float32)
    acc_out = jnp.zeros((w_out.shape[0], D), jnp.float32)
    acc_gate_up = jnp.zeros((2, D, ff_cols), jnp.float32)
    acc_down = jnp.zeros((ff_cols, D), jnp.float32)
    layer_outs = []
    input_grads = []
    for micro_idx in range(tokens.shape[0]):
        weights = fetch_weights(w_qkv, w_out, w_gate_up, w_down)
        qkv_all, out_all, gate_up_all, down_weight_full = weights
        rows_f32 = tokens[micro_idx].astype(jnp.float32)
        scale_attn = rms_scale(rows_f32)
        pre_attn = rows_f32 * scale_attn
        normed = (pre_attn * both_gains[0]).astype(jnp.bfloat16)
        piece_rows = lax.all_gather(normed, "tensor", axis=0, tiled=True)
        made = jnp.einsum("lsd,cde->lsce", piece_rows, qkv_all, preferred_element_type=jnp.float32)
        qkv_low = made.astype(jnp.bfloat16)
        attended, log_total = attention_forward(qkv_low, labels_every[micro_idx], key_spans)
        rows_now = lax.slice_in_dim(attended, 0, local_rows * lax.axis_size("tensor"), axis=0)
        attn_part = lax.psum_scatter(
            jnp.einsum("lsc,cd->lsd", rows_now, out_all, preferred_element_type=jnp.float32).astype(
                jnp.bfloat16
            ),
            "tensor",
            scatter_dimension=0,
            tiled=True,
        ).astype(jnp.float32)
        hidden = rows_f32 + attn_part
        scale_mlp = rms_scale(hidden)
        pre_mlp = hidden * scale_mlp
        normed_mlp = (pre_mlp * both_gains[1]).astype(jnp.bfloat16)
        expand_piece_rows = lax.all_gather(normed_mlp, "tensor", axis=0, tiled=True)
        gate_up = jnp.einsum(
            "lsd,cdf->lscf", expand_piece_rows, gate_up_all, preferred_element_type=jnp.float32
        )
        gate_part = gate_up[:, :, 0]
        up_part = gate_up[:, :, 1]
        sigmoid_gate = jax.nn.sigmoid(gate_part)
        activated = gate_part * sigmoid_gate
        mixed_lowp_rows = (activated * up_part).astype(jnp.bfloat16)
        down_rows_now = lax.slice_in_dim(
            mixed_lowp_rows, 0, local_rows * lax.axis_size("tensor"), axis=0
        )
        mlp_part = lax.psum_scatter(
            jnp.einsum(
                "meg,gp->mep", down_rows_now, down_weight_full, preferred_element_type=jnp.float32
            ).astype(jnp.bfloat16),
            "tensor",
            scatter_dimension=0,
            tiled=True,
        ).astype(jnp.float32)
        layer_outs.append((hidden + mlp_part).astype(jnp.bfloat16))
        qkv_all, out_all, gate_up_all, down_weight_full = fetch_weights(
            w_qkv, w_out, w_gate_up, w_down
        )
        grad_rows = out_grad[micro_idx]
        down_piece_rows = lax.all_gather(grad_rows, "tensor", axis=0, tiled=True)
        d_mixed = jnp.einsum(
            "xum,tm->xut", down_piece_rows, down_weight_full, preferred_element_type=jnp.float32
        )
        acc_down = acc_down + jnp.einsum(
            "zmp,zme->pe", mixed_lowp_rows, down_piece_rows, preferred_element_type=jnp.float32
        )
        d_gate = d_mixed * up_part * sigmoid_gate * (1.0 + gate_part * (1.0 - sigmoid_gate))
        d_up = d_mixed * activated
        d_gate_up = jnp.stack([d_gate, d_up], 2).astype(jnp.bfloat16)
        acc_gate_up = acc_gate_up + jnp.einsum(
            "lsd,lscf->cdf", expand_piece_rows, d_gate_up, preferred_element_type=jnp.float32
        )
        mlp_rows_now = lax.slice_in_dim(d_gate_up, 0, local_rows * lax.axis_size("tensor"), axis=0)
        d_normed_mlp = lax.psum_scatter(
            jnp.einsum(
                "lscf,cdf->lsd", mlp_rows_now, gate_up_all, preferred_element_type=jnp.float32
            ).astype(jnp.bfloat16),
            "tensor",
            scatter_dimension=0,
            tiled=True,
        ).astype(jnp.float32)
        gain_mlp_part = jnp.sum(d_normed_mlp * pre_mlp, axis=(0, 1))
        d_hidden = grad_rows.astype(jnp.float32) + norm_backward_pass(
            d_normed_mlp, pre_mlp, scale_mlp, both_gains[1]
        )
        attention_gradient_lowp = d_hidden.astype(jnp.bfloat16)
        out_piece_rows = lax.all_gather(attention_gradient_lowp, "tensor", axis=0, tiled=True)
        out_made = jnp.einsum(
            "lsd,cd->lsc", out_piece_rows, out_all, preferred_element_type=jnp.float32
        )
        d_attended = out_made.astype(jnp.bfloat16)
        acc_out = acc_out + jnp.einsum(
            "lsc,lsd->cd", attended, out_piece_rows, preferred_element_type=jnp.float32
        )
        d_qkv = attention_backward(
            qkv_low, labels_every[micro_idx], log_total, d_attended, key_spans
        )
        acc_qkv = acc_qkv + jnp.einsum(
            "lsd,lsce->cde", piece_rows, d_qkv, preferred_element_type=jnp.float32
        )
        d_normed = lax.psum_scatter(
            jnp.einsum("lsce,cde->lsd", d_qkv, qkv_all, preferred_element_type=jnp.float32).astype(
                jnp.bfloat16
            ),
            "tensor",
            scatter_dimension=0,
            tiled=True,
        ).astype(jnp.float32)
        gain_attn_part = jnp.sum(d_normed * pre_attn, axis=(0, 1))
        input_grads.append(
            d_hidden + norm_backward_pass(d_normed, pre_attn, scale_attn, both_gains[0])
        )
        acc_gain = acc_gain + jnp.stack([gain_attn_part, gain_mlp_part])
    gain_rows, qkv_rows, out_rows_sum, gate_up_rows, down_rows_sum = (
        lax.psum_scatter(
            acc_gain.astype(jnp.bfloat16), "fsdp", scatter_dimension=1, tiled=True
        ).astype(jnp.float32),
        lax.psum_scatter(
            acc_qkv.astype(jnp.bfloat16), "fsdp", scatter_dimension=1, tiled=True
        ).astype(jnp.float32),
        lax.psum_scatter(
            acc_out.astype(jnp.bfloat16), "fsdp", scatter_dimension=1, tiled=True
        ).astype(jnp.float32),
        lax.psum_scatter(
            acc_gate_up.astype(jnp.bfloat16), "fsdp", scatter_dimension=1, tiled=True
        ).astype(jnp.float32),
        lax.psum_scatter(
            acc_down.astype(jnp.bfloat16), "fsdp", scatter_dimension=1, tiled=True
        ).astype(jnp.float32),
    )
    gain_shares = lax.psum_scatter(gain_rows, "tensor", scatter_dimension=1, tiled=True)
    return (
        jnp.stack(layer_outs, 0),
        jnp.stack(input_grads, 0),
        gain_shares[0],
        qkv_rows,
        out_rows_sum,
        gain_shares[1],
        gate_up_rows,
        down_rows_sum,
    )


def solution(mesh):
    return jax.shard_map(
        local,
        mesh=mesh,
        in_specs=(
            P(None, "tensor", "fsdp", None),
            P(None, "fsdp", None),
            P(("fsdp", "tensor")),
            P(None, "fsdp", "tensor"),
            P("tensor", "fsdp"),
            P(("fsdp", "tensor")),
            P(None, "fsdp", "tensor"),
            P("tensor", "fsdp"),
            P(None, "tensor", "fsdp", None),
        ),
        out_specs=(
            P(None, "tensor", "fsdp", None),
            P(None, "tensor", "fsdp", None),
            P(("fsdp", "tensor")),
            P(None, "fsdp", "tensor"),
            P("tensor", "fsdp"),
            P(("fsdp", "tensor")),
            P(None, "fsdp", "tensor"),
            P("tensor", "fsdp"),
        ),
        check_vma=False,
    )
```

profile of v0, /device:TPU:0, one launch (start us, length us, event | category | flops | bytes accessed | tf_op | source)
XLA Modules:
  0.0 1468.2 jit_solution(14414753728371076220)
XLA Ops:
  10.0 69.7 %all-gather.2 = f32[32,32,2]{1,2,0:T(2,128)S(1)} all-gather(f32[1,32,2]{1,2,0:T(2,128)S(1)} %maximum_bitcast_fusion), channel_id=1, replica_groups=mesh['fsdp'=16,'tensor'=2] {'fsdp','tensor'}, dimensions={0}, use_global_device_ids=true | all-gather | bytes 8448 | tf_op jit(solution)/shard_map/all_gather | solution.py:143
  89.9 23.7 %all-gather.16.cloned.1.call-done = bf16[1024,1,1024]{2,0,1:T(8,128)(2,1)} async-done(((bf16[512,1,1024]{2,0,1:T(8,128)(2,1)}), bf16[1024,1,1024]{2,0,1:T(8,128)(2,1)}) %all-gather.16.cloned.1.call-update) | async-done | bytes 2097168 | tf_op jit(solution)/shard_map/all_gather | solution.py:169
  113.5 47.4 %all-gather.18.cloned.1.call-done = bf16[3,1024,512]{2,1,0:T(8,128)(2,1)} async-done(((bf16[3,64,512]{2,1,0:T(8,128)(2,1)}), bf16[3,1024,512]{2,1,0:T(8,128)(2,1)}) %all-gather.18.cloned.1.call-update) | async-done | bytes 3145744 | tf_op jit(solution)/shard_map/all_gather | solution.py:134
  204.0 29.9 %all-gather.28.cloned.1.call-done = bf16[1024,1,1024]{2,0,1:T(8,128)(2,1)} async-done(((bf16[512,1,1024]{2,0,1:T(8,128)(2,1)}), bf16[1024,1,1024]{2,0,1:T(8,128)(2,1)}) %all-gather.28.cloned.1.call-update) | async-done | bytes 2097168 | tf_op jit(solution)/shard_map/all_gather | solution.py:169
  272.3 32.1 %reduce-scatter.21.cloned.1.call-done = bf16[512,1,1024]{2,0,1:T(8,128)(2,1)} async-done(((bf16[1024,1,1024]{2,0,1:T(8,128)(2,1)}), bf16[512,1,1024]{2,0,1:T(8,128)(2,1)}) %reduce-scatter.21.cloned.1.call-update) | async-done | bytes 1048592 | tf_op jit(solution)/shard_map/reduce_scatter | solution.py:174
  314.8 27.4 %all-gather.30.cloned.1.call-done = bf16[1024,1,1024]{2,0,1:T(8,128)(2,1)} async-done(((bf16[512,1,1024]{2,0,1:T(8,128)(2,1)}), bf16[1024,1,1024]{2,0,1:T(8,128)(2,1)}) %all-gather.30.cloned.1.call-update) | async-done | bytes 2097168 | tf_op jit(solution)/shard_map/all_gather | solution.py:186
  342.2 77.1 %all-gather.24.cloned.1.call-done = bf16[2,1024,2048]{2,1,0:T(8,128)(2,1)} async-done(((bf16[2,64,2048]{2,1,0:T(8,128)(2,1)}), bf16[2,1024,2048]{2,1,0:T(8,128)(2,1)}) %all-gather.24.cloned.1.call-update) | async-done | bytes 8388624 | tf_op jit(solution)/shard_map/all_gather | solution.py:136
  419.4 16.4 %convolution_bitcast_fusion = f32[1024,1,2,2048]{3,0,2,1:T(8,128)} fusion(bf16[2,1024,2048]{2,1,0:T(8,128)(2,1)} %all-gather.24.cloned.1.call-done, bf16[1024,1,1024]{2,0,1:T(8,128)(2,1)} %all-gather.30.cloned.1.call-done), kind=kOutput, calls=%fused_computation.79 | convolution fusion | flops 8589934592 | bytes 27262976 | tf_op jit(solution)/shard_map/lsd,cdf->lscf/dot_general | solution.py:187
  435.8 17.1 %all-gather.38.cloned.1.call-done = bf16[1,1024,1,1024]{3,1,2,0:T(8,128)(2,1)} async-done(((bf16[1,512,1,1024]{3,1,2,0:T(8,128)(2,1)}), bf16[1,1024,1,1024]{3,1,2,0:T(8,128)(2,1)}) %all-gather.38.cloned.1.call-update) | async-done | bytes 2097168 | tf_op jit(solution)/shard_map/all_gather | solution.py:211
  452.9 52.6 %all-gather.26.cloned.1.call-done = bf16[2048,1024]{0,1:T(8,128)(2,1)} async-done(((bf16[2048,64]{0,1:T(8,128)(2,1)}), bf16[2048,1024]{0,1:T(8,128)(2,1)}) %all-gather.26.cloned.1.call-update) | async-done | bytes 4194320 | tf_op jit(solution)/shard_map/all_gather | solution.py:137
  505.5 13.0 fusion.55
  521.9 10.1 fusion.130
  532.1 7.2 all-gather.22.cloned.1.call-done
  539.3 16.1 %convolution_bitcast_fusion.1 = f32[1024,1,2,2048]{3,0,2,1:T(8,128)} fusion(bf16[2,1024,2048]{2,1,0:T(8,128)(2,1)} %all-gather.24.cloned.1.call-done, bf16[1024,1,1024]{2,0,1:T(8,128)(2,1)} %all-gather.22.cloned.1.call-done), kind=kOutput, calls=%fused_computation.80 | convolution fusion | flops 8589934592 | bytes 27262976 | tf_op jit(solution)/shard_map/lsd,cdf->lscf/dot_general | solution.py:187
  555.4 18.4 %all-gather.36.cloned.1.call-done = bf16[1,1024,1,1024]{3,1,2,0:T(8,128)(2,1)} async-done(((bf16[1,512,1,1024]{3,1,2,0:T(8,128)(2,1)}), bf16[1,1024,1,1024]{3,1,2,0:T(8,128)(2,1)}) %all-gather.36.cloned.1.call-update) | async-done | bytes 2097168 | tf_op jit(solution)/shard_map/all_gather | solution.py:211
  573.8 12.9 fusion.54
  590.1 12.3 fusion.128
  602.7 13.0 convert_bitcast_fusion
  615.9 26.7 %reduce-scatter.25.cloned.1.call-done = bf16[512,1,1024]{2,0,1:T(8,128)(2,1)} async-done(((bf16[1024,1,1024]{2,0,1:T(8,128)(2,1)}), bf16[512,1,1024]{2,0,1:T(8,128)(2,1)}) %reduce-scatter.25.cloned.1.call-update) | async-done | bytes 1048592 | tf_op jit(solution)/shard_map/reduce_scatter | solution.py:225
  646.5 30.0 %reduce-scatter.23.cloned.1.call-done = bf16[512,1,1024]{2,0,1:T(8,128)(2,1)} async-done(((bf16[1024,1,1024]{2,0,1:T(8,128)(2,1)}), bf16[512,1,1024]{2,0,1:T(8,128)(2,1)}) %reduce-scatter.23.cloned.1.call-update) | async-done | bytes 1048592 | tf_op jit(solution)/shard_map/reduce_scatter | solution.py:198
  682.0 32.6 %all-gather.34.cloned.1.call-done = bf16[1024,1,1024]{2,0,1:T(8,128)(2,1)} async-done(((bf16[512,1,1024]{2,0,1:T(8,128)(2,1)}), bf16[1024,1,1024]{2,0,1:T(8,128)(2,1)}) %all-gather.34.cloned.1.call-update) | async-done | bytes 2097168 | tf_op jit(solution)/shard_map/all_gather | solution.py:238
  717.9 12.9 multiply_reduce_fusion.1
  730.8 12.5 multiply_reduce_fusion
  743.3 29.1 %multiply_convert_fusion = (bf16[8,512,1024]{2,1,0:T(8,128)(2,1)}, bf16[8,512,1024]{2,1,0:T(8,128)(2,1)}) fusion(f32[8,512,1024]{2,1,0:T(8,128)} %get-tuple-element.372, f32[8,512,1024]{2,1,0:T(8,128)} %copy-done.3, f32[8,512]{1,0:T(8,128)S(1)} %get-tuple-element.371, f32[8,512]{1,0:T(8,128)S(1)} %log_add_fusion, pred[512,1024]{1,0:T(8,128)(4,1)S(1)} %copy-done.26, ...), kind=kLoop, calls=%fused_computation.1 | loop fusion | flops 50331648 | bytes 85000192 | tf_op jit(solution)/shard_map/while/body/eval_jaxpr/convert_element_type | solution.py:89
  782.3 9.3 fusion.25
  795.4 9.1 fusion.29
  804.5 12.7 multiply_reduce_fusion.2
  817.3 9.0 add_convert_fusion.4
  828.5 7.3 fusion.152
  848.8 7.6 fusion.131
  856.5 13.0 multiply_reduce_fusion.3
  869.6 29.4 %multiply_convert_fusion.2 = (bf16[8,512,1024]{2,1,0:T(8,128)(2,1)}, bf16[8,512,1024]{2,1,0:T(8,128)(2,1)}) fusion(f32[8,512,1024]{2,1,0:T(8,128)} %get-tuple-element.368, f32[8,512,1024]{2,1,0:T(8,128)} %copy-done.1, f32[8,512]{1,0:T(8,128)S(1)} %get-tuple-element.367, f32[8,512]{1,0:T(8,128)S(1)} %log_add_fusion.2, pred[512,1024]{1,0:T(8,128)(4,1)S(1)} %copy-done.21, ...), kind=kLoop, calls=%fused_computation.7 | loop fusion | flops 50331648 | bytes 85000192 | tf_op jit(solution)/shard_map/while/body/eval_jaxpr/convert_element_type | solution.py:89
  899.0 9.5 add_convert_fusion.5
  938.3 7.0 fusion.129
  945.6 15.1 %fusion.50 = f32[2048,1024]{0,1:T(8,128)} fusion(f32[1024,1,2,2048]{3,0,2,1:T(8,128)} %convolution_bitcast_fusion, bf16[1,1024,1,1024]{3,1,2,0:T(8,128)(2,1)} %all-gather.38.cloned.1.call-done), kind=kOutput, calls=%fused_computation.90 | convolution fusion | flops 4307550208 | bytes 27262976 | tf_op jit(solution)/shard_map/zmp,zme->pe/dot_general | solution.py:215
  960.7 16.6 %reduce-scatter.27.cloned.1.call-done = bf16[512,1,1024]{2,0,1:T(8,128)(2,1)} async-done(((bf16[1024,1,1024]{2,0,1:T(8,128)(2,1)}), bf16[512,1,1024]{2,0,1:T(8,128)(2,1)}) %reduce-scatter.27.cloned.1.call-update) | async-done | bytes 1048592 | tf_op jit(solution)/shard_map/reduce_scatter | solution.py:252
  981.3 14.2 add_convert_fusion.1
  1001.6 12.8 convert_bitcast_fusion.2
  1014.5 16.3 %fusion.42 = f32[2,2048,1024]{2,1,0:T(8,128)} fusion(bf16[1024,1,2048]{2,0,1:T(8,128)(2,1)} %copy-done.86, bf16[1024,1,2048]{2,0,1:T(8,128)(2,1)} %copy-done.85, bf16[1024,1,1024]{2,0,1:T(8,128)(2,1)} %all-gather.22.cloned.1.call-done), kind=kOutput, calls=%fused_computation.83 | convolution fusion | flops 8594128896 | bytes 27262976 | tf_op jit(solution)/shard_map/lsd,lscf->cdf/dot_general | solution.py:221
  1030.7 17.5 %fusion.8 = bf16[2,1024,2048]{1,2,0:T(8,128)(2,1)} fusion(f32[2,2048,1024]{2,1,0:T(8,128)} %fusion.42, bf16[1024,1,2048]{2,0,1:T(8,128)(2,1)} %copy-done.84, bf16[1024,1,2048]{2,0,1:T(8,128)(2,1)} %copy-done.83, bf16[1024,1,1024]{2,0,1:T(8,128)(2,1)} %all-gather.30.cloned.1.call-done), kind=kOutput, calls=%fused_computation.33 | convolution fusion | flops 8602517504 | bytes 35651584 | tf_op jit(solution)/shard_map/lsd,lscf->cdf/dot_general | solution.py:221
  1048.3 22.1 %copy.74 = bf16[2,1024,2048]{2,0,1:T(2,128)(2,1)} copy(bf16[2,1024,2048]{1,2,0:T(8,128)(2,1)} %fusion.8) | data formatting | bytes 16777216 | tf_op jit(solution)/shard_map/convert_element_type | solution.py:276
  1070.4 8.8 fusion.115
  1080.8 9.3 fusion.58
  1090.0 7.8 copy.71
  1099.8 13.1 reduce-scatter.35.cloned.1.call-done
  1114.7 58.2 %reduce-scatter.33.cloned.1.call-done = bf16[512,64]{0,1:T(8,128)(2,1)} async-done(((bf16[512,1024]{0,1:T(8,128)(2,1)}), bf16[512,64]{0,1:T(8,128)(2,1)}) %reduce-scatter.33.cloned.1.call-update) | async-done | bytes 65552 | tf_op jit(solution)/shard_map/reduce_scatter | solution.py:272
  1178.5 28.2 %reduce-scatter.19.cloned.1.call-done = bf16[512,1,1024]{2,0,1:T(8,128)(2,1)} async-done(((bf16[1024,1,1024]{2,0,1:T(8,128)(2,1)}), bf16[512,1,1024]{2,0,1:T(8,128)(2,1)}) %reduce-scatter.19.cloned.1.call-update) | async-done | bytes 1048592 | tf_op jit(solution)/shard_map/reduce_scatter | solution.py:198
  1221.2 235.2 %all-reduce.5.cloned.1.call-done = (bf16[3,1024,512]{2,0,1:T(4,128)(2,1)}, bf16[2,1024,2048]{2,0,1:T(2,128)(2,1)}) async-done(((bf16[3,1024,512]{2,0,1:T(4,128)(2,1)}, bf16[2,1024,2048]{2,0,1:T(2,128)(2,1)}), (bf16[3,1024,512]{2,0,1:T(4,128)(2,1)}, bf16[2,1024,2048]{2,0,1:T(2,128)(2,1)})) %all-reduce.5.cloned.1.call-update) | async-done | bytes 11534352
  (327 shorter events, 222.5 us)
Async XLA Ops:
  7.2 106.4 %all-gather.16.cloned.1.call-start = ((), (), s32[]{:S(2)}) async-start(), calls=%async_computation.12 | async-start | bytes 3145728 | tf_op jit(solution)/shard_map/all_gather | solution.py:169
  7.2 79.3 %copy-start.76 = (s32[2,1,3]{2,1,0:T(1,128)S(1)}, s32[2,1,3]{2,1,0:T(1,128)}, u32[]{:S(2)}) copy-start(s32[2,1,3]{2,1,0:T(1,128)} %param.42) | copy-start | bytes 76
  9.3 79.1 %copy-start.66 = (f32[512]{0:T(512)}, f32[512]{0:T(512)S(1)}, u32[]{:S(2)}) copy-start(f32[512]{0:T(512)S(1)} %add_rsqrt_fusion.3) | copy-start | bytes 6148
  9.3 79.1 %copy-start.68 = (f32[512]{0:T(512)}, f32[512]{0:T(512)S(1)}, u32[]{:S(2)}) copy-start(f32[512]{0:T(512)S(1)} %add_rsqrt_fusion.1) | copy-start | bytes 6148
  84.4 76.6 %all-gather.18.cloned.1.call-start = ((), (), s32[]{:S(2)}) async-start(), calls=%async_computation.13 | async-start | bytes 3342336 | tf_op jit(solution)/shard_map/all_gather | solution.py:134
  85.1 114.8 %all-gather.20.cloned.1.call-start = ((), (), s32[]{:S(2)}) async-start(), calls=%async_computation.14 | async-start | bytes 1114112 | tf_op jit(solution)/shard_map/all_gather | solution.py:135
  85.9 148.1 %all-gather.28.cloned.1.call-start = ((), (), s32[]{:S(2)}) async-start(), calls=%async_computation.20 | async-start | bytes 3145728 | tf_op jit(solution)/shard_map/all_gather | solution.py:169
  86.5 185.8 %reduce-scatter.17.cloned.1.call-start = ((), (), s32[]{:S(2)}) async-start(), calls=%async_computation.15 | async-start | bytes 3145728 | tf_op jit(solution)/shard_map/reduce_scatter | solution.py:174
  88.4 159.3 %copy-start.25 = (pred[512,1024]{1,0:T(8,128)(4,1)}, pred[512,1024]{1,0:T(8,128)(4,1)S(1)}, u32[]{:S(2)}) copy-start(pred[512,1024]{1,0:T(8,128)(4,1)S(1)} %get-tuple-element.356) | copy-start | bytes 1572868
  88.4 173.6 %copy-start.22 = (pred[512,1024]{1,0:T(8,128)(4,1)}, pred[512,1024]{1,0:T(8,128)(4,1)S(1)}, u32[]{:S(2)}) copy-start(pred[512,1024]{1,0:T(8,128)(4,1)S(1)} %get-tuple-element.355) | copy-start | bytes 1572868
  89.8 84.9 %copy-start.19 = (pred[512,1024]{1,0:T(8,128)(4,1)}, pred[512,1024]{1,0:T(8,128)(4,1)S(1)}, u32[]{:S(2)}) copy-start(pred[512,1024]{1,0:T(8,128)(4,1)S(1)} %get-tuple-element.354) | copy-start | bytes 1572868
  89.9 99.6 %copy-start.17 = (pred[512,1024]{1,0:T(8,128)(4,1)}, pred[512,1024]{1,0:T(8,128)(4,1)S(1)}, u32[]{:S(2)}) copy-start(pred[512,1024]{1,0:T(8,128)(4,1)S(1)} %get-tuple-element.353) | copy-start | bytes 1572868
  203.8 100.6 %reduce-scatter.21.cloned.1.call-start = ((), (), s32[]{:S(2)}) async-start(), calls=%async_computation.21 | async-start | bytes 3145728 | tf_op jit(solution)/shard_map/reduce_scatter | solution.py:174
  272.2 70.1 %all-gather.30.cloned.1.call-start = ((), (), s32[]{:S(2)}) async-start(), calls=%async_computation.22 | async-start | bytes 3145728 | tf_op jit(solution)/shard_map/all_gather | solution.py:186
  309.0 110.4 %all-gather.24.cloned.1.call-start = ((), (), s32[]{:S(2)}) async-start(), calls=%async_computation.17 | async-start | bytes 8912896 | tf_op jit(solution)/shard_map/all_gather | solution.py:136
  309.7 143.2 %all-gather.38.cloned.1.call-start = ((), (), s32[]{:S(2)}) async-start(), calls=%async_computation.33 | async-start | bytes 3145728 | tf_op jit(solution)/shard_map/all_gather | solution.py:211
  312.9 192.6 %all-gather.26.cloned.1.call-start = ((), (), s32[]{:S(2)}) async-start(), calls=%async_computation.18 | async-start | bytes 4456448 | tf_op jit(solution)/shard_map/all_gather | solution.py:137
  313.5 225.8 %all-gather.22.cloned.1.call-start = ((), (), s32[]{:S(2)}) async-start(), calls=%async_computation.16 | async-start | bytes 3145728 | tf_op jit(solution)/shard_map/all_gather | solution.py:186
  314.2 259.6 %all-gather.36.cloned.1.call-start = ((), (), s32[]{:S(2)}) async-start(), calls=%async_computation.32 | async-start | bytes 3145728 | tf_op jit(solution)/shard_map/all_gather | solution.py:211
  314.8 301.1 %reduce-scatter.29.cloned.1.call-start = ((), (), s32[]{:S(2)}) async-start(), calls=%async_computation.27 | async-start | bytes 3145728 | tf_op jit(solution)/shard_map/reduce_scatter | solution.py:225
  532.0 110.5 %reduce-scatter.25.cloned.1.call-start = ((), (), s32[]{:S(2)}) async-start(), calls=%async_computation.24 | async-start | bytes 3145728 | tf_op jit(solution)/shard_map/reduce_scatter | solution.py:225
  602.4 40.1 %copy-start.5 = (bf16[2,512,1,1024]{3,1,2,0:T(8,128)(2,1)S(1)}, bf16[2,512,1,1024]{3,1,2,0:T(8,128)(2,1)}, u32[]{:S(2)}) copy-start(bf16[2,512,1,1024]{3,1,2,0:T(8,128)(2,1)} %param.41) | copy-start | bytes 6291460
  602.4 40.1 %copy-start.9 = (bf16[512,1,1024]{2,0,1:T(8,128)(2,1)S(1)}, bf16[512,1,1024]{2,0,1:T(8,128)(2,1)}, u32[]{:S(2)}) copy-start(bf16[512,1,1024]{2,0,1:T(8,128)(2,1)} %reduce-scatter.17.cloned.1.call-done) | copy-start | bytes 3145732
  602.5 40.1 %copy-start.40 = (f32[1,1024]{1,0:T(1,128)S(1)}, f32[1,1024]{1,0:T(1,128)}, u32[]{:S(2)}) copy-start(f32[1,1024]{1,0:T(1,128)} %get-tuple-element.345) | copy-start | bytes 12292
  602.5 40.1 %copy-start.61 = (f32[512]{0:T(512)S(1)}, f32[512]{0:T(512)}, u32[]{:S(2)}) copy-start(f32[512]{0:T(512)} %copy-done.60) | copy-start | bytes 6148
  602.5 40.1 %copy-start.64 = (f32[512]{0:T(512)S(1)}, f32[512]{0:T(512)}, u32[]{:S(2)}) copy-start(f32[512]{0:T(512)} %copy-done.63) | copy-start | bytes 6148
  602.5 74.0 %reduce-scatter.23.cloned.1.call-start = ((), (), s32[]{:S(2)}) async-start(), calls=%async_computation.23 | async-start | bytes 3145728 | tf_op jit(solution)/shard_map/reduce_scatter | solution.py:198
  615.8 98.8 %all-gather.34.cloned.1.call-start = ((), (), s32[]{:S(2)}) async-start(), calls=%async_computation.28 | async-start | bytes 3145728 | tf_op jit(solution)/shard_map/all_gather | solution.py:238
  646.5 35.0 %copy-start.47 = (f32[8,512]{1,0:T(8,128)S(1)}, f32[8,512]{1,0:T(8,128)}, u32[]{:S(2)}) copy-start(f32[8,512]{1,0:T(8,128)} %copy-done.46) | copy-start | bytes 49156
  646.5 35.0 %copy-start.57 = (f32[8,512]{1,0:T(8,128)S(1)}, f32[8,512]{1,0:T(8,128)}, u32[]{:S(2)}) copy-start(f32[8,512]{1,0:T(8,128)} %copy-done.56) | copy-start | bytes 49156
  646.5 35.0 %copy-start.49 = (f32[8,512]{1,0:T(8,128)S(1)}, f32[8,512]{1,0:T(8,128)}, u32[]{:S(2)}) copy-start(f32[8,512]{1,0:T(8,128)} %copy-done.48) | copy-start | bytes 49156
  646.5 35.0 %copy-start.59 = (f32[8,512]{1,0:T(8,128)S(1)}, f32[8,512]{1,0:T(8,128)}, u32[]{:S(2)}) copy-start(f32[8,512]{1,0:T(8,128)} %copy-done.58) | copy-start | bytes 49156
  681.3 110.2 %all-gather.32.cloned.1.call-start = ((), (), s32[]{:S(2)}) async-start(), calls=%async_computation.25 | async-start | bytes 3145728 | tf_op jit(solution)/shard_map/all_gather | solution.py:238
  681.9 36.0 %copy-start.15 = (bf16[1024,3,512]{0,2,1:T(8,128)(2,1)S(1)}, bf16[1024,3,512]{0,2,1:T(8,128)(2,1)}, u32[]{:S(2)}) copy-start(bf16[1024,3,512]{0,2,1:T(8,128)(2,1)} %copy-done.14) | copy-start | bytes 9437188
  681.9 278.7 %reduce-scatter.31.cloned.1.call-start = ((), (), s32[]{:S(2)}) async-start(), calls=%async_computation.29 | async-start | bytes 3145728 | tf_op jit(solution)/shard_map/reduce_scatter | solution.py:252
  856.5 120.8 %reduce-scatter.27.cloned.1.call-start = ((), (), s32[]{:S(2)}) async-start(), calls=%async_computation.26 | async-start | bytes 3145728 | tf_op jit(solution)/shard_map/reduce_scatter | solution.py:252
  945.4 133.8 %reduce-scatter.37.cloned.1.call-start = ((), (), s32[]{:S(2)}) async-start(), calls=%async_computation.34 | async-start | bytes 278528
  981.3 131.6 %reduce-scatter.35.cloned.1.call-start = ((), (), s32[]{:S(2)}) async-start(), calls=%async_computation.31 | async-start | bytes 4456448 | tf_op jit(solution)/shard_map/reduce_scatter | solution.py:278
  995.5 177.3 %reduce-scatter.33.cloned.1.call-start = ((), (), s32[]{:S(2)}) async-start(), calls=%async_computation.30 | async-start | bytes 1114112 | tf_op jit(solution)/shard_map/reduce_scatter | solution.py:272
  1001.3 205.4 %reduce-scatter.19.cloned.1.call-start = ((), (), s32[]{:S(2)}) async-start(), calls=%async_computation.19 | async-start | bytes 3145728 | tf_op jit(solution)/shard_map/reduce_scatter | solution.py:198
  1014.4 204.8 %reduce-scatter.39.cloned.1.call-start = ((), (), s32[]{:S(2)}) async-start(), calls=%async_computation.35 | async-start | bytes 49152
  1080.7 375.7 %all-reduce.5.cloned.1.call-start = ((), (), s32[]{:S(2)}) async-start(), calls=%async_computation.36 | async-start | bytes 25165824
  1097.9 76.5 %copy-start.41 = (f32[1,1024]{1,0:T(1,128)S(1)}, f32[1,1024]{1,0:T(1,128)}, u32[]{:S(2)}) copy-start(f32[1,1024]{1,0:T(1,128)} %get-tuple-element.345) | copy-start | bytes 12292
  1097.9 76.5 %copy-start.65 = (f32[512]{0:T(512)S(1)}, f32[512]{0:T(512)}, u32[]{:S(2)}) copy-start(f32[512]{0:T(512)} %copy-done.63) | copy-start | bytes 6148
  1097.9 76.5 %copy-start.73 = (f32[512]{0:T(512)S(1)}, f32[512]{0:T(512)}, u32[]{:S(2)}) copy-start(f32[512]{0:T(512)} %copy-done.72) | copy-start | bytes 6148
  1097.9 108.8 %copy-start.10 = (bf16[512,1,1024]{2,0,1:T(8,128)(2,1)S(1)}, bf16[512,1,1024]{2,0,1:T(8,128)(2,1)}, u32[]{:S(2)}) copy-start(bf16[512,1,1024]{2,0,1:T(8,128)(2,1)} %reduce-scatter.17.cloned.1.call-done) | copy-start | bytes 3145732
  1097.9 108.8 %copy-start.62 = (f32[512]{0:T(512)S(1)}, f32[512]{0:T(512)}, u32[]{:S(2)}) copy-start(f32[512]{0:T(512)} %copy-done.60) | copy-start | bytes 6148
  1097.9 108.8 %copy-start.71 = (f32[512]{0:T(512)S(1)}, f32[512]{0:T(512)}, u32[]{:S(2)}) copy-start(f32[512]{0:T(512)} %copy-done.70) | copy-start | bytes 6148
  (64 other events, 840.5 us)
Sparse Core Ops, SparseCore 0:
  84.5 28.9 all-gather.15
  115.7 45.1 all-gather.17
  163.1 36.7 all-gather.19
  201.9 32.0 all-gather.27
  236.6 31.8 reduce-scatter.16
  272.3 32.0 reduce-scatter.20
  309.1 33.0 all-gather.29
  344.4 74.9 all-gather.23
  421.5 31.3 all-gather.37
  454.9 50.5 all-gather.25
  507.6 31.6 all-gather.21
  540.7 33.1 all-gather.35
  576.1 31.8 reduce-scatter.28
  610.7 31.8 reduce-scatter.24
  644.6 31.8 reduce-scatter.22
  681.4 33.1 all-gather.33
  716.6 33.1 all-gather.31
  856.6 31.8 reduce-scatter.30
  945.4 31.8 reduce-scatter.26
  981.6 55.3 reduce-scatter.36
  1041.3 71.4 reduce-scatter.34
  1116.5 56.3 reduce-scatter.32
  1175.8 30.8 reduce-scatter.18
  1209.3 9.8 reduce-scatter.38
  1223.2 233.1 all-reduce.4
where the time goes:
time: 1480 us; the launch traced here: 1470 us
  waiting for transfers between devices  783 us (53%)
  matrix products  400 us (27%)
  other arithmetic  121 us (8%)
  local copies, waits for them, and re-layouts  76.2 us (5%)
  blocking collectives  69.7 us (5%)
  between operations  16.1 us (1%)
    unnamed x28, waiting for transfers between devices  240 us
    all_gather x1, waiting for transfers between devices, fetch_weights(): lax.all_gather(w_gate_up, 'fsdp', axis=1, tiled=True)  77.1 us
    all_gather x1, blocking collectives, local(): lax.all_gather(jnp.stack([gain_attn, gain_mlp]), ('fsdp', 'tensor'), axis...  69.7 us
    convert_element_type x2, other arithmetic, attend_backward(): d_scores = (attn_probs * (d_probs - row_dot)).astype(jnp.bfloat16)  58.6 us
    reduce_scatter x2, waiting for transfers between devices, local(): lax.psum_scatter(jnp.einsum('meg,gp->mep', down_rows_now, down_weight_ful...  58.2 us
    reduce_scatter x1, waiting for transfers between devices, local(): lax.psum_scatter(acc_out.astype(jnp.bfloat16), 'fsdp', scatter_dimension=...  58.2 us
    all_gather x2, waiting for transfers between devices, local(): piece_rows = lax.all_gather(normed, 'tensor', axis=0, tiled=True)  53.6 us
    all_gather x1, waiting for transfers between devices, fetch_weights(): lax.all_gather(w_down, 'fsdp', axis=1, tiled=True)  52.6 us
  transfers between devices with their start and end apart: 25, of which 19 were waited for; matrix products, arithmetic and copies ran while one was open for 34% of the time, Pallas kernels for 0%

commit v1 on v0

--- a/solution.py
+++ b/solution.py
@@ -1,6 +1,8 @@
 import jax
 import jax.numpy as jnp
 from jax import lax
+from jax.experimental import pallas as pl
+from jax.experimental.pallas import tpu as pltpu
 from jax.sharding import PartitionSpec as P
 
 D = 1024
@@ -292,9 +294,742 @@
     )
 
 
+BF = jnp.bfloat16
+F32 = jnp.float32
+TILE = 256
+
+
+def dot_f32(a, b, ca, cb):
+    return lax.dot_general(a, b, (((ca,), (cb,)), ((), ())), preferred_element_type=F32)
+
+
+def call(body, name, ids, ins, in_specs, outs, out_specs, grid, scratch=(), flops=0):
+    moved = sum(a.size * a.dtype.itemsize for a in ins) + sum(
+        o.size * o.dtype.itemsize for o in outs
+    )
+    return pl.pallas_call(
+        body,
+        name=name,
+        out_shape=outs,
+        grid_spec=pltpu.PrefetchScalarGridSpec(
+            num_scalar_prefetch=1,
+            grid=grid,
+            in_specs=in_specs,
+            out_specs=out_specs,
+            scratch_shapes=list(scratch),
+        ),
+        compiler_params=pltpu.CompilerParams(
+            dimension_semantics=("arbitrary",) * len(grid), vmem_limit_bytes=56 * 2**20
+        ),
+        cost_estimate=pl.CostEstimate(flops=flops, bytes_accessed=moved, transcendentals=0),
+    )(ids, *ins)
+
+
+def shape(dims, dtype):
+    return jax.ShapeDtypeStruct(dims, dtype)
+
+
+def whole(dims):
+    zeros = (0,) * len(dims)
+    return pl.BlockSpec(dims, lambda *_: zeros)
+
+
+def store_transposed(ids, value, blocks_ref, out_ref):
+    count, height = blocks_ref.shape[0], blocks_ref.shape[1]
+    step = 128 // height
+    for c in range(value.shape[1] // 128):
+        part = value[:, c * 128 : (c + 1) * 128]
+        blocks_ref[c * step : (c + 1) * step] = part.T.reshape(step, height, part.shape[0])
+    for core in range(2):
+        for pair in range(count // 2):
+            source = 2 * (pair ^ ids[1]) + (core ^ ids[2])
+            out_ref[core * (count // 2) + pair] = blocks_ref[source]
+
+
+def rows_of(ref):
+    block = ref[...]
+    return block.reshape(block.shape[0] * block.shape[2], block.shape[3])
+
+
+def make_qkv(ids, x, gain, packed, fsdp, half):
+    length, width = x.shape
+    height = width // fsdp
+
+    def body(ids, x_ref, gain_ref, w_ref, qkv_ref, xt_ref, xn_ref, blocks_ref):
+        @pl.when((pl.program_id(0) == 0) & (pl.program_id(1) == 0))
+        def _():
+            for r in range(0, length, TILE):
+                rows = x_ref[r : r + TILE].astype(F32)
+                xn_ref[r : r + TILE] = (rows * rms_scale(rows) * gain_ref[...]).astype(BF)
+            store_transposed(ids, xn_ref[...], blocks_ref, xt_ref)
+
+        factor = jnp.where(pl.program_id(0) == 0, HEAD_DIM ** (-0.5), 1.0)
+        w = rows_of(w_ref)
+        for r in range(0, length, TILE):
+            made = dot_f32(xn_ref[r : r + TILE], w, 1, 0)
+            qkv_ref[0, r : r + TILE] = (made * factor).astype(BF)
+
+    return call(
+        body,
+        "qkv",
+        ids,
+        (x, gain, packed),
+        [
+            whole((length, width)),
+            whole((1, width)),
+            pl.BlockSpec((fsdp, 1, height, half), lambda c, t, ids: (0, t, c, 0)),
+        ],
+        (shape((3, length, width), BF), shape((fsdp, height, length), BF)),
+        [
+            pl.BlockSpec((1, length, half), lambda c, t, ids: (c, 0, t)),
+            whole((fsdp, height, length)),
+        ],
+        (3, width // half),
+        (pltpu.VMEM((length, width), BF), pltpu.VMEM((fsdp, height, length), BF)),
+        flops=2 * length * width * 3 * width,
+    )
+
+
+def lane_mask(values, head):
+    lanes = lax.broadcasted_iota(jnp.int32, values.shape, 1)
+    return jnp.where(lanes // HEAD_DIM == head, values, jnp.zeros_like(values))
+
+
+def attend(ids, qkv):
+    length, width = qkv.shape[1:]
+    tiles = length // TILE
+    pair = 2 * HEAD_DIM
+
+    def body(ids, q_ref, k_ref, v_ref, o_ref, ot_ref, e_ref, inv_ref, bias_ref, s_ref):
+        @pl.when(pl.program_id(0) == 0)
+        def _():
+            for i in range(tiles):
+                keys = i * TILE + lax.broadcasted_iota(jnp.int32, (2 * TILE, TILE), 0)
+                rows = i * TILE + lax.broadcasted_iota(jnp.int32, (2 * TILE, TILE), 1)
+                seen = keys <= rows
+                for p in range(3):
+                    start = ids[3 + p]
+                    inside = (keys >= start) & (keys < start + PIECE)
+                    inside &= (rows >= start) & (rows < start + PIECE)
+                    seen |= inside
+                bias_ref[i] = jnp.where(seen, 0.0, masked_score)
+
+        k = k_ref[0]
+        vt = v_ref[0].T
+        for i in range(tiles):
+            used = min(i + 2, tiles)
+            q_rows = q_ref[0, i * TILE : (i + 1) * TILE]
+            parts = []
+            for head in range(2):
+                slot = (2 * i + head) % 2
+                q_head = lane_mask(q_rows, head)
+                top = None
+                for j in range(used):
+                    s = dot_f32(k[j * TILE : (j + 1) * TILE], q_head, 1, 1)
+                    if j >= i:
+                        s = s + bias_ref[i, (j - i) * TILE : (j - i + 1) * TILE]
+                    s_ref[slot, j] = s
+                    now = jnp.max(s.reshape(TILE // 8, 8, TILE), axis=0)
+                    top = now if top is None else jnp.maximum(top, now)
+                top = jnp.max(top, axis=0, keepdims=True)
+                total = None
+                out = None
+                for j in range(used):
+                    e = jnp.exp(s_ref[slot, j] - top)
+                    now = jnp.sum(e.reshape(TILE // 8, 8, TILE), axis=0)
+                    total = now if total is None else total + now
+                    low = e.astype(BF)
+                    e_ref[head, j * TILE : (j + 1) * TILE, i * TILE : (i + 1) * TILE] = low
+                    now = dot_f32(
+                        vt[head * HEAD_DIM : (head + 1) * HEAD_DIM, j * TILE : (j + 1) * TILE],
+                        low,
+                        1,
+                        0,
+                    )
+                    out = now if out is None else out + now
+                inv = 1.0 / jnp.sum(total, axis=0, keepdims=True)
+                inv_ref[0, head : head + 1, i * TILE : (i + 1) * TILE] = inv
+                parts.append(out * inv)
+            both = jnp.concatenate(parts, axis=0)
+            ot_ref[:, i * TILE : (i + 1) * TILE] = both.astype(BF)
+            o_ref[i * TILE : (i + 1) * TILE] = both.T.astype(BF)
+
+    spec = [
+        pl.BlockSpec((1, length, pair), lambda p, ids, c=c: (c, 0, p)) for c in range(3)
+    ]
+    heads = width // HEAD_DIM
+    return call(
+        body,
+        "attend",
+        ids,
+        (qkv, qkv, qkv),
+        spec,
+        (
+            shape((length, width), BF),
+            shape((width, length), BF),
+            shape((heads, length, length), BF),
+            shape((heads // 2, 2, length), F32),
+        ),
+        [
+            pl.BlockSpec((length, pair), lambda p, ids: (0, p)),
+            pl.BlockSpec((pair, length), lambda p, ids: (p, 0)),
+            pl.BlockSpec((2, length, length), lambda p, ids: (p, 0, 0)),
+            pl.BlockSpec((1, 2, length), lambda p, ids: (p, 0, 0)),
+        ],
+        (heads // 2,),
+        (
+            pltpu.VMEM((tiles, 2 * TILE, TILE), F32),
+            pltpu.VMEM((2, tiles, TILE, TILE), F32),
+        ),
+        flops=4 * length * length * width,
+    )
+
+
+def attend_back(ids, qkv, d_heads, ot, e, inv):
+    length, width = qkv.shape[1:]
+    tiles = length // TILE
+    pair = 2 * HEAD_DIM
+
+    def body(ids, q_ref, k_ref, v_ref, d_ref, ot_ref, e_ref, inv_ref, out_ref, ds_ref, dq_ref):
+        k = k_ref[0]
+        v = v_ref[0]
+        kt = k.T
+        dt = d_ref[...].astype(F32).T
+        q_heads = []
+        d_scaled = []
+        deltas = []
+        for head in range(2):
+            span = slice(head * HEAD_DIM, (head + 1) * HEAD_DIM)
+            inv_row = inv_ref[0, head : head + 1]
+            mine = dt[span] * inv_row
+            deltas.append(jnp.sum(mine * ot_ref[span].astype(F32), axis=0, keepdims=True))
+            blank = jnp.zeros((HEAD_DIM, length), BF)
+            mine = mine.astype(BF)
+            d_scaled.append(
+                jnp.concatenate([mine, blank] if head == 0 else [blank, mine], axis=0)
+            )
+            q_heads.append(lane_mask(q_ref[0], head))
+        dq_ref[...] = jnp.zeros_like(dq_ref)
+        for j in range(tiles):
+            keys = slice(j * TILE, (j + 1) * TILE)
+            first = max(j - 1, 0) * TILE
+            d_key = None
+            d_value = None
+            for head in range(2):
+                for r in range(first, length, TILE):
+                    cols = slice(r, r + TILE)
+                    dp = dot_f32(v[keys], d_scaled[head][:, cols], 1, 0)
+                    weights = e_ref[head, keys, cols].astype(F32)
+                    ds_ref[j % 2, head, :, cols] = (
+                        weights * (dp - deltas[head][:, cols])
+                    ).astype(BF)
+                ds = ds_ref[j % 2, head, :, first:length]
+                now = dot_f32(ds, q_heads[head][first:length], 1, 0)
+                d_key = now if d_key is None else d_key + now
+                now = dot_f32(e_ref[head, keys, first:length], d_scaled[head][:, first:length], 1, 1)
+                d_value = now if d_value is None else d_value + now
+                rows = slice(head * HEAD_DIM, (head + 1) * HEAD_DIM)
+                dq_ref[rows, first:length] += dot_f32(kt[rows, keys], ds, 1, 0)
+            out_ref[1, keys] = d_key.astype(BF)
+            out_ref[2, keys] = d_value.astype(BF)
+        out_ref[0] = (dq_ref[...] * HEAD_DIM ** (-0.5)).T.astype(BF)
+
+    spec = [
+        pl.BlockSpec((1, length, pair), lambda p, ids, c=c: (c, 0, p)) for c in range(3)
+    ]
+    heads = width // HEAD_DIM
+    return call(
+        body,
+        "attend_back",
+        ids,
+        (qkv, qkv, qkv, d_heads, ot, e, inv),
+        spec
+        + [
+            pl.BlockSpec((length, pair), lambda p, ids: (0, p)),
+            pl.BlockSpec((pair, length), lambda p, ids: (p, 0)),
+            pl.BlockSpec((2, length, length), lambda p, ids: (p, 0, 0)),
+            pl.BlockSpec((1, 2, length), lambda p, ids: (p, 0, 0)),
+        ],
+        (shape((3, length, width), BF),),
+        [pl.BlockSpec((3, length, pair), lambda p, ids: (0, 0, p))],
+        (heads // 2,),
+        (pltpu.VMEM((2, 2, TILE, length), BF), pltpu.VMEM((pair, length), F32)),
+        flops=8 * length * length * width,
+    )[0]
+
+
+def out_project(ids, attended, packed, x, gain, fsdp, half):
+    length, width = x.shape
+    height = width // fsdp
+    parts = width // half
+
+    def body(ids, a_ref, w_ref, x_ref, gain_ref, hidden_ref, hn_ref, ht_ref, blocks_ref):
+        for r in range(0, length, TILE):
+            total = x_ref[r : r + TILE].astype(F32)
+            for t in range(parts):
+                w = w_ref[:, t].reshape(width, half)
+                total += dot_f32(a_ref[r : r + TILE, t * half : (t + 1) * half], w, 1, 1)
+            hidden_ref[r : r + TILE] = total
+            hn_ref[r : r + TILE] = (total * rms_scale(total) * gain_ref[...]).astype(BF)
+        store_transposed(ids, hn_ref[...], blocks_ref, ht_ref)
+
+    return call(
+        body,
+        "out_project",
+        ids,
+        (attended, packed, x, gain),
+        [
+            whole((length, width)),
+            pl.BlockSpec((fsdp, parts, height, half), lambda g, ids: (0, 0, 3, 0)),
+            whole((length, width)),
+            whole((1, width)),
+        ],
+        (
+            shape((length, width), F32),
+            shape((length, width), BF),
+            shape((fsdp, height, length), BF),
+        ),
+        [whole((length, width)), whole((length, width)), whole((fsdp, height, length))],
+        (1,),
+        (pltpu.VMEM((fsdp, height, length), BF),),
+        flops=2 * length * width * width,
+    )
+
+
+def feed_forward(ids, hn, grad, packed, fsdp):
+    length, width = hn.shape
+    height = width // fsdp
+    half = packed.shape[3]
+    parts = packed.shape[1]
+    tile = 256
+    per = half // tile
+
+    def body(ids, hn_ref, g_ref, w_ref, mixed_ref, d_ref, gt_ref, blocks_ref):
+        @pl.when((pl.program_id(0) == 0) & (pl.program_id(1) == 0))
+        def _():
+            store_transposed(ids, g_ref[...], blocks_ref, gt_ref)
+
+        w = w_ref[:, 0]
+        w_gate, w_up, w_down = [
+            w[:, c * height : (c + 1) * height].reshape(width, tile) for c in range(3)
+        ]
+        for r in range(0, length, TILE):
+            rows = hn_ref[r : r + TILE]
+            gate = dot_f32(rows, w_gate, 1, 0)
+            up = dot_f32(rows, w_up, 1, 0)
+            d_mixed = dot_f32(g_ref[r : r + TILE], w_down, 1, 0)
+            sig = jax.nn.sigmoid(gate)
+            act = gate * sig
+            mixed_ref[r : r + TILE] = (act * up).astype(BF)
+            d_ref[0, r : r + TILE] = (d_mixed * up * sig * (1.0 + gate * (1.0 - sig))).astype(BF)
+            d_ref[1, r : r + TILE] = (d_mixed * act).astype(BF)
+
+    return call(
+        body,
+        "feed_forward",
+        ids,
+        (hn, grad, packed),
+        [
+            whole((length, width)),
+            whole((length, width)),
+            pl.BlockSpec((fsdp, 1, 3 * height, tile), lambda t, n, ids: (0, t, 0, n)),
+        ],
+        (
+            shape((length, parts * half), BF),
+            shape((2, length, parts * half), BF),
+            shape((fsdp, height, length), BF),
+        ),
+        [
+            pl.BlockSpec((length, tile), lambda t, n, ids: (0, t * per + n)),
+            pl.BlockSpec((2, length, tile), lambda t, n, ids: (0, 0, t * per + n)),
+            whole((fsdp, height, length)),
+        ],
+        (parts, per),
+        (pltpu.VMEM((fsdp, height, length), BF),),
+        flops=6 * length * width * parts * half,
+    )
+
+
+def feed_forward_out(ids, mixed, packed, hidden, fsdp):
+    length, width = hidden.shape
+    height = width // fsdp
+    half = packed.shape[3]
+    parts = packed.shape[1]
+    tile = 512
+    per = half // tile
+    kept = length // parts
+
+    def body(ids, m_ref, w_ref, hidden_ref, keep_ref, send_ref, acc_ref):
+        first = (pl.program_id(0) == 0) & (pl.program_id(1) == 0)
+        last = (pl.program_id(0) == parts - 1) & (pl.program_id(1) == per - 1)
+
+        @pl.when(first)
+        def _():
+            acc_ref[...] = hidden_ref[...]
+
+        w = rows_of(w_ref)
+        for r in range(0, length, TILE):
+            acc_ref[r : r + TILE] += dot_f32(m_ref[r : r + TILE], w, 1, 1)
+
+        @pl.when(last)
+        def _():
+            keep_ref[...] = acc_ref[pl.ds(pl.multiple_of(ids[0] * kept, kept), kept)].astype(BF)
+            send_ref[...] = acc_ref[
+                pl.ds(pl.multiple_of((1 - ids[0]) * kept, kept), kept)
+            ].astype(BF)
+
+    return call(
+        body,
+        "feed_forward_out",
+        ids,
+        (mixed, packed, hidden),
+        [
+            pl.BlockSpec((length, tile), lambda t, n, ids: (0, t * per + n)),
+            pl.BlockSpec((fsdp, 1, height, tile), lambda t, n, ids: (0, t, 2, n)),
+            whole((length, width)),
+        ],
+        (shape((kept, width), BF), shape((kept, width), BF)),
+        [whole((kept, width)), whole((kept, width))],
+        (parts, per),
+        (pltpu.VMEM((length, width), F32),),
+        flops=2 * length * width * parts * half,
+    )
+
+
+def weight_grad(ids, name, left, right, index, parts, tile, extra=None):
+    fsdp, height, length = left.shape
+    half = right.shape[2] // parts
+    tile = min(tile, half)
+    per = half // tile
+    rows = height if extra is None else height + 8
+    hop = fsdp // 2
+
+    def body(ids, l_ref, r_ref, *refs):
+        right_tile = r_ref[0]
+        outs = refs[-2:]
+        for b in range(0, fsdp, 4):
+            block = l_ref[b : b + 4].reshape(4 * height, length)
+            made = dot_f32(block, right_tile, 1, 0).astype(BF).reshape(4, height, tile)
+            out = outs[b // hop]
+            out[0, b % hop : b % hop + 4, :height] = made
+        if extra is not None:
+            for core in range(2):
+                for pair in range(hop):
+                    source = 2 * (pair ^ ids[1]) + (core ^ ids[2])
+                    outs[core][0, pair, height:] = refs[0][source, 0]
+
+    ins = [left, right]
+    specs = [
+        whole((fsdp, height, length)),
+        pl.BlockSpec((1, length, tile), lambda t, n, ids: (index, 0, t * per + n)),
+    ]
+    if extra is not None:
+        ins.append(extra)
+        specs.append(pl.BlockSpec((fsdp, 1, 8, tile), lambda t, n, ids: (0, t, 0, n)))
+    out_spec = pl.BlockSpec((1, hop, rows, tile), lambda t, n, ids: (t ^ ids[0], 0, 0, n))
+    return call(
+        body,
+        name,
+        ids,
+        tuple(ins),
+        specs,
+        (shape((parts, hop, rows, half), BF),) * 2,
+        [out_spec, out_spec],
+        (parts, per),
+        flops=2 * length * fsdp * height * parts * half,
+    )
+
+
+def feed_forward_back(ids, d_gate_up, packed, hidden, grad, gain, fsdp):
+    length, width = hidden.shape
+    height = width // fsdp
+    half = packed.shape[3]
+    parts = packed.shape[1]
+    tile = 512
+    per = half // tile
+
+    def body(
+        ids, d_ref, w_ref, hidden_ref, g_ref, gain_ref, dh_ref, low_ref, lt_ref, gg_ref, acc_ref, blocks_ref
+    ):
+        first = (pl.program_id(0) == 0) & (pl.program_id(1) == 0)
+        last = (pl.program_id(0) == parts - 1) & (pl.program_id(1) == per - 1)
+
+        @pl.when(first)
+        def _():
+            acc_ref[...] = jnp.zeros_like(acc_ref)
+
+        w = w_ref[:, 0]
+        w_gate, w_up = [w[:, c * height : (c + 1) * height].reshape(width, tile) for c in range(2)]
+        for r in range(0, length, TILE):
+            acc_ref[r : r + TILE] += dot_f32(d_ref[0, r : r + TILE], w_gate, 1, 1) + dot_f32(
+                d_ref[1, r : r + TILE], w_up, 1, 1
+            )
+
+        @pl.when(last)
+        def _():
+            total = jnp.zeros((1, width), F32)
+            for r in range(0, length, TILE):
+                rows = hidden_ref[r : r + TILE]
+                scale = rms_scale(rows)
+                normed = rows * scale
+                d_normed = acc_ref[r : r + TILE]
+                total += jnp.sum(d_normed * normed, axis=0, keepdims=True)
+                dh = g_ref[r : r + TILE].astype(F32) + norm_backward_pass(
+                    d_normed, normed, scale, gain_ref[...]
+                )
+                dh_ref[r : r + TILE] = dh
+                low_ref[r : r + TILE] = dh.astype(BF)
+            gg_ref[...] = total
+            store_transposed(ids, low_ref[...], blocks_ref, lt_ref)
+
+    return call(
+        body,
+        "feed_forward_back",
+        ids,
+        (d_gate_up, packed, hidden, grad, gain),
+        [
+            pl.BlockSpec((2, length, tile), lambda t, n, ids: (0, 0, t * per + n)),
+            pl.BlockSpec((fsdp, 1, 2 * height, tile), lambda t, n, ids: (0, t, 0, n)),
+            whole((length, width)),
+            whole((length, width)),
+            whole((1, width)),
+        ],
+        (
+            shape((length, width), F32),
+            shape((length, width), BF),
+            shape((fsdp, height, length), BF),
+            shape((1, width), F32),
+        ),
+        [
+            whole((length, width)),
+            whole((length, width)),
+            whole((fsdp, height, length)),
+            whole((1, width)),
+        ],
+        (parts, per),
+        (pltpu.VMEM((length, width), F32), pltpu.VMEM((fsdp, height, length), BF)),
+        flops=4 * length * width * parts * half,
+    )
+
+
+def out_project_back(ids, d_attn, packed, fsdp):
+    length, width = d_attn.shape
+    height = width // fsdp
+    half = packed.shape[3]
+    parts = packed.shape[1]
+
+    def body(ids, d_ref, w_ref, out_ref):
+        w = rows_of(w_ref)
+        for r in range(0, length, TILE):
+            out_ref[r : r + TILE] = dot_f32(d_ref[r : r + TILE], w, 1, 0).astype(BF)
+
+    return call(
+        body,
+        "out_project_back",
+        ids,
+        (d_attn, packed),
+        [
+            whole((length, width)),
+            pl.BlockSpec((fsdp, 1, height, half), lambda t, ids: (0, t, 3, 0)),
+        ],
+        (shape((length, width), BF),),
+        [pl.BlockSpec((length, half), lambda t, ids: (0, t))],
+        (parts,),
+        flops=2 * length * width * width,
+    )[0]
+
+
+def qkv_back(ids, d_qkv, packed, x, dh, gain, fsdp):
+    length, width = x.shape
+    height = width // fsdp
+    half = packed.shape[3]
+    parts = packed.shape[1]
+    kept = length // parts
+
+    def body(ids, d_ref, w_ref, x_ref, dh_ref, gain_ref, keep_ref, send_ref, gg_ref, acc_ref):
+        first = (pl.program_id(0) == 0) & (pl.program_id(1) == 0)
+        last = (pl.program_id(0) == 2) & (pl.program_id(1) == parts - 1)
+
+        @pl.when(first)
+        def _():
+            acc_ref[...] = jnp.zeros_like(acc_ref)
+
+        w = rows_of(w_ref)
+        for r in range(0, length, TILE):
+            acc_ref[r : r + TILE] += dot_f32(d_ref[0, r : r + TILE], w, 1, 1)
+
+        @pl.when(last)
+        def _():
+            total = jnp.zeros((1, width), F32)
+            for r in range(0, length, TILE):
+                rows = x_ref[r : r + TILE].astype(F32)
+                scale = rms_scale(rows)
+                normed = rows * scale
+                d_normed = acc_ref[r : r + TILE]
+                total += jnp.sum(d_normed * normed, axis=0, keepdims=True)
+                acc_ref[r : r + TILE] = dh_ref[r : r + TILE] + norm_backward_pass(
+                    d_normed, normed, scale, gain_ref[...]
+                )
+            gg_ref[...] = total
+            keep_ref[...] = acc_ref[pl.ds(pl.multiple_of(ids[0] * kept, kept), kept)]
+            send_ref[...] = acc_ref[
+                pl.ds(pl.multiple_of((1 - ids[0]) * kept, kept), kept)
+            ].astype(BF)
+
+    return call(
+        body,
+        "qkv_back",
+        ids,
+        (d_qkv, packed, x, dh, gain),
+        [
+            pl.BlockSpec((1, length, half), lambda c, t, ids: (c, 0, t)),
+            pl.BlockSpec((fsdp, 1, height, half), lambda c, t, ids: (0, t, c, 0)),
+            whole((length, width)),
+            whole((length, width)),
+            whole((1, width)),
+        ],
+        (shape((kept, width), F32), shape((kept, width), BF), shape((1, width), F32)),
+        [whole((kept, width)), whole((kept, width)), whole((1, width))],
+        (3, parts),
+        (pltpu.VMEM((length, width), F32),),
+        flops=6 * length * width * width,
+    )
+
+
+def swap(value, bit):
+    if bit == 0:
+        return lax.ppermute(value, "tensor", [(0, 1), (1, 0)])
+    return lax.ppermute(
+        value, "fsdp", [(i, i ^ bit) for i in range(lax.axis_size("fsdp"))]
+    )
+
+
+def scatter_sum(keep, send, order):
+    bits = keep.shape[1].bit_length() - 1
+    dims = (2,) * (bits + 1)
+    got = swap(send, 1)
+    total = keep.reshape(dims + keep.shape[2:]).astype(F32) + got.reshape(
+        dims + keep.shape[2:]
+    ).astype(F32)
+    axes = [0] + [2 << b for b in reversed(range(bits))]
+    for bit in order:
+        at = axes.index(bit)
+        low = total.astype(BF)
+        mine = lax.index_in_dim(low, 0, at, keepdims=False)
+        other = lax.index_in_dim(low, 1, at, keepdims=False)
+        axes.remove(bit)
+        total = mine.astype(F32) + swap(other, bit).astype(F32)
+    return total
+
+
+def three_parts(values):
+    high = values.astype(BF)
+    rest = values - high.astype(F32)
+    middle = rest.astype(BF)
+    return jnp.stack([high, middle, (rest - middle.astype(F32)).astype(BF)], -1)
+
+
+def local_sequence(
+    tokens, piece_starts, gain_attn, w_qkv, w_out, gain_mlp, w_gate_up, w_down, out_grad
+):
+    fsdp = lax.axis_size("fsdp")
+    parts = lax.axis_size("tensor")
+    me_f = lax.axis_index("fsdp")
+    me_t = lax.axis_index("tensor")
+    local_rows = tokens.shape[1]
+    height = w_qkv.shape[1]
+    half = w_qkv.shape[2]
+    share = gain_attn.shape[0]
+    order_down, order_gate, order_up = (2, 0, 4, 8), (0, 4, 8, 2), (4, 8, 2, 0)
+
+    starts = lax.dynamic_index_in_dim(piece_starts, me_t, 0, keepdims=False)[0]
+    ids = jnp.concatenate([jnp.stack([me_t, me_f // 2, me_f % 2]).astype(jnp.int32), starts])
+
+    def sequence_of(rows):
+        rows = rows.reshape(parts, local_rows, D)
+        mine = lax.dynamic_index_in_dim(rows, me_t, 0, keepdims=False)
+        got = swap(lax.dynamic_index_in_dim(rows, 1 - me_t, 0, keepdims=False), 0)
+        return jnp.where(
+            me_t == 0, jnp.concatenate([mine, got]), jnp.concatenate([got, mine])
+        )
+
+    def micro_rows(keep, got):
+        both = jnp.where(me_t == 0, jnp.stack([keep, got]), jnp.stack([got, keep]))
+        return both.reshape(tokens.shape)
+
+    gains = three_parts(jnp.stack([gain_attn, gain_mlp])).reshape(1, -1)
+    gains = jnp.pad(gains, ((0, 7), (0, half - gains.shape[1])))
+    mine = jnp.concatenate([w_qkv.reshape(3 * height, half), w_out.T, gains])
+    attn_w = lax.all_gather(mine, ("fsdp", "tensor"), axis=0, tiled=False)
+    attn_w = attn_w.reshape(fsdp, parts, 4 * height + 8, half)
+    gains = attn_w[:, :, 4 * height, : 6 * share].reshape(fsdp * parts, 2, share, 3)
+    gains = jnp.sum(gains.astype(F32), axis=3)
+    gain_one, gain_two = [gains[:, i].reshape(1, D) for i in range(2)]
+
+    mine = jnp.concatenate([w_gate_up.reshape(2 * height, -1), w_down.T])
+    ff_w = lax.all_gather(mine, ("fsdp", "tensor"), axis=0, tiled=False)
+    ff_w = ff_w.reshape(fsdp, parts, 3 * height, -1)
+
+    x = sequence_of(tokens)
+    grad = sequence_of(out_grad)
+
+    qkv, xt = make_qkv(ids, x, gain_one, attn_w, fsdp, half)
+    attended, ot, e, inv = attend(ids, qkv)
+    hidden, hn, ht = out_project(ids, attended, attn_w, x, gain_two, fsdp, half)
+    mixed, d_gate_up, gt = feed_forward(ids, hn, grad, ff_w, fsdp)
+
+    down = weight_grad(ids, "grad_down", gt, mixed[None], 0, parts, 512)
+    down = scatter_sum(*down, order_down)
+    gate = weight_grad(ids, "grad_gate", ht, d_gate_up, 0, parts, 512)
+    gate = scatter_sum(*gate, order_gate)
+    up = weight_grad(ids, "grad_up", ht, d_gate_up, 1, parts, 512)
+    up = scatter_sum(*up, order_up)
+
+    dh, d_attn, dt, gain_two_grad = feed_forward_back(
+        ids, d_gate_up, ff_w, hidden, grad, gain_two, fsdp
+    )
+    d_attended = out_project_back(ids, d_attn, attn_w, fsdp)
+    out = weight_grad(ids, "grad_out", dt, attended[None], 0, parts, 512)
+    out = scatter_sum(*out, order_down)
+    keep, send = feed_forward_out(ids, mixed, ff_w, hidden, fsdp)
+    layer_out = micro_rows(keep, swap(send, 0))
+
+    d_qkv = attend_back(ids, qkv, d_attended, ot, e, inv)
+    keep, send, gain_one_grad = qkv_back(ids, d_qkv, attn_w, x, dh, gain_one, fsdp)
+    input_grad = micro_rows(keep, swap(send, 0).astype(F32))
+
+    gain_grads = jnp.stack([gain_one_grad[0], gain_two_grad[0]]).reshape(2, fsdp, parts, share)
+    gain_grads = gain_grads.transpose(1, 2, 0, 3).reshape(fsdp, parts, 1, 2 * share)
+    gain_grads = jnp.pad(gain_grads, ((0, 0), (0, 0), (0, 7), (0, half - 2 * share))).astype(BF)
+    three = []
+    for c, order in enumerate((order_down, order_gate, order_up)):
+        pieces = weight_grad(
+            ids, "grad_qkv", xt, d_qkv, c, parts, 512, gain_grads if c == 2 else None
+        )
+        three.append(scatter_sum(*pieces, order))
+    gain_shares = three[2][height, : 2 * share].reshape(2, share)
+    three[2] = three[2][:height]
+    return (
+        layer_out,
+        input_grad,
+        gain_shares[0],
+        jnp.stack(three),
+        out.T,
+        gain_shares[1],
+        jnp.stack([gate, up]),
+        down.T,
+    )
+
+
+def local_any(tokens, *rest):
+    if lax.axis_size("tensor") == tokens.shape[0] == 2 and tokens.shape[2] == 1:
+        return local_sequence(tokens, *rest)
+    return local(tokens, *rest)
+
+
 def solution(mesh):
     return jax.shard_map(
-        local,
+        local_any,
         mesh=mesh,
         in_specs=(
             P(None, "tensor", "fsdp", None),

time: 1480 us -> 732 us (0.49)
  waiting for transfers between devices: 783 us -> 339 us
  matrix products: 400 us -> 0 us
  Pallas kernels: 0 us -> 275 us
  other arithmetic: 121 us -> 39.2 us
  blocking collectives: 69.7 us -> 0 us
  local copies, waits for them, and re-layouts: 76.2 us -> 21.2 us
  starting transfers between devices: 1.78 us -> 36.3 us
    dot_general x48 -> x0, matrix products: 400 us -> none  [the longest x4 51.1 us: attend_backward(): jnp.einsum('qhd,khd->hqk', block_d, values_all, preferred_element_type=jn...]
    pallas_call x0 -> x16, Pallas kernels: none -> 275 us  [call(): pl.pallas_call(body, name=name, out_shape=outs, grid_spec=pltpu.PrefetchS...]
    unnamed x28 -> x2, waiting for transfers between devices: 240 us -> 0.03 us
    ppermute x0 -> x39, waiting for transfers between devices: none -> 230 us  [the longest x28 141 us: swap(): lax.ppermute(value, 'fsdp', [(i, i ^ bit) for i in range(lax.axis_size('f...]
    all_gather x12 -> x2, waiting for transfers between devices: 338 us -> 110 us  [the longest x1 89.2 us: local_sequence(): ff_w = lax.all_gather(mine, ('fsdp', 'tensor'), axis=0, tiled=False)]
    reduce_scatter x10 -> x0, waiting for transfers between devices: 205 us -> none  [the longest x2 58.2 us: local(): lax.psum_scatter(jnp.einsum('meg,gp->mep', down_rows_now, down_weight_ful...]
    all_gather x1 -> x0, blocking collectives: 69.7 us -> none  [local(): lax.all_gather(jnp.stack([gain_attn, gain_mlp]), ('fsdp', 'tensor'), axis...]
    convert_element_type x10 -> x31, other arithmetic: 74.8 us -> 21.1 us  [the longest x28 18.7 us: scatter_sum(): low = total.astype(BF)]
  transfers between devices with their start and end apart: 25 -> 41, of which waited for: 19 -> 28; matrix products, arithmetic and copies ran while one was open for 34% -> 7% of each run, Pallas kernels for 0% -> 14%
where the time goes in v1:
time: 732 us; the launch traced here: 726 us
  waiting for transfers between devices  339 us (46%)
  Pallas kernels  275 us (38%)
  other arithmetic  39.2 us (5%)
  starting transfers between devices  36.3 us (5%)
  local copies, waits for them, and re-layouts  21.2 us (3%)
  between operations  15.2 us (2%)
    pallas_call x16, Pallas kernels, call(): pl.pallas_call(body, name=name, out_shape=outs, grid_spec=pltpu.PrefetchS...  275 us
    ppermute x28, waiting for transfers between devices, swap(): lax.ppermute(value, 'fsdp', [(i, i ^ bit) for i in range(lax.axis_size('f...  141 us
    all_gather x1, waiting for transfers between devices, local_sequence(): ff_w = lax.all_gather(mine, ('fsdp', 'tensor'), axis=0, tiled=False)  89.2 us
    ppermute x11, waiting for transfers between devices, swap(): return lax.ppermute(value, 'tensor', [(0, 1), (1, 0)])  88.9 us
    all_gather x1, waiting for transfers between devices, local_sequence(): attn_w = lax.all_gather(mine, ('fsdp', 'tensor'), axis=0, tiled=False)  20.4 us
    ppermute x28, starting transfers between devices, swap(): lax.ppermute(value, 'fsdp', [(i, i ^ bit) for i in range(lax.axis_size('f...  19.7 us
    convert_element_type x28, other arithmetic, scatter_sum(): low = total.astype(BF)  18.7 us
    ppermute x11, starting transfers between devices, swap(): return lax.ppermute(value, 'tensor', [(0, 1), (1, 0)])  16.5 us
  transfers between devices with their start and end apart: 41, of which 28 were waited for; matrix products, arithmetic and copies ran while one was open for 7% of the time, Pallas kernels for 14%

profile of v1, /device:TPU:0, one launch (start us, length us, event | category | flops | bytes accessed | tf_op | source)
XLA Modules:
  0.0 725.9 jit_solution(8931426837345860288)
XLA Ops:
  12.8 2.8 dynamic-slice_bitcast_fusion.3
  15.6 3.0 collective-permute-start
  20.4 26.0 %collective-permute-done = bf16[512,1024]{1,0:T(8,128)(2,1)S(1)} collective-permute-done((bf16[512,1024]{1,0:T(8,128)(2,1)}, bf16[512,1024]{1,0:T(8,128)(2,1)S(1)}, u32[]{:S(2)}, u32[]{:S(2)}) %collective-permute-start) | collective-permute-done | bytes 1048608 | tf_op jit(solution)/shard_map/ppermute | solution.py:901
  46.4 2.3 maximum_select_fusion.1.x_ref
  48.7 26.1 %collective-permute-done.1 = bf16[512,1024]{1,0:T(8,128)(2,1)} collective-permute-done((bf16[512,1024]{1,0:T(8,128)(2,1)}, bf16[512,1024]{1,0:T(8,128)(2,1)}, u32[]{:S(2)}, u32[]{:S(2)}) %collective-permute-start.1) | collective-permute-done | bytes 1048608 | tf_op jit(solution)/shard_map/ppermute | solution.py:901
  74.7 4.0 maximum_select_fusion.2.g_ref
  78.7 20.4 %all-gather.5.cloned.1.call-done = bf16[8448,512]{1,0:T(8,128)(2,1)} async-done(((bf16[264,512]{1,0:T(8,128)(2,1)}), bf16[8448,512]{1,0:T(8,128)(2,1)}) %all-gather.5.cloned.1.call-update) | async-done | bytes 8650768 | tf_op jit(solution)/shard_map/all_gather | solution.py:963
  103.0 14.2 %qkv.1 = (bf16[3,1024,1024]{2,1,0:T(8,128)(2,1)}, bf16[16,64,1024]{2,1,0:T(8,128)(2,1)}) custom-call(s32[6]{0:T(128)} %pad_add_fusion.ids, bf16[1024,1024]{1,0:T(8,128)(2,1)} %maximum_select_fusion.1.x_ref, f32[1,1024]{1,0:T(1,128)} %reshape_squeeze.8.gain_ref, bf16[16,2,264,512]{3,2,1,0:T(8,128)(2,1)} %bitcast.251), custom_call_target="tpu_custom_call" | custom-call | flops 6442450944 | bytes 19140608 | tf_op jit(solution)/shard_map/qkv/pallas_call | solution.py:310
  117.2 40.8 %attend.1 = (bf16[1024,1024]{1,0:T(8,128)(2,1)}, bf16[1024,1024]{1,0:T(8,128)(2,1)}, bf16[16,1024,1024]{2,1,0:T(8,128)(2,1)}, f32[8,2,1024]{2,1,0:T(2,128)}) custom-call(s32[6]{0:T(128)} %pad_add_fusion.ids, bf16[3,1024,1024]{2,1,0:T(8,128)(2,1)} %get-tuple-element.43.q_ref.k_ref.v_ref, bf16[3,1024,1024]{2,1,0:T(8,128)(2,1)} %get-tuple-element.43.q_ref.k_ref.v_ref, ...), custom_call_target="tpu_custom_call" | custom-call | flops 4294967296 | bytes 56688640 | tf_op jit(solution)/shard_map/attend/pallas_call | solution.py:310
  158.0 9.3 %out_project.1 = (f32[1024,1024]{1,0:T(8,128)}, bf16[1024,1024]{1,0:T(8,128)(2,1)}, bf16[16,64,1024]{2,1,0:T(8,128)(2,1)}) custom-call(s32[6]{0:T(128)} %pad_add_fusion.ids, bf16[1024,1024]{1,0:T(8,128)(2,1)} %get-tuple-element.44.a_ref, bf16[16,2,264,512]{3,2,1,0:T(8,128)(2,1)} %bitcast.252, bf16[1024,1024]{1,0:T(8,128)(2,1)} %maximum_select_fusion.1.x_ref, ...), custom_call_target="tpu_custom_call" | custom-call | flops 2147483648 | bytes 21237760 | tf_op jit(solution)/shard_map/out_project/pallas_call | solution.py:310
  167.4 89.2 %all-gather.7.cloned.1.call-done = bf16[6144,2048]{1,0:T(8,128)(2,1)} async-done(((bf16[192,2048]{1,0:T(8,128)(2,1)}), bf16[6144,2048]{1,0:T(8,128)(2,1)}) %all-gather.7.cloned.1.call-update) | async-done | bytes 25165840 | tf_op jit(solution)/shard_map/all_gather | solution.py:970
  256.5 37.4 %feed_forward.1 = (bf16[1024,4096]{1,0:T(8,128)(2,1)}, bf16[2,1024,4096]{2,1,0:T(8,128)(2,1)}, bf16[16,64,1024]{2,1,0:T(8,128)(2,1)}) custom-call(s32[6]{0:T(128)} %pad_add_fusion.ids, bf16[1024,1024]{1,0:T(8,128)(2,1)} %get-tuple-element.45.hn_ref, bf16[1024,1024]{1,0:T(8,128)(2,1)} %maximum_select_fusion.2.g_ref, bf16[16,2,192,2048]{3,2,1,0:T(8,128)(2,1)} %bitcast.255), custom_call_target="tpu_custom_call" | custom-call | flops 25769803776 | bytes 56623104 | tf_op jit(solution)/shard_map/feed_forward/pallas_call | solution.py:310
  294.0 14.1 %grad_up.1 = (bf16[2,8,64,2048]{3,2,1,0:T(8,128)(2,1)}, bf16[2,8,64,2048]{3,2,1,0:T(8,128)(2,1)}) custom-call(s32[6]{0:T(128)} %pad_add_fusion.ids, bf16[16,64,1024]{2,1,0:T(8,128)(2,1)} %get-tuple-element.70.l_ref, bf16[2,1024,4096]{2,1,0:T(8,128)(2,1)} %get-tuple-element.50.d_ref.r_ref), custom_call_target="tpu_custom_call" | custom-call | flops 8589934592 | bytes 27262976 | tf_op jit(solution)/shard_map/grad_up/pallas_call | solution.py:310
  308.1 14.1 %grad_gate.1 = (bf16[2,8,64,2048]{3,2,1,0:T(8,128)(2,1)}, bf16[2,8,64,2048]{3,2,1,0:T(8,128)(2,1)}) custom-call(s32[6]{0:T(128)} %pad_add_fusion.ids, bf16[16,64,1024]{2,1,0:T(8,128)(2,1)} %get-tuple-element.70.l_ref, bf16[2,1024,4096]{2,1,0:T(8,128)(2,1)} %get-tuple-element.50.d_ref.r_ref), custom_call_target="tpu_custom_call" | custom-call | flops 8589934592 | bytes 27262976 | tf_op jit(solution)/shard_map/grad_gate/pallas_call | solution.py:310
  322.2 30.5 %feed_forward_back.1 = (f32[1024,1024]{1,0:T(8,128)}, bf16[1024,1024]{1,0:T(8,128)(2,1)}, bf16[16,64,1024]{2,1,0:T(8,128)(2,1)}, f32[1,1024]{1,0:T(1,128)}) custom-call(s32[6]{0:T(128)} %pad_add_fusion.ids, bf16[2,1024,4096]{2,1,0:T(8,128)(2,1)} %get-tuple-element.50.d_ref.r_ref, bf16[16,2,192,2048]{3,2,1,0:T(8,128)(2,1)} %bitcast.256, ...), custom_call_target="tpu_custom_call" | custom-call | flops 17179869184 | bytes 56631296 | tf_op jit(solution)/shard_map/feed_forward_back/pallas_call | solution.py:310
  352.7 16.8 %feed_forward_out.1 = (bf16[512,1024]{1,0:T(8,128)(2,1)}, bf16[512,1024]{1,0:T(8,128)(2,1)}) custom-call(s32[6]{0:T(128)} %pad_add_fusion.ids, bf16[1024,4096]{1,0:T(8,128)(2,1)} %get-tuple-element.46.m_ref, bf16[16,2,192,2048]{3,2,1,0:T(8,128)(2,1)} %bitcast.257, f32[1024,1024]{1,0:T(8,128)} %get-tuple-element.47.hidden_ref), custom_call_target="tpu_custom_call" | custom-call | flops 8589934592 | bytes 39845888 | tf_op jit(solution)/shard_map/feed_forward_out/pallas_call | solution.py:310
  369.5 6.1 out_project_back.1.d_ref
  375.6 36.2 %attend_back.1.d_ref.r_ref = bf16[3,1024,1024]{2,1,0:T(8,128)(2,1)} custom-call(s32[6]{0:T(128)} %pad_add_fusion.ids, bf16[3,1024,1024]{2,1,0:T(8,128)(2,1)} %get-tuple-element.43.q_ref.k_ref.v_ref, bf16[3,1024,1024]{2,1,0:T(8,128)(2,1)} %get-tuple-element.43.q_ref.k_ref.v_ref, bf16[3,1024,1024]{2,1,0:T(8,128)(2,1)} %get-tuple-element.43.q_ref.k_ref.v_ref, ...), custom_call_target="tpu_custom_call" | custom-call | flops 8589934592 | bytes 62980096 | tf_op jit(solution)/shard_map/attend_back/pallas_call | solution.py:310
  411.7 17.0 %qkv_back.1 = (f32[512,1024]{1,0:T(8,128)}, bf16[512,1024]{1,0:T(8,128)(2,1)}, f32[1,1024]{1,0:T(1,128)}) custom-call(s32[6]{0:T(128)} %pad_add_fusion.ids, bf16[3,1024,1024]{2,1,0:T(8,128)(2,1)} %attend_back.1.d_ref.r_ref, bf16[16,2,264,512]{3,2,1,0:T(8,128)(2,1)} %bitcast.254, bf16[1024,1024]{1,0:T(8,128)(2,1)} %maximum_select_fusion.1.x_ref, ...), custom_call_target="tpu_custom_call" | custom-call | flops 6442450944 | bytes 24387584 | tf_op jit(solution)/shard_map/qkv_back/pallas_call | solution.py:310
  431.7 6.0 grad_out.1
  437.7 6.0 grad_qkv.5
  444.4 6.1 grad_qkv.3
  451.0 14.1 %grad_down.1 = (bf16[2,8,64,2048]{3,2,1,0:T(8,128)(2,1)}, bf16[2,8,64,2048]{3,2,1,0:T(8,128)(2,1)}) custom-call(s32[6]{0:T(128)} %pad_add_fusion.ids, bf16[16,64,1024]{2,1,0:T(8,128)(2,1)} %get-tuple-element.75.l_ref, bf16[1,1024,4096]{2,1,0:T(8,128)(2,1)} %bitcast.260), custom_call_target="tpu_custom_call" | custom-call | flops 8589934592 | bytes 18874368 | tf_op jit(solution)/shard_map/grad_down/pallas_call | solution.py:310
  465.2 6.1 grad_qkv.4
  471.3 6.4 collective-permute-done.3
  478.8 6.3 copy.68
  496.8 9.6 %collective-permute-done.20 = bf16[2,2,2,64,512]{4,3,1,2,0:T(8,128)(2,1)S(1)} collective-permute-done((bf16[2,2,2,64,512]{4,3,1,2,0:T(8,128)(2,1)S(1)}, bf16[2,2,2,64,512]{4,3,1,2,0:T(8,128)(2,1)S(1)}, u32[]{:S(2)}, u32[]{:S(2)}) %collective-permute-start.20) | collective-permute-done | bytes 524320 | tf_op jit(solution)/shard_map/ppermute | solution.py:902
  509.4 10.5 %collective-permute-done.10 = bf16[2,2,2,64,512]{4,3,1,2,0:T(8,128)(2,1)S(1)} collective-permute-done((bf16[2,2,2,64,512]{4,3,1,2,0:T(8,128)(2,1)S(1)}, bf16[2,2,2,64,512]{4,3,1,2,0:T(8,128)(2,1)S(1)}, u32[]{:S(2)}, u32[]{:S(2)}) %collective-permute-start.10) | collective-permute-done | bytes 524320 | tf_op jit(solution)/shard_map/ppermute | solution.py:902
  524.3 2.6 collective-permute-done.21
  533.4 5.5 collective-permute-done.22
  538.8 2.7 collective-permute-start.17
  541.6 8.1 %collective-permute-done.17 = bf16[2,64,512]{2,1,0:T(8,128)(2,1)S(1)} collective-permute-done((bf16[2,64,512]{2,1,0:T(8,128)(2,1)S(1)}, bf16[2,64,512]{2,1,0:T(8,128)(2,1)S(1)}, u32[]{:S(2)}, u32[]{:S(2)}) %collective-permute-start.17) | collective-permute-done | bytes 131104 | tf_op jit(solution)/shard_map/ppermute | solution.py:902
  549.7 5.0 collective-permute-done.12
  554.7 5.5 collective-permute-done.23
  567.5 3.1 collective-permute-done.7
  572.8 2.3 collective-permute-done.8
  576.5 2.5 add_convert_fusion
  581.9 2.3 add_convert_fusion.1
  587.7 3.7 add_convert_fusion.2
  594.1 28.4 %collective-permute-done.35 = bf16[2,2,2,64,2048]{4,3,1,2,0:T(8,128)(2,1)S(1)} collective-permute-done((bf16[2,2,2,64,2048]{4,3,1,2,0:T(8,128)(2,1)S(1)}, bf16[2,2,2,64,2048]{4,3,1,2,0:T(8,128)(2,1)S(1)}, u32[]{:S(2)}, u32[]{:S(2)}) %collective-permute-start.35) | collective-permute-done | bytes 2097184 | tf_op jit(solution)/shard_map/ppermute | solution.py:902
  625.3 5.1 collective-permute-done.30
  632.3 8.3 %collective-permute-done.25 = bf16[2,2,2,64,2048]{4,3,2,0,1:T(8,128)(2,1)S(1)} collective-permute-done((bf16[2,2,2,64,2048]{4,3,2,0,1:T(8,128)(2,1)S(1)}, bf16[2,2,2,64,2048]{4,3,2,0,1:T(8,128)(2,1)S(1)}, u32[]{:S(2)}, u32[]{:S(2)}) %collective-permute-start.25) | collective-permute-done | bytes 2097184 | tf_op jit(solution)/shard_map/ppermute | solution.py:901
  642.2 14.8 %collective-permute-done.36 = bf16[2,2,64,2048]{3,2,0,1:T(8,128)(2,1)S(1)} collective-permute-done((bf16[2,2,64,2048]{3,2,0,1:T(8,128)(2,1)S(1)}, bf16[2,2,64,2048]{3,2,0,1:T(8,128)(2,1)S(1)}, u32[]{:S(2)}, u32[]{:S(2)}) %collective-permute-start.36) | collective-permute-done | bytes 1048608 | tf_op jit(solution)/shard_map/ppermute | solution.py:901
  657.8 14.7 %collective-permute-done.31 = bf16[2,2,64,2048]{3,2,0,1:T(8,128)(2,1)S(1)} collective-permute-done((bf16[2,2,64,2048]{3,2,0,1:T(8,128)(2,1)S(1)}, bf16[2,2,64,2048]{3,2,0,1:T(8,128)(2,1)S(1)}, u32[]{:S(2)}, u32[]{:S(2)}) %collective-permute-start.31) | collective-permute-done | bytes 1048608 | tf_op jit(solution)/shard_map/ppermute | solution.py:902
  674.5 13.8 %collective-permute-done.26 = bf16[2,2,64,2048]{3,2,1,0:T(8,128)(2,1)S(1)} collective-permute-done((bf16[2,2,64,2048]{3,2,1,0:T(8,128)(2,1)S(1)}, bf16[2,2,64,2048]{3,2,1,0:T(8,128)(2,1)S(1)}, u32[]{:S(2)}, u32[]{:S(2)}) %collective-permute-start.26) | collective-permute-done | bytes 1048608 | tf_op jit(solution)/shard_map/ppermute | solution.py:902
  688.8 5.8 collective-permute-done.37
  696.3 13.7 %collective-permute-done.27 = bf16[2,64,2048]{2,1,0:T(8,128)(2,1)S(1)} collective-permute-done((bf16[2,64,2048]{2,1,0:T(8,128)(2,1)S(1)}, bf16[2,64,2048]{2,1,0:T(8,128)(2,1)S(1)}, u32[]{:S(2)}, u32[]{:S(2)}) %collective-permute-start.27) | collective-permute-done | bytes 524320 | tf_op jit(solution)/shard_map/ppermute | solution.py:902
  711.1 5.6 collective-permute-done.28
  (181 shorter events, 75.9 us)
Async XLA Ops:
  7.2 12.6 %copy-start = (s32[2,1,3]{2,1,0:T(1,128)S(1)}, s32[2,1,3]{2,1,0:T(1,128)}, u32[]{:S(2)}) copy-start(s32[2,1,3]{2,1,0:T(1,128)} %param.10) | copy-start | bytes 76
  7.2 92.0 %all-gather.5.cloned.1.call-start = ((), (), s32[]{:S(2)}) async-start(), calls=%async_computation | async-start | bytes 8921088 | tf_op jit(solution)/shard_map/all_gather | solution.py:963
  10.6 245.9 %all-gather.7.cloned.1.call-start = ((), (), s32[]{:S(2)}) async-start(), calls=%async_computation.1 | async-start | bytes 25952256 | tf_op jit(solution)/shard_map/all_gather | solution.py:970
  12.8 5.8 copy-start.5
  15.6 30.7 %collective-permute-start = (bf16[512,1024]{1,0:T(8,128)(2,1)}, bf16[512,1024]{1,0:T(8,128)(2,1)S(1)}, u32[]{:S(2)}, u32[]{:S(2)}) collective-permute-start(bf16[512,1024]{1,0:T(8,128)(2,1)} %get-tuple-element.113), channel_id=1, source_target_pairs={{0,1},{1,0},{2,3},{3,2},{4,5},{5,4},{6,7},{7,6},{8,9},{9,8},{10,11... | collective-permute-start | bytes 3145736 | tf_op jit(solution)/shard_map/ppermute | solution.py:901
  19.7 55.0 %collective-permute-start.1 = (bf16[512,1024]{1,0:T(8,128)(2,1)}, bf16[512,1024]{1,0:T(8,128)(2,1)}, u32[]{:S(2)}, u32[]{:S(2)}) collective-permute-start(bf16[512,1024]{1,0:T(8,128)(2,1)} %get-tuple-element.111), channel_id=1, source_target_pairs={{0,1},{1,0},{2,3},{3,2},{4,5},{5,4},{6,7},{7,6},{8,9},{9,8},{10,11... | collective-permute-start | bytes 3145736 | tf_op jit(solution)/shard_map/ppermute | solution.py:901
  411.7 17.7 %copy-start.11 = (f32[1,1024]{1,0:T(1,128)S(1)}, f32[1,1024]{1,0:T(1,128)}, u32[]{:S(2)}) copy-start(f32[1,1024]{1,0:T(1,128)} %get-tuple-element.60) | copy-start | bytes 12292
  429.6 62.5 %collective-permute-start.2 = (bf16[512,1024]{1,0:T(8,128)(2,1)}, bf16[512,1024]{1,0:T(8,128)(2,1)S(1)}, u32[]{:S(2)}, u32[]{:S(2)}) collective-permute-start(bf16[512,1024]{1,0:T(8,128)(2,1)} %get-tuple-element.49), channel_id=1, source_target_pairs={{0,1},{1,0},{2,3},{3,2},{4,5},{5,4},{6,7},{7,6},{8,9},{9,8},{10,11... | collective-permute-start | bytes 3145736 | tf_op jit(solution)/shard_map/ppermute | solution.py:901
  431.2 46.5 %collective-permute-start.3 = (bf16[512,1024]{1,0:T(8,128)(2,1)}, bf16[512,1024]{1,0:T(8,128)(2,1)S(1)}, u32[]{:S(2)}, u32[]{:S(2)}) collective-permute-start(bf16[512,1024]{1,0:T(8,128)(2,1)} %get-tuple-element.57), channel_id=1, source_target_pairs={{0,1},{1,0},{2,3},{3,2},{4,5},{5,4},{6,7},{7,6},{8,9},{9,8},{10,11... | collective-permute-start | bytes 3145736 | tf_op jit(solution)/shard_map/ppermute | solution.py:901
  437.7 47.4 %collective-permute-start.19 = (bf16[2,8,64,512]{3,2,1,0:T(8,128)(2,1)}, bf16[2,8,64,512]{3,2,1,0:T(8,128)(2,1)}, u32[]{:S(2)}, u32[]{:S(2)}) collective-permute-start(bf16[2,8,64,512]{3,2,1,0:T(8,128)(2,1)} %get-tuple-element.69), channel_id=1, source_target_pairs={{0,2},{2,0},{4,6},{6,4},{8,10},{10,8},{12,14},{14,12},{16,18},{18,... | collective-permute-start | bytes 3145736 | tf_op jit(solution)/shard_map/ppermute | solution.py:902
  450.5 44.7 %collective-permute-start.4 = (bf16[2,8,72,512]{3,2,1,0:T(8,128)(2,1)}, bf16[2,8,72,512]{3,2,1,0:T(8,128)(2,1)S(1)}, u32[]{:S(2)}, u32[]{:S(2)}) collective-permute-start(bf16[2,8,72,512]{3,2,1,0:T(8,128)(2,1)} %get-tuple-element.62), channel_id=1, source_target_pairs={{0,2},{2,0},{4,6},{6,4},{8,10},{10,8},{12,14},{14,12},{16,18},{18,... | collective-permute-start | bytes 3538952 | tf_op jit(solution)/shard_map/ppermute | solution.py:902
  451.0 36.5 %collective-permute-start.14 = (bf16[2,8,64,512]{3,2,1,0:T(8,128)(2,1)}, bf16[2,8,64,512]{3,2,1,0:T(8,128)(2,1)}, u32[]{:S(2)}, u32[]{:S(2)}) collective-permute-start(bf16[2,8,64,512]{3,2,1,0:T(8,128)(2,1)} %get-tuple-element.66), channel_id=1, source_target_pairs={{0,2},{2,0},{4,6},{6,4},{8,10},{10,8},{12,14},{14,12},{16,18},{18,... | collective-permute-start | bytes 3145736 | tf_op jit(solution)/shard_map/ppermute | solution.py:902
  471.3 6.6 copy-start.6
  477.7 11.7 %collective-permute-start.9 = (bf16[2,8,64,512]{3,2,1,0:T(8,128)(2,1)}, bf16[2,8,64,512]{3,2,1,0:T(8,128)(2,1)}, u32[]{:S(2)}, u32[]{:S(2)}) collective-permute-start(bf16[2,8,64,512]{3,2,1,0:T(8,128)(2,1)} %get-tuple-element.64), channel_id=1, source_target_pairs={{0,2},{2,0},{4,6},{6,4},{8,10},{10,8},{12,14},{14,12},{16,18},{18,... | collective-permute-start | bytes 3145736 | tf_op jit(solution)/shard_map/ppermute | solution.py:902
  485.1 91.4 %collective-permute-start.34 = (bf16[2,8,64,2048]{3,2,1,0:T(8,128)(2,1)}, bf16[2,8,64,2048]{3,2,1,0:T(8,128)(2,1)S(1)}, u32[]{:S(2)}, u32[]{:S(2)}) collective-permute-start(bf16[2,8,64,2048]{3,2,1,0:T(8,128)(2,1)} %get-tuple-element.77), channel_id=1, source_target_pairs={{0,2},{2,0},{4,6},{6,4},{8,10},{10,8},{12,14},{14,12},{16,18},{18,... | collective-permute-start | bytes 12582920 | tf_op jit(solution)/shard_map/ppermute | solution.py:902
  487.5 94.4 %collective-permute-start.29 = (bf16[2,8,64,2048]{3,2,1,0:T(8,128)(2,1)}, bf16[2,8,64,2048]{3,2,1,0:T(8,128)(2,1)S(1)}, u32[]{:S(2)}, u32[]{:S(2)}) collective-permute-start(bf16[2,8,64,2048]{3,2,1,0:T(8,128)(2,1)} %get-tuple-element.74), channel_id=1, source_target_pairs={{0,2},{2,0},{4,6},{6,4},{8,10},{10,8},{12,14},{14,12},{16,18},{18,... | collective-permute-start | bytes 12582920 | tf_op jit(solution)/shard_map/ppermute | solution.py:902
  489.5 96.8 %collective-permute-start.24 = (bf16[2,8,64,2048]{3,2,1,0:T(8,128)(2,1)}, bf16[2,8,64,2048]{3,2,1,0:T(8,128)(2,1)}, u32[]{:S(2)}, u32[]{:S(2)}) collective-permute-start(bf16[2,8,64,2048]{3,2,1,0:T(8,128)(2,1)} %get-tuple-element.72), channel_id=1, source_target_pairs={{0,2},{2,0},{4,6},{6,4},{8,10},{10,8},{12,14},{14,12},{16,18},{18,... | collective-permute-start | bytes 12582920 | tf_op jit(solution)/shard_map/ppermute | solution.py:902
  492.1 14.3 %collective-permute-start.20 = (bf16[2,2,2,64,512]{4,3,1,2,0:T(8,128)(2,1)S(1)}, bf16[2,2,2,64,512]{4,3,1,2,0:T(8,128)(2,1)S(1)}, u32[]{:S(2)}, u32[]{:S(2)}) collective-permute-start(bf16[2,2,2,64,512]{4,3,1,2,0:T(8,128)(2,1)S(1)} %bitcast.276), channel_id=1, source_target_pairs={{0,4},{2,6},{4,0},{6,2},{8,12},{10,14},{12,8},{14,10},{16,20},{18,... | collective-permute-start | bytes 1572872 | tf_op jit(solution)/shard_map/ppermute | solution.py:902
  495.3 14.0 %collective-permute-start.15 = (bf16[2,2,2,64,512]{4,3,2,0,1:T(8,128)(2,1)S(1)}, bf16[2,2,2,64,512]{4,3,2,0,1:T(8,128)(2,1)S(1)}, u32[]{:S(2)}, u32[]{:S(2)}) collective-permute-start(bf16[2,2,2,64,512]{4,3,2,0,1:T(8,128)(2,1)S(1)} %copy.58), channel_id=1, source_target_pairs={{0,1},{1,0},{2,3},{3,2},{4,5},{5,4},{6,7},{7,6},{8,9},{9,8},{10,11... | collective-permute-start | bytes 1572872 | tf_op jit(solution)/shard_map/ppermute | solution.py:901
  506.4 13.5 %collective-permute-start.10 = (bf16[2,2,2,64,512]{4,3,1,2,0:T(8,128)(2,1)S(1)}, bf16[2,2,2,64,512]{4,3,1,2,0:T(8,128)(2,1)S(1)}, u32[]{:S(2)}, u32[]{:S(2)}) collective-permute-start(bf16[2,2,2,64,512]{4,3,1,2,0:T(8,128)(2,1)S(1)} %bitcast.275), channel_id=1, source_target_pairs={{0,4},{2,6},{4,0},{6,2},{8,12},{10,14},{12,8},{14,10},{16,20},{18,... | collective-permute-start | bytes 1572872 | tf_op jit(solution)/shard_map/ppermute | solution.py:902
  509.2 14.6 %collective-permute-start.5 = (bf16[2,2,2,72,512]{4,3,0,2,1:T(8,128)(2,1)S(1)}, bf16[2,2,2,72,512]{4,3,0,2,1:T(8,128)(2,1)S(1)}, u32[]{:S(2)}, u32[]{:S(2)}) collective-permute-start(bf16[2,2,2,72,512]{4,3,0,2,1:T(8,128)(2,1)S(1)} %bitcast.273), channel_id=1, source_target_pairs={{0,8},{2,10},{4,12},{6,14},{8,0},{10,2},{12,4},{14,6},{16,24},{18,... | collective-permute-start | bytes 1769480 | tf_op jit(solution)/shard_map/ppermute | solution.py:902
  519.9 6.9 collective-permute-start.21
  523.8 6.6 collective-permute-start.16
  526.9 6.4 collective-permute-start.11
  530.4 32.8 %collective-permute-start.6 = (bf16[2,2,72,512]{3,2,0,1:T(8,128)(2,1)S(1)}, bf16[2,2,72,512]{3,2,0,1:T(8,128)(2,1)S(1)}, u32[]{:S(2)}, u32[]{:S(2)}) collective-permute-start(bf16[2,2,72,512]{3,2,0,1:T(8,128)(2,1)S(1)} %slice_bitcast_fusion.12), channel_id=1, source_target_pairs={{0,16},{2,18},{4,20},{6,22},{8,24},{10,26},{12,28},{14,30},{16,0},... | collective-permute-start | bytes 884744 | tf_op jit(solution)/shard_map/ppermute | solution.py:902
  533.2 5.6 collective-permute-start.22
  538.8 10.8 %collective-permute-start.17 = (bf16[2,64,512]{2,1,0:T(8,128)(2,1)S(1)}, bf16[2,64,512]{2,1,0:T(8,128)(2,1)S(1)}, u32[]{:S(2)}, u32[]{:S(2)}) collective-permute-start(bf16[2,64,512]{2,1,0:T(8,128)(2,1)S(1)} %slice_bitcast_fusion.31), channel_id=1, source_target_pairs={{0,16},{2,18},{4,20},{6,22},{8,24},{10,26},{12,28},{14,30},{16,0},... | collective-permute-start | bytes 393224 | tf_op jit(solution)/shard_map/ppermute | solution.py:902
  549.6 5.0 collective-permute-start.12
  554.7 5.6 collective-permute-start.23
  554.7 21.9 %copy-start.4 = (bf16[2,8,64,2048]{3,2,1,0:T(8,128)(2,1)S(1)}, bf16[2,8,64,2048]{3,2,1,0:T(8,128)(2,1)}, u32[]{:S(2)}) copy-start(bf16[2,8,64,2048]{3,2,1,0:T(8,128)(2,1)} %get-tuple-element.76) | copy-start | bytes 12582916
  560.3 5.2 collective-permute-start.18
  563.2 9.6 %collective-permute-start.13 = (bf16[64,512]{1,0:T(8,128)(2,1)S(1)}, bf16[64,512]{1,0:T(8,128)(2,1)S(1)}, u32[]{:S(2)}, u32[]{:S(2)}) collective-permute-start(bf16[64,512]{1,0:T(8,128)(2,1)S(1)} %slice_bitcast_fusion.41), channel_id=1, source_target_pairs={{0,16},{2,18},{4,20},{6,22},{8,24},{10,26},{12,28},{14,30},{16,0},... | collective-permute-start | bytes 196616 | tf_op jit(solution)/shard_map/ppermute | solution.py:902
  565.4 5.1 collective-permute-start.7
  570.6 4.5 collective-permute-start.8
  579.9 42.6 %collective-permute-start.35 = (bf16[2,2,2,64,2048]{4,3,1,2,0:T(8,128)(2,1)S(1)}, bf16[2,2,2,64,2048]{4,3,1,2,0:T(8,128)(2,1)S(1)}, u32[]{:S(2)}, u32[]{:S(2)}) collective-permute-start(bf16[2,2,2,64,2048]{4,3,1,2,0:T(8,128)(2,1)S(1)} %bitcast.266), channel_id=1, source_target_pairs={{0,4},{2,6},{4,0},{6,2},{8,12},{10,14},{12,8},{14,10},{16,20},{18,... | collective-permute-start | bytes 6291464 | tf_op jit(solution)/shard_map/ppermute | solution.py:902
  584.8 3.0 copy-start.2
  586.3 44.2 %collective-permute-start.30 = (bf16[2,2,2,64,2048]{4,3,0,2,1:T(8,128)(2,1)}, bf16[2,2,2,64,2048]{4,3,0,2,1:T(8,128)(2,1)S(1)}, u32[]{:S(2)}, u32[]{:S(2)}) collective-permute-start(bf16[2,2,2,64,2048]{4,3,0,2,1:T(8,128)(2,1)} %bitcast.245), channel_id=1, source_target_pairs={{0,8},{2,10},{4,12},{6,14},{8,0},{10,2},{12,4},{14,6},{16,24},{18,... | collective-permute-start | bytes 6291464 | tf_op jit(solution)/shard_map/ppermute | solution.py:902
  592.0 48.6 %collective-permute-start.25 = (bf16[2,2,2,64,2048]{4,3,2,0,1:T(8,128)(2,1)S(1)}, bf16[2,2,2,64,2048]{4,3,2,0,1:T(8,128)(2,1)S(1)}, u32[]{:S(2)}, u32[]{:S(2)}) collective-permute-start(bf16[2,2,2,64,2048]{4,3,2,0,1:T(8,128)(2,1)S(1)} %copy.62), channel_id=1, source_target_pairs={{0,1},{1,0},{2,3},{3,2},{4,5},{5,4},{6,7},{7,6},{8,9},{9,8},{10,11... | collective-permute-start | bytes 6291464 | tf_op jit(solution)/shard_map/ppermute | solution.py:901
  623.5 33.5 %collective-permute-start.36 = (bf16[2,2,64,2048]{3,2,0,1:T(8,128)(2,1)S(1)}, bf16[2,2,64,2048]{3,2,0,1:T(8,128)(2,1)S(1)}, u32[]{:S(2)}, u32[]{:S(2)}) collective-permute-start(bf16[2,2,64,2048]{3,2,0,1:T(8,128)(2,1)S(1)} %slice_bitcast_fusion), channel_id=1, source_target_pairs={{0,1},{1,0},{2,3},{3,2},{4,5},{5,4},{6,7},{7,6},{8,9},{9,8},{10,11... | collective-permute-start | bytes 3145736 | tf_op jit(solution)/shard_map/ppermute | solution.py:901
  631.4 41.1 %collective-permute-start.31 = (bf16[2,2,64,2048]{3,2,0,1:T(8,128)(2,1)S(1)}, bf16[2,2,64,2048]{3,2,0,1:T(8,128)(2,1)S(1)}, u32[]{:S(2)}, u32[]{:S(2)}) collective-permute-start(bf16[2,2,64,2048]{3,2,0,1:T(8,128)(2,1)S(1)} %slice_bitcast_fusion.2), channel_id=1, source_target_pairs={{0,16},{2,18},{4,20},{6,22},{8,24},{10,26},{12,28},{14,30},{16,0},... | collective-permute-start | bytes 3145736 | tf_op jit(solution)/shard_map/ppermute | solution.py:902
  641.6 46.7 %collective-permute-start.26 = (bf16[2,2,64,2048]{3,2,1,0:T(8,128)(2,1)S(1)}, bf16[2,2,64,2048]{3,2,1,0:T(8,128)(2,1)S(1)}, u32[]{:S(2)}, u32[]{:S(2)}) collective-permute-start(bf16[2,2,64,2048]{3,2,1,0:T(8,128)(2,1)S(1)} %slice_bitcast_fusion.4), channel_id=1, source_target_pairs={{0,8},{2,10},{4,12},{6,14},{8,0},{10,2},{12,4},{14,6},{16,24},{18,... | collective-permute-start | bytes 3145736 | tf_op jit(solution)/shard_map/ppermute | solution.py:902
  657.5 37.1 %collective-permute-start.37 = (bf16[2,64,2048]{2,1,0:T(8,128)(2,1)S(1)}, bf16[2,64,2048]{2,1,0:T(8,128)(2,1)S(1)}, u32[]{:S(2)}, u32[]{:S(2)}) collective-permute-start(bf16[2,64,2048]{2,1,0:T(8,128)(2,1)S(1)} %slice_bitcast_fusion.6), channel_id=1, source_target_pairs={{0,8},{2,10},{4,12},{6,14},{8,0},{10,2},{12,4},{14,6},{16,24},{18,... | collective-permute-start | bytes 1572872 | tf_op jit(solution)/shard_map/ppermute | solution.py:902
  673.0 21.8 %collective-permute-start.32 = (bf16[2,64,2048]{2,1,0:T(8,128)(2,1)S(1)}, bf16[2,64,2048]{2,1,0:T(8,128)(2,1)S(1)}, u32[]{:S(2)}, u32[]{:S(2)}) collective-permute-start(bf16[2,64,2048]{2,1,0:T(8,128)(2,1)S(1)} %slice_bitcast_fusion.8), channel_id=1, source_target_pairs={{0,4},{2,6},{4,0},{6,2},{8,12},{10,14},{12,8},{14,10},{16,20},{18,... | collective-permute-start | bytes 1572872 | tf_op jit(solution)/shard_map/ppermute | solution.py:902
  688.7 21.3 %collective-permute-start.27 = (bf16[2,64,2048]{2,1,0:T(8,128)(2,1)S(1)}, bf16[2,64,2048]{2,1,0:T(8,128)(2,1)S(1)}, u32[]{:S(2)}, u32[]{:S(2)}) collective-permute-start(bf16[2,64,2048]{2,1,0:T(8,128)(2,1)S(1)} %slice_bitcast_fusion.10), channel_id=1, source_target_pairs={{0,16},{2,18},{4,20},{6,22},{8,24},{10,26},{12,28},{14,30},{16,0},... | collective-permute-start | bytes 1572872 | tf_op jit(solution)/shard_map/ppermute | solution.py:902
  694.7 23.1 %collective-permute-start.38 = (bf16[64,2048]{1,0:T(8,128)(2,1)S(1)}, bf16[64,2048]{1,0:T(8,128)(2,1)S(1)}, u32[]{:S(2)}, u32[]{:S(2)}) collective-permute-start(bf16[64,2048]{1,0:T(8,128)(2,1)S(1)} %slice_bitcast_fusion.14), channel_id=1, source_target_pairs={{0,16},{2,18},{4,20},{6,22},{8,24},{10,26},{12,28},{14,30},{16,0},... | collective-permute-start | bytes 786440 | tf_op jit(solution)/shard_map/ppermute | solution.py:902
  695.0 16.0 %collective-permute-start.33 = (bf16[64,2048]{1,0:T(8,128)(2,1)S(1)}, bf16[64,2048]{1,0:T(8,128)(2,1)S(1)}, u32[]{:S(2)}, u32[]{:S(2)}) collective-permute-start(bf16[64,2048]{1,0:T(8,128)(2,1)S(1)} %slice_bitcast_fusion.16), channel_id=1, source_target_pairs={{0,1},{1,0},{2,3},{3,2},{4,5},{5,4},{6,7},{7,6},{8,9},{9,8},{10,11... | collective-permute-start | bytes 786440 | tf_op jit(solution)/shard_map/ppermute | solution.py:901
  710.2 6.4 collective-permute-start.28
  711.0 7.6 %copy-start.1 = (s32[2,1,3]{2,1,0:T(1,128)S(1)}, s32[2,1,3]{2,1,0:T(1,128)}, u32[]{:S(2)}) copy-start(s32[2,1,3]{2,1,0:T(1,128)} %param.10) | copy-start | bytes 76
  (5 other events, 10.4 us)
Sparse Core Ops, SparseCore 0:
  11.5 87.6 all-gather.4
  102.0 154.4 all-gather.6

commit v2 on v0

--- a/solution.py
+++ b/solution.py
@@ -1,6 +1,8 @@
 import jax
 import jax.numpy as jnp
 from jax import lax
+from jax.experimental import pallas as pl
+from jax.experimental.pallas import tpu as pltpu
 from jax.sharding import PartitionSpec as P
 
 D = 1024
@@ -292,9 +294,1034 @@
     )
 
 
+BF = jnp.bfloat16
+F32 = jnp.float32
+TILE = 256
+UNITS = 512
+CORE, TENSOR, X, Z_NEAR, Z_FAR = 1, 0, 2, 4, 8
+
+
+def dot_f32(a, b, ca, cb):
+    return lax.dot_general(a, b, (((ca,), (cb,)), ((), ())), preferred_element_type=F32)
+
+
+def call(body, name, ids, ins, in_specs, outs, out_specs, grid, scratch=(), aliases=None):
+    return pl.pallas_call(
+        body,
+        name=name,
+        out_shape=outs,
+        grid_spec=pltpu.PrefetchScalarGridSpec(
+            num_scalar_prefetch=1,
+            grid=grid,
+            in_specs=in_specs,
+            out_specs=out_specs,
+            scratch_shapes=list(scratch),
+        ),
+        input_output_aliases=aliases or {},
+        compiler_params=pltpu.CompilerParams(
+            dimension_semantics=("arbitrary",) * len(grid), vmem_limit_bytes=56 * 2**20
+        ),
+        cost_estimate=pl.CostEstimate(flops=1024, bytes_accessed=1024, transcendentals=0),
+    )(ids, *ins)
+
+
+def shape(dims, dtype):
+    return jax.ShapeDtypeStruct(dims, dtype)
+
+
+def whole(dims):
+    zeros = (0,) * len(dims)
+    return pl.BlockSpec(dims, lambda *_: zeros)
+
+
+IN_PLACE = pl.BlockSpec(memory_space=pl.ANY)
+
+
+def store_transposed(ids, value, blocks_ref, out_ref):
+    count, height = blocks_ref.shape[0], blocks_ref.shape[1]
+    step = 128 // height
+    for c in range(value.shape[1] // 128):
+        part = value[:, c * 128 : (c + 1) * 128]
+        blocks_ref[c * step : (c + 1) * step] = part.T.reshape(step, height, part.shape[0])
+    for core in range(2):
+        for pair in range(count // 2):
+            source = 2 * (pair ^ ids[1]) + (core ^ ids[2])
+            out_ref[core * (count // 2) + pair] = blocks_ref[source]
+
+
+def position(order, f, t):
+    at = 0
+    for k, bit in enumerate(order):
+        value = t if bit == TENSOR else (f // bit) % 2
+        at = at + value * 2**k
+    return at
+
+
+def swap(value, bit):
+    if bit == TENSOR:
+        return lax.ppermute(value, "tensor", [(0, 1), (1, 0)])
+    return lax.ppermute(value, "fsdp", [(i, i ^ bit) for i in range(lax.axis_size("fsdp"))])
+
+
+class Gathered:
+    def __init__(self, mine, order):
+        self.order = order
+        self.left = [*order, CORE]
+        self.held = mine
+        self.rows = mine.shape
+        self.ready = False
+        self.begin()
+
+    def begin(self):
+        self.got = swap(self.held, self.left[0])
+
+    def advance(self):
+        if self.left.pop(0) == CORE:
+            self.pair = [a.reshape((-1,) + self.rows) for a in (self.held, self.got)]
+            self.ready = True
+        else:
+            self.held = jnp.stack([self.held, self.got])
+            self.begin()
+
+
+class Summed:
+    def __init__(self, keep, send, order):
+        dims = (2,) * 4 + keep.shape[2:]
+        axes = (TENSOR, Z_FAR, Z_NEAR, X)
+        self.arrays = [(keep.reshape(dims), axes)]
+        self.axes = axes
+        self.left = list(order)
+        self.got = swap(send.reshape(dims), CORE)
+        self.bit = None
+
+    def received(self):
+        self.arrays.append((self.got, self.axes))
+        self.bit = self.left.pop(0) if self.left else None
+        self.axes = tuple(a for a in self.axes if a != self.bit)
+
+
+def halve(ids, sums):
+    for s in sums:
+        s.received()
+    last = sums[0].bit is None
+    depth = 0 if last else max(len(s.axes) for s in sums)
+    blocks = 2**depth
+    ins, in_specs, outs, out_specs, counts = [], [], [], [], []
+    for s in sums:
+        rows, columns = s.arrays[0][0].shape[-2:]
+
+        def index(axes, g, now=s.axes, bit=s.bit):
+            at = []
+            for a in axes:
+                if last or a not in now:
+                    at.append(int(a == bit))
+                else:
+                    at.append(g // 2 ** (depth - 1 - now.index(a)) % 2)
+            return (*at, 0, 0)
+
+        for array, axes in s.arrays:
+            ins.append(array)
+            in_specs.append(
+                pl.BlockSpec(
+                    (None,) * len(axes) + (rows, columns),
+                    lambda g, ids, axes=axes, index=index: index(axes, g),
+                )
+            )
+        counts.append(len(s.arrays))
+        lead = () if last else (2,) * len(s.axes)
+        outs.append(shape(lead + (rows, columns), F32 if last else BF))
+        out_specs.append(
+            pl.BlockSpec(
+                (None,) * len(lead) + (rows, columns),
+                lambda g, ids, axes=() if last else s.axes, index=index: index(axes, g),
+            )
+        )
+
+    def body(ids, *refs):
+        out_refs = refs[len(ins) :]
+        at = 0
+        for out_ref, count in zip(out_refs, counts):
+            rows = out_ref.shape[0]
+            for r in range(0, rows, 64):
+                total = refs[at][r : r + 64].astype(F32)
+                for k in range(1, count):
+                    total += refs[at + k][r : r + 64].astype(F32)
+                out_ref[r : r + 64] = total.astype(out_ref.dtype)
+            at += count
+
+    made = call(body, "halve", ids, tuple(ins), in_specs, tuple(outs), out_specs, (blocks,))
+    for s, value in zip(sums, made):
+        if last:
+            s.result = value
+        else:
+            s.got = swap(value, s.bit)
+    return made
+
+
+def after(values, running):
+    running = [r for r in running if not r.ready]
+    values, got = lax.optimization_barrier((values, [r.got for r in running]))
+    for r, g in zip(running, got):
+        r.got = g
+        r.advance()
+    return values
+
+
+def gathered_rows(ids, refs, order, part, height):
+    mine = position(order, ids[3], ids[0])
+    flipped = ids[2] == 1
+    blocks = []
+    for pair in range(refs[0].shape[0] // 2):
+        at = position(order, 2 * pair, part) ^ mine
+        a, b = [ref[at, :height] for ref in refs]
+        blocks += [jnp.where(flipped, b, a), jnp.where(flipped, a, b)]
+    return jnp.concatenate(blocks, axis=0)
+
+
+def make_qkv(ids, rows, gots, gain, gathered):
+    parts, local_rows, width = rows.shape
+    length = parts * local_rows
+    fsdp = gathered[0].pair[0].shape[0]
+    height = width // fsdp
+    half = width // parts
+
+    piece = local_rows // len(gots)
+
+    def body(ids, rows_ref, gain_ref, *refs):
+        qkv_ref, xt_ref, x_ref, xn_ref, blocks_ref = refs[-5:]
+        x_ref[pl.ds(pl.multiple_of(ids[0] * local_rows, local_rows), local_rows)] = rows_ref[0]
+        for k in range(len(gots)):
+            first = pl.multiple_of((1 - ids[0]) * local_rows + k * piece, piece)
+            x_ref[pl.ds(first, piece)] = refs[6 + k][...]
+        for r in range(0, length, TILE):
+            rows = x_ref[r : r + TILE].astype(F32)
+            xn_ref[r : r + TILE] = (rows * rms_scale(rows) * gain_ref[...]).astype(BF)
+        for c in range(3):
+            for t in range(parts):
+                w = gathered_rows(ids, refs[2 * c : 2 * c + 2], gathered[c].order, t, height)
+                for r in range(0, length, TILE):
+                    made = dot_f32(xn_ref[r : r + TILE], w, 1, 0)
+                    if c == 0:
+                        made = made * HEAD_DIM ** (-0.5)
+                    qkv_ref[c, r : r + TILE, t * half : (t + 1) * half] = made.astype(BF)
+        store_transposed(ids, xn_ref[...], blocks_ref, xt_ref)
+
+    weights = [a for g in gathered for a in g.pair]
+    return call(
+        body,
+        "qkv",
+        ids,
+        (rows, gain, *weights, *gots),
+        [pl.BlockSpec((1, local_rows, width), lambda g, ids: (ids[0], 0, 0)), whole((1, width))]
+        + [whole(a.shape) for a in (*weights, *gots)],
+        (
+            shape((3, length, width), BF),
+            shape((fsdp, height, length), BF),
+            shape((length, width), BF),
+        ),
+        [whole((3, length, width)), whole((fsdp, height, length)), whole((length, width))],
+        (1,),
+        (pltpu.VMEM((length, width), BF), pltpu.VMEM((fsdp, height, length), BF)),
+    )
+
+
+def store_natural(value, out_ref):
+    height = out_ref.shape[-2]
+    step = 128 // height
+    for c in range(value.shape[1] // 128):
+        part = value[:, c * 128 : (c + 1) * 128]
+        out_ref[c * step : (c + 1) * step] = part.T.reshape(step, height, part.shape[0])
+
+
+def join_rows(ids, rows, got, fsdp):
+    parts, local_rows, width = rows.shape
+    length = parts * local_rows
+    height = width // fsdp
+
+    def body(ids, rows_ref, got_ref, out_ref, t_ref):
+        out_ref[0, pl.ds(pl.multiple_of(ids[0] * local_rows, local_rows), local_rows)] = rows_ref[
+            0
+        ]
+        out_ref[
+            0, pl.ds(pl.multiple_of((1 - ids[0]) * local_rows, local_rows), local_rows)
+        ] = got_ref[0]
+        store_natural(out_ref[0], t_ref.at[0])
+
+    spec = pl.BlockSpec((1, local_rows, width), lambda s, ids: (s ^ ids[0], 0, 0))
+    return call(
+        body,
+        "join_rows",
+        ids,
+        (rows, got),
+        [spec, spec],
+        (shape((parts, length, width), BF), shape((parts, fsdp, height, length), BF)),
+        [
+            pl.BlockSpec((1, length, width), lambda s, ids: (s, 0, 0)),
+            pl.BlockSpec((1, fsdp, height, length), lambda s, ids: (s, 0, 0, 0)),
+        ],
+        (parts,),
+    )
+
+
+def transposed(ids, rows, fsdp):
+    length, width = rows.shape
+    height = width // fsdp
+
+    def body(ids, rows_ref, t_ref):
+        store_natural(rows_ref[...], t_ref)
+
+    return call(
+        body,
+        "transposed",
+        ids,
+        (rows,),
+        [whole((length, width))],
+        (shape((fsdp, height, length), BF),),
+        [whole((fsdp, height, length))],
+        (1,),
+    )[0]
+
+
+def lane_mask(values, head):
+    lanes = lax.broadcasted_iota(jnp.int32, values.shape, 1)
+    return jnp.where(lanes // HEAD_DIM == head, values, jnp.zeros_like(values))
+
+
+def attend(ids, qkv):
+    length, width = qkv.shape[1:]
+    tiles = length // TILE
+    pair = 2 * HEAD_DIM
+    heads = width // HEAD_DIM
+
+    def body(ids, q_ref, k_ref, v_ref, *refs):
+        o_ref, ot_ref, e_ref, inv_ref, bias_ref, s_ref = refs[-6:]
+
+        @pl.when(pl.program_id(0) == 0)
+        def _():
+            for i in range(tiles):
+                keys = i * TILE + lax.broadcasted_iota(jnp.int32, (2 * TILE, TILE), 0)
+                rows = i * TILE + lax.broadcasted_iota(jnp.int32, (2 * TILE, TILE), 1)
+                seen = keys <= rows
+                for p in range(3):
+                    start = ids[4 + p]
+                    inside = (keys >= start) & (keys < start + PIECE)
+                    inside &= (rows >= start) & (rows < start + PIECE)
+                    seen |= inside
+                bias_ref[i] = jnp.where(seen, 0.0, masked_score)
+
+        k = k_ref[0]
+        vt = v_ref[0].T
+        for i in range(tiles):
+            used = min(i + 2, tiles)
+            q_rows = q_ref[0, i * TILE : (i + 1) * TILE]
+            parts = []
+            for head in range(2):
+                slot = (2 * i + head) % 2
+                q_head = lane_mask(q_rows, head)
+                top = None
+                for j in range(used):
+                    s = dot_f32(k[j * TILE : (j + 1) * TILE], q_head, 1, 1)
+                    if j >= i:
+                        s = s + bias_ref[i, (j - i) * TILE : (j - i + 1) * TILE]
+                    s_ref[slot, j] = s
+                    now = jnp.max(s.reshape(TILE // 8, 8, TILE), axis=0)
+                    top = now if top is None else jnp.maximum(top, now)
+                top = jnp.max(top, axis=0, keepdims=True)
+                total = None
+                out = None
+                for j in range(used):
+                    e = jnp.exp(s_ref[slot, j] - top)
+                    now = jnp.sum(e.reshape(TILE // 8, 8, TILE), axis=0)
+                    total = now if total is None else total + now
+                    low = e.astype(BF)
+                    e_ref[head, j * TILE : (j + 1) * TILE, i * TILE : (i + 1) * TILE] = low
+                    now = dot_f32(
+                        vt[head * HEAD_DIM : (head + 1) * HEAD_DIM, j * TILE : (j + 1) * TILE],
+                        low,
+                        1,
+                        0,
+                    )
+                    out = now if out is None else out + now
+                inv = 1.0 / jnp.sum(total, axis=0, keepdims=True)
+                inv_ref[0, head : head + 1, i * TILE : (i + 1) * TILE] = inv
+                parts.append(out * inv)
+            both = jnp.concatenate(parts, axis=0)
+            ot_ref[:, i * TILE : (i + 1) * TILE] = both.astype(BF)
+            o_ref[i * TILE : (i + 1) * TILE] = both.T.astype(BF)
+
+    spec = [
+        pl.BlockSpec((1, length, pair), lambda p, ids, c=c: (c, 0, p)) for c in range(3)
+    ]
+    return call(
+        body,
+        "attend",
+        ids,
+        (qkv, qkv, qkv),
+        spec,
+        (
+            shape((length, width), BF),
+            shape((width, length), BF),
+            shape((heads, length, length), BF),
+            shape((heads // 2, 2, length), F32),
+        ),
+        [
+            pl.BlockSpec((length, pair), lambda p, ids: (0, p)),
+            pl.BlockSpec((pair, length), lambda p, ids: (p, 0)),
+            pl.BlockSpec((2, length, length), lambda p, ids: (p, 0, 0)),
+            pl.BlockSpec((1, 2, length), lambda p, ids: (p, 0, 0)),
+        ],
+        (heads // 2,),
+        (
+            pltpu.VMEM((tiles, 2 * TILE, TILE), F32),
+            pltpu.VMEM((2, tiles, TILE, TILE), F32),
+        ),
+    )
+
+
+def attend_back(ids, qkv, d_heads, saved):
+    length, width = qkv.shape[1:]
+    tiles = length // TILE
+    pair = 2 * HEAD_DIM
+    heads = width // HEAD_DIM
+
+    def body(ids, q_ref, k_ref, v_ref, d_ref, ot_ref, e_ref, inv_ref, *refs):
+        out_ref, ds_ref, dq_ref = refs[-3:]
+        k = k_ref[0]
+        v = v_ref[0]
+        kt = k.T
+        dt = d_ref[...].astype(F32).T
+        q_heads = []
+        d_scaled = []
+        deltas = []
+        for head in range(2):
+            span = slice(head * HEAD_DIM, (head + 1) * HEAD_DIM)
+            inv_row = inv_ref[0, head : head + 1]
+            mine = dt[span] * inv_row
+            deltas.append(jnp.sum(mine * ot_ref[span].astype(F32), axis=0, keepdims=True))
+            blank = jnp.zeros((HEAD_DIM, length), BF)
+            mine = mine.astype(BF)
+            d_scaled.append(
+                jnp.concatenate([mine, blank] if head == 0 else [blank, mine], axis=0)
+            )
+            q_heads.append(lane_mask(q_ref[0], head))
+        dq_ref[...] = jnp.zeros_like(dq_ref)
+        for j in range(tiles):
+            keys = slice(j * TILE, (j + 1) * TILE)
+            first = max(j - 1, 0) * TILE
+            d_key = None
+            d_value = None
+            for head in range(2):
+                for r in range(first, length, TILE):
+                    cols = slice(r, r + TILE)
+                    dp = dot_f32(v[keys], d_scaled[head][:, cols], 1, 0)
+                    weights = e_ref[head, keys, cols].astype(F32)
+                    ds_ref[j % 2, head, :, cols] = (
+                        weights * (dp - deltas[head][:, cols])
+                    ).astype(BF)
+                ds = ds_ref[j % 2, head, :, first:length]
+                now = dot_f32(ds, q_heads[head][first:length], 1, 0)
+                d_key = now if d_key is None else d_key + now
+                now = dot_f32(
+                    e_ref[head, keys, first:length], d_scaled[head][:, first:length], 1, 1
+                )
+                d_value = now if d_value is None else d_value + now
+                rows = slice(head * HEAD_DIM, (head + 1) * HEAD_DIM)
+                dq_ref[rows, first:length] += dot_f32(kt[rows, keys], ds, 1, 0)
+            out_ref[1, keys] = d_key.astype(BF)
+            out_ref[2, keys] = d_value.astype(BF)
+        out_ref[0] = (dq_ref[...] * HEAD_DIM ** (-0.5)).T.astype(BF)
+
+    spec = [
+        pl.BlockSpec((1, length, pair), lambda p, ids, c=c: (c, 0, p)) for c in range(3)
+    ]
+    return call(
+        body,
+        "attend_back",
+        ids,
+        (qkv, qkv, qkv, d_heads, *saved),
+        spec
+        + [
+            pl.BlockSpec((length, pair), lambda p, ids: (0, p)),
+            pl.BlockSpec((pair, length), lambda p, ids: (p, 0)),
+            pl.BlockSpec((2, length, length), lambda p, ids: (p, 0, 0)),
+            pl.BlockSpec((1, 2, length), lambda p, ids: (p, 0, 0)),
+        ],
+        (shape((3, length, width), BF),),
+        [pl.BlockSpec((3, length, pair), lambda p, ids: (0, 0, p))],
+        (heads // 2,),
+        (pltpu.VMEM((2, 2, TILE, length), BF), pltpu.VMEM((pair, length), F32)),
+    )[0]
+
+
+def out_project(ids, attended, gathered, x, gain):
+    length, width = x.shape
+    fsdp = gathered.pair[0].shape[0]
+    height = width // fsdp
+    parts = 2
+    half = width // parts
+
+    def body(ids, a_ref, wa_ref, wb_ref, x_ref, gain_ref, hidden_ref, hn_ref, ht_ref):
+        w = [
+            gathered_rows(ids, (wa_ref, wb_ref), gathered.order, t, height) for t in range(parts)
+        ]
+        for r in range(0, length, TILE):
+            total = x_ref[r : r + TILE].astype(F32)
+            for t in range(parts):
+                total += dot_f32(a_ref[r : r + TILE, t * half : (t + 1) * half], w[t], 1, 1)
+            hidden_ref[r : r + TILE] = total
+            hn_ref[r : r + TILE] = (total * rms_scale(total) * gain_ref[...]).astype(BF)
+        store_natural(hn_ref[...], ht_ref)
+
+    return call(
+        body,
+        "out_project",
+        ids,
+        (attended, *gathered.pair, x, gain),
+        [whole((length, width))]
+        + [whole(a.shape) for a in gathered.pair]
+        + [whole((length, width)), whole((1, width))],
+        (
+            shape((length, width), F32),
+            shape((length, width), BF),
+            shape((fsdp, height, length), BF),
+        ),
+        [whole((length, width)), whole((length, width)), whole((fsdp, height, length))],
+        (1,),
+    )
+
+
+def feed_forward(ids, hn, grads, which, packed):
+    length, width = hn.shape
+    fsdp, rows, units = packed.shape
+    height = rows // 3
+    tile = 256
+
+    def body(ids, hn_ref, g_ref, w_ref, out_ref):
+        w_gate, w_up, w_down = [
+            w_ref[:, c * height : (c + 1) * height].reshape(width, tile) for c in range(3)
+        ]
+        for r in range(0, length, TILE):
+            rows = hn_ref[r : r + TILE]
+            gate = dot_f32(rows, w_gate, 1, 0)
+            up = dot_f32(rows, w_up, 1, 0)
+            d_mixed = dot_f32(g_ref[0, r : r + TILE], w_down, 1, 0)
+            sig = jax.nn.sigmoid(gate)
+            act = gate * sig
+            out_ref[0, r : r + TILE] = (
+                d_mixed * up * sig * (1.0 + gate * (1.0 - sig))
+            ).astype(BF)
+            out_ref[1, r : r + TILE] = (d_mixed * act).astype(BF)
+            out_ref[2, r : r + TILE] = (act * up).astype(BF)
+
+    return call(
+        body,
+        "feed_forward",
+        ids,
+        (hn, grads, packed),
+        [
+            whole((length, width)),
+            pl.BlockSpec((1, length, width), lambda n, ids: (which, 0, 0)),
+            pl.BlockSpec((fsdp, rows, tile), lambda n, ids: (0, 0, n)),
+        ],
+        (shape((3, length, units), BF),),
+        [pl.BlockSpec((3, length, tile), lambda n, ids: (0, 0, n))],
+        (units // tile,),
+    )[0]
+
+
+def feed_forward_out(ids, own, theirs, packed, hidden):
+    length, width = hidden.shape
+    fsdp, rows, units = packed.shape
+    height = rows // 3
+    per = units // UNITS
+    kept = length // 2
+
+    def body(ids, own_ref, theirs_ref, w_ref, hidden_ref, keep_ref, send_ref, acc_ref):
+        first = pl.program_id(1) == 0
+
+        @pl.when(first & (pl.program_id(0) == 0))
+        def _():
+            acc_ref[...] = hidden_ref[...]
+
+        @pl.when(first & (pl.program_id(0) == 1))
+        def _():
+            acc_ref[...] = jnp.zeros_like(acc_ref)
+
+        w = w_ref[...].reshape(width, UNITS)
+
+        def add(m_ref):
+            for r in range(0, length, TILE):
+                acc_ref[r : r + TILE] += dot_f32(m_ref[0, r : r + TILE], w, 1, 1)
+
+        pl.when(pl.program_id(0) == 0)(lambda: add(own_ref))
+        pl.when(pl.program_id(0) == 1)(lambda: add(theirs_ref))
+
+        @pl.when(pl.program_id(1) == per - 1)
+        def _():
+            keep_ref[0] = acc_ref[pl.ds(pl.multiple_of(ids[0] * kept, kept), kept)]
+            send_ref[0] = acc_ref[
+                pl.ds(pl.multiple_of((1 - ids[0]) * kept, kept), kept)
+            ].astype(BF)
+
+    out_spec = pl.BlockSpec((1, kept, width), lambda s, n, ids: (s ^ ids[0], 0, 0))
+    return call(
+        body,
+        "feed_forward_out",
+        ids,
+        (own, theirs, packed, hidden),
+        [
+            pl.BlockSpec((1, length, UNITS), lambda s, n, ids: (2, 0, jnp.where(s == 0, n, per - 1))),
+            pl.BlockSpec((1, length, UNITS), lambda s, n, ids: (2, 0, jnp.where(s == 1, n, 0))),
+            pl.BlockSpec((fsdp, height, UNITS), lambda s, n, ids: (0, 2, n)),
+            whole((length, width)),
+        ],
+        (shape((2, kept, width), F32), shape((2, kept, width), BF)),
+        [out_spec, out_spec],
+        (2, per),
+        (pltpu.VMEM((length, width), F32),),
+    )
+
+
+def feed_forward_grads(ids, hn_t, hn_t_theirs, grads_t, own, theirs):
+    fsdp, height, length = hn_t.shape
+    units = own.shape[2]
+    per = units // UNITS
+
+    def body(ids, h_ref, h2_ref, g_ref, own_ref, theirs_ref, out_ref):
+        def make(a_ref, b_ref):
+            for f in range(0, fsdp, 4):
+                a = a_ref[f : f + 4].reshape(4 * height, length)
+                b = b_ref[f : f + 4].reshape(4 * height, length)
+                made = dot_f32(a, own_ref[0], 1, 0) + dot_f32(b, theirs_ref[0], 1, 0)
+                out_ref[f : f + 4] = made.astype(BF).reshape(4, height, UNITS)
+
+        pl.when(pl.program_id(0) < 2)(lambda: make(h_ref, h2_ref))
+        pl.when(pl.program_id(0) == 2)(lambda: make(g_ref.at[0], g_ref.at[1]))
+
+    side = pl.BlockSpec((1, length, UNITS), lambda c, n, ids: (c, 0, n))
+    return call(
+        body,
+        "feed_forward_grads",
+        ids,
+        (hn_t, hn_t_theirs, grads_t, own, theirs),
+        [whole(hn_t.shape), whole(hn_t.shape), whole(grads_t.shape), side, side],
+        (shape((fsdp, 3 * height, units), BF),),
+        [pl.BlockSpec((fsdp, height, UNITS), lambda c, n, ids: (0, c, n))],
+        (3, per),
+    )[0]
+
+
+def weight_grad(ids, name, sources):
+    fsdp, height, length = sources[0][0].shape
+    parts = 2
+    half = sources[0][1].shape[2] // parts
+    tile = min(UNITS, half)
+    per = half // tile
+    hop = fsdp // 2
+
+    def body(ids, *refs):
+        outs = refs[-2:]
+        for k in range(len(sources)):
+            l_ref, r_ref = refs[2 * k : 2 * k + 2]
+
+            @pl.when(pl.program_id(0) == k)
+            def _(l_ref=l_ref, r_ref=r_ref):
+                right_tile = r_ref[0]
+                for b in range(0, fsdp, 4):
+                    block = l_ref[b : b + 4].reshape(4 * height, length)
+                    made = dot_f32(block, right_tile, 1, 0).astype(BF)
+                    outs[b // hop][0, b % hop : b % hop + 4] = made.reshape(4, height, tile)
+
+    ins, specs = [], []
+    for k, (left, right, index) in enumerate(sources):
+        ins += [left, right]
+
+        def columns(c, t, n, ids, k=k, index=index):
+            at = n * parts + t
+            at = jnp.where(c == k, at, 0 if k else half * parts // tile - 1)
+            return (index, 0, at)
+
+        specs += [whole(left.shape), pl.BlockSpec((1, length, tile), columns)]
+    spec = pl.BlockSpec((1, hop, height, tile), lambda c, t, n, ids: (t ^ ids[0], 0, c, n))
+    return call(
+        body,
+        name,
+        ids,
+        tuple(ins),
+        specs,
+        (shape((parts, hop, len(sources) * height, half), BF),) * 2,
+        [spec, spec],
+        (len(sources), parts, per),
+    )
+
+
+def feed_forward_back(ids, stacked, packed, cut=None):
+    length = stacked.shape[1]
+    fsdp, rows, units = packed.shape
+    height = rows // 3
+    width = fsdp * height
+    per = units // UNITS
+
+    def body(ids, d_ref, w_ref, *refs):
+        acc_ref = refs[-1]
+
+        @pl.when(pl.program_id(0) == 0)
+        def _():
+            acc_ref[...] = jnp.zeros_like(acc_ref)
+
+        w_gate, w_up = [
+            w_ref[:, c * height : (c + 1) * height].reshape(width, UNITS) for c in range(2)
+        ]
+        for r in range(0, length, TILE):
+            acc_ref[r : r + TILE] += dot_f32(d_ref[0, r : r + TILE], w_gate, 1, 1) + dot_f32(
+                d_ref[1, r : r + TILE], w_up, 1, 1
+            )
+
+        @pl.when(pl.program_id(0) == per - 1)
+        def _():
+            if cut is None:
+                refs[0][...] = acc_ref[...]
+            else:
+                refs[0][...] = acc_ref[:cut].astype(BF)
+                refs[1][...] = acc_ref[cut:].astype(BF)
+
+    outs = [shape((length, width), F32)]
+    if cut is not None:
+        outs = [shape((cut, width), BF), shape((length - cut, width), BF)]
+    return call(
+        body,
+        "feed_forward_back",
+        ids,
+        (stacked, packed),
+        [
+            pl.BlockSpec((2, length, UNITS), lambda n, ids: (0, 0, n)),
+            pl.BlockSpec((fsdp, 2 * height, UNITS), lambda n, ids: (0, 0, n)),
+        ],
+        tuple(outs),
+        [whole(o.shape) for o in outs],
+        (per,),
+        (pltpu.VMEM((length, width), F32),),
+    )
+
+
+def norm_and_project_back(ids, share, gots, hidden, grads, gain, gathered):
+    length, width = hidden.shape
+    fsdp = gathered.pair[0].shape[0]
+    height = width // fsdp
+    parts = 2
+    half = width // parts
+
+    cut = gots[0].shape[0]
+
+    def body(ids, share_ref, got_ref, tail_ref, hidden_ref, g_ref, gain_ref, wa_ref, wb_ref, *refs):
+        dh_ref, lt_ref, out_ref, low_ref = refs
+        for r in range(0, length, TILE):
+            rows = hidden_ref[r : r + TILE]
+            scale = rms_scale(rows)
+            normed = rows * scale
+            theirs = got_ref[r : r + TILE] if r < cut else tail_ref[r - cut : r - cut + TILE]
+            d_normed = share_ref[r : r + TILE] + theirs.astype(F32)
+            dh = g_ref[0, r : r + TILE].astype(F32) + norm_backward_pass(
+                d_normed, normed, scale, gain_ref[...]
+            )
+            dh_ref[r : r + TILE] = dh
+            low_ref[r : r + TILE] = dh.astype(BF)
+        for t in range(parts):
+            w = gathered_rows(ids, (wa_ref, wb_ref), gathered.order, t, height)
+            for r in range(0, length, TILE):
+                out_ref[r : r + TILE, t * half : (t + 1) * half] = dot_f32(
+                    low_ref[r : r + TILE], w, 1, 0
+                ).astype(BF)
+        store_natural(low_ref[...], lt_ref)
+
+    square = whole((length, width))
+    return call(
+        body,
+        "norm_and_project_back",
+        ids,
+        (share, *gots, hidden, grads, gain, *gathered.pair),
+        [
+            square,
+            *[whole(g.shape) for g in gots],
+            square,
+            pl.BlockSpec((1, length, width), lambda g, ids: (0, 0, 0)),
+            whole((1, width)),
+        ]
+        + [whole(a.shape) for a in gathered.pair],
+        (
+            shape((length, width), F32),
+            shape((fsdp, height, length), BF),
+            shape((length, width), BF),
+        ),
+        [square, whole((fsdp, height, length)), square],
+        (1,),
+        (pltpu.VMEM((length, width), BF),),
+    )
+
+
+def out_grad_halves(ids, left, right):
+    fsdp, height, length = left.shape
+    half = right.shape[1] // 2
+
+    def body(ids, l_ref, r_ref, keep_ref, send_ref):
+        def make(out_ref):
+            for f in range(0, fsdp, 4):
+                a = l_ref[f : f + 4].reshape(4 * height, length)
+                out_ref[f : f + 4] = (
+                    dot_f32(a, r_ref[...], 1, 0).astype(BF).reshape(4, height, half)
+                )
+
+        pl.when(pl.program_id(0) == 0)(lambda: make(send_ref))
+        pl.when(pl.program_id(0) == 1)(lambda: make(keep_ref))
+
+    blocks = whole((fsdp, height, half))
+    return call(
+        body,
+        "grad_out",
+        ids,
+        (left, right),
+        [whole(left.shape), pl.BlockSpec((length, half), lambda s, ids: (0, (1 - s) ^ ids[0]))],
+        (shape((fsdp, height, half), BF),) * 2,
+        [blocks, blocks],
+        (2,),
+    )
+
+
+def store_lines(out_ref, values):
+    lines = values.shape[1] // 128
+    for n in range(lines):
+        out_ref[0, pl.ds(n, values.shape[0], stride=lines)] = values[:, n * 128 : (n + 1) * 128]
+
+
+def qkv_back(ids, d_qkv, gathered, x, dh, gain, sent):
+    length, width = x.shape
+    fsdp = gathered[1].pair[0].shape[0]
+    height = width // fsdp
+    parts = 2
+    half = width // parts
+    kept = length // parts
+
+    def body(ids, d_ref, *refs):
+        x_ref, dh_ref, gain_ref, out_ref, acc_ref = refs[-5:]
+        for c in range(3):
+            for t in range(parts):
+                w = gathered_rows(ids, refs[2 * c : 2 * c + 2], gathered[c].order, t, height)
+                for r in range(0, kept, TILE):
+                    part = dot_f32(d_ref[c, r : r + TILE, t * half : (t + 1) * half], w, 1, 1)
+                    if c == 0 and t == 0:
+                        acc_ref[r : r + TILE] = part
+                    else:
+                        acc_ref[r : r + TILE] += part
+        for r in range(0, kept, TILE):
+            rows = x_ref[r : r + TILE].astype(F32)
+            scale = rms_scale(rows)
+            normed = rows * scale
+            d_normed = acc_ref[r : r + TILE]
+            acc_ref[r : r + TILE] = dh_ref[r : r + TILE] + norm_backward_pass(
+                d_normed, normed, scale, gain_ref[...]
+            )
+        if sent:
+            out_ref[...] = acc_ref[...].astype(BF)
+        else:
+            store_lines(out_ref, acc_ref)
+
+    def rows(ids):
+        return 1 - ids[0] if sent else ids[0]
+
+    weights = [a for g in gathered for a in g.pair]
+    lines = kept * width // 128
+    return call(
+        body,
+        "qkv_back",
+        ids,
+        (d_qkv, *weights, x, dh, gain),
+        [pl.BlockSpec((3, kept, width), lambda g, ids: (0, rows(ids), 0))]
+        + [whole(a.shape) for a in weights]
+        + [pl.BlockSpec((kept, width), lambda g, ids: (rows(ids), 0))] * 2
+        + [whole((1, width))],
+        (shape((kept, width), BF) if sent else shape((parts, lines, 128), F32),),
+        [
+            whole((kept, width))
+            if sent
+            else pl.BlockSpec((1, lines, 128), lambda g, ids: (ids[0], 0, 0)),
+        ],
+        (1,),
+        (pltpu.VMEM((kept, width), F32),),
+    )[0]
+
+
+def place_rows(ids, got, lines):
+    kept, width = got.shape
+
+    def body(ids, got_ref, _, out_ref, wide_ref):
+        wide_ref[...] = got_ref[...].astype(F32)
+        store_lines(out_ref, wide_ref)
+
+    return call(
+        body,
+        "place_rows",
+        ids,
+        (got, lines),
+        [whole((kept, width)), IN_PLACE],
+        (shape(lines.shape, F32),),
+        [pl.BlockSpec((1,) + lines.shape[1:], lambda g, ids: (1 - ids[0], 0, 0))],
+        (1,),
+        (pltpu.VMEM((kept, width), F32),),
+        aliases={2: 0},
+    )[0]
+
+
+def three_parts(values):
+    high = values.astype(BF)
+    rest = values - high.astype(F32)
+    middle = rest.astype(BF)
+    return jnp.stack([high, middle, (rest - middle.astype(F32)).astype(BF)], -1)
+
+
+def local_sequence(
+    tokens, piece_starts, gain_attn, w_qkv, w_out, gain_mlp, w_gate_up, w_down, out_grad
+):
+    fsdp = lax.axis_size("fsdp")
+    parts = lax.axis_size("tensor")
+    me_f = lax.axis_index("fsdp")
+    me_t = lax.axis_index("tensor")
+    local_rows = tokens.shape[1]
+    height = w_qkv.shape[1]
+    half = w_qkv.shape[2]
+    share = gain_attn.shape[0]
+
+    starts = lax.dynamic_index_in_dim(piece_starts, me_t, 0, keepdims=False)[0]
+    ids = jnp.stack([me_t, me_f // 2, me_f % 2, me_f]).astype(jnp.int32)
+    ids = jnp.concatenate([ids, starts])
+    rows_in = tokens.reshape(parts, local_rows, D)
+    grads_in = out_grad.reshape(parts, local_rows, D)
+
+    def other(rows):
+        return lax.dynamic_index_in_dim(rows, 1 - me_t, 0, keepdims=False)
+
+    wk = Gathered(w_qkv[1], (TENSOR, Z_FAR, X, Z_NEAR))
+    wv = Gathered(w_qkv[2], (TENSOR, Z_NEAR, Z_FAR, X))
+    gains = three_parts(jnp.stack([gain_attn, gain_mlp])).reshape(1, -1)
+    gains = jnp.pad(gains, ((0, 7), (0, half - gains.shape[1])))
+    wq = Gathered(jnp.concatenate([w_qkv[0], gains]), (Z_FAR, X, Z_NEAR, TENSOR))
+    o_mine = w_out.T
+    ff_mine = jnp.concatenate([w_gate_up.reshape(2 * height, -1), w_down.T])
+    aways = jnp.split(other(rows_in), 2)
+    three = [wq, wk, wv]
+    o_mine = after(o_mine, three)
+    wo = Gathered(o_mine, (Z_FAR, TENSOR, Z_NEAR, X))
+    got_one = swap(aways[0], TENSOR)
+    got_one, aways[1] = after((got_one, aways[1]), [*three, wo])
+    got_two = swap(aways[1], TENSOR)
+    got_two = after(got_two, [*three, wo])
+    ff_mine = after(ff_mine, [*three, wo])
+    packed = lax.all_gather(ff_mine, "fsdp", axis=0, tiled=False)
+    got_rows = after((got_one, got_two), three)
+
+    each = jnp.arange(fsdp * parts)
+    each_f, each_t = each // parts, each % parts
+    at = position(wq.order, each_f, each_t) ^ position(wq.order, me_f, me_t)
+    at = at + fsdp * ((each_f ^ me_f) % 2)
+    gains = jnp.concatenate([a[:, height, : 6 * share] for a in wq.pair])[at]
+    gains = jnp.sum(gains.reshape(fsdp * parts, 2, share, 3).astype(F32), axis=3)
+    gain_one, gain_two = [gains[:, i].reshape(1, D) for i in range(2)]
+
+    qkv, xt, x = make_qkv(ids, rows_in, got_rows, gain_one, (wq, wk, wv))
+    _, away = lax.optimization_barrier((got_rows, grads_in))
+    got_grads = swap(away, TENSOR)
+    qkv = after(qkv, [wo])
+    attended, *saved = after(attend(ids, qkv), [wo])
+    hidden, hn, ht = out_project(ids, attended, wo, x, gain_two)
+    hn_theirs = swap(hn, TENSOR)
+    grads, gt = join_rows(ids, grads_in, got_grads, fsdp)
+    hn, grads, packed = lax.optimization_barrier((hn, grads, packed))
+
+    own = feed_forward(ids, hn, grads, 0, packed)
+    own, hn_theirs = lax.optimization_barrier((own, hn_theirs))
+    theirs = feed_forward(ids, hn_theirs, grads, 1, packed)
+    ht_theirs = transposed(ids, hn_theirs, fsdp)
+    *d_theirs, = feed_forward_back(ids, theirs, packed, local_rows * parts * 3 // 4)
+    d_theirs, ht_theirs, own = lax.optimization_barrier((d_theirs, ht_theirs, own))
+    got_one = swap(d_theirs[0], TENSOR)
+    made = feed_forward_grads(ids, ht, ht_theirs, gt, own, theirs)
+    made, own, got_one, d_tail = lax.optimization_barrier((made, own, got_one, d_theirs[1]))
+    summed = lax.psum_scatter(made, "fsdp", scatter_dimension=0, tiled=False)
+    got_two = swap(d_tail, TENSOR)
+    share_own = feed_forward_back(ids, own, packed)[0]
+    share_own, got_two = lax.optimization_barrier((share_own, got_two))
+    dh, dt, d_attended = norm_and_project_back(
+        ids, share_own, (got_one, got_two), hidden, grads, gain_two, wo
+    )
+
+    def join(values, sums):
+        values, gots = lax.optimization_barrier((values, [s.got for s in sums]))
+        for s, g in zip(sums, gots):
+            s.got = g
+        made = halve(ids, sums)
+        return lax.optimization_barrier((values, made))[0]
+
+    o_keep, o_send = out_grad_halves(ids, dt, attended)
+    o_send, d_attended, own, theirs = lax.optimization_barrier((o_send, d_attended, own, theirs))
+    o_got = swap(o_send, TENSOR)
+    keep_out, send_out = feed_forward_out(ids, own, theirs, packed, hidden)
+    d_attended, send_out, o_got = lax.optimization_barrier((d_attended, send_out, o_got))
+    o_sum = (o_keep.astype(F32) + o_got.astype(F32)).astype(BF)
+    got_out = swap(send_out, TENSOR)
+    d_qkv = attend_back(ids, qkv, d_attended, saved)
+
+    orders = (
+        (X, Z_NEAR, Z_FAR, TENSOR),
+        (Z_NEAR, X, TENSOR, Z_FAR),
+        (TENSOR, Z_FAR, X, Z_NEAR),
+    )
+    sums = []
+    for c, order in enumerate(orders):
+        made = weight_grad(ids, "grad_qkv", [(xt, d_qkv, c)])
+        made, d_qkv = lax.optimization_barrier((made, d_qkv))
+        sums.append(Summed(*made, order))
+    d_qkv = join(d_qkv, sums)
+    sent = qkv_back(ids, d_qkv, (wq, wk, wv), x, dh, gain_one, True)
+    sent, d_qkv, got_out, summed, o_sum = join((sent, d_qkv, got_out, summed, o_sum), sums)
+    o_sum = lax.psum_scatter(o_sum, "fsdp", scatter_dimension=0, tiled=False)
+    layer_out = (keep_out + got_out.astype(F32)).astype(BF).reshape(tokens.shape)
+    got_grad = swap(sent, TENSOR)
+    lines = qkv_back(ids, d_qkv, (wq, wk, wv), x, dh, gain_one, False)
+    lines = join(lines, sums)
+    halve(ids, sums)
+    halve(ids, sums)
+
+    input_grad = place_rows(ids, got_grad, lines).reshape(tokens.shape)
+    qkv_grad = jnp.stack([s.result for s in sums])
+    summed = summed.astype(F32)
+    gate_up_grad = summed[: 2 * height].reshape(w_gate_up.shape)
+    from_qkv = jnp.sum(w_qkv.astype(F32) * qkv_grad, axis=(0, 2))
+    from_gate_up = jnp.sum(w_gate_up.astype(F32) * gate_up_grad, axis=(0, 2))
+    both = jnp.stack([from_qkv, from_gate_up]).reshape(2, parts, share)
+    mine = lax.dynamic_index_in_dim(both, me_t, 1, keepdims=False)
+    theirs = lax.dynamic_index_in_dim(both, 1 - me_t, 1, keepdims=False)
+    mine = mine + swap(theirs, TENSOR)
+    return (
+        layer_out,
+        input_grad,
+        mine[0] / gain_attn,
+        qkv_grad,
+        o_sum.astype(F32).T,
+        mine[1] / gain_mlp,
+        gate_up_grad,
+        summed[2 * height :].T,
+    )
+
+
+def local_any(tokens, *rest):
+    sizes = (lax.axis_size("tensor"), tokens.shape[0], tokens.shape[2], lax.axis_size("fsdp"))
+    if sizes == (2, 2, 1, 16):
+        return local_sequence(tokens, *rest)
+    return local(tokens, *rest)
+
+
 def solution(mesh):
     return jax.shard_map(
-        local,
+        local_any,
         mesh=mesh,
         in_specs=(
             P(None, "tensor", "fsdp", None),

time: 1480 us -> 513 us (0.35)
  waiting for transfers between devices: 783 us -> 83.7 us
  matrix products: 400 us -> 0 us
  Pallas kernels: 0 us -> 318 us
  other arithmetic: 121 us -> 20.8 us
  blocking collectives: 69.7 us -> 0 us
  local copies, waits for them, and re-layouts: 76.2 us -> 19.2 us
  starting transfers between devices: 1.78 us -> 46.8 us
    dot_general x48 -> x0, matrix products: 400 us -> none  [the longest x4 51.1 us: attend_backward(): jnp.einsum('qhd,khd->hqk', block_d, values_all, preferred_element_type=jn...]
    all_gather x12 -> x1, waiting for transfers between devices: 338 us -> 11.4 us  [local_sequence(): packed = lax.all_gather(ff_mine, 'fsdp', axis=0, tiled=False)]
    pallas_call x0 -> x25, Pallas kernels: none -> 318 us  [call(): pl.pallas_call(body, name=name, out_shape=outs, grid_spec=pltpu.PrefetchS...]
    unnamed x28 -> x3, waiting for transfers between devices: 240 us -> 0.05 us
    reduce_scatter x10 -> x2, waiting for transfers between devices: 205 us -> 8.03 us  [the longest x1 8.03 us: local_sequence(): o_sum = lax.psum_scatter(o_sum, 'fsdp', scatter_dimension=0, tiled=False)]
    convert_element_type x10 -> x4, other arithmetic: 74.8 us -> 2.86 us  [the longest x1 1.34 us: local_sequence(): o_sum = (o_keep.astype(F32) + o_got.astype(F32)).astype(BF)]
    all_gather x1 -> x0, blocking collectives: 69.7 us -> none  [local(): lax.all_gather(jnp.stack([gain_attn, gain_mlp]), ('fsdp', 'tensor'), axis...]
    ppermute x0 -> x45, waiting for transfers between devices: none -> 64.2 us  [the longest x28 33.4 us: swap(): lax.ppermute(value, 'fsdp', [(i, i ^ bit) for i in range(lax.axis_size('f...]
  transfers between devices with their start and end apart: 25 -> 48, of which waited for: 19 -> 19; matrix products, arithmetic and copies ran while one was open for 34% -> 5% of each run, Pallas kernels for 0% -> 55%
where the time goes in v2:
time: 513 us; the launch traced here: 503 us
  Pallas kernels  318 us (62%)
  waiting for transfers between devices  83.7 us (16%)
  starting transfers between devices  46.8 us (9%)
  other arithmetic  20.8 us (4%)
  local copies, waits for them, and re-layouts  19.2 us (4%)
  between operations  14.7 us (3%)
    pallas_call x25, Pallas kernels, call(): pl.pallas_call(body, name=name, out_shape=outs, grid_spec=pltpu.PrefetchS...  318 us
    ppermute x28, waiting for transfers between devices, swap(): lax.ppermute(value, 'fsdp', [(i, i ^ bit) for i in range(lax.axis_size('f...  33.4 us
    ppermute x17, waiting for transfers between devices, swap(): return lax.ppermute(value, 'tensor', [(0, 1), (1, 0)])  30.8 us
    ppermute x28, starting transfers between devices, swap(): lax.ppermute(value, 'fsdp', [(i, i ^ bit) for i in range(lax.axis_size('f...  27.9 us
    ppermute x17, starting transfers between devices, swap(): return lax.ppermute(value, 'tensor', [(0, 1), (1, 0)])  18.8 us
    unnamed x92, local copies, waits for them, and re-layouts  11.8 us
    all_gather x1, waiting for transfers between devices, local_sequence(): packed = lax.all_gather(ff_mine, 'fsdp', axis=0, tiled=False)  11.4 us
  transfers between devices with their start and end apart: 48, of which 19 were waited for; matrix products, arithmetic and copies ran while one was open for 5% of the time, Pallas kernels for 55%

profile of v2, /device:TPU:0, one launch (start us, length us, event | category | flops | bytes accessed | tf_op | source)
XLA Modules:
  0.0 503.5 jit_solution(15649943629465654344)
XLA Ops:
  8.2 3.0 collective-permute-start.1
  12.9 3.1 collective-permute-start
  18.9 2.5 collective-permute-start.5
  23.0 2.2 collective-permute-start.6
  25.3 5.4 %collective-permute-done.7 = bf16[64,512]{1,0:T(8,128)(2,1)S(1)} collective-permute-done((bf16[64,512]{1,0:T(8,128)(2,1)S(1)}, bf16[64,512]{1,0:T(8,128)(2,1)S(1)}, u32[]{:S(2)}, u32[]{:S(2)}) %collective-permute-start.7) | collective-permute-done | bytes 65568 | tf_op jit(solution)/shard_map/ppermute | solution.py:363
  37.2 7.7 %collective-permute-done.12 = bf16[2,64,512]{2,1,0:T(8,128)(2,1)S(1)} collective-permute-done((bf16[2,64,512]{2,1,0:T(8,128)(2,1)S(1)}, bf16[2,64,512]{2,1,0:T(8,128)(2,1)S(1)}, u32[]{:S(2)}, u32[]{:S(2)}) %collective-permute-start.12) | collective-permute-done | bytes 131104 | tf_op jit(solution)/shard_map/ppermute | solution.py:362
  44.9 2.2 collective-permute-done.11
  53.6 12.4 %collective-permute-done.16 = bf16[2,2,64,512]{3,2,1,0:T(8,128)(2,1)} collective-permute-done((bf16[2,2,64,512]{3,2,1,0:T(8,128)(2,1)S(1)}, bf16[2,2,64,512]{3,2,1,0:T(8,128)(2,1)}, u32[]{:S(2)}, u32[]{:S(2)}) %collective-permute-start.16) | collective-permute-done | bytes 262176 | tf_op jit(solution)/shard_map/ppermute | solution.py:363
  71.2 2.0 fusion.29
  76.7 15.4 %qkv.1 = (bf16[3,1024,1024]{2,1,0:T(8,128)(2,1)}, bf16[16,64,1024]{2,1,0:T(8,128)(2,1)}, bf16[1024,1024]{1,0:T(8,128)(2,1)}) custom-call(s32[7]{0:T(128)} %concatenate.37.ids, bf16[2,512,1024]{2,1,0:T(8,128)(2,1)} %bitcast.149, f32[1,1024]{1,0:T(1,128)} %reshape_squeeze.6.gain_ref.refs_8_, bf16[16,72,512]{2,1,0:T(8,128)(2,1)} %bitcast.137, ...), custom_call_target="tpu_custom_call" | custom-call | flops 1024 | bytes 1024 | tf_op jit(solution)/shard_map/qkv/pallas_call | solution.py:309
  97.3 41.0 %attend.1 = (bf16[1024,1024]{1,0:T(8,128)(2,1)}, bf16[1024,1024]{1,0:T(8,128)(2,1)}, bf16[16,1024,1024]{2,1,0:T(8,128)(2,1)}, f32[8,2,1024]{2,1,0:T(2,128)}) custom-call(s32[7]{0:T(128)} %concatenate.37.ids, bf16[3,1024,1024]{2,1,0:T(8,128)(2,1)} %get-tuple-element.162.q_ref.k_ref.v_ref, bf16[3,1024,1024]{2,1,0:T(8,128)(2,1)} %get-tuple-element.162.q_ref.k_ref.v_ref, ...), custom_call_target="tpu_custom_call" | custom-call | flops 1024 | bytes 1024 | tf_op jit(solution)/shard_map/attend/pallas_call | solution.py:309
  139.3 9.3 %out_project.1 = (f32[1024,1024]{1,0:T(8,128)}, bf16[1024,1024]{1,0:T(8,128)(2,1)}, bf16[16,64,1024]{2,1,0:T(8,128)(2,1)}) custom-call(s32[7]{0:T(128)} %concatenate.37.ids, bf16[1024,1024]{1,0:T(8,128)(2,1)} %get-tuple-element.168.a_ref.r_ref, bf16[16,64,512]{2,1,0:T(8,128)(2,1)} %bitcast.147, bf16[16,64,512]{2,1,0:T(8,128)(2,1)} %bitcast.154, ...), custom_call_target="tpu_custom_call" | custom-call | flops 1024 | bytes 1024 | tf_op jit(solution)/shard_map/out_project/pallas_call | solution.py:309
  150.4 5.7 %join_rows.1 = (bf16[2,1024,1024]{2,1,0:T(8,128)(2,1)}, bf16[2,16,64,1024]{3,2,1,0:T(8,128)(2,1)}) custom-call(s32[7]{0:T(128)} %concatenate.37.ids, bf16[2,512,1024]{2,1,0:T(8,128)(2,1)} %bitcast.158, bf16[2,512,1024]{2,1,0:T(8,128)(2,1)} %copy-done.21), custom_call_target="tpu_custom_call" | custom-call | flops 1024 | bytes 1024 | tf_op jit(solution)/shard_map/join_rows/pallas_call | solution.py:309
  156.1 11.4 %all-gather.3.cloned.1.call-done = bf16[3072,2048]{1,0:T(8,128)(2,1)} async-done(((bf16[192,2048]{1,0:T(8,128)(2,1)}), bf16[3072,2048]{1,0:T(8,128)(2,1)}) %all-gather.3.cloned.1.call-update) | async-done | bytes 12582928 | tf_op jit(solution)/shard_map/all_gather | solution.py:1218
  167.5 20.2 %feed_forward.2.own_ref.d_ref = bf16[3,1024,2048]{2,1,0:T(8,128)(2,1)} custom-call(s32[7]{0:T(128)} %concatenate.37.ids, bf16[1024,1024]{1,0:T(8,128)(2,1)} %get-tuple-element.176.hn_ref, bf16[2,1024,1024]{2,1,0:T(8,128)(2,1)} %get-tuple-element.177.g_ref, bf16[16,192,2048]{2,1,0:T(8,128)(2,1)} %bitcast.116), custom_call_target="tpu_custom_call" | custom-call | flops 1024 | bytes 1024 | tf_op jit(solution)/shard_map/feed_forward/pallas_call | solution.py:309
  187.7 8.8 %collective-permute-done.23.hn_ref.rows_ref = bf16[1024,1024]{1,0:T(8,128)(2,1)S(1)} collective-permute-done((bf16[1024,1024]{1,0:T(8,128)(2,1)}, bf16[1024,1024]{1,0:T(8,128)(2,1)S(1)}, u32[]{:S(2)}, u32[]{:S(2)}) %collective-permute-start.23) | collective-permute-done | bytes 2097184 | tf_op jit(solution)/shard_map/ppermute | solution.py:362
  197.8 20.6 %feed_forward.3.d_ref.theirs_ref = bf16[3,1024,2048]{2,1,0:T(8,128)(2,1)} custom-call(s32[7]{0:T(128)} %concatenate.37.ids, bf16[1024,1024]{1,0:T(8,128)(2,1)} %copy-done.12, bf16[2,1024,1024]{2,1,0:T(8,128)(2,1)} %get-tuple-element.177.g_ref, bf16[16,192,2048]{2,1,0:T(8,128)(2,1)} %bitcast.117), custom_call_target="tpu_custom_call" | custom-call | flops 1024 | bytes 1024 | tf_op jit(solution)/shard_map/feed_forward/pallas_call | solution.py:309
  218.3 4.2 transposed.1.h2_ref
  222.5 14.3 %feed_forward_back.2 = (bf16[768,1024]{1,0:T(8,128)(2,1)}, bf16[256,1024]{1,0:T(8,128)(2,1)}) custom-call(s32[7]{0:T(128)} %concatenate.37.ids, bf16[3,1024,2048]{2,1,0:T(8,128)(2,1)} %feed_forward.3.d_ref.theirs_ref, bf16[16,192,2048]{2,1,0:T(8,128)(2,1)} %bitcast.118), custom_call_target="tpu_custom_call" | custom-call | flops 1024 | bytes 1024 | tf_op jit(solution)/shard_map/feed_forward_back/pallas_call | solution.py:309
  237.4 34.4 %feed_forward_grads.1 = bf16[16,192,2048]{2,1,0:T(8,128)(2,1)} custom-call(s32[7]{0:T(128)} %concatenate.37.ids, bf16[16,64,1024]{2,1,0:T(8,128)(2,1)} %get-tuple-element.171.h_ref, bf16[16,64,1024]{2,1,0:T(8,128)(2,1)} %transposed.1.h2_ref, bf16[2,16,64,1024]{3,2,1,0:T(8,128)(2,1)} %get-tuple-element.184.g_ref, ...), custom_call_target="tpu_custom_call" | custom-call | flops 1024 | bytes 1024 | tf_op jit(solution)/shard_map/feed_forward_grads/pallas_call | solution.py:309
  274.5 15.9 %feed_forward_back.3.share_ref = f32[1024,1024]{1,0:T(8,128)} custom-call(s32[7]{0:T(128)} %concatenate.37.ids, bf16[3,1024,2048]{2,1,0:T(8,128)(2,1)} %feed_forward.2.own_ref.d_ref, bf16[16,192,2048]{2,1,0:T(8,128)(2,1)} %bitcast.119), custom_call_target="tpu_custom_call" | custom-call | flops 1024 | bytes 1024 | tf_op jit(solution)/shard_map/feed_forward_back/pallas_call | solution.py:309
  291.2 12.8 %norm_and_project_back.1 = (f32[1024,1024]{1,0:T(8,128)}, bf16[16,64,1024]{2,1,0:T(8,128)(2,1)}, bf16[1024,1024]{1,0:T(8,128)(2,1)}) custom-call(s32[7]{0:T(128)} %concatenate.37.ids, f32[1024,1024]{1,0:T(8,128)} %feed_forward_back.3.share_ref, bf16[768,1024]{1,0:T(8,128)(2,1)} %copy-done.24, bf16[256,1024]{1,0:T(8,128)(2,1)} %copy-done.35, ...), custom_call_target="tpu_custom_call" | custom-call | flops 1024 | bytes 1024 | tf_op jit(solution)/shard_map/norm_and_project_back/pallas_call | solution.py:309
  304.0 6.8 %grad_out.1 = (bf16[16,64,512]{2,1,0:T(8,128)(2,1)}, bf16[16,64,512]{2,1,0:T(8,128)(2,1)}) custom-call(s32[7]{0:T(128)} %concatenate.37.ids, bf16[16,64,1024]{2,1,0:T(8,128)(2,1)} %get-tuple-element.194.l_ref, bf16[1024,1024]{1,0:T(8,128)(2,1)} %get-tuple-element.168.a_ref.r_ref), custom_call_target="tpu_custom_call" | custom-call | flops 1024 | bytes 1024 | tf_op jit(solution)/shard_map/grad_out/pallas_call | solution.py:309
  310.8 1.8 collective-permute-start.26
  312.6 19.3 %feed_forward_out.1 = (f32[2,512,1024]{2,1,0:T(8,128)}, bf16[2,512,1024]{2,1,0:T(8,128)(2,1)}) custom-call(s32[7]{0:T(128)} %concatenate.37.ids, bf16[3,1024,2048]{2,1,0:T(8,128)(2,1)} %feed_forward.2.own_ref.d_ref, bf16[3,1024,2048]{2,1,0:T(8,128)(2,1)} %feed_forward.3.d_ref.theirs_ref, bf16[16,192,2048]{2,1,0:T(8,128)(2,1)} %bitcast.120, ...), custom_call_target="tpu_custom_call" | custom-call | flops 1024 | bytes 1024 | tf_op jit(solution)/shard_map/feed_forward_out/pallas_call | solution.py:309
  331.9 4.2 collective-permute-done.26
  336.4 36.3 %attend_back.1.refs_1_.d_ref = bf16[3,1024,1024]{2,1,0:T(8,128)(2,1)} custom-call(s32[7]{0:T(128)} %concatenate.37.ids, bf16[3,1024,1024]{2,1,0:T(8,128)(2,1)} %get-tuple-element.162.q_ref.k_ref.v_ref, bf16[3,1024,1024]{2,1,0:T(8,128)(2,1)} %get-tuple-element.162.q_ref.k_ref.v_ref, bf16[3,1024,1024]{2,1,0:T(8,128)(2,1)} %get-tuple-element.162.q_ref.k_ref.v_ref, ...), custom_call_target="tpu_custom_call" | custom-call | flops 1024 | bytes 1024 | tf_op jit(solution)/shard_map/attend_back/pallas_call | solution.py:309
  372.7 5.9 %grad_qkv.3 = (bf16[2,8,64,512]{3,2,1,0:T(8,128)(2,1)}, bf16[2,8,64,512]{3,2,1,0:T(8,128)(2,1)}) custom-call(s32[7]{0:T(128)} %concatenate.37.ids, bf16[16,64,1024]{2,1,0:T(8,128)(2,1)} %get-tuple-element.200.refs_0_, bf16[3,1024,1024]{2,1,0:T(8,128)(2,1)} %attend_back.1.refs_1_.d_ref), custom_call_target="tpu_custom_call" | custom-call | flops 1024 | bytes 1024 | tf_op jit(solution)/shard_map/grad_qkv/pallas_call | solution.py:309
  378.6 5.9 %grad_qkv.4 = (bf16[2,8,64,512]{3,2,1,0:T(8,128)(2,1)}, bf16[2,8,64,512]{3,2,1,0:T(8,128)(2,1)}) custom-call(s32[7]{0:T(128)} %concatenate.37.ids, bf16[16,64,1024]{2,1,0:T(8,128)(2,1)} %get-tuple-element.200.refs_0_, bf16[3,1024,1024]{2,1,0:T(8,128)(2,1)} %attend_back.1.refs_1_.d_ref), custom_call_target="tpu_custom_call" | custom-call | flops 1024 | bytes 1024 | tf_op jit(solution)/shard_map/grad_qkv/pallas_call | solution.py:309
  384.6 6.1 %grad_qkv.5 = (bf16[2,8,64,512]{3,2,1,0:T(8,128)(2,1)}, bf16[2,8,64,512]{3,2,1,0:T(8,128)(2,1)}) custom-call(s32[7]{0:T(128)} %concatenate.37.ids, bf16[16,64,1024]{2,1,0:T(8,128)(2,1)} %get-tuple-element.200.refs_0_, bf16[3,1024,1024]{2,1,0:T(8,128)(2,1)} %attend_back.1.refs_1_.d_ref), custom_call_target="tpu_custom_call" | custom-call | flops 1024 | bytes 1024 | tf_op jit(solution)/shard_map/grad_qkv/pallas_call | solution.py:309
  391.3 3.2 collective-permute-done.29.refs_5_.refs_7_.refs_9_.refs_11_.refs_13_
  396.0 6.5 %halve.5 = (bf16[2,2,2,64,512]{4,3,2,1,0:T(8,128)(2,1)}, bf16[2,2,2,64,512]{4,3,2,1,0:T(8,128)(2,1)}, bf16[2,2,2,64,512]{4,3,2,1,0:T(8,128)(2,1)}) custom-call(s32[7]{0:T(128)} %concatenate.37.ids, bf16[2,2,2,2,64,512]{5,4,3,2,1,0:T(8,128)(2,1)} %bitcast.121, bf16[2,2,2,2,64,512]{5,4,3,2,1,0:T(8,128)(2,1)} %copy-done.2, ...), custom_call_target="tpu_custom_call" | custom-call | flops 1024 | bytes 1024 | tf_op jit(solution)/shard_map/halve/pallas_call | solution.py:309
  402.7 1.8 collective-permute-start.32
  407.2 10.3 %qkv_back.2 = bf16[512,1024]{1,0:T(8,128)(2,1)} custom-call(s32[7]{0:T(128)} %concatenate.37.ids, bf16[3,1024,1024]{2,1,0:T(8,128)(2,1)} %attend_back.1.refs_1_.d_ref, bf16[16,72,512]{2,1,0:T(8,128)(2,1)} %bitcast.138, bf16[16,72,512]{2,1,0:T(8,128)(2,1)} %bitcast.43.refs_1_, bf16[16,64,512]{2,1,0:T(8,128)(2,1)} %bitcast.144, ...), custom_call_target="tpu_custom_call" | custom-call | flops 1024 | bytes 1024 | tf_op jit(solution)/shard_map/qkv_back/pallas_call | solution.py:309
  419.2 4.5 halve.6
  427.2 10.8 %qkv_back.3._ = f32[2,4096,128]{2,1,0:T(8,128)} custom-call(s32[7]{0:T(128)} %concatenate.37.ids, bf16[3,1024,1024]{2,1,0:T(8,128)(2,1)} %attend_back.1.refs_1_.d_ref, bf16[16,72,512]{2,1,0:T(8,128)(2,1)} %bitcast.139, bf16[16,72,512]{2,1,0:T(8,128)(2,1)} %bitcast.43.refs_1_, bf16[16,64,512]{2,1,0:T(8,128)(2,1)} %bitcast.145, ...), custom_call_target="tpu_custom_call" | custom-call | flops 1024 | bytes 1024 | tf_op jit(solution)/shard_map/qkv_back/pallas_call | solution.py:309
  440.4 2.8 halve.7
  444.2 1.7 collective-permute-start.39
  447.3 3.2 collective-permute-done.38.refs_4_
  451.8 2.7 halve.8
  456.7 2.1 collective-permute-start.43
  459.9 1.9 collective-permute-done.42.refs_11_
  463.0 2.8 halve.9
  465.8 1.9 multiply_reduce_fusion.1
  468.1 5.0 fusion
  473.1 8.4 %collective-permute-done.44 = f32[2,32]{1,0:T(2,128)S(1)} collective-permute-done((f32[2,32]{1,0:T(2,128)S(1)}, f32[2,32]{1,0:T(2,128)S(1)}, u32[]{:S(2)}, u32[]{:S(2)}) %collective-permute-start.44) | collective-permute-done | bytes 288 | tf_op jit(solution)/shard_map/ppermute | solution.py:362
  483.1 3.9 place_rows.1
  487.0 8.0 %reduce-scatter.5.cloned.1.call-done = bf16[1,64,512]{2,1,0:T(8,128)(2,1)} async-done(((bf16[16,64,512]{2,1,0:T(8,128)(2,1)}), bf16[1,64,512]{2,1,0:T(8,128)(2,1)}) %reduce-scatter.5.cloned.1.call-update) | async-done | bytes 65552 | tf_op jit(solution)/shard_map/reduce_scatter | solution.py:1285
  (223 shorter events, 66.4 us)
Async XLA Ops:
  7.2 160.3 %all-gather.3.cloned.1.call-start = ((), (), s32[]{:S(2)}) async-start(), calls=%async_computation.4 | async-start | bytes 13369344 | tf_op jit(solution)/shard_map/all_gather | solution.py:1218
  8.2 10.7 %collective-permute-start.1 = (bf16[64,512]{1,0:T(8,128)(2,1)S(1)}, bf16[64,512]{1,0:T(8,128)(2,1)S(1)}, u32[]{:S(2)}, u32[]{:S(2)}) collective-permute-start(bf16[64,512]{1,0:T(8,128)(2,1)S(1)} %get-tuple-element.319), channel_id=1, source_target_pairs={{0,1},{1,0},{2,3},{3,2},{4,5},{5,4},{6,7},{7,6},{8,9},{9,8},{10,11... | collective-permute-start | bytes 196616 | tf_op jit(solution)/shard_map/ppermute | solution.py:362
  11.2 7.7 %collective-permute-start.2 = (bf16[64,512]{1,0:T(8,128)(2,1)S(1)}, bf16[64,512]{1,0:T(8,128)(2,1)S(1)}, u32[]{:S(2)}, u32[]{:S(2)}) collective-permute-start(bf16[64,512]{1,0:T(8,128)(2,1)S(1)} %get-tuple-element.320), channel_id=1, source_target_pairs={{0,1},{1,0},{2,3},{3,2},{4,5},{5,4},{6,7},{7,6},{8,9},{9,8},{10,11... | collective-permute-start | bytes 196616 | tf_op jit(solution)/shard_map/ppermute | solution.py:362
  12.9 5.9 %collective-permute-start = (bf16[72,512]{1,0:T(8,128)(2,1)S(1)}, bf16[72,512]{1,0:T(8,128)(2,1)S(1)}, u32[]{:S(2)}, u32[]{:S(2)}) collective-permute-start(bf16[72,512]{1,0:T(8,128)(2,1)S(1)} %get-tuple-element.332), channel_id=1, source_target_pairs={{0,16},{2,18},{4,20},{6,22},{8,24},{10,26},{12,28},{14,30},{16,0},... | collective-permute-start | bytes 221192 | tf_op jit(solution)/shard_map/ppermute | solution.py:363
  17.3 13.4 %collective-permute-start.3 = (bf16[256,1024]{1,0:T(8,128)(2,1)S(1)}, bf16[256,1024]{1,0:T(8,128)(2,1)S(1)}, u32[]{:S(2)}, u32[]{:S(2)}) collective-permute-start(bf16[256,1024]{1,0:T(8,128)(2,1)S(1)} %get-tuple-element.301), channel_id=1, source_target_pairs={{0,1},{1,0},{2,3},{3,2},{4,5},{5,4},{6,7},{7,6},{8,9},{9,8},{10,11... | collective-permute-start | bytes 1572872 | tf_op jit(solution)/shard_map/ppermute | solution.py:362
  18.9 11.8 %collective-permute-start.5 = (bf16[2,64,512]{2,1,0:T(8,128)(2,1)S(1)}, bf16[2,64,512]{2,1,0:T(8,128)(2,1)S(1)}, u32[]{:S(2)}, u32[]{:S(2)}) collective-permute-start(bf16[2,64,512]{2,1,0:T(8,128)(2,1)S(1)} %get-tuple-element.330), channel_id=1, source_target_pairs={{0,16},{2,18},{4,20},{6,22},{8,24},{10,26},{12,28},{14,30},{16,0},... | collective-permute-start | bytes 393224 | tf_op jit(solution)/shard_map/ppermute | solution.py:363
  21.5 9.2 %collective-permute-start.4 = (bf16[2,72,512]{2,1,0:T(8,128)(2,1)S(1)}, bf16[2,72,512]{2,1,0:T(8,128)(2,1)S(1)}, u32[]{:S(2)}, u32[]{:S(2)}) collective-permute-start(bf16[2,72,512]{2,1,0:T(8,128)(2,1)S(1)} %get-tuple-element.324), channel_id=1, source_target_pairs={{0,4},{2,6},{4,0},{6,2},{8,12},{10,14},{12,8},{14,10},{16,20},{18,... | collective-permute-start | bytes 442376 | tf_op jit(solution)/shard_map/ppermute | solution.py:363
  23.0 7.6 %collective-permute-start.6 = (bf16[2,64,512]{2,1,0:T(8,128)(2,1)S(1)}, bf16[2,64,512]{2,1,0:T(8,128)(2,1)S(1)}, u32[]{:S(2)}, u32[]{:S(2)}) collective-permute-start(bf16[2,64,512]{2,1,0:T(8,128)(2,1)S(1)} %get-tuple-element.328), channel_id=1, source_target_pairs={{0,8},{2,10},{4,12},{6,14},{8,0},{10,2},{12,4},{14,6},{16,24},{18,... | collective-permute-start | bytes 393224 | tf_op jit(solution)/shard_map/ppermute | solution.py:363
  25.3 5.4 %collective-permute-start.7 = (bf16[64,512]{1,0:T(8,128)(2,1)S(1)}, bf16[64,512]{1,0:T(8,128)(2,1)S(1)}, u32[]{:S(2)}, u32[]{:S(2)}) collective-permute-start(bf16[64,512]{1,0:T(8,128)(2,1)S(1)} %bitcast.172), channel_id=1, source_target_pairs={{0,16},{2,18},{4,20},{6,22},{8,24},{10,26},{12,28},{14,30},{16,0},... | collective-permute-start | bytes 196616 | tf_op jit(solution)/shard_map/ppermute | solution.py:363
  30.7 16.4 %collective-permute-start.8 = (bf16[256,1024]{1,0:T(8,128)(2,1)S(1)}, bf16[256,1024]{1,0:T(8,128)(2,1)}, u32[]{:S(2)}, u32[]{:S(2)}) collective-permute-start(bf16[256,1024]{1,0:T(8,128)(2,1)S(1)} %get-tuple-element.142), channel_id=1, source_target_pairs={{0,1},{1,0},{2,3},{3,2},{4,5},{5,4},{6,7},{7,6},{8,9},{9,8},{10,11... | collective-permute-start | bytes 1572872 | tf_op jit(solution)/shard_map/ppermute | solution.py:362
  32.3 14.8 %collective-permute-start.9 = (bf16[2,2,72,512]{3,2,1,0:T(8,128)(2,1)S(1)}, bf16[2,2,72,512]{3,2,1,0:T(8,128)(2,1)S(1)}, u32[]{:S(2)}, u32[]{:S(2)}) collective-permute-start(bf16[2,2,72,512]{3,2,1,0:T(8,128)(2,1)S(1)} %get-tuple-element.311), channel_id=1, source_target_pairs={{0,8},{2,10},{4,12},{6,14},{8,0},{10,2},{12,4},{14,6},{16,24},{18,... | collective-permute-start | bytes 884744 | tf_op jit(solution)/shard_map/ppermute | solution.py:363
  33.4 11.5 %collective-permute-start.10 = (bf16[2,2,64,512]{3,2,1,0:T(8,128)(2,1)S(1)}, bf16[2,2,64,512]{3,2,1,0:T(8,128)(2,1)S(1)}, u32[]{:S(2)}, u32[]{:S(2)}) collective-permute-start(bf16[2,2,64,512]{3,2,1,0:T(8,128)(2,1)S(1)} %get-tuple-element.317), channel_id=1, source_target_pairs={{0,4},{2,6},{4,0},{6,2},{8,12},{10,14},{12,8},{14,10},{16,20},{18,... | collective-permute-start | bytes 786440 | tf_op jit(solution)/shard_map/ppermute | solution.py:363
  35.0 12.1 %collective-permute-start.11 = (bf16[2,2,64,512]{3,2,1,0:T(8,128)(2,1)S(1)}, bf16[2,2,64,512]{3,2,1,0:T(8,128)(2,1)S(1)}, u32[]{:S(2)}, u32[]{:S(2)}) collective-permute-start(bf16[2,2,64,512]{3,2,1,0:T(8,128)(2,1)S(1)} %get-tuple-element.315), channel_id=1, source_target_pairs={{0,16},{2,18},{4,20},{6,22},{8,24},{10,26},{12,28},{14,30},{16,0},... | collective-permute-start | bytes 786440 | tf_op jit(solution)/shard_map/ppermute | solution.py:363
  36.4 8.4 %collective-permute-start.12 = (bf16[2,64,512]{2,1,0:T(8,128)(2,1)S(1)}, bf16[2,64,512]{2,1,0:T(8,128)(2,1)S(1)}, u32[]{:S(2)}, u32[]{:S(2)}) collective-permute-start(bf16[2,64,512]{2,1,0:T(8,128)(2,1)S(1)} %get-tuple-element.326), channel_id=1, source_target_pairs={{0,1},{1,0},{2,3},{3,2},{4,5},{5,4},{6,7},{7,6},{8,9},{9,8},{10,11... | collective-permute-start | bytes 393224 | tf_op jit(solution)/shard_map/ppermute | solution.py:362
  48.0 18.1 %collective-permute-start.14 = (bf16[2,2,2,64,512]{4,3,2,1,0:T(8,128)(2,1)S(1)}, bf16[2,2,2,64,512]{4,3,2,1,0:T(8,128)(2,1)}, u32[]{:S(2)}, u32[]{:S(2)}) collective-permute-start(bf16[2,2,2,64,512]{4,3,2,1,0:T(8,128)(2,1)S(1)} %get-tuple-element.309), channel_id=1, source_target_pairs={{0,8},{2,10},{4,12},{6,14},{8,0},{10,2},{12,4},{14,6},{16,24},{18,... | collective-permute-start | bytes 1572872 | tf_op jit(solution)/shard_map/ppermute | solution.py:363
  48.1 18.0 %collective-permute-start.13 = (bf16[2,2,2,72,512]{4,3,2,1,0:T(8,128)(2,1)S(1)}, bf16[2,2,2,72,512]{4,3,2,1,0:T(8,128)(2,1)S(1)}, u32[]{:S(2)}, u32[]{:S(2)}) collective-permute-start(bf16[2,2,2,72,512]{4,3,2,1,0:T(8,128)(2,1)S(1)} %get-tuple-element.303), channel_id=1, source_target_pairs={{0,1},{1,0},{2,3},{3,2},{4,5},{5,4},{6,7},{7,6},{8,9},{9,8},{10,11... | collective-permute-start | bytes 1769480 | tf_op jit(solution)/shard_map/ppermute | solution.py:362
  50.0 16.1 %collective-permute-start.15 = (bf16[2,2,2,64,512]{4,3,2,1,0:T(8,128)(2,1)}, bf16[2,2,2,64,512]{4,3,2,1,0:T(8,128)(2,1)}, u32[]{:S(2)}, u32[]{:S(2)}) collective-permute-start(bf16[2,2,2,64,512]{4,3,2,1,0:T(8,128)(2,1)} %get-tuple-element.307), channel_id=1, source_target_pairs={{0,4},{2,6},{4,0},{6,2},{8,12},{10,14},{12,8},{14,10},{16,20},{18,... | collective-permute-start | bytes 1572872 | tf_op jit(solution)/shard_map/ppermute | solution.py:363
  51.4 14.6 %collective-permute-start.16 = (bf16[2,2,64,512]{3,2,1,0:T(8,128)(2,1)S(1)}, bf16[2,2,64,512]{3,2,1,0:T(8,128)(2,1)}, u32[]{:S(2)}, u32[]{:S(2)}) collective-permute-start(bf16[2,2,64,512]{3,2,1,0:T(8,128)(2,1)S(1)} %get-tuple-element.313), channel_id=1, source_target_pairs={{0,8},{2,10},{4,12},{6,14},{8,0},{10,2},{12,4},{14,6},{16,24},{18,... | collective-permute-start | bytes 786440 | tf_op jit(solution)/shard_map/ppermute | solution.py:363
  66.1 352.3 %reduce-scatter.3.cloned.1.call-start = ((), (), s32[]{:S(2)}) async-start(), calls=%async_computation.2 | async-start | bytes 13369344 | tf_op jit(solution)/shard_map/reduce_scatter | solution.py:1248
  68.1 5.1 %collective-permute-start.19 = (bf16[2,2,2,2,64,512]{5,4,3,2,1,0:T(8,128)(2,1)S(1)}, bf16[2,2,2,2,64,512]{5,4,3,2,1,0:T(8,128)(2,1)}, u32[]{:S(2)}, u32[]{:S(2)}) collective-permute-start(bf16[2,2,2,2,64,512]{5,4,3,2,1,0:T(8,128)(2,1)S(1)} %pad_maximum_fusion.2), channel_id=1, source_target_pairs={{0,2},{2,0},{4,6},{6,4},{8,10},{10,8},{12,14},{14,12},{16,18},{18,... | collective-permute-start | bytes 3145736 | tf_op jit(solution)/shard_map/ppermute | solution.py:363
  68.4 5.8 %collective-permute-start.17 = (bf16[2,2,2,2,72,512]{5,4,3,2,1,0:T(8,128)(2,1)S(1)}, bf16[2,2,2,2,72,512]{5,4,3,2,1,0:T(8,128)(2,1)}, u32[]{:S(2)}, u32[]{:S(2)}) collective-permute-start(bf16[2,2,2,2,72,512]{5,4,3,2,1,0:T(8,128)(2,1)S(1)} %pad_maximum_fusion), channel_id=1, source_target_pairs={{0,2},{2,0},{4,6},{6,4},{8,10},{10,8},{12,14},{14,12},{16,18},{18,... | collective-permute-start | bytes 3538952 | tf_op jit(solution)/shard_map/ppermute | solution.py:363
  70.1 4.1 collective-permute-start.18
  73.2 20.5 %collective-permute-start.20 = (bf16[2,2,2,64,512]{4,3,2,1,0:T(8,128)(2,1)}, bf16[2,2,2,64,512]{4,3,2,1,0:T(8,128)(2,1)}, u32[]{:S(2)}, u32[]{:S(2)}) collective-permute-start(bf16[2,2,2,64,512]{4,3,2,1,0:T(8,128)(2,1)} %get-tuple-element.305), channel_id=1, source_target_pairs={{0,4},{2,6},{4,0},{6,2},{8,12},{10,14},{12,8},{14,10},{16,20},{18,... | collective-permute-start | bytes 1572872 | tf_op jit(solution)/shard_map/ppermute | solution.py:363
  94.9 43.4 %collective-permute-start.21 = (bf16[2,2,2,2,64,512]{5,4,3,2,1,0:T(8,128)(2,1)S(1)}, bf16[2,2,2,2,64,512]{5,4,3,2,1,0:T(8,128)(2,1)S(1)}, u32[]{:S(2)}, u32[]{:S(2)}) collective-permute-start(bf16[2,2,2,2,64,512]{5,4,3,2,1,0:T(8,128)(2,1)S(1)} %pad_maximum_fusion.3), channel_id=1, source_target_pairs={{0,2},{2,0},{4,6},{6,4},{8,10},{10,8},{12,14},{14,12},{16,18},{18,... | collective-permute-start | bytes 3145736 | tf_op jit(solution)/shard_map/ppermute | solution.py:363
  95.8 53.3 %collective-permute-start.22 = (bf16[2,512,1024]{2,1,0:T(8,128)(2,1)}, bf16[2,512,1024]{2,1,0:T(8,128)(2,1)S(1)}, u32[]{:S(2)}, u32[]{:S(2)}) collective-permute-start(bf16[2,512,1024]{2,1,0:T(8,128)(2,1)} %bitcast.157), channel_id=1, source_target_pairs={{0,1},{1,0},{2,3},{3,2},{4,5},{5,4},{6,7},{7,6},{8,9},{9,8},{10,11... | collective-permute-start | bytes 6291464 | tf_op jit(solution)/shard_map/ppermute | solution.py:362
  148.6 47.9 %collective-permute-start.23 = (bf16[1024,1024]{1,0:T(8,128)(2,1)}, bf16[1024,1024]{1,0:T(8,128)(2,1)S(1)}, u32[]{:S(2)}, u32[]{:S(2)}) collective-permute-start(bf16[1024,1024]{1,0:T(8,128)(2,1)} %get-tuple-element.176.hn_ref), channel_id=1, source_target_pairs={{0,1},{1,0},{2,3},{3,2},{4,5},{5,4},{6,7},{7,6},{8,9},{9,8},{10,11... | collective-permute-start | bytes 6291464 | tf_op jit(solution)/shard_map/ppermute | solution.py:362
  236.8 35.8 %collective-permute-start.24 = (bf16[768,1024]{1,0:T(8,128)(2,1)}, bf16[768,1024]{1,0:T(8,128)(2,1)S(1)}, u32[]{:S(2)}, u32[]{:S(2)}) collective-permute-start(bf16[768,1024]{1,0:T(8,128)(2,1)} %get-tuple-element.186), channel_id=1, source_target_pairs={{0,1},{1,0},{2,3},{3,2},{4,5},{5,4},{6,7},{7,6},{8,9},{9,8},{10,11... | collective-permute-start | bytes 4718600 | tf_op jit(solution)/shard_map/ppermute | solution.py:362
  273.7 221.3 %reduce-scatter.5.cloned.1.call-start = ((), (), s32[]{:S(2)}) async-start(), calls=%async_computation.3 | async-start | bytes 1114112 | tf_op jit(solution)/shard_map/reduce_scatter | solution.py:1285
  273.7 16.7 %collective-permute-start.25 = (bf16[256,1024]{1,0:T(8,128)(2,1)S(1)}, bf16[256,1024]{1,0:T(8,128)(2,1)S(1)}, u32[]{:S(2)}, u32[]{:S(2)}) collective-permute-start(bf16[256,1024]{1,0:T(8,128)(2,1)S(1)} %copy-done.44), channel_id=1, source_target_pairs={{0,1},{1,0},{2,3},{3,2},{4,5},{5,4},{6,7},{7,6},{8,9},{9,8},{10,11... | collective-permute-start | bytes 1572872 | tf_op jit(solution)/shard_map/ppermute | solution.py:362
  310.8 25.4 %collective-permute-start.26 = (bf16[16,64,512]{2,1,0:T(8,128)(2,1)}, bf16[16,64,512]{2,1,0:T(8,128)(2,1)S(1)}, u32[]{:S(2)}, u32[]{:S(2)}) collective-permute-start(bf16[16,64,512]{2,1,0:T(8,128)(2,1)} %get-tuple-element.203), channel_id=1, source_target_pairs={{0,1},{1,0},{2,3},{3,2},{4,5},{5,4},{6,7},{7,6},{8,9},{9,8},{10,11... | collective-permute-start | bytes 3145736 | tf_op jit(solution)/shard_map/ppermute | solution.py:362
  336.1 82.2 %collective-permute-start.30 = (bf16[2,512,1024]{2,1,0:T(8,128)(2,1)}, bf16[2,512,1024]{2,1,0:T(8,128)(2,1)}, u32[]{:S(2)}, u32[]{:S(2)}) collective-permute-start(bf16[2,512,1024]{2,1,0:T(8,128)(2,1)} %get-tuple-element.232), channel_id=1, source_target_pairs={{0,1},{1,0},{2,3},{3,2},{4,5},{5,4},{6,7},{7,6},{8,9},{9,8},{10,11... | collective-permute-start | bytes 6291464 | tf_op jit(solution)/shard_map/ppermute | solution.py:362
  378.6 12.7 %collective-permute-start.27 = (bf16[2,2,2,2,64,512]{5,4,3,2,1,0:T(8,128)(2,1)}, bf16[2,2,2,2,64,512]{5,4,3,2,1,0:T(8,128)(2,1)S(1)}, u32[]{:S(2)}, u32[]{:S(2)}) collective-permute-start(bf16[2,2,2,2,64,512]{5,4,3,2,1,0:T(8,128)(2,1)} %bitcast.183), channel_id=1, source_target_pairs={{0,2},{2,0},{4,6},{6,4},{8,10},{10,8},{12,14},{14,12},{16,18},{18,... | collective-permute-start | bytes 3145736 | tf_op jit(solution)/shard_map/ppermute | solution.py:363
  390.7 3.8 collective-permute-start.29
  391.2 3.8 collective-permute-start.28
  402.5 15.0 %collective-permute-start.31 = (bf16[2,2,2,64,512]{4,3,2,1,0:T(8,128)(2,1)}, bf16[2,2,2,64,512]{4,3,2,1,0:T(8,128)(2,1)S(1)}, u32[]{:S(2)}, u32[]{:S(2)}) collective-permute-start(bf16[2,2,2,64,512]{4,3,2,1,0:T(8,128)(2,1)} %get-tuple-element.227), channel_id=1, source_target_pairs={{0,4},{2,6},{4,0},{6,2},{8,12},{10,14},{12,8},{14,10},{16,20},{18,... | collective-permute-start | bytes 1572872 | tf_op jit(solution)/shard_map/ppermute | solution.py:363
  402.7 14.8 %collective-permute-start.32 = (bf16[2,2,2,64,512]{4,3,2,1,0:T(8,128)(2,1)}, bf16[2,2,2,64,512]{4,3,2,1,0:T(8,128)(2,1)S(1)}, u32[]{:S(2)}, u32[]{:S(2)}) collective-permute-start(bf16[2,2,2,64,512]{4,3,2,1,0:T(8,128)(2,1)} %get-tuple-element.228), channel_id=1, source_target_pairs={{0,8},{2,10},{4,12},{6,14},{8,0},{10,2},{12,4},{14,6},{16,24},{18,... | collective-permute-start | bytes 1572872 | tf_op jit(solution)/shard_map/ppermute | solution.py:363
  404.5 13.8 %collective-permute-start.33 = (bf16[2,2,2,64,512]{4,3,2,1,0:T(8,128)(2,1)}, bf16[2,2,2,64,512]{4,3,2,1,0:T(8,128)(2,1)S(1)}, u32[]{:S(2)}, u32[]{:S(2)}) collective-permute-start(bf16[2,2,2,64,512]{4,3,2,1,0:T(8,128)(2,1)} %get-tuple-element.229), channel_id=1, source_target_pairs={{0,1},{1,0},{2,3},{3,2},{4,5},{5,4},{6,7},{7,6},{8,9},{9,8},{10,11... | collective-permute-start | bytes 1572872 | tf_op jit(solution)/shard_map/ppermute | solution.py:362
  423.6 14.6 %collective-permute-start.35 = (bf16[2,2,64,512]{3,2,1,0:T(8,128)(2,1)}, bf16[2,2,64,512]{3,2,1,0:T(8,128)(2,1)S(1)}, u32[]{:S(2)}, u32[]{:S(2)}) collective-permute-start(bf16[2,2,64,512]{3,2,1,0:T(8,128)(2,1)} %get-tuple-element.244), channel_id=1, source_target_pairs={{0,8},{2,10},{4,12},{6,14},{8,0},{10,2},{12,4},{14,6},{16,24},{18,... | collective-permute-start | bytes 786440 | tf_op jit(solution)/shard_map/ppermute | solution.py:363
  424.2 14.0 %collective-permute-start.36 = (bf16[2,2,64,512]{3,2,1,0:T(8,128)(2,1)}, bf16[2,2,64,512]{3,2,1,0:T(8,128)(2,1)S(1)}, u32[]{:S(2)}, u32[]{:S(2)}) collective-permute-start(bf16[2,2,64,512]{3,2,1,0:T(8,128)(2,1)} %get-tuple-element.245), channel_id=1, source_target_pairs={{0,4},{2,6},{4,0},{6,2},{8,12},{10,14},{12,8},{14,10},{16,20},{18,... | collective-permute-start | bytes 786440 | tf_op jit(solution)/shard_map/ppermute | solution.py:363
  425.8 13.9 %collective-permute-start.37 = (bf16[2,2,64,512]{3,2,1,0:T(8,128)(2,1)}, bf16[2,2,64,512]{3,2,1,0:T(8,128)(2,1)S(1)}, u32[]{:S(2)}, u32[]{:S(2)}) collective-permute-start(bf16[2,2,64,512]{3,2,1,0:T(8,128)(2,1)} %get-tuple-element.246), channel_id=1, source_target_pairs={{0,16},{2,18},{4,20},{6,22},{8,24},{10,26},{12,28},{14,30},{16,0},... | collective-permute-start | bytes 786440 | tf_op jit(solution)/shard_map/ppermute | solution.py:363
  443.2 7.3 %collective-permute-start.38 = (bf16[2,64,512]{2,1,0:T(8,128)(2,1)}, bf16[2,64,512]{2,1,0:T(8,128)(2,1)S(1)}, u32[]{:S(2)}, u32[]{:S(2)}) collective-permute-start(bf16[2,64,512]{2,1,0:T(8,128)(2,1)} %get-tuple-element.254), channel_id=1, source_target_pairs={{0,16},{2,18},{4,20},{6,22},{8,24},{10,26},{12,28},{14,30},{16,0},... | collective-permute-start | bytes 393224 | tf_op jit(solution)/shard_map/ppermute | solution.py:363
  444.2 6.3 %collective-permute-start.39 = (bf16[2,64,512]{2,1,0:T(8,128)(2,1)}, bf16[2,64,512]{2,1,0:T(8,128)(2,1)S(1)}, u32[]{:S(2)}, u32[]{:S(2)}) collective-permute-start(bf16[2,64,512]{2,1,0:T(8,128)(2,1)} %get-tuple-element.255), channel_id=1, source_target_pairs={{0,1},{1,0},{2,3},{3,2},{4,5},{5,4},{6,7},{7,6},{8,9},{9,8},{10,11... | collective-permute-start | bytes 393224 | tf_op jit(solution)/shard_map/ppermute | solution.py:362
  445.9 5.2 %collective-permute-start.40 = (bf16[2,64,512]{2,1,0:T(8,128)(2,1)}, bf16[2,64,512]{2,1,0:T(8,128)(2,1)S(1)}, u32[]{:S(2)}, u32[]{:S(2)}) collective-permute-start(bf16[2,64,512]{2,1,0:T(8,128)(2,1)} %get-tuple-element.256), channel_id=1, source_target_pairs={{0,4},{2,6},{4,0},{6,2},{8,12},{10,14},{12,8},{14,10},{16,20},{18,... | collective-permute-start | bytes 393224 | tf_op jit(solution)/shard_map/ppermute | solution.py:363
  454.5 5.4 %collective-permute-start.41 = (bf16[64,512]{1,0:T(8,128)(2,1)}, bf16[64,512]{1,0:T(8,128)(2,1)S(1)}, u32[]{:S(2)}, u32[]{:S(2)}) collective-permute-start(bf16[64,512]{1,0:T(8,128)(2,1)} %get-tuple-element.258), channel_id=1, source_target_pairs={{0,1},{1,0},{2,3},{3,2},{4,5},{5,4},{6,7},{7,6},{8,9},{9,8},{10,11... | collective-permute-start | bytes 196616 | tf_op jit(solution)/shard_map/ppermute | solution.py:362
  455.7 6.1 %collective-permute-start.42 = (bf16[64,512]{1,0:T(8,128)(2,1)}, bf16[64,512]{1,0:T(8,128)(2,1)S(1)}, u32[]{:S(2)}, u32[]{:S(2)}) collective-permute-start(bf16[64,512]{1,0:T(8,128)(2,1)} %get-tuple-element.259), channel_id=1, source_target_pairs={{0,16},{2,18},{4,20},{6,22},{8,24},{10,26},{12,28},{14,30},{16,0},... | collective-permute-start | bytes 196616 | tf_op jit(solution)/shard_map/ppermute | solution.py:363
  456.7 5.0 collective-permute-start.43
  459.2 22.9 %collective-permute-start.34 = (bf16[512,1024]{1,0:T(8,128)(2,1)S(1)}, bf16[512,1024]{1,0:T(8,128)(2,1)S(1)}, u32[]{:S(2)}, u32[]{:S(2)}) collective-permute-start(bf16[512,1024]{1,0:T(8,128)(2,1)S(1)} %copy-done.25), channel_id=1, source_target_pairs={{0,1},{1,0},{2,3},{3,2},{4,5},{5,4},{6,7},{7,6},{8,9},{9,8},{10,11... | collective-permute-start | bytes 3145736 | tf_op jit(solution)/shard_map/ppermute | solution.py:362
  467.9 13.6 %collective-permute-start.44 = (f32[2,32]{1,0:T(2,128)S(1)}, f32[2,32]{1,0:T(2,128)S(1)}, u32[]{:S(2)}, u32[]{:S(2)}) collective-permute-start(f32[2,32]{1,0:T(2,128)S(1)} %bitcast.182), channel_id=1, source_target_pairs={{0,1},{1,0},{2,3},{3,2},{4,5},{5,4},{6,7},{7,6},{8,9},{9,8},{10,11... | collective-permute-start | bytes 776 | tf_op jit(solution)/shard_map/ppermute | solution.py:362
  (45 other events, 309.5 us)
Sparse Core Ops, SparseCore 0:
  66.2 101.2 all-gather.2
  272.7 132.2 reduce-scatter.2
  438.2 56.7 reduce-scatter.4

commit v3 on v2

--- a/solution.py
+++ b/solution.py
@@ -1,3 +1,5 @@
+import itertools
+
 import jax
 import jax.numpy as jnp
 from jax import lax
@@ -298,6 +300,7 @@
 F32 = jnp.float32
 TILE = 256
 UNITS = 512
+O_ROWS = (16, 16, 32)
 CORE, TENSOR, X, Z_NEAR, Z_FAR = 1, 0, 2, 4, 8
 
 
@@ -374,11 +377,17 @@
 
     def begin(self):
         self.got = swap(self.held, self.left[0])
+        if len(self.left) == 2:
+            self.early = swap(self.held, CORE)
 
     def advance(self):
         if self.left.pop(0) == CORE:
-            self.pair = [a.reshape((-1,) + self.rows) for a in (self.held, self.got)]
+            arrays = (self.held, self.last, self.early, self.got)
+            self.arrays = [a.reshape((-1,) + self.rows) for a in arrays]
             self.ready = True
+        elif self.left == [CORE]:
+            self.last = self.got
+            self.got = swap(self.last, CORE)
         else:
             self.held = jnp.stack([self.held, self.got])
             self.begin()
@@ -403,55 +412,43 @@
 def halve(ids, sums):
     for s in sums:
         s.received()
-    last = sums[0].bit is None
-    depth = 0 if last else max(len(s.axes) for s in sums)
-    blocks = 2**depth
+    steps = 2 if any(s.axes for s in sums) else 1
     ins, in_specs, outs, out_specs, counts = [], [], [], [], []
     for s in sums:
         rows, columns = s.arrays[0][0].shape[-2:]
-
-        def index(axes, g, now=s.axes, bit=s.bit):
-            at = []
-            for a in axes:
-                if last or a not in now:
-                    at.append(int(a == bit))
-                else:
-                    at.append(g // 2 ** (depth - 1 - now.index(a)) % 2)
-            return (*at, 0, 0)
+        split = s.axes[0] if steps == 2 and s.axes else None
+
+        def spec(axes, now=s.axes, bit=s.bit, split=split, tail=(rows, columns)):
+            block = tuple(2 if a in now and a != split else None for a in axes)
+
+            def index(g, ids):
+                at = tuple(g if a == split else int(a == bit and a not in now) for a in axes)
+                return (*at, 0, 0)
+
+            return pl.BlockSpec(block + tail, index)
 
         for array, axes in s.arrays:
             ins.append(array)
-            in_specs.append(
-                pl.BlockSpec(
-                    (None,) * len(axes) + (rows, columns),
-                    lambda g, ids, axes=axes, index=index: index(axes, g),
-                )
-            )
+            in_specs.append(spec(axes))
         counts.append(len(s.arrays))
-        lead = () if last else (2,) * len(s.axes)
-        outs.append(shape(lead + (rows, columns), F32 if last else BF))
-        out_specs.append(
-            pl.BlockSpec(
-                (None,) * len(lead) + (rows, columns),
-                lambda g, ids, axes=() if last else s.axes, index=index: index(axes, g),
-            )
-        )
+        kind = F32 if s.bit is None else BF
+        outs.append(shape((2,) * len(s.axes) + (rows, columns), kind))
+        out_specs.append(spec(s.axes))
 
     def body(ids, *refs):
         out_refs = refs[len(ins) :]
         at = 0
         for out_ref, count in zip(out_refs, counts):
-            rows = out_ref.shape[0]
-            for r in range(0, rows, 64):
-                total = refs[at][r : r + 64].astype(F32)
+            for where in itertools.product(range(2), repeat=len(out_ref.shape) - 2):
+                total = refs[at][where].astype(F32)
                 for k in range(1, count):
-                    total += refs[at + k][r : r + 64].astype(F32)
-                out_ref[r : r + 64] = total.astype(out_ref.dtype)
+                    total += refs[at + k][where].astype(F32)
+                out_ref[where] = total.astype(out_ref.dtype)
             at += count
 
-    made = call(body, "halve", ids, tuple(ins), in_specs, tuple(outs), out_specs, (blocks,))
+    made = call(body, "halve", ids, tuple(ins), in_specs, tuple(outs), out_specs, (steps,))
     for s, value in zip(sums, made):
-        if last:
+        if s.bit is None:
             s.result = value
         else:
             s.got = swap(value, s.bit)
@@ -467,61 +464,90 @@
     return values
 
 
-def gathered_rows(ids, refs, order, part, height):
+def gathered_rows(ids, refs, order, part, low, high):
     mine = position(order, ids[3], ids[0])
+    count = refs[0].shape[0]
     flipped = ids[2] == 1
     blocks = []
-    for pair in range(refs[0].shape[0] // 2):
+    for pair in range(count):
         at = position(order, 2 * pair, part) ^ mine
-        a, b = [ref[at, :height] for ref in refs]
+        late = at >= count
+        at = at % count
+        held, last, early, other = [ref[at, low:high] for ref in refs]
+        a, b = jnp.where(late, last, held), jnp.where(late, other, early)
         blocks += [jnp.where(flipped, b, a), jnp.where(flipped, a, b)]
-    return jnp.concatenate(blocks, axis=0)
-
-
-def make_qkv(ids, rows, gots, gain, gathered):
+    return blocks
+
+
+def make_qkv(ids, rows, gots, gain, gathered, height):
     parts, local_rows, width = rows.shape
     length = parts * local_rows
-    fsdp = gathered[0].pair[0].shape[0]
-    height = width // fsdp
+    fsdp = width // height
     half = width // parts
-
-    piece = local_rows // len(gots)
+    per = local_rows // TILE
 
     def body(ids, rows_ref, gain_ref, *refs):
-        qkv_ref, xt_ref, x_ref, xn_ref, blocks_ref = refs[-5:]
-        x_ref[pl.ds(pl.multiple_of(ids[0] * local_rows, local_rows), local_rows)] = rows_ref[0]
-        for k in range(len(gots)):
-            first = pl.multiple_of((1 - ids[0]) * local_rows + k * piece, piece)
-            x_ref[pl.ds(first, piece)] = refs[6 + k][...]
-        for r in range(0, length, TILE):
-            rows = x_ref[r : r + TILE].astype(F32)
-            xn_ref[r : r + TILE] = (rows * rms_scale(rows) * gain_ref[...]).astype(BF)
+        qkv_ref, xt_ref, x_ref, w_ref, wo_ref, blocks_ref = refs[-6:]
+        step = pl.program_id(0)
+
+        @pl.when(step == 0)
+        def _():
+            for t in range(parts):
+                pieces = []
+                for c in range(3):
+                    args = (ids, refs[4 * c : 4 * c + 4], gathered[c].order, t)
+                    w_ref[c, t] = jnp.concatenate(gathered_rows(*args, 0, height), axis=0)
+                    pieces.append(gathered_rows(*args, height, height + O_ROWS[c]))
+                blocks = [block for of_one in zip(*pieces) for block in of_one]
+                wo_ref[t] = jnp.concatenate(blocks, axis=0)
+
+        @pl.when(step // per == ids[0])
+        def _():
+            x_ref[...] = rows_ref[0]
+
+        for k in range(per):
+
+            @pl.when((step // per != ids[0]) & (step % per == k))
+            def _(k=k):
+                x_ref[...] = refs[12 + k][...]
+
+        values = x_ref[...].astype(F32)
+        xn = (values * rms_scale(values) * gain_ref[...]).astype(BF)
         for c in range(3):
             for t in range(parts):
-                w = gathered_rows(ids, refs[2 * c : 2 * c + 2], gathered[c].order, t, height)
-                for r in range(0, length, TILE):
-                    made = dot_f32(xn_ref[r : r + TILE], w, 1, 0)
-                    if c == 0:
-                        made = made * HEAD_DIM ** (-0.5)
-                    qkv_ref[c, r : r + TILE, t * half : (t + 1) * half] = made.astype(BF)
-        store_transposed(ids, xn_ref[...], blocks_ref, xt_ref)
-
-    weights = [a for g in gathered for a in g.pair]
+                made = dot_f32(xn, w_ref[c, t], 1, 0)
+                if c == 0:
+                    made = made * HEAD_DIM ** (-0.5)
+                qkv_ref[c, :, t * half : (t + 1) * half] = made.astype(BF)
+        store_transposed(ids, xn, blocks_ref, xt_ref)
+
+    weights = [a for g in gathered for a in g.arrays]
     return call(
         body,
         "qkv",
         ids,
         (rows, gain, *weights, *gots),
-        [pl.BlockSpec((1, local_rows, width), lambda g, ids: (ids[0], 0, 0)), whole((1, width))]
+        [
+            pl.BlockSpec((1, TILE, width), lambda r, ids: (ids[0], r % per, 0)),
+            whole((1, width)),
+        ]
         + [whole(a.shape) for a in (*weights, *gots)],
         (
             shape((3, length, width), BF),
             shape((fsdp, height, length), BF),
             shape((length, width), BF),
+            shape((3, parts, width, half), BF),
+            shape((parts, width, half), BF),
         ),
-        [whole((3, length, width)), whole((fsdp, height, length)), whole((length, width))],
-        (1,),
-        (pltpu.VMEM((length, width), BF), pltpu.VMEM((fsdp, height, length), BF)),
+        [
+            pl.BlockSpec((3, TILE, width), lambda r, ids: (0, r, 0)),
+            pl.BlockSpec((fsdp, height, TILE), lambda r, ids: (0, 0, r)),
+            pl.BlockSpec((TILE, width), lambda r, ids: (r, 0)),
+            whole((3, parts, width, half)),
+            whole((parts, width, half)),
+        ],
+        (length // TILE,),
+        (pltpu.VMEM((fsdp, height, TILE), BF),),
     )
 
 
@@ -533,19 +559,15 @@
         out_ref[c * step : (c + 1) * step] = part.T.reshape(step, height, part.shape[0])
 
 
-def join_rows(ids, rows, got, fsdp):
+def join_rows(ids, rows, got):
     parts, local_rows, width = rows.shape
     length = parts * local_rows
-    height = width // fsdp
-
-    def body(ids, rows_ref, got_ref, out_ref, t_ref):
-        out_ref[0, pl.ds(pl.multiple_of(ids[0] * local_rows, local_rows), local_rows)] = rows_ref[
-            0
-        ]
-        out_ref[
-            0, pl.ds(pl.multiple_of((1 - ids[0]) * local_rows, local_rows), local_rows)
-        ] = got_ref[0]
-        store_natural(out_ref[0], t_ref.at[0])
+
+    def body(ids, rows_ref, got_ref, out_ref):
+        mine = pl.multiple_of(ids[0] * local_rows, local_rows)
+        out_ref[0, pl.ds(mine, local_rows)] = rows_ref[0]
+        rest = pl.multiple_of((1 - ids[0]) * local_rows, local_rows)
+        out_ref[0, pl.ds(rest, local_rows)] = got_ref[0]
 
     spec = pl.BlockSpec((1, local_rows, width), lambda s, ids: (s ^ ids[0], 0, 0))
     return call(
@@ -554,31 +576,9 @@
         ids,
         (rows, got),
         [spec, spec],
-        (shape((parts, length, width), BF), shape((parts, fsdp, height, length), BF)),
-        [
-            pl.BlockSpec((1, length, width), lambda s, ids: (s, 0, 0)),
-            pl.BlockSpec((1, fsdp, height, length), lambda s, ids: (s, 0, 0, 0)),
-        ],
+        (shape((parts, length, width), BF),),
+        [pl.BlockSpec((1, length, width), lambda s, ids: (s, 0, 0))],
         (parts,),
-    )
-
-
-def transposed(ids, rows, fsdp):
-    length, width = rows.shape
-    height = width // fsdp
-
-    def body(ids, rows_ref, t_ref):
-        store_natural(rows_ref[...], t_ref)
-
-    return call(
-        body,
-        "transposed",
-        ids,
-        (rows,),
-        [whole((length, width))],
-        (shape((fsdp, height, length), BF),),
-        [whole((fsdp, height, length))],
-        (1,),
     )[0]
 
 
@@ -611,43 +611,56 @@
 
         k = k_ref[0]
         vt = v_ref[0].T
-        for i in range(tiles):
-            used = min(i + 2, tiles)
-            q_rows = q_ref[0, i * TILE : (i + 1) * TILE]
-            parts = []
-            for head in range(2):
-                slot = (2 * i + head) % 2
-                q_head = lane_mask(q_rows, head)
-                top = None
-                for j in range(used):
-                    s = dot_f32(k[j * TILE : (j + 1) * TILE], q_head, 1, 1)
-                    if j >= i:
-                        s = s + bias_ref[i, (j - i) * TILE : (j - i + 1) * TILE]
-                    s_ref[slot, j] = s
-                    now = jnp.max(s.reshape(TILE // 8, 8, TILE), axis=0)
-                    top = now if top is None else jnp.maximum(top, now)
-                top = jnp.max(top, axis=0, keepdims=True)
-                total = None
-                out = None
-                for j in range(used):
-                    e = jnp.exp(s_ref[slot, j] - top)
-                    now = jnp.sum(e.reshape(TILE // 8, 8, TILE), axis=0)
-                    total = now if total is None else total + now
-                    low = e.astype(BF)
-                    e_ref[head, j * TILE : (j + 1) * TILE, i * TILE : (i + 1) * TILE] = low
-                    now = dot_f32(
-                        vt[head * HEAD_DIM : (head + 1) * HEAD_DIM, j * TILE : (j + 1) * TILE],
-                        low,
-                        1,
-                        0,
-                    )
-                    out = now if out is None else out + now
-                inv = 1.0 / jnp.sum(total, axis=0, keepdims=True)
-                inv_ref[0, head : head + 1, i * TILE : (i + 1) * TILE] = inv
-                parts.append(out * inv)
-            both = jnp.concatenate(parts, axis=0)
-            ot_ref[:, i * TILE : (i + 1) * TILE] = both.astype(BF)
-            o_ref[i * TILE : (i + 1) * TILE] = both.T.astype(BF)
+        slots = s_ref.shape[0]
+        todo = [(i, head) for i in range(tiles) for head in range(2)]
+        state = {}
+
+        def score(n):
+            i, head = todo[n]
+            q_head = lane_mask(q_ref[0, i * TILE : (i + 1) * TILE], head)
+            top = None
+            for j in range(min(i + 2, tiles)):
+                s = dot_f32(k[j * TILE : (j + 1) * TILE], q_head, 1, 1)
+                if j >= i:
+                    s = s + bias_ref[i, (j - i) * TILE : (j - i + 1) * TILE]
+                s_ref[n % slots, j] = s
+                now = jnp.max(s.reshape(TILE // 8, 8, TILE), axis=0)
+                top = now if top is None else jnp.maximum(top, now)
+            state[n] = jnp.max(top, axis=0, keepdims=True)
+
+        def soften(n):
+            i, head = todo[n]
+            total = None
+            for j in range(min(i + 2, tiles)):
+                e = jnp.exp(s_ref[n % slots, j] - state[n])
+                now = jnp.sum(e.reshape(TILE // 8, 8, TILE), axis=0)
+                total = now if total is None else total + now
+                e_ref[head, j * TILE : (j + 1) * TILE, i * TILE : (i + 1) * TILE] = e.astype(BF)
+            state[n] = 1.0 / jnp.sum(total, axis=0, keepdims=True)
+            inv_ref[0, head : head + 1, i * TILE : (i + 1) * TILE] = state[n]
+
+        def gather_values(n):
+            i, head = todo[n]
+            used = min(i + 2, tiles) * TILE
+            out = dot_f32(
+                vt[head * HEAD_DIM : (head + 1) * HEAD_DIM, :used],
+                e_ref[head, :used, i * TILE : (i + 1) * TILE],
+                1,
+                0,
+            )
+            state[n] = out * state[n]
+            if head == 1:
+                both = jnp.concatenate([state[n - 1], state[n]], axis=0)
+                ot_ref[:, i * TILE : (i + 1) * TILE] = both.astype(BF)
+                o_ref[i * TILE : (i + 1) * TILE] = both.T.astype(BF)
+
+        for n in range(len(todo) + 2):
+            if n < len(todo):
+                score(n)
+            if 1 <= n <= len(todo):
+                soften(n - 1)
+            if n >= 2:
+                gather_values(n - 2)
 
     spec = [
         pl.BlockSpec((1, length, pair), lambda p, ids, c=c: (c, 0, p)) for c in range(3)
@@ -673,7 +686,7 @@
         (heads // 2,),
         (
             pltpu.VMEM((tiles, 2 * TILE, TILE), F32),
-            pltpu.VMEM((2, tiles, TILE, TILE), F32),
+            pltpu.VMEM((4, tiles, TILE, TILE), F32),
         ),
     )
 
@@ -705,30 +718,38 @@
             )
             q_heads.append(lane_mask(q_ref[0], head))
         dq_ref[...] = jnp.zeros_like(dq_ref)
-        for j in range(tiles):
+        sums = {}
+
+        def scores_back(j, head):
             keys = slice(j * TILE, (j + 1) * TILE)
+            for r in range(max(j - 1, 0) * TILE, length, TILE):
+                cols = slice(r, r + TILE)
+                dp = dot_f32(v[keys], d_scaled[head][:, cols], 1, 0)
+                weights = e_ref[head, keys, cols].astype(F32)
+                ds_ref[j % 2, head, :, cols] = (weights * (dp - deltas[head][:, cols])).astype(BF)
+
+        def operands_back(j, head):
+            keys = slice(j * TILE, (j + 1) * TILE)
+            rows = slice(head * HEAD_DIM, (head + 1) * HEAD_DIM)
             first = max(j - 1, 0) * TILE
-            d_key = None
-            d_value = None
-            for head in range(2):
-                for r in range(first, length, TILE):
-                    cols = slice(r, r + TILE)
-                    dp = dot_f32(v[keys], d_scaled[head][:, cols], 1, 0)
-                    weights = e_ref[head, keys, cols].astype(F32)
-                    ds_ref[j % 2, head, :, cols] = (
-                        weights * (dp - deltas[head][:, cols])
-                    ).astype(BF)
-                ds = ds_ref[j % 2, head, :, first:length]
-                now = dot_f32(ds, q_heads[head][first:length], 1, 0)
-                d_key = now if d_key is None else d_key + now
-                now = dot_f32(
-                    e_ref[head, keys, first:length], d_scaled[head][:, first:length], 1, 1
-                )
-                d_value = now if d_value is None else d_value + now
-                rows = slice(head * HEAD_DIM, (head + 1) * HEAD_DIM)
-                dq_ref[rows, first:length] += dot_f32(kt[rows, keys], ds, 1, 0)
-            out_ref[1, keys] = d_key.astype(BF)
-            out_ref[2, keys] = d_value.astype(BF)
+            ds = ds_ref[j % 2, head, :, first:length]
+            d_key = dot_f32(ds, q_heads[head][first:length], 1, 0)
+            d_value = dot_f32(
+                e_ref[head, keys, first:length], d_scaled[head][:, first:length], 1, 1
+            )
+            dq_ref[rows, first:length] += dot_f32(kt[rows, keys], ds, 1, 0)
+            if head == 0:
+                sums[j] = (d_key, d_value)
+            else:
+                out_ref[1, keys] = (sums[j][0] + d_key).astype(BF)
+                out_ref[2, keys] = (sums[j][1] + d_value).astype(BF)
+
+        todo = [(j, head) for j in range(tiles) for head in range(2)]
+        for n in range(len(todo) + 1):
+            if n < len(todo):
+                scores_back(*todo[n])
+            if n >= 1:
+                operands_back(*todo[n - 1])
         out_ref[0] = (dq_ref[...] * HEAD_DIM ** (-0.5)).T.astype(BF)
 
     spec = [
@@ -753,40 +774,27 @@
     )[0]
 
 
-def out_project(ids, attended, gathered, x, gain):
+def out_project(ids, attended, w_out, x, gain):
     length, width = x.shape
-    fsdp = gathered.pair[0].shape[0]
-    height = width // fsdp
-    parts = 2
-    half = width // parts
-
-    def body(ids, a_ref, wa_ref, wb_ref, x_ref, gain_ref, hidden_ref, hn_ref, ht_ref):
-        w = [
-            gathered_rows(ids, (wa_ref, wb_ref), gathered.order, t, height) for t in range(parts)
-        ]
-        for r in range(0, length, TILE):
-            total = x_ref[r : r + TILE].astype(F32)
-            for t in range(parts):
-                total += dot_f32(a_ref[r : r + TILE, t * half : (t + 1) * half], w[t], 1, 1)
-            hidden_ref[r : r + TILE] = total
-            hn_ref[r : r + TILE] = (total * rms_scale(total) * gain_ref[...]).astype(BF)
-        store_natural(hn_ref[...], ht_ref)
-
+    parts, _, half = w_out.shape
+
+    def body(ids, a_ref, w_ref, x_ref, gain_ref, hidden_ref, hn_ref):
+        total = x_ref[...].astype(F32)
+        for t in range(parts):
+            total += dot_f32(a_ref[:, t * half : (t + 1) * half], w_ref[t], 1, 1)
+        hidden_ref[...] = total
+        hn_ref[...] = (total * rms_scale(total) * gain_ref[...]).astype(BF)
+
+    tile = pl.BlockSpec((TILE, width), lambda r, ids: (r, 0))
     return call(
         body,
         "out_project",
         ids,
-        (attended, *gathered.pair, x, gain),
-        [whole((length, width))]
-        + [whole(a.shape) for a in gathered.pair]
-        + [whole((length, width)), whole((1, width))],
-        (
-            shape((length, width), F32),
-            shape((length, width), BF),
-            shape((fsdp, height, length), BF),
-        ),
-        [whole((length, width)), whole((length, width)), whole((fsdp, height, length))],
-        (1,),
+        (attended, w_out, x, gain),
+        [tile, whole(w_out.shape), tile, whole((1, width))],
+        (shape((length, width), F32), shape((length, width), BF)),
+        [tile, tile],
+        (length // TILE,),
     )
 
 
@@ -795,8 +803,13 @@
     fsdp, rows, units = packed.shape
     height = rows // 3
     tile = 256
-
-    def body(ids, hn_ref, g_ref, w_ref, out_ref):
+    steps = units // tile
+    columns = width // steps
+
+    def body(ids, hn_ref, g_ref, w_ref, out_ref, ht_ref, gt_ref):
+        first = pl.multiple_of(pl.program_id(0) * columns, columns)
+        store_natural(hn_ref[:, pl.ds(first, columns)], ht_ref)
+        store_natural(g_ref[0, :, pl.ds(first, columns)], gt_ref)
         w_gate, w_up, w_down = [
             w_ref[:, c * height : (c + 1) * height].reshape(width, tile) for c in range(3)
         ]
@@ -823,71 +836,88 @@
             pl.BlockSpec((1, length, width), lambda n, ids: (which, 0, 0)),
             pl.BlockSpec((fsdp, rows, tile), lambda n, ids: (0, 0, n)),
         ],
-        (shape((3, length, units), BF),),
-        [pl.BlockSpec((3, length, tile), lambda n, ids: (0, 0, n))],
-        (units // tile,),
-    )[0]
+        (
+            shape((3, length, units), BF),
+            shape((fsdp, height, length), BF),
+            shape((fsdp, height, length), BF),
+        ),
+        [
+            pl.BlockSpec((3, length, tile), lambda n, ids: (0, 0, n)),
+            pl.BlockSpec((columns // height, height, length), lambda n, ids: (n, 0, 0)),
+            pl.BlockSpec((columns // height, height, length), lambda n, ids: (n, 0, 0)),
+        ],
+        (steps,),
+    )
 
 
 def feed_forward_out(ids, own, theirs, packed, hidden):
     length, width = hidden.shape
     fsdp, rows, units = packed.shape
     height = rows // 3
-    per = units // UNITS
     kept = length // 2
-
-    def body(ids, own_ref, theirs_ref, w_ref, hidden_ref, keep_ref, send_ref, acc_ref):
-        first = pl.program_id(1) == 0
-
-        @pl.when(first & (pl.program_id(0) == 0))
+    per = kept // TILE
+
+    def body(ids, own_ref, theirs_ref, w_ref, hidden_ref, keep_ref, send_ref):
+        w = w_ref[...].reshape(width, units)
+        mine = pl.program_id(0) == 0
+        keeps = pl.program_id(1) >= per
+
+        @pl.when(mine & keeps)
         def _():
-            acc_ref[...] = hidden_ref[...]
-
-        @pl.when(first & (pl.program_id(0) == 1))
+            keep_ref[0] = hidden_ref[...] + dot_f32(own_ref[0], w, 1, 1)
+
+        @pl.when(mine & ~keeps)
         def _():
-            acc_ref[...] = jnp.zeros_like(acc_ref)
-
-        w = w_ref[...].reshape(width, UNITS)
-
-        def add(m_ref):
-            for r in range(0, length, TILE):
-                acc_ref[r : r + TILE] += dot_f32(m_ref[0, r : r + TILE], w, 1, 1)
-
-        pl.when(pl.program_id(0) == 0)(lambda: add(own_ref))
-        pl.when(pl.program_id(0) == 1)(lambda: add(theirs_ref))
-
-        @pl.when(pl.program_id(1) == per - 1)
+            send_ref[0] = (hidden_ref[...] + dot_f32(own_ref[0], w, 1, 1)).astype(BF)
+
+        @pl.when(~mine & keeps)
         def _():
-            keep_ref[0] = acc_ref[pl.ds(pl.multiple_of(ids[0] * kept, kept), kept)]
-            send_ref[0] = acc_ref[
-                pl.ds(pl.multiple_of((1 - ids[0]) * kept, kept), kept)
-            ].astype(BF)
-
-    out_spec = pl.BlockSpec((1, kept, width), lambda s, n, ids: (s ^ ids[0], 0, 0))
+            keep_ref[0] = dot_f32(theirs_ref[0], w, 1, 1)
+
+        @pl.when(~mine & ~keeps)
+        def _():
+            send_ref[0] = dot_f32(theirs_ref[0], w, 1, 1).astype(BF)
+
+    def row(j, ids):
+        return jnp.where(j < per, (1 - ids[0]) * per + j, ids[0] * per + j - per)
+
     return call(
         body,
         "feed_forward_out",
         ids,
         (own, theirs, packed, hidden),
         [
-            pl.BlockSpec((1, length, UNITS), lambda s, n, ids: (2, 0, jnp.where(s == 0, n, per - 1))),
-            pl.BlockSpec((1, length, UNITS), lambda s, n, ids: (2, 0, jnp.where(s == 1, n, 0))),
-            pl.BlockSpec((fsdp, height, UNITS), lambda s, n, ids: (0, 2, n)),
-            whole((length, width)),
+            pl.BlockSpec(
+                (1, TILE, units),
+                lambda s, j, ids: (2, row(jnp.where(s == 0, j, 2 * per - 1), ids), 0),
+            ),
+            pl.BlockSpec(
+                (1, TILE, units), lambda s, j, ids: (2, row(jnp.where(s == 1, j, 0), ids), 0)
+            ),
+            pl.BlockSpec((fsdp, height, units), lambda s, j, ids: (0, 2, 0)),
+            pl.BlockSpec(
+                (TILE, width), lambda s, j, ids: (row(jnp.where(s == 0, j, 2 * per - 1), ids), 0)
+            ),
         ],
         (shape((2, kept, width), F32), shape((2, kept, width), BF)),
-        [out_spec, out_spec],
-        (2, per),
-        (pltpu.VMEM((length, width), F32),),
-    )
-
-
-def feed_forward_grads(ids, hn_t, hn_t_theirs, grads_t, own, theirs):
+        [
+            pl.BlockSpec(
+                (1, TILE, width), lambda s, j, ids: (s ^ ids[0], jnp.maximum(j - per, 0), 0)
+            ),
+            pl.BlockSpec(
+                (1, TILE, width), lambda s, j, ids: (s ^ ids[0], jnp.minimum(j, per - 1), 0)
+            ),
+        ],
+        (2, 2 * per),
+    )
+
+
+def feed_forward_grads(ids, hn_t, hn_t_theirs, grads_t, grads_t_theirs, own, theirs):
     fsdp, height, length = hn_t.shape
     units = own.shape[2]
     per = units // UNITS
 
-    def body(ids, h_ref, h2_ref, g_ref, own_ref, theirs_ref, out_ref):
+    def body(ids, h_ref, h2_ref, g_ref, g2_ref, own_ref, theirs_ref, out_ref):
         def make(a_ref, b_ref):
             for f in range(0, fsdp, 4):
                 a = a_ref[f : f + 4].reshape(4 * height, length)
@@ -896,15 +926,15 @@
                 out_ref[f : f + 4] = made.astype(BF).reshape(4, height, UNITS)
 
         pl.when(pl.program_id(0) < 2)(lambda: make(h_ref, h2_ref))
-        pl.when(pl.program_id(0) == 2)(lambda: make(g_ref.at[0], g_ref.at[1]))
+        pl.when(pl.program_id(0) == 2)(lambda: make(g_ref, g2_ref))
 
     side = pl.BlockSpec((1, length, UNITS), lambda c, n, ids: (c, 0, n))
     return call(
         body,
         "feed_forward_grads",
         ids,
-        (hn_t, hn_t_theirs, grads_t, own, theirs),
-        [whole(hn_t.shape), whole(hn_t.shape), whole(grads_t.shape), side, side],
+        (hn_t, hn_t_theirs, grads_t, grads_t_theirs, own, theirs),
+        [whole(hn_t.shape)] * 4 + [side, side],
         (shape((fsdp, 3 * height, units), BF),),
         [pl.BlockSpec((fsdp, height, UNITS), lambda c, n, ids: (0, c, n))],
         (3, per),
@@ -955,8 +985,9 @@
     )
 
 
-def feed_forward_back(ids, stacked, packed, cut=None):
-    length = stacked.shape[1]
+def feed_forward_back(ids, stacked, packed, half=None):
+    length = stacked.shape[1] if half is None else stacked.shape[1] // 2
+    at = half or 0
     fsdp, rows, units = packed.shape
     height = rows // 3
     width = fsdp * height
@@ -979,111 +1010,76 @@
 
         @pl.when(pl.program_id(0) == per - 1)
         def _():
-            if cut is None:
-                refs[0][...] = acc_ref[...]
-            else:
-                refs[0][...] = acc_ref[:cut].astype(BF)
-                refs[1][...] = acc_ref[cut:].astype(BF)
-
-    outs = [shape((length, width), F32)]
-    if cut is not None:
-        outs = [shape((cut, width), BF), shape((length - cut, width), BF)]
+            refs[0][...] = acc_ref[...].astype(refs[0].dtype)
+
     return call(
         body,
         "feed_forward_back",
         ids,
         (stacked, packed),
         [
-            pl.BlockSpec((2, length, UNITS), lambda n, ids: (0, 0, n)),
+            pl.BlockSpec((2, length, UNITS), lambda n, ids: (0, at, n)),
             pl.BlockSpec((fsdp, 2 * height, UNITS), lambda n, ids: (0, 0, n)),
         ],
-        tuple(outs),
-        [whole(o.shape) for o in outs],
+        (shape((length, width), F32 if half is None else BF),),
+        [whole((length, width))],
         (per,),
         (pltpu.VMEM((length, width), F32),),
-    )
-
-
-def norm_and_project_back(ids, share, gots, hidden, grads, gain, gathered):
+    )[0]
+
+
+def norm_and_project_back(ids, share, gots, hidden, grads, gain, w_out):
     length, width = hidden.shape
-    fsdp = gathered.pair[0].shape[0]
+    parts, _, half = w_out.shape
+    fsdp = lax.axis_size("fsdp")
     height = width // fsdp
-    parts = 2
-    half = width // parts
-
-    cut = gots[0].shape[0]
-
-    def body(ids, share_ref, got_ref, tail_ref, hidden_ref, g_ref, gain_ref, wa_ref, wb_ref, *refs):
-        dh_ref, lt_ref, out_ref, low_ref = refs
-        for r in range(0, length, TILE):
-            rows = hidden_ref[r : r + TILE]
-            scale = rms_scale(rows)
-            normed = rows * scale
-            theirs = got_ref[r : r + TILE] if r < cut else tail_ref[r - cut : r - cut + TILE]
-            d_normed = share_ref[r : r + TILE] + theirs.astype(F32)
-            dh = g_ref[0, r : r + TILE].astype(F32) + norm_backward_pass(
-                d_normed, normed, scale, gain_ref[...]
-            )
-            dh_ref[r : r + TILE] = dh
-            low_ref[r : r + TILE] = dh.astype(BF)
+    cut = gots[0].shape[0] // TILE
+
+    def body(ids, share_ref, got_ref, tail_ref, hidden_ref, g_ref, gain_ref, w_ref, *refs):
+        dh_ref, lt_ref, out_ref, blocks_ref, got_scr = refs
+
+        @pl.when(pl.program_id(0) < cut)
+        def _():
+            got_scr[...] = got_ref[...]
+
+        @pl.when(pl.program_id(0) >= cut)
+        def _():
+            got_scr[...] = tail_ref[...]
+
+        rows = hidden_ref[...]
+        scale = rms_scale(rows)
+        normed = rows * scale
+        d_normed = share_ref[...] + got_scr[...].astype(F32)
+        dh = g_ref[0].astype(F32) + norm_backward_pass(d_normed, normed, scale, gain_ref[...])
+        dh_ref[...] = dh
+        low = dh.astype(BF)
         for t in range(parts):
-            w = gathered_rows(ids, (wa_ref, wb_ref), gathered.order, t, height)
-            for r in range(0, length, TILE):
-                out_ref[r : r + TILE, t * half : (t + 1) * half] = dot_f32(
-                    low_ref[r : r + TILE], w, 1, 0
-                ).astype(BF)
-        store_natural(low_ref[...], lt_ref)
-
-    square = whole((length, width))
+            out_ref[:, t * half : (t + 1) * half] = dot_f32(low, w_ref[t], 1, 0).astype(BF)
+        store_transposed(ids, low, blocks_ref, lt_ref)
+
+    tile = pl.BlockSpec((TILE, width), lambda r, ids: (r, 0))
     return call(
         body,
         "norm_and_project_back",
         ids,
-        (share, *gots, hidden, grads, gain, *gathered.pair),
+        (share, *gots, hidden, grads, gain, w_out),
         [
-            square,
-            *[whole(g.shape) for g in gots],
-            square,
-            pl.BlockSpec((1, length, width), lambda g, ids: (0, 0, 0)),
+            tile,
+            pl.BlockSpec((TILE, width), lambda r, ids: (jnp.minimum(r, cut - 1), 0)),
+            pl.BlockSpec((TILE, width), lambda r, ids: (jnp.maximum(r - cut, 0), 0)),
+            tile,
+            pl.BlockSpec((1, TILE, width), lambda r, ids: (0, r, 0)),
             whole((1, width)),
-        ]
-        + [whole(a.shape) for a in gathered.pair],
+            whole(w_out.shape),
+        ],
         (
             shape((length, width), F32),
             shape((fsdp, height, length), BF),
             shape((length, width), BF),
         ),
-        [square, whole((fsdp, height, length)), square],
-        (1,),
-        (pltpu.VMEM((length, width), BF),),
-    )
-
-
-def out_grad_halves(ids, left, right):
-    fsdp, height, length = left.shape
-    half = right.shape[1] // 2
-
-    def body(ids, l_ref, r_ref, keep_ref, send_ref):
-        def make(out_ref):
-            for f in range(0, fsdp, 4):
-                a = l_ref[f : f + 4].reshape(4 * height, length)
-                out_ref[f : f + 4] = (
-                    dot_f32(a, r_ref[...], 1, 0).astype(BF).reshape(4, height, half)
-                )
-
-        pl.when(pl.program_id(0) == 0)(lambda: make(send_ref))
-        pl.when(pl.program_id(0) == 1)(lambda: make(keep_ref))
-
-    blocks = whole((fsdp, height, half))
-    return call(
-        body,
-        "grad_out",
-        ids,
-        (left, right),
-        [whole(left.shape), pl.BlockSpec((length, half), lambda s, ids: (0, (1 - s) ^ ids[0]))],
-        (shape((fsdp, height, half), BF),) * 2,
-        [blocks, blocks],
-        (2,),
+        [tile, pl.BlockSpec((fsdp, height, TILE), lambda r, ids: (0, 0, r)), tile],
+        (length // TILE,),
+        (pltpu.VMEM((fsdp, height, TILE), BF), pltpu.VMEM((TILE, width), BF)),
     )
 
 
@@ -1093,60 +1089,51 @@
         out_ref[0, pl.ds(n, values.shape[0], stride=lines)] = values[:, n * 128 : (n + 1) * 128]
 
 
-def qkv_back(ids, d_qkv, gathered, x, dh, gain, sent):
+def qkv_back(ids, d_qkv, weights, x, dh, gain, sent):
     length, width = x.shape
-    fsdp = gathered[1].pair[0].shape[0]
-    height = width // fsdp
-    parts = 2
-    half = width // parts
+    parts, _, half = weights.shape[1:]
     kept = length // parts
-
-    def body(ids, d_ref, *refs):
-        x_ref, dh_ref, gain_ref, out_ref, acc_ref = refs[-5:]
+    per = kept // TILE
+
+    def body(ids, d_ref, w_ref, x_ref, dh_ref, gain_ref, out_ref, acc_ref):
+        d_normed = None
         for c in range(3):
             for t in range(parts):
-                w = gathered_rows(ids, refs[2 * c : 2 * c + 2], gathered[c].order, t, height)
-                for r in range(0, kept, TILE):
-                    part = dot_f32(d_ref[c, r : r + TILE, t * half : (t + 1) * half], w, 1, 1)
-                    if c == 0 and t == 0:
-                        acc_ref[r : r + TILE] = part
-                    else:
-                        acc_ref[r : r + TILE] += part
-        for r in range(0, kept, TILE):
-            rows = x_ref[r : r + TILE].astype(F32)
-            scale = rms_scale(rows)
-            normed = rows * scale
-            d_normed = acc_ref[r : r + TILE]
-            acc_ref[r : r + TILE] = dh_ref[r : r + TILE] + norm_backward_pass(
-                d_normed, normed, scale, gain_ref[...]
-            )
+                part = dot_f32(d_ref[c, :, t * half : (t + 1) * half], w_ref[c, t], 1, 1)
+                d_normed = part if d_normed is None else d_normed + part
+        rows = x_ref[...].astype(F32)
+        scale = rms_scale(rows)
+        made = dh_ref[...] + norm_backward_pass(d_normed, rows * scale, scale, gain_ref[...])
         if sent:
-            out_ref[...] = acc_ref[...].astype(BF)
+            out_ref[...] = made.astype(BF)
         else:
+            acc_ref[...] = made
             store_lines(out_ref, acc_ref)
 
-    def rows(ids):
-        return 1 - ids[0] if sent else ids[0]
-
-    weights = [a for g in gathered for a in g.pair]
+    def rows(r, ids):
+        return per * (1 - ids[0] if sent else ids[0]) + r
+
     lines = kept * width // 128
     return call(
         body,
         "qkv_back",
         ids,
-        (d_qkv, *weights, x, dh, gain),
-        [pl.BlockSpec((3, kept, width), lambda g, ids: (0, rows(ids), 0))]
-        + [whole(a.shape) for a in weights]
-        + [pl.BlockSpec((kept, width), lambda g, ids: (rows(ids), 0))] * 2
-        + [whole((1, width))],
+        (d_qkv, weights, x, dh, gain),
+        [
+            pl.BlockSpec((3, TILE, width), lambda r, ids: (0, rows(r, ids), 0)),
+            whole(weights.shape),
+            pl.BlockSpec((TILE, width), lambda r, ids: (rows(r, ids), 0)),
+            pl.BlockSpec((TILE, width), lambda r, ids: (rows(r, ids), 0)),
+            whole((1, width)),
+        ],
         (shape((kept, width), BF) if sent else shape((parts, lines, 128), F32),),
         [
-            whole((kept, width))
+            pl.BlockSpec((TILE, width), lambda r, ids: (r, 0))
             if sent
-            else pl.BlockSpec((1, lines, 128), lambda g, ids: (ids[0], 0, 0)),
+            else pl.BlockSpec((1, lines // per, 128), lambda r, ids: (ids[0], r, 0)),
         ],
-        (1,),
-        (pltpu.VMEM((kept, width), F32),),
+        (per,),
+        (pltpu.VMEM((TILE, width), F32),),
     )[0]
 
 
@@ -1199,22 +1186,23 @@
     def other(rows):
         return lax.dynamic_index_in_dim(rows, 1 - me_t, 0, keepdims=False)
 
-    wk = Gathered(w_qkv[1], (TENSOR, Z_FAR, X, Z_NEAR))
-    wv = Gathered(w_qkv[2], (TENSOR, Z_NEAR, Z_FAR, X))
+    o_mine = jnp.split(w_out.T, (O_ROWS[0], O_ROWS[0] + O_ROWS[1]))
+    wk = Gathered(jnp.concatenate([w_qkv[1], o_mine[1]]), (TENSOR, Z_FAR, X, Z_NEAR))
+    wv = Gathered(jnp.concatenate([w_qkv[2], o_mine[2]]), (TENSOR, Z_NEAR, Z_FAR, X))
     gains = three_parts(jnp.stack([gain_attn, gain_mlp])).reshape(1, -1)
     gains = jnp.pad(gains, ((0, 7), (0, half - gains.shape[1])))
-    wq = Gathered(jnp.concatenate([w_qkv[0], gains]), (Z_FAR, X, Z_NEAR, TENSOR))
-    o_mine = w_out.T
+    wq = Gathered(
+        jnp.concatenate([w_qkv[0], o_mine[0], gains]), (Z_FAR, X, Z_NEAR, TENSOR)
+    )
     ff_mine = jnp.concatenate([w_gate_up.reshape(2 * height, -1), w_down.T])
     aways = jnp.split(other(rows_in), 2)
     three = [wq, wk, wv]
-    o_mine = after(o_mine, three)
-    wo = Gathered(o_mine, (Z_FAR, TENSOR, Z_NEAR, X))
+    aways[0] = after(aways[0], three)
     got_one = swap(aways[0], TENSOR)
-    got_one, aways[1] = after((got_one, aways[1]), [*three, wo])
+    got_one, aways[1] = after((got_one, aways[1]), three)
     got_two = swap(aways[1], TENSOR)
-    got_two = after(got_two, [*three, wo])
-    ff_mine = after(ff_mine, [*three, wo])
+    got_two = after(got_two, three)
+    ff_mine = after(ff_mine, three)
     packed = lax.all_gather(ff_mine, "fsdp", axis=0, tiled=False)
     got_rows = after((got_one, got_two), three)
 
@@ -1222,35 +1210,38 @@
     each_f, each_t = each // parts, each % parts
     at = position(wq.order, each_f, each_t) ^ position(wq.order, me_f, me_t)
     at = at + fsdp * ((each_f ^ me_f) % 2)
-    gains = jnp.concatenate([a[:, height, : 6 * share] for a in wq.pair])[at]
+    row = height + O_ROWS[0]
+    gains = jnp.concatenate([a[:, row, : 6 * share] for a in wq.arrays])[at]
     gains = jnp.sum(gains.reshape(fsdp * parts, 2, share, 3).astype(F32), axis=3)
     gain_one, gain_two = [gains[:, i].reshape(1, D) for i in range(2)]
 
-    qkv, xt, x = make_qkv(ids, rows_in, got_rows, gain_one, (wq, wk, wv))
+    qkv, xt, x, w_all, wo_all = make_qkv(ids, rows_in, got_rows, gain_one, three, height)
     _, away = lax.optimization_barrier((got_rows, grads_in))
     got_grads = swap(away, TENSOR)
-    qkv = after(qkv, [wo])
-    attended, *saved = after(attend(ids, qkv), [wo])
-    hidden, hn, ht = out_project(ids, attended, wo, x, gain_two)
+    attended, *saved = attend(ids, qkv)
+    hidden, hn = out_project(ids, attended, wo_all, x, gain_two)
     hn_theirs = swap(hn, TENSOR)
-    grads, gt = join_rows(ids, grads_in, got_grads, fsdp)
+    grads = join_rows(ids, grads_in, got_grads)
     hn, grads, packed = lax.optimization_barrier((hn, grads, packed))
 
-    own = feed_forward(ids, hn, grads, 0, packed)
+    own, ht, gt = feed_forward(ids, hn, grads, 0, packed)
     own, hn_theirs = lax.optimization_barrier((own, hn_theirs))
-    theirs = feed_forward(ids, hn_theirs, grads, 1, packed)
-    ht_theirs = transposed(ids, hn_theirs, fsdp)
-    *d_theirs, = feed_forward_back(ids, theirs, packed, local_rows * parts * 3 // 4)
-    d_theirs, ht_theirs, own = lax.optimization_barrier((d_theirs, ht_theirs, own))
-    got_one = swap(d_theirs[0], TENSOR)
-    made = feed_forward_grads(ids, ht, ht_theirs, gt, own, theirs)
-    made, own, got_one, d_tail = lax.optimization_barrier((made, own, got_one, d_theirs[1]))
+    theirs, ht_theirs, gt_theirs = feed_forward(ids, hn_theirs, grads, 1, packed)
+    d_one = feed_forward_back(ids, theirs, packed, 0)
+    d_one, theirs, own = lax.optimization_barrier((d_one, theirs, own))
+    got_one = swap(d_one, TENSOR)
+    made = feed_forward_grads(ids, ht, ht_theirs, gt, gt_theirs, own, theirs)
+    made, own, theirs, got_one = lax.optimization_barrier((made, own, theirs, got_one))
     summed = lax.psum_scatter(made, "fsdp", scatter_dimension=0, tiled=False)
-    got_two = swap(d_tail, TENSOR)
-    share_own = feed_forward_back(ids, own, packed)[0]
-    share_own, got_two = lax.optimization_barrier((share_own, got_two))
+    d_two = feed_forward_back(ids, theirs, packed, 1)
+    d_two, own, theirs = lax.optimization_barrier((d_two, own, theirs))
+    got_two = swap(d_two, TENSOR)
+    share_own = feed_forward_back(ids, own, packed)
+    share_own, own, theirs = lax.optimization_barrier((share_own, own, theirs))
+    keep_out, send_out = feed_forward_out(ids, own, theirs, packed, hidden)
+    share_own, got_two, send_out = lax.optimization_barrier((share_own, got_two, send_out))
     dh, dt, d_attended = norm_and_project_back(
-        ids, share_own, (got_one, got_two), hidden, grads, gain_two, wo
+        ids, share_own, (got_one, got_two), hidden, grads, gain_two, wo_all
     )
 
     def join(values, sums):
@@ -1260,18 +1251,17 @@
         made = halve(ids, sums)
         return lax.optimization_barrier((values, made))[0]
 
-    o_keep, o_send = out_grad_halves(ids, dt, attended)
-    o_send, d_attended, own, theirs = lax.optimization_barrier((o_send, d_attended, own, theirs))
-    o_got = swap(o_send, TENSOR)
-    keep_out, send_out = feed_forward_out(ids, own, theirs, packed, hidden)
-    d_attended, send_out, o_got = lax.optimization_barrier((d_attended, send_out, o_got))
-    o_sum = (o_keep.astype(F32) + o_got.astype(F32)).astype(BF)
+    o_sum = weight_grad(ids, "grad_out", [(dt, attended[None], 0)])
+    o_sum, d_attended, send_out = lax.optimization_barrier((o_sum, d_attended, send_out))
+    o_sum = Summed(*o_sum, (X, Z_NEAR, TENSOR, Z_FAR))
     got_out = swap(send_out, TENSOR)
     d_qkv = attend_back(ids, qkv, d_attended, saved)
 
+    d_qkv = join(d_qkv, [o_sum])
+
     orders = (
-        (X, Z_NEAR, Z_FAR, TENSOR),
-        (Z_NEAR, X, TENSOR, Z_FAR),
+        (X, Z_NEAR, TENSOR, Z_FAR),
+        (Z_NEAR, X, Z_FAR, TENSOR),
         (TENSOR, Z_FAR, X, Z_NEAR),
     )
     sums = []
@@ -1280,18 +1270,17 @@
         made, d_qkv = lax.optimization_barrier((made, d_qkv))
         sums.append(Summed(*made, order))
     d_qkv = join(d_qkv, sums)
-    sent = qkv_back(ids, d_qkv, (wq, wk, wv), x, dh, gain_one, True)
-    sent, d_qkv, got_out, summed, o_sum = join((sent, d_qkv, got_out, summed, o_sum), sums)
-    o_sum = lax.psum_scatter(o_sum, "fsdp", scatter_dimension=0, tiled=False)
+    sums.append(o_sum)
+    sent = qkv_back(ids, d_qkv, w_all, x, dh, gain_one, True)
+    sent, d_qkv, got_out = join((sent, d_qkv, got_out), sums)
     layer_out = (keep_out + got_out.astype(F32)).astype(BF).reshape(tokens.shape)
     got_grad = swap(sent, TENSOR)
-    lines = qkv_back(ids, d_qkv, (wq, wk, wv), x, dh, gain_one, False)
-    lines = join(lines, sums)
+    lines = qkv_back(ids, d_qkv, w_all, x, dh, gain_one, False)
+    lines, summed = join((lines, summed), sums)
     halve(ids, sums)
-    halve(ids, sums)
-
-    input_grad = place_rows(ids, got_grad, lines).reshape(tokens.shape)
-    qkv_grad = jnp.stack([s.result for s in sums])
+    lines, got_grad = lax.optimization_barrier((lines, got_grad))
+    input_grad = join(place_rows(ids, got_grad, lines), sums).reshape(tokens.shape)
+    qkv_grad = jnp.stack([s.result for s in sums[:3]])
     summed = summed.astype(F32)
     gate_up_grad = summed[: 2 * height].reshape(w_gate_up.shape)
     from_qkv = jnp.sum(w_qkv.astype(F32) * qkv_grad, axis=(0, 2))
@@ -1305,7 +1294,7 @@
         input_grad,
         mine[0] / gain_attn,
         qkv_grad,
-        o_sum.astype(F32).T,
+        o_sum.result.T,
         mine[1] / gain_mlp,
         gate_up_grad,
         summed[2 * height :].T,

time: 513 us -> 484 us (0.943)
  Pallas kernels: 318 us -> 302 us
  other arithmetic: 20.8 us -> 9.63 us
    ppermute x17 -> x16, waiting for transfers between devices: 30.8 us -> 1.43 us  [swap(): return lax.ppermute(value, 'tensor', [(0, 1), (1, 0)])]
    ppermute x28 -> x31, waiting for transfers between devices: 33.4 us -> 54.1 us  [swap(): lax.ppermute(value, 'fsdp', [(i, i ^ bit) for i in range(lax.axis_size('f...]
    all_gather x1, waiting for transfers between devices: 11.4 us -> 30.7 us  [local_sequence(): packed = lax.all_gather(ff_mine, 'fsdp', axis=0, tiled=False)]
    pallas_call x25 -> x26, Pallas kernels: 318 us -> 302 us  [call(): pl.pallas_call(body, name=name, out_shape=outs, grid_spec=pltpu.PrefetchS...]
    reduce_scatter x1 -> x0, waiting for transfers between devices: 8.03 us -> none  [local_sequence(): o_sum = lax.psum_scatter(o_sum, 'fsdp', scatter_dimension=0, tiled=False)]
    another operation x17 -> x12, other arithmetic: 7.67 us -> 0.47 us  [advance(): self.held = jnp.stack([self.held, self.got])]
    ppermute x17 -> x16, starting transfers between devices: 18.8 us -> 16.5 us  [swap(): return lax.ppermute(value, 'tensor', [(0, 1), (1, 0)])]
    unnamed x92 -> x89, local copies, waits for them, and re-layouts: 11.8 us -> 11.1 us
  transfers between devices with their start and end apart: 48 -> 49, of which waited for: 19 -> 16; matrix products, arithmetic and copies ran while one was open for 5% -> 3% of each run, Pallas kernels for 55% -> 56%
where the time goes in v3:
time: 484 us; the launch traced here: 479 us
  Pallas kernels  302 us (62%)
  waiting for transfers between devices  86.2 us (18%)
  starting transfers between devices  44.9 us (9%)
  local copies, waits for them, and re-layouts  21.3 us (4%)
  between operations  14.8 us (3%)
  other arithmetic  9.63 us (2%)
    pallas_call x26, Pallas kernels, call(): pl.pallas_call(body, name=name, out_shape=outs, grid_spec=pltpu.PrefetchS...  302 us
    ppermute x31, waiting for transfers between devices, swap(): lax.ppermute(value, 'fsdp', [(i, i ^ bit) for i in range(lax.axis_size('f...  54.1 us
    all_gather x1, waiting for transfers between devices, local_sequence(): packed = lax.all_gather(ff_mine, 'fsdp', axis=0, tiled=False)  30.7 us
    ppermute x31, starting transfers between devices, swap(): lax.ppermute(value, 'fsdp', [(i, i ^ bit) for i in range(lax.axis_size('f...  28.4 us
    ppermute x16, starting transfers between devices, swap(): return lax.ppermute(value, 'tensor', [(0, 1), (1, 0)])  16.5 us
    unnamed x89, local copies, waits for them, and re-layouts  11.1 us
  transfers between devices with their start and end apart: 49, of which 16 were waited for; matrix products, arithmetic and copies ran while one was open for 3% of the time, Pallas kernels for 56%

profile of v3, /device:TPU:0, one launch (start us, length us, event | category | flops | bytes accessed | tf_op | source)
XLA Modules:
  0.0 479.0 jit_solution(16491112256220701317)
XLA Ops:
  8.9 3.0 collective-permute-start.2
  14.5 3.1 collective-permute-start
  18.9 2.8 collective-permute-done
  23.2 1.6 collective-permute-start.4
  25.5 3.4 collective-permute-start.5
  29.0 4.8 %collective-permute-done.5 = bf16[2,80,512]{2,1,0:T(8,128)(2,1)S(1)} collective-permute-done((bf16[2,80,512]{2,1,0:T(8,128)(2,1)S(1)}, bf16[2,80,512]{2,1,0:T(8,128)(2,1)S(1)}, u32[]{:S(2)}, u32[]{:S(2)}) %collective-permute-start.5) | collective-permute-done | bytes 163872 | tf_op jit(solution)/shard_map/ppermute | solution.py:366
  33.9 2.4 collective-permute-start.8
  36.8 3.7 collective-permute-start.10
  42.1 5.6 %collective-permute-done.9 = bf16[2,2,80,512]{3,2,1,0:T(8,128)(2,1)S(1)} collective-permute-done((bf16[2,2,80,512]{3,2,1,0:T(8,128)(2,1)S(1)}, bf16[2,2,80,512]{3,2,1,0:T(8,128)(2,1)S(1)}, u32[]{:S(2)}, u32[]{:S(2)}) %collective-permute-start.9) | collective-permute-done | bytes 327712 | tf_op jit(solution)/shard_map/ppermute | solution.py:366
  48.7 7.3 %collective-permute-done.10 = bf16[2,2,96,512]{3,2,1,0:T(8,128)(2,1)S(1)} collective-permute-done((bf16[2,2,96,512]{3,2,1,0:T(8,128)(2,1)S(1)}, bf16[2,2,96,512]{3,2,1,0:T(8,128)(2,1)S(1)}, u32[]{:S(2)}, u32[]{:S(2)}) %collective-permute-start.10) | collective-permute-done | bytes 393248 | tf_op jit(solution)/shard_map/ppermute | solution.py:366
  60.4 11.0 %collective-permute-done.12 = bf16[2,2,2,80,512]{4,3,2,1,0:T(8,128)(2,1)} collective-permute-done((bf16[2,2,2,80,512]{4,3,2,1,0:T(8,128)(2,1)S(1)}, bf16[2,2,2,80,512]{4,3,2,1,0:T(8,128)(2,1)}, u32[]{:S(2)}, u32[]{:S(2)}) %collective-permute-start.12) | collective-permute-done | bytes 655392 | tf_op jit(solution)/shard_map/ppermute | solution.py:366
  75.5 2.5 collective-permute-done.16
  82.0 18.3 %qkv.1 = (bf16[3,1024,1024]{2,1,0:T(8,128)(2,1)}, bf16[16,64,1024]{2,1,0:T(8,128)(2,1)}, bf16[1024,1024]{1,0:T(8,128)(2,1)}, bf16[3,2,1024,512]{3,2,1,0:T(8,128)(2,1)}, bf16[2,1024,512]{2,1,0:T(8,128)(2,1)}) custom-call(s32[7]{0:T(128)} %concatenate.43.ids, bf16[2,512,1024]{2,1,0:T(8,128)(2,1)} %bitcast.135, f32[1,1024]{1,0:T(1,128)} %reshape_squeeze.6.gain_ref, ...), custom_call_target="tpu_custom_call" | custom-call | flops 1024 | bytes 1024 | tf_op jit(solution)/shard_map/qkv/pallas_call | solution.py:312
  100.3 29.7 %attend.1 = (bf16[1024,1024]{1,0:T(8,128)(2,1)}, bf16[1024,1024]{1,0:T(8,128)(2,1)}, bf16[16,1024,1024]{2,1,0:T(8,128)(2,1)}, f32[8,2,1024]{2,1,0:T(2,128)}) custom-call(s32[7]{0:T(128)} %concatenate.43.ids, bf16[3,1024,1024]{2,1,0:T(8,128)(2,1)} %get-tuple-element.169.q_ref.k_ref.v_ref, bf16[3,1024,1024]{2,1,0:T(8,128)(2,1)} %get-tuple-element.169.q_ref.k_ref.v_ref, ...), custom_call_target="tpu_custom_call" | custom-call | flops 1024 | bytes 1024 | tf_op jit(solution)/shard_map/attend/pallas_call | solution.py:312
  130.7 8.1 %out_project.1 = (f32[1024,1024]{1,0:T(8,128)}, bf16[1024,1024]{1,0:T(8,128)(2,1)}) custom-call(s32[7]{0:T(128)} %concatenate.43.ids, bf16[1024,1024]{1,0:T(8,128)(2,1)} %get-tuple-element.170.a_ref, bf16[2,1024,512]{2,1,0:T(8,128)(2,1)} %get-tuple-element.171.w_ref, bf16[1024,1024]{1,0:T(8,128)(2,1)} %get-tuple-element.172.x_ref, ...), custom_call_target="tpu_custom_call" | custom-call | flops 1024 | bytes 1024 | tf_op jit(solution)/shard_map/out_project/pallas_call | solution.py:312
  139.5 4.3 join_rows.1.g_ref
  143.8 30.7 %all-gather.3.cloned.1.call-done = bf16[3072,2048]{1,0:T(8,128)(2,1)} async-done(((bf16[192,2048]{1,0:T(8,128)(2,1)}), bf16[3072,2048]{1,0:T(8,128)(2,1)}) %all-gather.3.cloned.1.call-update) | async-done | bytes 12582928 | tf_op jit(solution)/shard_map/all_gather | solution.py:1206
  174.6 20.3 %feed_forward.2 = (bf16[3,1024,2048]{2,1,0:T(8,128)(2,1)}, bf16[16,64,1024]{2,1,0:T(8,128)(2,1)}, bf16[16,64,1024]{2,1,0:T(8,128)(2,1)}) custom-call(s32[7]{0:T(128)} %concatenate.43.ids, bf16[1024,1024]{1,0:T(8,128)(2,1)} %get-tuple-element.176.hn_ref, bf16[2,1024,1024]{2,1,0:T(8,128)(2,1)} %join_rows.1.g_ref, bf16[16,192,2048]{2,1,0:T(8,128)(2,1)} %bitcast.107), custom_call_target="tpu_custom_call" | custom-call | flops 1024 | bytes 1024 | tf_op jit(solution)/shard_map/feed_forward/pallas_call | solution.py:312
  196.3 20.4 %feed_forward.3 = (bf16[3,1024,2048]{2,1,0:T(8,128)(2,1)}, bf16[16,64,1024]{2,1,0:T(8,128)(2,1)}, bf16[16,64,1024]{2,1,0:T(8,128)(2,1)}) custom-call(s32[7]{0:T(128)} %concatenate.43.ids, bf16[1024,1024]{1,0:T(8,128)(2,1)} %copy-done.22, bf16[2,1024,1024]{2,1,0:T(8,128)(2,1)} %join_rows.1.g_ref, bf16[16,192,2048]{2,1,0:T(8,128)(2,1)} %bitcast.108), custom_call_target="tpu_custom_call" | custom-call | flops 1024 | bytes 1024 | tf_op jit(solution)/shard_map/feed_forward/pallas_call | solution.py:312
  216.6 10.1 %feed_forward_back.3 = bf16[512,1024]{1,0:T(8,128)(2,1)} custom-call(s32[7]{0:T(128)} %concatenate.43.ids, bf16[3,1024,2048]{2,1,0:T(8,128)(2,1)} %get-tuple-element.195.d_ref.theirs_ref, bf16[16,192,2048]{2,1,0:T(8,128)(2,1)} %bitcast.109), custom_call_target="tpu_custom_call" | custom-call | flops 1024 | bytes 1024 | tf_op jit(solution)/shard_map/feed_forward_back/pallas_call | solution.py:312
  228.1 34.3 %feed_forward_grads.1 = bf16[16,192,2048]{2,1,0:T(8,128)(2,1)} custom-call(s32[7]{0:T(128)} %concatenate.43.ids, bf16[16,64,1024]{2,1,0:T(8,128)(2,1)} %get-tuple-element.179.h_ref, bf16[16,64,1024]{2,1,0:T(8,128)(2,1)} %get-tuple-element.182.h2_ref, bf16[16,64,1024]{2,1,0:T(8,128)(2,1)} %get-tuple-element.183.g_ref, ...), custom_call_target="tpu_custom_call" | custom-call | flops 1024 | bytes 1024 | tf_op jit(solution)/shard_map/feed_forward_grads/pallas_call | solution.py:312
  263.4 11.0 %feed_forward_back.4 = bf16[512,1024]{1,0:T(8,128)(2,1)} custom-call(s32[7]{0:T(128)} %concatenate.43.ids, bf16[3,1024,2048]{2,1,0:T(8,128)(2,1)} %get-tuple-element.195.d_ref.theirs_ref, bf16[16,192,2048]{2,1,0:T(8,128)(2,1)} %bitcast.110), custom_call_target="tpu_custom_call" | custom-call | flops 1024 | bytes 1024 | tf_op jit(solution)/shard_map/feed_forward_back/pallas_call | solution.py:312
  274.4 16.1 %feed_forward_back.5.share_ref = f32[1024,1024]{1,0:T(8,128)} custom-call(s32[7]{0:T(128)} %concatenate.43.ids, bf16[3,1024,2048]{2,1,0:T(8,128)(2,1)} %get-tuple-element.194.own_ref.d_ref, bf16[16,192,2048]{2,1,0:T(8,128)(2,1)} %bitcast.111), custom_call_target="tpu_custom_call" | custom-call | flops 1024 | bytes 1024 | tf_op jit(solution)/shard_map/feed_forward_back/pallas_call | solution.py:312
  290.5 19.1 %feed_forward_out.1 = (f32[2,512,1024]{2,1,0:T(8,128)}, bf16[2,512,1024]{2,1,0:T(8,128)(2,1)}) custom-call(s32[7]{0:T(128)} %concatenate.43.ids, bf16[3,1024,2048]{2,1,0:T(8,128)(2,1)} %get-tuple-element.194.own_ref.d_ref, bf16[3,1024,2048]{2,1,0:T(8,128)(2,1)} %get-tuple-element.195.d_ref.theirs_ref, bf16[16,192,2048]{2,1,0:T(8,128)(2,1)} %bitcast.112, ...), custom_call_target="tpu_custom_call" | custom-call | flops 1024 | bytes 1024 | tf_op jit(solution)/shard_map/feed_forward_out/pallas_call | solution.py:312
  310.6 12.0 %norm_and_project_back.1 = (f32[1024,1024]{1,0:T(8,128)}, bf16[16,64,1024]{2,1,0:T(8,128)(2,1)}, bf16[1024,1024]{1,0:T(8,128)(2,1)}) custom-call(s32[7]{0:T(128)} %concatenate.43.ids, f32[1024,1024]{1,0:T(8,128)} %feed_forward_back.5.share_ref, bf16[512,1024]{1,0:T(8,128)(2,1)} %copy-done.23, bf16[512,1024]{1,0:T(8,128)(2,1)} %copy-done.24, ...), custom_call_target="tpu_custom_call" | custom-call | flops 1024 | bytes 1024 | tf_op jit(solution)/shard_map/norm_and_project_back/pallas_call | solution.py:312
  322.5 6.2 %grad_out.1 = (bf16[2,8,64,512]{3,2,1,0:T(8,128)(2,1)}, bf16[2,8,64,512]{3,2,1,0:T(8,128)(2,1)}) custom-call(s32[7]{0:T(128)} %concatenate.43.ids, bf16[16,64,1024]{2,1,0:T(8,128)(2,1)} %get-tuple-element.205.refs_0_, bf16[1,1024,1024]{2,1,0:T(8,128)(2,1)} %bitcast.134), custom_call_target="tpu_custom_call" | custom-call | flops 1024 | bytes 1024 | tf_op jit(solution)/shard_map/grad_out/pallas_call | solution.py:312
  328.7 2.2 collective-permute-start.28
  330.9 31.9 %attend_back.1.refs_1_.d_ref = bf16[3,1024,1024]{2,1,0:T(8,128)(2,1)} custom-call(s32[7]{0:T(128)} %concatenate.43.ids, bf16[3,1024,1024]{2,1,0:T(8,128)(2,1)} %get-tuple-element.169.q_ref.k_ref.v_ref, bf16[3,1024,1024]{2,1,0:T(8,128)(2,1)} %get-tuple-element.169.q_ref.k_ref.v_ref, bf16[3,1024,1024]{2,1,0:T(8,128)(2,1)} %get-tuple-element.169.q_ref.k_ref.v_ref, ...), custom_call_target="tpu_custom_call" | custom-call | flops 1024 | bytes 1024 | tf_op jit(solution)/shard_map/attend_back/pallas_call | solution.py:312
  363.7 2.9 halve.6
  366.6 5.9 %grad_qkv.3 = (bf16[2,8,64,512]{3,2,1,0:T(8,128)(2,1)}, bf16[2,8,64,512]{3,2,1,0:T(8,128)(2,1)}) custom-call(s32[7]{0:T(128)} %concatenate.43.ids, bf16[16,64,1024]{2,1,0:T(8,128)(2,1)} %get-tuple-element.198.refs_0_, bf16[3,1024,1024]{2,1,0:T(8,128)(2,1)} %attend_back.1.refs_1_.d_ref), custom_call_target="tpu_custom_call" | custom-call | flops 1024 | bytes 1024 | tf_op jit(solution)/shard_map/grad_qkv/pallas_call | solution.py:312
  372.6 6.0 %grad_qkv.4 = (bf16[2,8,64,512]{3,2,1,0:T(8,128)(2,1)}, bf16[2,8,64,512]{3,2,1,0:T(8,128)(2,1)}) custom-call(s32[7]{0:T(128)} %concatenate.43.ids, bf16[16,64,1024]{2,1,0:T(8,128)(2,1)} %get-tuple-element.198.refs_0_, bf16[3,1024,1024]{2,1,0:T(8,128)(2,1)} %attend_back.1.refs_1_.d_ref), custom_call_target="tpu_custom_call" | custom-call | flops 1024 | bytes 1024 | tf_op jit(solution)/shard_map/grad_qkv/pallas_call | solution.py:312
  378.6 6.3 %grad_qkv.5 = (bf16[2,8,64,512]{3,2,1,0:T(8,128)(2,1)}, bf16[2,8,64,512]{3,2,1,0:T(8,128)(2,1)}) custom-call(s32[7]{0:T(128)} %concatenate.43.ids, bf16[16,64,1024]{2,1,0:T(8,128)(2,1)} %get-tuple-element.198.refs_0_, bf16[3,1024,1024]{2,1,0:T(8,128)(2,1)} %attend_back.1.refs_1_.d_ref), custom_call_target="tpu_custom_call" | custom-call | flops 1024 | bytes 1024 | tf_op jit(solution)/shard_map/grad_qkv/pallas_call | solution.py:312
  385.5 3.1 collective-permute-done.27.refs_5_.refs_7_.refs_9_.refs_11_.refs_13_
  390.1 3.5 halve.7
  394.2 9.4 %qkv_back.2 = bf16[512,1024]{1,0:T(8,128)(2,1)} custom-call(s32[7]{0:T(128)} %concatenate.43.ids, bf16[3,1024,1024]{2,1,0:T(8,128)(2,1)} %attend_back.1.refs_1_.d_ref, bf16[3,2,1024,512]{3,2,1,0:T(8,128)(2,1)} %get-tuple-element.242.w_ref, bf16[1024,1024]{1,0:T(8,128)(2,1)} %get-tuple-element.172.x_ref, f32[1024,1024]{1,0:T(8,128)} %get-tuple-element.243.dh_ref, ...), custom_call_target="tpu_custom_call" | custom-call | flops 1024 | bytes 1024 | tf_op jit(solution)/shard_map/qkv_back/pallas_call | solution.py:312
  403.6 7.4 %collective-permute-done.29.refs_2_ = bf16[2,2,2,64,512]{4,3,2,1,0:T(8,128)(2,1)S(1)} collective-permute-done((bf16[2,2,2,64,512]{4,3,2,1,0:T(8,128)(2,1)}, bf16[2,2,2,64,512]{4,3,2,1,0:T(8,128)(2,1)S(1)}, u32[]{:S(2)}, u32[]{:S(2)}) %collective-permute-start.29) | collective-permute-done | bytes 524320 | tf_op jit(solution)/shard_map/ppermute | solution.py:366
  412.7 3.5 halve.8
  417.0 1.7 collective-permute-start.35
  420.1 9.8 %qkv_back.3._ = f32[2,4096,128]{2,1,0:T(8,128)} custom-call(s32[7]{0:T(128)} %concatenate.43.ids, bf16[3,1024,1024]{2,1,0:T(8,128)(2,1)} %attend_back.1.refs_1_.d_ref, bf16[3,2,1024,512]{3,2,1,0:T(8,128)(2,1)} %get-tuple-element.242.w_ref, bf16[1024,1024]{1,0:T(8,128)(2,1)} %get-tuple-element.172.x_ref, f32[1024,1024]{1,0:T(8,128)} %get-tuple-element.243.dh_ref, ...), custom_call_target="tpu_custom_call" | custom-call | flops 1024 | bytes 1024 | tf_op jit(solution)/shard_map/qkv_back/pallas_call | solution.py:312
  431.5 4.3 collective-permute-done.36.refs_15_.refs_18_.refs_21_
  436.4 3.5 halve.9
  440.0 1.7 collective-permute-start.38
  443.8 3.8 fusion
  447.7 1.6 collective-permute-done.39.refs_9_.refs_10_
  450.7 2.8 halve.10
  457.4 3.8 place_rows.1
  462.7 3.0 halve.11
  465.8 1.9 multiply_reduce_fusion.1
  (219 shorter events, 52.5 us)
Async XLA Ops:
  7.2 167.4 %all-gather.3.cloned.1.call-start = ((), (), s32[]{:S(2)}) async-start(), calls=%async_computation.2 | async-start | bytes 13369344 | tf_op jit(solution)/shard_map/all_gather | solution.py:1206
  8.9 12.8 %collective-permute-start.2 = (bf16[96,512]{1,0:T(8,128)(2,1)S(1)}, bf16[96,512]{1,0:T(8,128)(2,1)S(1)}, u32[]{:S(2)}, u32[]{:S(2)}) collective-permute-start(bf16[96,512]{1,0:T(8,128)(2,1)S(1)} %get-tuple-element.356), channel_id=1, source_target_pairs={{0,1},{1,0},{2,3},{3,2},{4,5},{5,4},{6,7},{7,6},{8,9},{9,8},{10,11... | collective-permute-start | bytes 294920 | tf_op jit(solution)/shard_map/ppermute | solution.py:365
  12.7 6.2 %collective-permute-start.1 = (bf16[80,512]{1,0:T(8,128)(2,1)S(1)}, bf16[80,512]{1,0:T(8,128)(2,1)S(1)}, u32[]{:S(2)}, u32[]{:S(2)}) collective-permute-start(bf16[80,512]{1,0:T(8,128)(2,1)S(1)} %get-tuple-element.360), channel_id=1, source_target_pairs={{0,1},{1,0},{2,3},{3,2},{4,5},{5,4},{6,7},{7,6},{8,9},{9,8},{10,11... | collective-permute-start | bytes 245768 | tf_op jit(solution)/shard_map/ppermute | solution.py:365
  14.5 7.2 %collective-permute-start = (bf16[88,512]{1,0:T(8,128)(2,1)S(1)}, bf16[88,512]{1,0:T(8,128)(2,1)S(1)}, u32[]{:S(2)}, u32[]{:S(2)}) collective-permute-start(bf16[88,512]{1,0:T(8,128)(2,1)S(1)} %get-tuple-element.358), channel_id=1, source_target_pairs={{0,16},{2,18},{4,20},{6,22},{8,24},{10,26},{12,28},{14,30},{16,0},... | collective-permute-start | bytes 270344 | tf_op jit(solution)/shard_map/ppermute | solution.py:366
  21.7 12.2 %collective-permute-start.3 = (bf16[256,1024]{1,0:T(8,128)(2,1)S(1)}, bf16[256,1024]{1,0:T(8,128)(2,1)S(1)}, u32[]{:S(2)}, u32[]{:S(2)}) collective-permute-start(bf16[256,1024]{1,0:T(8,128)(2,1)S(1)} %get-tuple-element.149), channel_id=1, source_target_pairs={{0,1},{1,0},{2,3},{3,2},{4,5},{5,4},{6,7},{7,6},{8,9},{9,8},{10,11... | collective-permute-start | bytes 1572872 | tf_op jit(solution)/shard_map/ppermute | solution.py:365
  23.2 10.6 %collective-permute-start.4 = (bf16[2,88,512]{2,1,0:T(8,128)(2,1)S(1)}, bf16[2,88,512]{2,1,0:T(8,128)(2,1)S(1)}, u32[]{:S(2)}, u32[]{:S(2)}) collective-permute-start(bf16[2,88,512]{2,1,0:T(8,128)(2,1)S(1)} %get-tuple-element.352), channel_id=1, source_target_pairs={{0,4},{2,6},{4,0},{6,2},{8,12},{10,14},{12,8},{14,10},{16,20},{18,... | collective-permute-start | bytes 540680 | tf_op jit(solution)/shard_map/ppermute | solution.py:366
  24.8 9.0 %collective-permute-start.6 = (bf16[2,96,512]{2,1,0:T(8,128)(2,1)S(1)}, bf16[2,96,512]{2,1,0:T(8,128)(2,1)S(1)}, u32[]{:S(2)}, u32[]{:S(2)}) collective-permute-start(bf16[2,96,512]{2,1,0:T(8,128)(2,1)S(1)} %get-tuple-element.347), channel_id=1, source_target_pairs={{0,8},{2,10},{4,12},{6,14},{8,0},{10,2},{12,4},{14,6},{16,24},{18,... | collective-permute-start | bytes 589832 | tf_op jit(solution)/shard_map/ppermute | solution.py:366
  25.5 8.3 %collective-permute-start.5 = (bf16[2,80,512]{2,1,0:T(8,128)(2,1)S(1)}, bf16[2,80,512]{2,1,0:T(8,128)(2,1)S(1)}, u32[]{:S(2)}, u32[]{:S(2)}) collective-permute-start(bf16[2,80,512]{2,1,0:T(8,128)(2,1)S(1)} %get-tuple-element.354), channel_id=1, source_target_pairs={{0,16},{2,18},{4,20},{6,22},{8,24},{10,26},{12,28},{14,30},{16,0},... | collective-permute-start | bytes 491528 | tf_op jit(solution)/shard_map/ppermute | solution.py:366
  33.9 14.8 %collective-permute-start.8 = (bf16[2,2,88,512]{3,2,1,0:T(8,128)(2,1)S(1)}, bf16[2,2,88,512]{3,2,1,0:T(8,128)(2,1)S(1)}, u32[]{:S(2)}, u32[]{:S(2)}) collective-permute-start(bf16[2,2,88,512]{3,2,1,0:T(8,128)(2,1)S(1)} %get-tuple-element.343), channel_id=1, source_target_pairs={{0,8},{2,10},{4,12},{6,14},{8,0},{10,2},{12,4},{14,6},{16,24},{18,... | collective-permute-start | bytes 1081352 | tf_op jit(solution)/shard_map/ppermute | solution.py:366
  36.3 19.7 %collective-permute-start.7 = (bf16[256,1024]{1,0:T(8,128)(2,1)S(1)}, bf16[256,1024]{1,0:T(8,128)(2,1)S(1)}, u32[]{:S(2)}, u32[]{:S(2)}) collective-permute-start(bf16[256,1024]{1,0:T(8,128)(2,1)S(1)} %get-tuple-element.153), channel_id=1, source_target_pairs={{0,1},{1,0},{2,3},{3,2},{4,5},{5,4},{6,7},{7,6},{8,9},{9,8},{10,11... | collective-permute-start | bytes 1572872 | tf_op jit(solution)/shard_map/ppermute | solution.py:365
  36.8 19.1 %collective-permute-start.10 = (bf16[2,2,96,512]{3,2,1,0:T(8,128)(2,1)S(1)}, bf16[2,2,96,512]{3,2,1,0:T(8,128)(2,1)S(1)}, u32[]{:S(2)}, u32[]{:S(2)}) collective-permute-start(bf16[2,2,96,512]{3,2,1,0:T(8,128)(2,1)S(1)} %get-tuple-element.341), channel_id=1, source_target_pairs={{0,16},{2,18},{4,20},{6,22},{8,24},{10,26},{12,28},{14,30},{16,0},... | collective-permute-start | bytes 1179656 | tf_op jit(solution)/shard_map/ppermute | solution.py:366
  40.6 7.1 %collective-permute-start.9 = (bf16[2,2,80,512]{3,2,1,0:T(8,128)(2,1)S(1)}, bf16[2,2,80,512]{3,2,1,0:T(8,128)(2,1)S(1)}, u32[]{:S(2)}, u32[]{:S(2)}) collective-permute-start(bf16[2,2,80,512]{3,2,1,0:T(8,128)(2,1)S(1)} %get-tuple-element.345), channel_id=1, source_target_pairs={{0,4},{2,6},{4,0},{6,2},{8,12},{10,14},{12,8},{14,10},{16,20},{18,... | collective-permute-start | bytes 983048 | tf_op jit(solution)/shard_map/ppermute | solution.py:366
  56.9 14.4 %collective-permute-start.13 = (bf16[2,2,2,96,512]{4,3,2,1,0:T(8,128)(2,1)S(1)}, bf16[2,2,2,96,512]{4,3,2,1,0:T(8,128)(2,1)S(1)}, u32[]{:S(2)}, u32[]{:S(2)}) collective-permute-start(bf16[2,2,2,96,512]{4,3,2,1,0:T(8,128)(2,1)S(1)} %pad_maximum_fusion.1), channel_id=1, source_target_pairs={{0,4},{2,6},{4,0},{6,2},{8,12},{10,14},{12,8},{14,10},{16,20},{18,... | collective-permute-start | bytes 2359304 | tf_op jit(solution)/shard_map/ppermute | solution.py:366
  58.6 12.8 %collective-permute-start.11 = (bf16[2,2,2,88,512]{4,3,2,1,0:T(8,128)(2,1)S(1)}, bf16[2,2,2,88,512]{4,3,2,1,0:T(8,128)(2,1)}, u32[]{:S(2)}, u32[]{:S(2)}) collective-permute-start(bf16[2,2,2,88,512]{4,3,2,1,0:T(8,128)(2,1)S(1)} %pad_maximum_fusion.2), channel_id=1, source_target_pairs={{0,1},{1,0},{2,3},{3,2},{4,5},{5,4},{6,7},{7,6},{8,9},{9,8},{10,11... | collective-permute-start | bytes 2162696 | tf_op jit(solution)/shard_map/ppermute | solution.py:365
  59.2 12.2 %collective-permute-start.12 = (bf16[2,2,2,80,512]{4,3,2,1,0:T(8,128)(2,1)S(1)}, bf16[2,2,2,80,512]{4,3,2,1,0:T(8,128)(2,1)}, u32[]{:S(2)}, u32[]{:S(2)}) collective-permute-start(bf16[2,2,2,80,512]{4,3,2,1,0:T(8,128)(2,1)S(1)} %pad_maximum_fusion.3), channel_id=1, source_target_pairs={{0,8},{2,10},{4,12},{6,14},{8,0},{10,2},{12,4},{14,6},{16,24},{18,... | collective-permute-start | bytes 1966088 | tf_op jit(solution)/shard_map/ppermute | solution.py:366
  71.4 364.3 %reduce-scatter.2.cloned.1.call-start = ((), (), s32[]{:S(2)}) async-start(), calls=%async_computation.1 | async-start | bytes 13369344 | tf_op jit(solution)/shard_map/reduce_scatter | solution.py:1235
  71.5 6.5 %collective-permute-start.17 = (bf16[2,2,2,96,512]{4,3,2,1,0:T(8,128)(2,1)S(1)}, bf16[2,2,2,96,512]{4,3,2,1,0:T(8,128)(2,1)}, u32[]{:S(2)}, u32[]{:S(2)}) collective-permute-start(bf16[2,2,2,96,512]{4,3,2,1,0:T(8,128)(2,1)S(1)} %collective-permute-done.13), channel_id=1, source_target_pairs={{0,2},{2,0},{4,6},{6,4},{8,10},{10,8},{12,14},{14,12},{16,18},{18,... | collective-permute-start | bytes 2359304 | tf_op jit(solution)/shard_map/ppermute | solution.py:366
  72.0 6.0 %collective-permute-start.15 = (bf16[2,2,2,88,512]{4,3,2,1,0:T(8,128)(2,1)}, bf16[2,2,2,88,512]{4,3,2,1,0:T(8,128)(2,1)}, u32[]{:S(2)}, u32[]{:S(2)}) collective-permute-start(bf16[2,2,2,88,512]{4,3,2,1,0:T(8,128)(2,1)} %collective-permute-done.11), channel_id=1, source_target_pairs={{0,2},{2,0},{4,6},{6,4},{8,10},{10,8},{12,14},{14,12},{16,18},{18,... | collective-permute-start | bytes 2162696 | tf_op jit(solution)/shard_map/ppermute | solution.py:366
  72.1 5.9 %collective-permute-start.16 = (bf16[2,2,2,80,512]{4,3,2,1,0:T(8,128)(2,1)}, bf16[2,2,2,80,512]{4,3,2,1,0:T(8,128)(2,1)}, u32[]{:S(2)}, u32[]{:S(2)}) collective-permute-start(bf16[2,2,2,80,512]{4,3,2,1,0:T(8,128)(2,1)} %collective-permute-done.12), channel_id=1, source_target_pairs={{0,2},{2,0},{4,6},{6,4},{8,10},{10,8},{12,14},{14,12},{16,18},{18,... | collective-permute-start | bytes 1966088 | tf_op jit(solution)/shard_map/ppermute | solution.py:366
  73.2 8.8 %collective-permute-start.18 = (bf16[2,2,2,80,512]{4,3,2,1,0:T(8,128)(2,1)S(1)}, bf16[2,2,2,80,512]{4,3,2,1,0:T(8,128)(2,1)}, u32[]{:S(2)}, u32[]{:S(2)}) collective-permute-start(bf16[2,2,2,80,512]{4,3,2,1,0:T(8,128)(2,1)S(1)} %pad_maximum_fusion.3), channel_id=1, source_target_pairs={{0,2},{2,0},{4,6},{6,4},{8,10},{10,8},{12,14},{14,12},{16,18},{18,... | collective-permute-start | bytes 1966088 | tf_op jit(solution)/shard_map/ppermute | solution.py:366
  73.8 8.1 %collective-permute-start.19 = (bf16[2,2,2,96,512]{4,3,2,1,0:T(8,128)(2,1)S(1)}, bf16[2,2,2,96,512]{4,3,2,1,0:T(8,128)(2,1)}, u32[]{:S(2)}, u32[]{:S(2)}) collective-permute-start(bf16[2,2,2,96,512]{4,3,2,1,0:T(8,128)(2,1)S(1)} %pad_maximum_fusion.1), channel_id=1, source_target_pairs={{0,2},{2,0},{4,6},{6,4},{8,10},{10,8},{12,14},{14,12},{16,18},{18,... | collective-permute-start | bytes 2359304 | tf_op jit(solution)/shard_map/ppermute | solution.py:366
  80.4 59.1 %collective-permute-start.20 = (bf16[2,512,1024]{2,1,0:T(8,128)(2,1)}, bf16[2,512,1024]{2,1,0:T(8,128)(2,1)}, u32[]{:S(2)}, u32[]{:S(2)}) collective-permute-start(bf16[2,512,1024]{2,1,0:T(8,128)(2,1)} %bitcast.145), channel_id=1, source_target_pairs={{0,1},{1,0},{2,3},{3,2},{4,5},{5,4},{6,7},{7,6},{8,9},{9,8},{10,11... | collective-permute-start | bytes 6291464 | tf_op jit(solution)/shard_map/ppermute | solution.py:365
  138.8 56.1 %collective-permute-start.21 = (bf16[1024,1024]{1,0:T(8,128)(2,1)}, bf16[1024,1024]{1,0:T(8,128)(2,1)S(1)}, u32[]{:S(2)}, u32[]{:S(2)}) collective-permute-start(bf16[1024,1024]{1,0:T(8,128)(2,1)} %get-tuple-element.176.hn_ref), channel_id=1, source_target_pairs={{0,1},{1,0},{2,3},{3,2},{4,5},{5,4},{6,7},{7,6},{8,9},{9,8},{10,11... | collective-permute-start | bytes 6291464 | tf_op jit(solution)/shard_map/ppermute | solution.py:365
  226.7 35.8 %collective-permute-start.22 = (bf16[512,1024]{1,0:T(8,128)(2,1)}, bf16[512,1024]{1,0:T(8,128)(2,1)S(1)}, u32[]{:S(2)}, u32[]{:S(2)}) collective-permute-start(bf16[512,1024]{1,0:T(8,128)(2,1)} %feed_forward_back.3), channel_id=1, source_target_pairs={{0,1},{1,0},{2,3},{3,2},{4,5},{5,4},{6,7},{7,6},{8,9},{9,8},{10,11... | collective-permute-start | bytes 3145736 | tf_op jit(solution)/shard_map/ppermute | solution.py:365
  274.4 35.2 %collective-permute-start.23 = (bf16[512,1024]{1,0:T(8,128)(2,1)}, bf16[512,1024]{1,0:T(8,128)(2,1)S(1)}, u32[]{:S(2)}, u32[]{:S(2)}) collective-permute-start(bf16[512,1024]{1,0:T(8,128)(2,1)} %feed_forward_back.4), channel_id=1, source_target_pairs={{0,1},{1,0},{2,3},{3,2},{4,5},{5,4},{6,7},{7,6},{8,9},{9,8},{10,11... | collective-permute-start | bytes 3145736 | tf_op jit(solution)/shard_map/ppermute | solution.py:365
  328.7 34.1 %collective-permute-start.24 = (bf16[2,2,2,2,64,512]{5,4,3,2,1,0:T(8,128)(2,1)}, bf16[2,2,2,2,64,512]{5,4,3,2,1,0:T(8,128)(2,1)S(1)}, u32[]{:S(2)}, u32[]{:S(2)}) collective-permute-start(bf16[2,2,2,2,64,512]{5,4,3,2,1,0:T(8,128)(2,1)} %bitcast.171), channel_id=1, source_target_pairs={{0,2},{2,0},{4,6},{6,4},{8,10},{10,8},{12,14},{14,12},{16,18},{18,... | collective-permute-start | bytes 3145736 | tf_op jit(solution)/shard_map/ppermute | solution.py:366
  328.7 74.9 %collective-permute-start.28 = (bf16[2,512,1024]{2,1,0:T(8,128)(2,1)S(1)}, bf16[2,512,1024]{2,1,0:T(8,128)(2,1)}, u32[]{:S(2)}, u32[]{:S(2)}) collective-permute-start(bf16[2,512,1024]{2,1,0:T(8,128)(2,1)S(1)} %copy-done.41), channel_id=1, source_target_pairs={{0,1},{1,0},{2,3},{3,2},{4,5},{5,4},{6,7},{7,6},{8,9},{9,8},{10,11... | collective-permute-start | bytes 6291464 | tf_op jit(solution)/shard_map/ppermute | solution.py:365
  372.6 12.9 %collective-permute-start.25 = (bf16[2,2,2,2,64,512]{5,4,3,2,1,0:T(8,128)(2,1)}, bf16[2,2,2,2,64,512]{5,4,3,2,1,0:T(8,128)(2,1)S(1)}, u32[]{:S(2)}, u32[]{:S(2)}) collective-permute-start(bf16[2,2,2,2,64,512]{5,4,3,2,1,0:T(8,128)(2,1)} %bitcast.169), channel_id=1, source_target_pairs={{0,2},{2,0},{4,6},{6,4},{8,10},{10,8},{12,14},{14,12},{16,18},{18,... | collective-permute-start | bytes 3145736 | tf_op jit(solution)/shard_map/ppermute | solution.py:366
  384.9 3.7 collective-permute-start.27
  385.4 3.8 collective-permute-start.26
  385.4 18.1 %collective-permute-start.32 = (bf16[2,2,2,64,512]{4,3,2,1,0:T(8,128)(2,1)S(1)}, bf16[2,2,2,64,512]{4,3,2,1,0:T(8,128)(2,1)S(1)}, u32[]{:S(2)}, u32[]{:S(2)}) collective-permute-start(bf16[2,2,2,64,512]{4,3,2,1,0:T(8,128)(2,1)S(1)} %copy-done.33), channel_id=1, source_target_pairs={{0,4},{2,6},{4,0},{6,2},{8,12},{10,14},{12,8},{14,10},{16,20},{18,... | collective-permute-start | bytes 1572872 | tf_op jit(solution)/shard_map/ppermute | solution.py:366
  393.6 17.3 %collective-permute-start.29 = (bf16[2,2,2,64,512]{4,3,2,1,0:T(8,128)(2,1)}, bf16[2,2,2,64,512]{4,3,2,1,0:T(8,128)(2,1)S(1)}, u32[]{:S(2)}, u32[]{:S(2)}) collective-permute-start(bf16[2,2,2,64,512]{4,3,2,1,0:T(8,128)(2,1)} %get-tuple-element.238), channel_id=1, source_target_pairs={{0,4},{2,6},{4,0},{6,2},{8,12},{10,14},{12,8},{14,10},{16,20},{18,... | collective-permute-start | bytes 1572872 | tf_op jit(solution)/shard_map/ppermute | solution.py:366
  393.6 17.3 %collective-permute-start.30 = (bf16[2,2,2,64,512]{4,3,2,1,0:T(8,128)(2,1)}, bf16[2,2,2,64,512]{4,3,2,1,0:T(8,128)(2,1)S(1)}, u32[]{:S(2)}, u32[]{:S(2)}) collective-permute-start(bf16[2,2,2,64,512]{4,3,2,1,0:T(8,128)(2,1)} %get-tuple-element.239), channel_id=1, source_target_pairs={{0,8},{2,10},{4,12},{6,14},{8,0},{10,2},{12,4},{14,6},{16,24},{18,... | collective-permute-start | bytes 1572872 | tf_op jit(solution)/shard_map/ppermute | solution.py:366
  394.2 16.8 %collective-permute-start.31 = (bf16[2,2,2,64,512]{4,3,2,1,0:T(8,128)(2,1)}, bf16[2,2,2,64,512]{4,3,2,1,0:T(8,128)(2,1)S(1)}, u32[]{:S(2)}, u32[]{:S(2)}) collective-permute-start(bf16[2,2,2,64,512]{4,3,2,1,0:T(8,128)(2,1)} %get-tuple-element.240), channel_id=1, source_target_pairs={{0,1},{1,0},{2,3},{3,2},{4,5},{5,4},{6,7},{7,6},{8,9},{9,8},{10,11... | collective-permute-start | bytes 1572872 | tf_op jit(solution)/shard_map/ppermute | solution.py:365
  416.3 41.1 %collective-permute-start.37 = (bf16[512,1024]{1,0:T(8,128)(2,1)}, bf16[512,1024]{1,0:T(8,128)(2,1)}, u32[]{:S(2)}, u32[]{:S(2)}) collective-permute-start(bf16[512,1024]{1,0:T(8,128)(2,1)} %qkv_back.2), channel_id=1, source_target_pairs={{0,1},{1,0},{2,3},{3,2},{4,5},{5,4},{6,7},{7,6},{8,9},{9,8},{10,11... | collective-permute-start | bytes 3145736 | tf_op jit(solution)/shard_map/ppermute | solution.py:365
  416.4 15.1 %collective-permute-start.33 = (bf16[2,2,64,512]{3,2,1,0:T(8,128)(2,1)}, bf16[2,2,64,512]{3,2,1,0:T(8,128)(2,1)S(1)}, u32[]{:S(2)}, u32[]{:S(2)}) collective-permute-start(bf16[2,2,64,512]{3,2,1,0:T(8,128)(2,1)} %get-tuple-element.252), channel_id=1, source_target_pairs={{0,8},{2,10},{4,12},{6,14},{8,0},{10,2},{12,4},{14,6},{16,24},{18,... | collective-permute-start | bytes 786440 | tf_op jit(solution)/shard_map/ppermute | solution.py:366
  416.4 15.0 %collective-permute-start.34 = (bf16[2,2,64,512]{3,2,1,0:T(8,128)(2,1)}, bf16[2,2,64,512]{3,2,1,0:T(8,128)(2,1)S(1)}, u32[]{:S(2)}, u32[]{:S(2)}) collective-permute-start(bf16[2,2,64,512]{3,2,1,0:T(8,128)(2,1)} %get-tuple-element.253), channel_id=1, source_target_pairs={{0,4},{2,6},{4,0},{6,2},{8,12},{10,14},{12,8},{14,10},{16,20},{18,... | collective-permute-start | bytes 786440 | tf_op jit(solution)/shard_map/ppermute | solution.py:366
  417.0 14.5 %collective-permute-start.35 = (bf16[2,2,64,512]{3,2,1,0:T(8,128)(2,1)}, bf16[2,2,64,512]{3,2,1,0:T(8,128)(2,1)S(1)}, u32[]{:S(2)}, u32[]{:S(2)}) collective-permute-start(bf16[2,2,64,512]{3,2,1,0:T(8,128)(2,1)} %get-tuple-element.254), channel_id=1, source_target_pairs={{0,16},{2,18},{4,20},{6,22},{8,24},{10,26},{12,28},{14,30},{16,0},... | collective-permute-start | bytes 786440 | tf_op jit(solution)/shard_map/ppermute | solution.py:366
  418.7 17.1 %collective-permute-start.36 = (bf16[2,2,64,512]{3,2,1,0:T(8,128)(2,1)}, bf16[2,2,64,512]{3,2,1,0:T(8,128)(2,1)S(1)}, u32[]{:S(2)}, u32[]{:S(2)}) collective-permute-start(bf16[2,2,64,512]{3,2,1,0:T(8,128)(2,1)} %get-tuple-element.255), channel_id=1, source_target_pairs={{0,8},{2,10},{4,12},{6,14},{8,0},{10,2},{12,4},{14,6},{16,24},{18,... | collective-permute-start | bytes 786440 | tf_op jit(solution)/shard_map/ppermute | solution.py:366
  440.0 7.7 %collective-permute-start.38 = (bf16[2,64,512]{2,1,0:T(8,128)(2,1)}, bf16[2,64,512]{2,1,0:T(8,128)(2,1)S(1)}, u32[]{:S(2)}, u32[]{:S(2)}) collective-permute-start(bf16[2,64,512]{2,1,0:T(8,128)(2,1)} %get-tuple-element.265), channel_id=1, source_target_pairs={{0,1},{1,0},{2,3},{3,2},{4,5},{5,4},{6,7},{7,6},{8,9},{9,8},{10,11... | collective-permute-start | bytes 393224 | tf_op jit(solution)/shard_map/ppermute | solution.py:365
  441.7 7.7 %collective-permute-start.39 = (bf16[2,64,512]{2,1,0:T(8,128)(2,1)}, bf16[2,64,512]{2,1,0:T(8,128)(2,1)S(1)}, u32[]{:S(2)}, u32[]{:S(2)}) collective-permute-start(bf16[2,64,512]{2,1,0:T(8,128)(2,1)} %get-tuple-element.266), channel_id=1, source_target_pairs={{0,16},{2,18},{4,20},{6,22},{8,24},{10,26},{12,28},{14,30},{16,0},... | collective-permute-start | bytes 393224 | tf_op jit(solution)/shard_map/ppermute | solution.py:366
  442.2 7.1 %collective-permute-start.40 = (bf16[2,64,512]{2,1,0:T(8,128)(2,1)}, bf16[2,64,512]{2,1,0:T(8,128)(2,1)S(1)}, u32[]{:S(2)}, u32[]{:S(2)}) collective-permute-start(bf16[2,64,512]{2,1,0:T(8,128)(2,1)} %get-tuple-element.267), channel_id=1, source_target_pairs={{0,4},{2,6},{4,0},{6,2},{8,12},{10,14},{12,8},{14,10},{16,20},{18,... | collective-permute-start | bytes 393224 | tf_op jit(solution)/shard_map/ppermute | solution.py:366
  443.4 5.9 %collective-permute-start.41 = (bf16[2,64,512]{2,1,0:T(8,128)(2,1)}, bf16[2,64,512]{2,1,0:T(8,128)(2,1)S(1)}, u32[]{:S(2)}, u32[]{:S(2)}) collective-permute-start(bf16[2,64,512]{2,1,0:T(8,128)(2,1)} %get-tuple-element.268), channel_id=1, source_target_pairs={{0,1},{1,0},{2,3},{3,2},{4,5},{5,4},{6,7},{7,6},{8,9},{9,8},{10,11... | collective-permute-start | bytes 393224 | tf_op jit(solution)/shard_map/ppermute | solution.py:365
  453.5 7.9 %collective-permute-start.42 = (bf16[64,512]{1,0:T(8,128)(2,1)}, bf16[64,512]{1,0:T(8,128)(2,1)S(1)}, u32[]{:S(2)}, u32[]{:S(2)}) collective-permute-start(bf16[64,512]{1,0:T(8,128)(2,1)} %get-tuple-element.273), channel_id=1, source_target_pairs={{0,16},{2,18},{4,20},{6,22},{8,24},{10,26},{12,28},{14,30},{16,0},... | collective-permute-start | bytes 196616 | tf_op jit(solution)/shard_map/ppermute | solution.py:366
  453.9 7.5 %collective-permute-start.43 = (bf16[64,512]{1,0:T(8,128)(2,1)}, bf16[64,512]{1,0:T(8,128)(2,1)S(1)}, u32[]{:S(2)}, u32[]{:S(2)}) collective-permute-start(bf16[64,512]{1,0:T(8,128)(2,1)} %get-tuple-element.274), channel_id=1, source_target_pairs={{0,1},{1,0},{2,3},{3,2},{4,5},{5,4},{6,7},{7,6},{8,9},{9,8},{10,11... | collective-permute-start | bytes 196616 | tf_op jit(solution)/shard_map/ppermute | solution.py:365
  455.2 6.2 %collective-permute-start.44 = (bf16[64,512]{1,0:T(8,128)(2,1)}, bf16[64,512]{1,0:T(8,128)(2,1)S(1)}, u32[]{:S(2)}, u32[]{:S(2)}) collective-permute-start(bf16[64,512]{1,0:T(8,128)(2,1)} %get-tuple-element.275), channel_id=1, source_target_pairs={{0,8},{2,10},{4,12},{6,14},{8,0},{10,2},{12,4},{14,6},{16,24},{18,... | collective-permute-start | bytes 196616 | tf_op jit(solution)/shard_map/ppermute | solution.py:366
  455.9 5.6 %collective-permute-start.45 = (bf16[64,512]{1,0:T(8,128)(2,1)}, bf16[64,512]{1,0:T(8,128)(2,1)S(1)}, u32[]{:S(2)}, u32[]{:S(2)}) collective-permute-start(bf16[64,512]{1,0:T(8,128)(2,1)} %get-tuple-element.276), channel_id=1, source_target_pairs={{0,16},{2,18},{4,20},{6,22},{8,24},{10,26},{12,28},{14,30},{16,0},... | collective-permute-start | bytes 196616 | tf_op jit(solution)/shard_map/ppermute | solution.py:366
  467.8 3.6 collective-permute-start.46
  (44 other events, 290.9 us)
Sparse Core Ops, SparseCore 0:
  71.5 102.9 all-gather.2
  262.6 132.0 reduce-scatter.1

commit v4 on v3

--- a/solution.py
+++ b/solution.py
@@ -300,7 +300,7 @@
 F32 = jnp.float32
 TILE = 256
 UNITS = 512
-O_ROWS = (16, 16, 32)
+O_ROWS = (16, 32, 16)
 CORE, TENSOR, X, Z_NEAR, Z_FAR = 1, 0, 2, 4, 8
 
 
@@ -464,19 +464,15 @@
     return values
 
 
-def gathered_rows(ids, refs, order, part, low, high):
-    mine = position(order, ids[3], ids[0])
+def gathered_pair(ids, refs, order, pair, part, low, high):
     count = refs[0].shape[0]
+    at = position(order, 2 * pair, part) ^ position(order, ids[3], ids[0])
+    late = at >= count
+    at = at % count
+    held, last, early, other = [ref[at, low:high] for ref in refs]
+    a, b = jnp.where(late, last, held), jnp.where(late, other, early)
     flipped = ids[2] == 1
-    blocks = []
-    for pair in range(count):
-        at = position(order, 2 * pair, part) ^ mine
-        late = at >= count
-        at = at % count
-        held, last, early, other = [ref[at, low:high] for ref in refs]
-        a, b = jnp.where(late, last, held), jnp.where(late, other, early)
-        blocks += [jnp.where(flipped, b, a), jnp.where(flipped, a, b)]
-    return blocks
+    return jnp.where(flipped, b, a), jnp.where(flipped, a, b)
 
 
 def make_qkv(ids, rows, gots, gain, gathered, height):
@@ -492,14 +488,24 @@
 
         @pl.when(step == 0)
         def _():
-            for t in range(parts):
-                pieces = []
-                for c in range(3):
-                    args = (ids, refs[4 * c : 4 * c + 4], gathered[c].order, t)
-                    w_ref[c, t] = jnp.concatenate(gathered_rows(*args, 0, height), axis=0)
-                    pieces.append(gathered_rows(*args, height, height + O_ROWS[c]))
-                blocks = [block for of_one in zip(*pieces) for block in of_one]
-                wo_ref[t] = jnp.concatenate(blocks, axis=0)
+            @pl.loop(0, fsdp // 2)
+            def _(pair):
+                for t in range(parts):
+                    first = 0
+                    for c in range(3):
+                        args = (ids, refs[4 * c : 4 * c + 4], gathered[c].order, pair, t)
+                        for core, rows in enumerate(gathered_pair(*args, 0, height)):
+                            start = pl.multiple_of((2 * pair + core) * height, height)
+                            w_ref[c, t, pl.ds(start, height)] = rows
+                        count = O_ROWS[c]
+                        if not count:
+                            continue
+                        for core, rows in enumerate(
+                            gathered_pair(*args, height, height + count)
+                        ):
+                            start = (2 * pair + core) * height + first
+                            wo_ref[t, pl.ds(pl.multiple_of(start, 16), count)] = rows
+                        first += count
 
         @pl.when(step // per == ids[0])
         def _():
@@ -806,10 +812,10 @@
     steps = units // tile
     columns = width // steps
 
-    def body(ids, hn_ref, g_ref, w_ref, out_ref, ht_ref, gt_ref):
+    def body(ids, hn_ref, g_ref, w_ref, out_ref, t_ref):
         first = pl.multiple_of(pl.program_id(0) * columns, columns)
-        store_natural(hn_ref[:, pl.ds(first, columns)], ht_ref)
-        store_natural(g_ref[0, :, pl.ds(first, columns)], gt_ref)
+        store_natural(hn_ref[:, pl.ds(first, columns)], t_ref.at[0])
+        store_natural(g_ref[0, :, pl.ds(first, columns)], t_ref.at[1])
         w_gate, w_up, w_down = [
             w_ref[:, c * height : (c + 1) * height].reshape(width, tile) for c in range(3)
         ]
@@ -838,13 +844,11 @@
         ],
         (
             shape((3, length, units), BF),
-            shape((fsdp, height, length), BF),
-            shape((fsdp, height, length), BF),
+            shape((2, fsdp, height, length), BF),
         ),
         [
             pl.BlockSpec((3, length, tile), lambda n, ids: (0, 0, n)),
-            pl.BlockSpec((columns // height, height, length), lambda n, ids: (n, 0, 0)),
-            pl.BlockSpec((columns // height, height, length), lambda n, ids: (n, 0, 0)),
+            pl.BlockSpec((2, columns // height, height, length), lambda n, ids: (0, n, 0, 0)),
         ],
         (steps,),
     )
@@ -862,21 +866,16 @@
         mine = pl.program_id(0) == 0
         keeps = pl.program_id(1) >= per
 
-        @pl.when(mine & keeps)
+        rows = jnp.where(mine, own_ref[0], theirs_ref[0])
+        made = dot_f32(rows, w, 1, 1) + jnp.where(mine, hidden_ref[...], 0.0)
+
+        @pl.when(keeps)
         def _():
-            keep_ref[0] = hidden_ref[...] + dot_f32(own_ref[0], w, 1, 1)
-
-        @pl.when(mine & ~keeps)
+            keep_ref[0] = made
+
+        @pl.when(~keeps)
         def _():
-            send_ref[0] = (hidden_ref[...] + dot_f32(own_ref[0], w, 1, 1)).astype(BF)
-
-        @pl.when(~mine & keeps)
-        def _():
-            keep_ref[0] = dot_f32(theirs_ref[0], w, 1, 1)
-
-        @pl.when(~mine & ~keeps)
-        def _():
-            send_ref[0] = dot_f32(theirs_ref[0], w, 1, 1).astype(BF)
+            send_ref[0] = made.astype(BF)
 
     def row(j, ids):
         return jnp.where(j < per, (1 - ids[0]) * per + j, ids[0] * per + j - per)
@@ -912,29 +911,26 @@
     )
 
 
-def feed_forward_grads(ids, hn_t, hn_t_theirs, grads_t, grads_t_theirs, own, theirs):
-    fsdp, height, length = hn_t.shape
+def feed_forward_grads(ids, own_t, theirs_t, own, theirs):
+    fsdp, height, length = own_t.shape[1:]
     units = own.shape[2]
     per = units // UNITS
 
-    def body(ids, h_ref, h2_ref, g_ref, g2_ref, own_ref, theirs_ref, out_ref):
-        def make(a_ref, b_ref):
-            for f in range(0, fsdp, 4):
-                a = a_ref[f : f + 4].reshape(4 * height, length)
-                b = b_ref[f : f + 4].reshape(4 * height, length)
-                made = dot_f32(a, own_ref[0], 1, 0) + dot_f32(b, theirs_ref[0], 1, 0)
-                out_ref[f : f + 4] = made.astype(BF).reshape(4, height, UNITS)
-
-        pl.when(pl.program_id(0) < 2)(lambda: make(h_ref, h2_ref))
-        pl.when(pl.program_id(0) == 2)(lambda: make(g_ref, g2_ref))
-
-    side = pl.BlockSpec((1, length, UNITS), lambda c, n, ids: (c, 0, n))
+    def body(ids, a_ref, b_ref, own_ref, theirs_ref, out_ref):
+        for f in range(0, fsdp, 4):
+            a = a_ref[0, f : f + 4].reshape(4 * height, length)
+            b = b_ref[0, f : f + 4].reshape(4 * height, length)
+            made = dot_f32(a, own_ref[0], 1, 0) + dot_f32(b, theirs_ref[0], 1, 0)
+            out_ref[f : f + 4] = made.astype(BF).reshape(4, height, UNITS)
+
+    left = pl.BlockSpec((1, fsdp, height, length), lambda c, n, ids: (c // 2, 0, 0, 0))
+    right = pl.BlockSpec((1, length, UNITS), lambda c, n, ids: (c, 0, n))
     return call(
         body,
         "feed_forward_grads",
         ids,
-        (hn_t, hn_t_theirs, grads_t, grads_t_theirs, own, theirs),
-        [whole(hn_t.shape)] * 4 + [side, side],
+        (own_t, theirs_t, own, theirs),
+        [left, left, right, right],
         (shape((fsdp, 3 * height, units), BF),),
         [pl.BlockSpec((fsdp, height, UNITS), lambda c, n, ids: (0, c, n))],
         (3, per),
@@ -1021,7 +1017,7 @@
             pl.BlockSpec((2, length, UNITS), lambda n, ids: (0, at, n)),
             pl.BlockSpec((fsdp, 2 * height, UNITS), lambda n, ids: (0, 0, n)),
         ],
-        (shape((length, width), F32 if half is None else BF),),
+        (shape((length, width), BF),),
         [whole((length, width))],
         (per,),
         (pltpu.VMEM((length, width), F32),),
@@ -1036,7 +1032,7 @@
     cut = gots[0].shape[0] // TILE
 
     def body(ids, share_ref, got_ref, tail_ref, hidden_ref, g_ref, gain_ref, w_ref, *refs):
-        dh_ref, lt_ref, out_ref, blocks_ref, got_scr = refs
+        low_ref, lt_ref, out_ref, blocks_ref, got_scr = refs
 
         @pl.when(pl.program_id(0) < cut)
         def _():
@@ -1049,10 +1045,10 @@
         rows = hidden_ref[...]
         scale = rms_scale(rows)
         normed = rows * scale
-        d_normed = share_ref[...] + got_scr[...].astype(F32)
+        d_normed = share_ref[...].astype(F32) + got_scr[...].astype(F32)
         dh = g_ref[0].astype(F32) + norm_backward_pass(d_normed, normed, scale, gain_ref[...])
-        dh_ref[...] = dh
         low = dh.astype(BF)
+        low_ref[...] = low
         for t in range(parts):
             out_ref[:, t * half : (t + 1) * half] = dot_f32(low, w_ref[t], 1, 0).astype(BF)
         store_transposed(ids, low, blocks_ref, lt_ref)
@@ -1073,7 +1069,7 @@
             whole(w_out.shape),
         ],
         (
-            shape((length, width), F32),
+            shape((length, width), BF),
             shape((fsdp, height, length), BF),
             shape((length, width), BF),
         ),
@@ -1103,7 +1099,7 @@
                 d_normed = part if d_normed is None else d_normed + part
         rows = x_ref[...].astype(F32)
         scale = rms_scale(rows)
-        made = dh_ref[...] + norm_backward_pass(d_normed, rows * scale, scale, gain_ref[...])
+        made = dh_ref[...].astype(F32) + norm_backward_pass(d_normed, rows * scale, scale, gain_ref[...])
         if sent:
             out_ref[...] = made.astype(BF)
         else:
@@ -1224,13 +1220,13 @@
     grads = join_rows(ids, grads_in, got_grads)
     hn, grads, packed = lax.optimization_barrier((hn, grads, packed))
 
-    own, ht, gt = feed_forward(ids, hn, grads, 0, packed)
+    own, own_t = feed_forward(ids, hn, grads, 0, packed)
     own, hn_theirs = lax.optimization_barrier((own, hn_theirs))
-    theirs, ht_theirs, gt_theirs = feed_forward(ids, hn_theirs, grads, 1, packed)
+    theirs, theirs_t = feed_forward(ids, hn_theirs, grads, 1, packed)
     d_one = feed_forward_back(ids, theirs, packed, 0)
     d_one, theirs, own = lax.optimization_barrier((d_one, theirs, own))
     got_one = swap(d_one, TENSOR)
-    made = feed_forward_grads(ids, ht, ht_theirs, gt, gt_theirs, own, theirs)
+    made = feed_forward_grads(ids, own_t, theirs_t, own, theirs)
     made, own, theirs, got_one = lax.optimization_barrier((made, own, theirs, got_one))
     summed = lax.psum_scatter(made, "fsdp", scatter_dimension=0, tiled=False)
     d_two = feed_forward_back(ids, theirs, packed, 1)

time: 484 us -> 478 us (0.988)
  transfers between devices with their start and end apart: 49 -> 49, of which waited for: 16 -> 19; matrix products, arithmetic and copies ran while one was open for 3% -> 3% of each run, Pallas kernels for 56% -> 56%
where the time goes in v4:
time: 478 us; the launch traced here: 474 us
  Pallas kernels  300 us (63%)
  waiting for transfers between devices  84.7 us (18%)
  starting transfers between devices  43 us (9%)
  local copies, waits for them, and re-layouts  21.5 us (4%)
  between operations  15 us (3%)
  other arithmetic  9.56 us (2%)
    pallas_call x26, Pallas kernels, call(): pl.pallas_call(body, name=name, out_shape=outs, grid_spec=pltpu.PrefetchS...  300 us
    ppermute x31, waiting for transfers between devices, swap(): lax.ppermute(value, 'fsdp', [(i, i ^ bit) for i in range(lax.axis_size('f...  53.3 us
    all_gather x1, waiting for transfers between devices, local_sequence(): packed = lax.all_gather(ff_mine, 'fsdp', axis=0, tiled=False)  28.5 us
    ppermute x31, starting transfers between devices, swap(): lax.ppermute(value, 'fsdp', [(i, i ^ bit) for i in range(lax.axis_size('f...  25.6 us
    ppermute x16, starting transfers between devices, swap(): return lax.ppermute(value, 'tensor', [(0, 1), (1, 0)])  17.3 us
    unnamed x89, local copies, waits for them, and re-layouts  11.3 us
  transfers between devices with their start and end apart: 49, of which 19 were waited for; matrix products, arithmetic and copies ran while one was open for 3% of the time, Pallas kernels for 56%

profile of v4, /device:TPU:0, one launch (start us, length us, event | category | flops | bytes accessed | tf_op | source)
XLA Modules:
  0.0 473.7 jit_solution(5048492434797549909)
XLA Ops:
  8.9 3.0 collective-permute-start.2
  13.6 2.7 collective-permute-start
  18.9 1.7 collective-permute-done
  22.3 1.6 collective-permute-start.4
  24.3 2.6 collective-permute-start.6
  26.9 5.0 %collective-permute-done.6 = bf16[2,80,512]{2,1,0:T(8,128)(2,1)S(1)} collective-permute-done((bf16[2,80,512]{2,1,0:T(8,128)(2,1)S(1)}, bf16[2,80,512]{2,1,0:T(8,128)(2,1)S(1)}, u32[]{:S(2)}, u32[]{:S(2)}) %collective-permute-start.6) | collective-permute-done | bytes 163872 | tf_op jit(solution)/shard_map/ppermute | solution.py:366
  31.9 1.8 collective-permute-done.5
  35.9 1.6 collective-permute-start.9
  37.5 2.9 collective-permute-start.10
  40.4 12.8 %collective-permute-done.10 = bf16[2,2,80,512]{3,2,1,0:T(8,128)(2,1)S(1)} collective-permute-done((bf16[2,2,80,512]{3,2,1,0:T(8,128)(2,1)S(1)}, bf16[2,2,80,512]{3,2,1,0:T(8,128)(2,1)S(1)}, u32[]{:S(2)}, u32[]{:S(2)}) %collective-permute-start.10) | collective-permute-done | bytes 327712 | tf_op jit(solution)/shard_map/ppermute | solution.py:366
  54.4 1.6 collective-permute-start.11
  57.6 12.2 %collective-permute-done.13 = bf16[2,2,2,80,512]{4,3,2,1,0:T(8,128)(2,1)} collective-permute-done((bf16[2,2,2,80,512]{4,3,2,1,0:T(8,128)(2,1)S(1)}, bf16[2,2,2,80,512]{4,3,2,1,0:T(8,128)(2,1)}, u32[]{:S(2)}, u32[]{:S(2)}) %collective-permute-start.13) | collective-permute-done | bytes 655392 | tf_op jit(solution)/shard_map/ppermute | solution.py:366
  74.2 2.5 collective-permute-done.17
  80.7 19.3 %qkv.1 = (bf16[3,1024,1024]{2,1,0:T(8,128)(2,1)}, bf16[16,64,1024]{2,1,0:T(8,128)(2,1)}, bf16[1024,1024]{1,0:T(8,128)(2,1)}, bf16[3,2,1024,512]{3,2,1,0:T(8,128)(2,1)}, bf16[2,1024,512]{2,1,0:T(8,128)(2,1)}) custom-call(s32[7]{0:T(128)} %concatenate.43.ids, bf16[2,512,1024]{2,1,0:T(8,128)(2,1)} %bitcast.135, f32[1,1024]{1,0:T(1,128)} %reshape_squeeze.6.gain_ref, ...), custom_call_target="tpu_custom_call" | custom-call | flops 1024 | bytes 1024 | tf_op jit(solution)/shard_map/qkv/pallas_call | solution.py:312
  100.0 29.7 %attend.1 = (bf16[1024,1024]{1,0:T(8,128)(2,1)}, bf16[1024,1024]{1,0:T(8,128)(2,1)}, bf16[16,1024,1024]{2,1,0:T(8,128)(2,1)}, f32[8,2,1024]{2,1,0:T(2,128)}) custom-call(s32[7]{0:T(128)} %concatenate.43.ids, bf16[3,1024,1024]{2,1,0:T(8,128)(2,1)} %get-tuple-element.167.q_ref.k_ref.v_ref, bf16[3,1024,1024]{2,1,0:T(8,128)(2,1)} %get-tuple-element.167.q_ref.k_ref.v_ref, ...), custom_call_target="tpu_custom_call" | custom-call | flops 1024 | bytes 1024 | tf_op jit(solution)/shard_map/attend/pallas_call | solution.py:312
  130.4 8.0 %out_project.1 = (f32[1024,1024]{1,0:T(8,128)}, bf16[1024,1024]{1,0:T(8,128)(2,1)}) custom-call(s32[7]{0:T(128)} %concatenate.43.ids, bf16[1024,1024]{1,0:T(8,128)(2,1)} %get-tuple-element.168.a_ref, bf16[2,1024,512]{2,1,0:T(8,128)(2,1)} %get-tuple-element.169.w_ref, bf16[1024,1024]{1,0:T(8,128)(2,1)} %get-tuple-element.170.x_ref, ...), custom_call_target="tpu_custom_call" | custom-call | flops 1024 | bytes 1024 | tf_op jit(solution)/shard_map/out_project/pallas_call | solution.py:312
  139.0 4.3 join_rows.1.g_ref
  143.4 28.5 %all-gather.3.cloned.1.call-done = bf16[3072,2048]{1,0:T(8,128)(2,1)} async-done(((bf16[192,2048]{1,0:T(8,128)(2,1)}), bf16[3072,2048]{1,0:T(8,128)(2,1)}) %all-gather.3.cloned.1.call-update) | async-done | bytes 12582928 | tf_op jit(solution)/shard_map/all_gather | solution.py:1202
  171.9 21.1 %feed_forward.2 = (bf16[3,1024,2048]{2,1,0:T(8,128)(2,1)}, bf16[2,16,64,1024]{3,2,1,0:T(8,128)(2,1)}) custom-call(s32[7]{0:T(128)} %concatenate.43.ids, bf16[1024,1024]{1,0:T(8,128)(2,1)} %get-tuple-element.174.hn_ref, bf16[2,1024,1024]{2,1,0:T(8,128)(2,1)} %join_rows.1.g_ref, bf16[16,192,2048]{2,1,0:T(8,128)(2,1)} %bitcast.107), custom_call_target="tpu_custom_call" | custom-call | flops 1024 | bytes 1024 | tf_op jit(solution)/shard_map/feed_forward/pallas_call | solution.py:312
  194.3 21.2 %feed_forward.3 = (bf16[3,1024,2048]{2,1,0:T(8,128)(2,1)}, bf16[2,16,64,1024]{3,2,1,0:T(8,128)(2,1)}) custom-call(s32[7]{0:T(128)} %concatenate.43.ids, bf16[1024,1024]{1,0:T(8,128)(2,1)} %copy-done.22, bf16[2,1024,1024]{2,1,0:T(8,128)(2,1)} %join_rows.1.g_ref, bf16[16,192,2048]{2,1,0:T(8,128)(2,1)} %bitcast.108), custom_call_target="tpu_custom_call" | custom-call | flops 1024 | bytes 1024 | tf_op jit(solution)/shard_map/feed_forward/pallas_call | solution.py:312
  215.5 10.0 %feed_forward_back.3 = bf16[512,1024]{1,0:T(8,128)(2,1)} custom-call(s32[7]{0:T(128)} %concatenate.43.ids, bf16[3,1024,2048]{2,1,0:T(8,128)(2,1)} %get-tuple-element.191.d_ref.theirs_ref, bf16[16,192,2048]{2,1,0:T(8,128)(2,1)} %bitcast.109), custom_call_target="tpu_custom_call" | custom-call | flops 1024 | bytes 1024 | tf_op jit(solution)/shard_map/feed_forward_back/pallas_call | solution.py:312
  227.1 33.9 %feed_forward_grads.1 = bf16[16,192,2048]{2,1,0:T(8,128)(2,1)} custom-call(s32[7]{0:T(128)} %concatenate.43.ids, bf16[2,16,64,1024]{3,2,1,0:T(8,128)(2,1)} %get-tuple-element.177.a_ref, bf16[2,16,64,1024]{3,2,1,0:T(8,128)(2,1)} %get-tuple-element.180.b_ref, bf16[3,1024,2048]{2,1,0:T(8,128)(2,1)} %get-tuple-element.190.own_ref.d_ref, ...), custom_call_target="tpu_custom_call" | custom-call | flops 1024 | bytes 1024 | tf_op jit(solution)/shard_map/feed_forward_grads/pallas_call | solution.py:312
  261.9 10.9 %feed_forward_back.4 = bf16[512,1024]{1,0:T(8,128)(2,1)} custom-call(s32[7]{0:T(128)} %concatenate.43.ids, bf16[3,1024,2048]{2,1,0:T(8,128)(2,1)} %get-tuple-element.191.d_ref.theirs_ref, bf16[16,192,2048]{2,1,0:T(8,128)(2,1)} %bitcast.110), custom_call_target="tpu_custom_call" | custom-call | flops 1024 | bytes 1024 | tf_op jit(solution)/shard_map/feed_forward_back/pallas_call | solution.py:312
  272.9 15.3 %feed_forward_back.5.share_ref = bf16[1024,1024]{1,0:T(8,128)(2,1)} custom-call(s32[7]{0:T(128)} %concatenate.43.ids, bf16[3,1024,2048]{2,1,0:T(8,128)(2,1)} %get-tuple-element.190.own_ref.d_ref, bf16[16,192,2048]{2,1,0:T(8,128)(2,1)} %bitcast.111), custom_call_target="tpu_custom_call" | custom-call | flops 1024 | bytes 1024 | tf_op jit(solution)/shard_map/feed_forward_back/pallas_call | solution.py:312
  288.2 17.0 %feed_forward_out.1 = (f32[2,512,1024]{2,1,0:T(8,128)}, bf16[2,512,1024]{2,1,0:T(8,128)(2,1)}) custom-call(s32[7]{0:T(128)} %concatenate.43.ids, bf16[3,1024,2048]{2,1,0:T(8,128)(2,1)} %get-tuple-element.190.own_ref.d_ref, bf16[3,1024,2048]{2,1,0:T(8,128)(2,1)} %get-tuple-element.191.d_ref.theirs_ref, bf16[16,192,2048]{2,1,0:T(8,128)(2,1)} %bitcast.112, ...), custom_call_target="tpu_custom_call" | custom-call | flops 1024 | bytes 1024 | tf_op jit(solution)/shard_map/feed_forward_out/pallas_call | solution.py:312
  306.3 10.9 %norm_and_project_back.1 = (bf16[1024,1024]{1,0:T(8,128)(2,1)}, bf16[16,64,1024]{2,1,0:T(8,128)(2,1)}, bf16[1024,1024]{1,0:T(8,128)(2,1)}) custom-call(s32[7]{0:T(128)} %concatenate.43.ids, bf16[1024,1024]{1,0:T(8,128)(2,1)} %feed_forward_back.5.share_ref, bf16[512,1024]{1,0:T(8,128)(2,1)} %copy-done.23, bf16[512,1024]{1,0:T(8,128)(2,1)} %copy-done.24, ...), custom_call_target="tpu_custom_call" | custom-call | flops 1024 | bytes 1024 | tf_op jit(solution)/shard_map/norm_and_project_back/pallas_call | solution.py:312
  317.2 6.2 %grad_out.1 = (bf16[2,8,64,512]{3,2,1,0:T(8,128)(2,1)}, bf16[2,8,64,512]{3,2,1,0:T(8,128)(2,1)}) custom-call(s32[7]{0:T(128)} %concatenate.43.ids, bf16[16,64,1024]{2,1,0:T(8,128)(2,1)} %get-tuple-element.201.refs_0_, bf16[1,1024,1024]{2,1,0:T(8,128)(2,1)} %bitcast.134), custom_call_target="tpu_custom_call" | custom-call | flops 1024 | bytes 1024 | tf_op jit(solution)/shard_map/grad_out/pallas_call | solution.py:312
  323.3 2.0 collective-permute-start.28
  325.3 32.0 %attend_back.1.refs_1_.d_ref = bf16[3,1024,1024]{2,1,0:T(8,128)(2,1)} custom-call(s32[7]{0:T(128)} %concatenate.43.ids, bf16[3,1024,1024]{2,1,0:T(8,128)(2,1)} %get-tuple-element.167.q_ref.k_ref.v_ref, bf16[3,1024,1024]{2,1,0:T(8,128)(2,1)} %get-tuple-element.167.q_ref.k_ref.v_ref, bf16[3,1024,1024]{2,1,0:T(8,128)(2,1)} %get-tuple-element.167.q_ref.k_ref.v_ref, ...), custom_call_target="tpu_custom_call" | custom-call | flops 1024 | bytes 1024 | tf_op jit(solution)/shard_map/attend_back/pallas_call | solution.py:312
  358.3 2.9 halve.6
  361.2 6.0 %grad_qkv.3 = (bf16[2,8,64,512]{3,2,1,0:T(8,128)(2,1)}, bf16[2,8,64,512]{3,2,1,0:T(8,128)(2,1)}) custom-call(s32[7]{0:T(128)} %concatenate.43.ids, bf16[16,64,1024]{2,1,0:T(8,128)(2,1)} %get-tuple-element.194.refs_0_, bf16[3,1024,1024]{2,1,0:T(8,128)(2,1)} %attend_back.1.refs_1_.d_ref), custom_call_target="tpu_custom_call" | custom-call | flops 1024 | bytes 1024 | tf_op jit(solution)/shard_map/grad_qkv/pallas_call | solution.py:312
  367.2 5.9 %grad_qkv.4 = (bf16[2,8,64,512]{3,2,1,0:T(8,128)(2,1)}, bf16[2,8,64,512]{3,2,1,0:T(8,128)(2,1)}) custom-call(s32[7]{0:T(128)} %concatenate.43.ids, bf16[16,64,1024]{2,1,0:T(8,128)(2,1)} %get-tuple-element.194.refs_0_, bf16[3,1024,1024]{2,1,0:T(8,128)(2,1)} %attend_back.1.refs_1_.d_ref), custom_call_target="tpu_custom_call" | custom-call | flops 1024 | bytes 1024 | tf_op jit(solution)/shard_map/grad_qkv/pallas_call | solution.py:312
  373.1 6.2 %grad_qkv.5 = (bf16[2,8,64,512]{3,2,1,0:T(8,128)(2,1)}, bf16[2,8,64,512]{3,2,1,0:T(8,128)(2,1)}) custom-call(s32[7]{0:T(128)} %concatenate.43.ids, bf16[16,64,1024]{2,1,0:T(8,128)(2,1)} %get-tuple-element.194.refs_0_, bf16[3,1024,1024]{2,1,0:T(8,128)(2,1)} %attend_back.1.refs_1_.d_ref), custom_call_target="tpu_custom_call" | custom-call | flops 1024 | bytes 1024 | tf_op jit(solution)/shard_map/grad_qkv/pallas_call | solution.py:312
  380.6 2.5 collective-permute-done.27.refs_5_.refs_7_.refs_9_.refs_11_.refs_13_
  384.6 3.5 halve.7
  389.3 9.3 %qkv_back.2 = bf16[512,1024]{1,0:T(8,128)(2,1)} custom-call(s32[7]{0:T(128)} %concatenate.43.ids, bf16[3,1024,1024]{2,1,0:T(8,128)(2,1)} %attend_back.1.refs_1_.d_ref, bf16[3,2,1024,512]{3,2,1,0:T(8,128)(2,1)} %get-tuple-element.238.w_ref, bf16[1024,1024]{1,0:T(8,128)(2,1)} %get-tuple-element.170.x_ref, bf16[1024,1024]{1,0:T(8,128)(2,1)} %get-tuple-element.239.dh_ref, ...), custom_call_target="tpu_custom_call" | custom-call | flops 1024 | bytes 1024 | tf_op jit(solution)/shard_map/qkv_back/pallas_call | solution.py:312
  398.6 6.8 %collective-permute-done.29.refs_2_ = bf16[2,2,2,64,512]{4,3,2,1,0:T(8,128)(2,1)S(1)} collective-permute-done((bf16[2,2,2,64,512]{4,3,2,1,0:T(8,128)(2,1)}, bf16[2,2,2,64,512]{4,3,2,1,0:T(8,128)(2,1)S(1)}, u32[]{:S(2)}, u32[]{:S(2)}) %collective-permute-start.29) | collective-permute-done | bytes 524320 | tf_op jit(solution)/shard_map/ppermute | solution.py:366
  407.2 3.5 halve.8
  413.4 1.7 collective-permute-start.36
  415.2 9.6 %qkv_back.3._ = f32[2,4096,128]{2,1,0:T(8,128)} custom-call(s32[7]{0:T(128)} %concatenate.43.ids, bf16[3,1024,1024]{2,1,0:T(8,128)(2,1)} %attend_back.1.refs_1_.d_ref, bf16[3,2,1024,512]{3,2,1,0:T(8,128)(2,1)} %get-tuple-element.238.w_ref, bf16[1024,1024]{1,0:T(8,128)(2,1)} %get-tuple-element.170.x_ref, bf16[1024,1024]{1,0:T(8,128)(2,1)} %get-tuple-element.239.dh_ref, ...), custom_call_target="tpu_custom_call" | custom-call | flops 1024 | bytes 1024 | tf_op jit(solution)/shard_map/qkv_back/pallas_call | solution.py:312
  426.0 4.3 collective-permute-done.36.refs_15_.refs_18_.refs_21_
  430.9 3.5 halve.9
  434.4 1.7 collective-permute-start.38
  438.5 3.8 fusion
  445.2 2.8 halve.10
  451.8 3.8 place_rows.1
  457.1 3.0 halve.11
  460.2 1.9 multiply_reduce_fusion.1
  (219 shorter events, 53.8 us)
Async XLA Ops:
  7.2 164.7 %all-gather.3.cloned.1.call-start = ((), (), s32[]{:S(2)}) async-start(), calls=%async_computation.2 | async-start | bytes 13369344 | tf_op jit(solution)/shard_map/all_gather | solution.py:1202
  8.9 10.0 %collective-permute-start.2 = (bf16[80,512]{1,0:T(8,128)(2,1)S(1)}, bf16[80,512]{1,0:T(8,128)(2,1)S(1)}, u32[]{:S(2)}, u32[]{:S(2)}) collective-permute-start(bf16[80,512]{1,0:T(8,128)(2,1)S(1)} %get-tuple-element.356), channel_id=1, source_target_pairs={{0,1},{1,0},{2,3},{3,2},{4,5},{5,4},{6,7},{7,6},{8,9},{9,8},{10,11... | collective-permute-start | bytes 245768 | tf_op jit(solution)/shard_map/ppermute | solution.py:365
  13.6 7.0 %collective-permute-start = (bf16[88,512]{1,0:T(8,128)(2,1)S(1)}, bf16[88,512]{1,0:T(8,128)(2,1)S(1)}, u32[]{:S(2)}, u32[]{:S(2)}) collective-permute-start(bf16[88,512]{1,0:T(8,128)(2,1)S(1)} %get-tuple-element.354), channel_id=1, source_target_pairs={{0,16},{2,18},{4,20},{6,22},{8,24},{10,26},{12,28},{14,30},{16,0},... | collective-permute-start | bytes 270344 | tf_op jit(solution)/shard_map/ppermute | solution.py:366
  17.0 4.7 collective-permute-start.1
  21.7 12.2 %collective-permute-start.3 = (bf16[256,1024]{1,0:T(8,128)(2,1)S(1)}, bf16[256,1024]{1,0:T(8,128)(2,1)S(1)}, u32[]{:S(2)}, u32[]{:S(2)}) collective-permute-start(bf16[256,1024]{1,0:T(8,128)(2,1)S(1)} %get-tuple-element.147), channel_id=1, source_target_pairs={{0,1},{1,0},{2,3},{3,2},{4,5},{5,4},{6,7},{7,6},{8,9},{9,8},{10,11... | collective-permute-start | bytes 1572872 | tf_op jit(solution)/shard_map/ppermute | solution.py:365
  22.3 9.7 %collective-permute-start.4 = (bf16[2,88,512]{2,1,0:T(8,128)(2,1)S(1)}, bf16[2,88,512]{2,1,0:T(8,128)(2,1)S(1)}, u32[]{:S(2)}, u32[]{:S(2)}) collective-permute-start(bf16[2,88,512]{2,1,0:T(8,128)(2,1)S(1)} %get-tuple-element.348), channel_id=1, source_target_pairs={{0,4},{2,6},{4,0},{6,2},{8,12},{10,14},{12,8},{14,10},{16,20},{18,... | collective-permute-start | bytes 540680 | tf_op jit(solution)/shard_map/ppermute | solution.py:366
  23.8 9.8 %collective-permute-start.5 = (bf16[2,96,512]{2,1,0:T(8,128)(2,1)S(1)}, bf16[2,96,512]{2,1,0:T(8,128)(2,1)S(1)}, u32[]{:S(2)}, u32[]{:S(2)}) collective-permute-start(bf16[2,96,512]{2,1,0:T(8,128)(2,1)S(1)} %get-tuple-element.343), channel_id=1, source_target_pairs={{0,16},{2,18},{4,20},{6,22},{8,24},{10,26},{12,28},{14,30},{16,0},... | collective-permute-start | bytes 589832 | tf_op jit(solution)/shard_map/ppermute | solution.py:366
  24.3 7.7 %collective-permute-start.6 = (bf16[2,80,512]{2,1,0:T(8,128)(2,1)S(1)}, bf16[2,80,512]{2,1,0:T(8,128)(2,1)S(1)}, u32[]{:S(2)}, u32[]{:S(2)}) collective-permute-start(bf16[2,80,512]{2,1,0:T(8,128)(2,1)S(1)} %get-tuple-element.350), channel_id=1, source_target_pairs={{0,8},{2,10},{4,12},{6,14},{8,0},{10,2},{12,4},{14,6},{16,24},{18,... | collective-permute-start | bytes 491528 | tf_op jit(solution)/shard_map/ppermute | solution.py:366
  34.0 19.3 %collective-permute-start.8 = (bf16[2,2,88,512]{3,2,1,0:T(8,128)(2,1)S(1)}, bf16[2,2,88,512]{3,2,1,0:T(8,128)(2,1)S(1)}, u32[]{:S(2)}, u32[]{:S(2)}) collective-permute-start(bf16[2,2,88,512]{3,2,1,0:T(8,128)(2,1)S(1)} %get-tuple-element.339), channel_id=1, source_target_pairs={{0,8},{2,10},{4,12},{6,14},{8,0},{10,2},{12,4},{14,6},{16,24},{18,... | collective-permute-start | bytes 1081352 | tf_op jit(solution)/shard_map/ppermute | solution.py:366
  35.4 17.9 %collective-permute-start.7 = (bf16[256,1024]{1,0:T(8,128)(2,1)S(1)}, bf16[256,1024]{1,0:T(8,128)(2,1)S(1)}, u32[]{:S(2)}, u32[]{:S(2)}) collective-permute-start(bf16[256,1024]{1,0:T(8,128)(2,1)S(1)} %get-tuple-element.151), channel_id=1, source_target_pairs={{0,1},{1,0},{2,3},{3,2},{4,5},{5,4},{6,7},{7,6},{8,9},{9,8},{10,11... | collective-permute-start | bytes 1572872 | tf_op jit(solution)/shard_map/ppermute | solution.py:365
  35.9 17.4 %collective-permute-start.9 = (bf16[2,2,96,512]{3,2,1,0:T(8,128)(2,1)S(1)}, bf16[2,2,96,512]{3,2,1,0:T(8,128)(2,1)S(1)}, u32[]{:S(2)}, u32[]{:S(2)}) collective-permute-start(bf16[2,2,96,512]{3,2,1,0:T(8,128)(2,1)S(1)} %get-tuple-element.337), channel_id=1, source_target_pairs={{0,4},{2,6},{4,0},{6,2},{8,12},{10,14},{12,8},{14,10},{16,20},{18,... | collective-permute-start | bytes 1179656 | tf_op jit(solution)/shard_map/ppermute | solution.py:366
  37.5 15.7 %collective-permute-start.10 = (bf16[2,2,80,512]{3,2,1,0:T(8,128)(2,1)S(1)}, bf16[2,2,80,512]{3,2,1,0:T(8,128)(2,1)S(1)}, u32[]{:S(2)}, u32[]{:S(2)}) collective-permute-start(bf16[2,2,80,512]{3,2,1,0:T(8,128)(2,1)S(1)} %get-tuple-element.341), channel_id=1, source_target_pairs={{0,16},{2,18},{4,20},{6,22},{8,24},{10,26},{12,28},{14,30},{16,0},... | collective-permute-start | bytes 983048 | tf_op jit(solution)/shard_map/ppermute | solution.py:366
  54.2 15.9 %collective-permute-start.12 = (bf16[2,2,2,96,512]{4,3,2,1,0:T(8,128)(2,1)S(1)}, bf16[2,2,2,96,512]{4,3,2,1,0:T(8,128)(2,1)S(1)}, u32[]{:S(2)}, u32[]{:S(2)}) collective-permute-start(bf16[2,2,2,96,512]{4,3,2,1,0:T(8,128)(2,1)S(1)} %pad_maximum_fusion.1), channel_id=1, source_target_pairs={{0,8},{2,10},{4,12},{6,14},{8,0},{10,2},{12,4},{14,6},{16,24},{18,... | collective-permute-start | bytes 2359304 | tf_op jit(solution)/shard_map/ppermute | solution.py:366
  54.4 15.6 %collective-permute-start.11 = (bf16[2,2,2,88,512]{4,3,2,1,0:T(8,128)(2,1)S(1)}, bf16[2,2,2,88,512]{4,3,2,1,0:T(8,128)(2,1)}, u32[]{:S(2)}, u32[]{:S(2)}) collective-permute-start(bf16[2,2,2,88,512]{4,3,2,1,0:T(8,128)(2,1)S(1)} %pad_maximum_fusion.2), channel_id=1, source_target_pairs={{0,1},{1,0},{2,3},{3,2},{4,5},{5,4},{6,7},{7,6},{8,9},{9,8},{10,11... | collective-permute-start | bytes 2162696 | tf_op jit(solution)/shard_map/ppermute | solution.py:365
  56.0 13.8 %collective-permute-start.13 = (bf16[2,2,2,80,512]{4,3,2,1,0:T(8,128)(2,1)S(1)}, bf16[2,2,2,80,512]{4,3,2,1,0:T(8,128)(2,1)}, u32[]{:S(2)}, u32[]{:S(2)}) collective-permute-start(bf16[2,2,2,80,512]{4,3,2,1,0:T(8,128)(2,1)S(1)} %pad_maximum_fusion.3), channel_id=1, source_target_pairs={{0,4},{2,6},{4,0},{6,2},{8,12},{10,14},{12,8},{14,10},{16,20},{18,... | collective-permute-start | bytes 1966088 | tf_op jit(solution)/shard_map/ppermute | solution.py:366
  70.1 360.1 %reduce-scatter.2.cloned.1.call-start = ((), (), s32[]{:S(2)}) async-start(), calls=%async_computation.1 | async-start | bytes 13369344 | tf_op jit(solution)/shard_map/reduce_scatter | solution.py:1231
  70.2 6.5 %collective-permute-start.16 = (bf16[2,2,2,96,512]{4,3,2,1,0:T(8,128)(2,1)S(1)}, bf16[2,2,2,96,512]{4,3,2,1,0:T(8,128)(2,1)}, u32[]{:S(2)}, u32[]{:S(2)}) collective-permute-start(bf16[2,2,2,96,512]{4,3,2,1,0:T(8,128)(2,1)S(1)} %collective-permute-done.12), channel_id=1, source_target_pairs={{0,2},{2,0},{4,6},{6,4},{8,10},{10,8},{12,14},{14,12},{16,18},{18,... | collective-permute-start | bytes 2359304 | tf_op jit(solution)/shard_map/ppermute | solution.py:366
  70.7 6.0 %collective-permute-start.15 = (bf16[2,2,2,88,512]{4,3,2,1,0:T(8,128)(2,1)}, bf16[2,2,2,88,512]{4,3,2,1,0:T(8,128)(2,1)}, u32[]{:S(2)}, u32[]{:S(2)}) collective-permute-start(bf16[2,2,2,88,512]{4,3,2,1,0:T(8,128)(2,1)} %collective-permute-done.11), channel_id=1, source_target_pairs={{0,2},{2,0},{4,6},{6,4},{8,10},{10,8},{12,14},{14,12},{16,18},{18,... | collective-permute-start | bytes 2162696 | tf_op jit(solution)/shard_map/ppermute | solution.py:366
  70.8 5.9 %collective-permute-start.17 = (bf16[2,2,2,80,512]{4,3,2,1,0:T(8,128)(2,1)}, bf16[2,2,2,80,512]{4,3,2,1,0:T(8,128)(2,1)}, u32[]{:S(2)}, u32[]{:S(2)}) collective-permute-start(bf16[2,2,2,80,512]{4,3,2,1,0:T(8,128)(2,1)} %collective-permute-done.13), channel_id=1, source_target_pairs={{0,2},{2,0},{4,6},{6,4},{8,10},{10,8},{12,14},{14,12},{16,18},{18,... | collective-permute-start | bytes 1966088 | tf_op jit(solution)/shard_map/ppermute | solution.py:366
  71.9 8.7 %collective-permute-start.19 = (bf16[2,2,2,80,512]{4,3,2,1,0:T(8,128)(2,1)S(1)}, bf16[2,2,2,80,512]{4,3,2,1,0:T(8,128)(2,1)}, u32[]{:S(2)}, u32[]{:S(2)}) collective-permute-start(bf16[2,2,2,80,512]{4,3,2,1,0:T(8,128)(2,1)S(1)} %pad_maximum_fusion.3), channel_id=1, source_target_pairs={{0,2},{2,0},{4,6},{6,4},{8,10},{10,8},{12,14},{14,12},{16,18},{18,... | collective-permute-start | bytes 1966088 | tf_op jit(solution)/shard_map/ppermute | solution.py:366
  72.6 8.1 %collective-permute-start.18 = (bf16[2,2,2,96,512]{4,3,2,1,0:T(8,128)(2,1)S(1)}, bf16[2,2,2,96,512]{4,3,2,1,0:T(8,128)(2,1)}, u32[]{:S(2)}, u32[]{:S(2)}) collective-permute-start(bf16[2,2,2,96,512]{4,3,2,1,0:T(8,128)(2,1)S(1)} %pad_maximum_fusion.1), channel_id=1, source_target_pairs={{0,2},{2,0},{4,6},{6,4},{8,10},{10,8},{12,14},{14,12},{16,18},{18,... | collective-permute-start | bytes 2359304 | tf_op jit(solution)/shard_map/ppermute | solution.py:366
  79.1 59.9 %collective-permute-start.20 = (bf16[2,512,1024]{2,1,0:T(8,128)(2,1)}, bf16[2,512,1024]{2,1,0:T(8,128)(2,1)}, u32[]{:S(2)}, u32[]{:S(2)}) collective-permute-start(bf16[2,512,1024]{2,1,0:T(8,128)(2,1)} %bitcast.145), channel_id=1, source_target_pairs={{0,1},{1,0},{2,3},{3,2},{4,5},{5,4},{6,7},{7,6},{8,9},{9,8},{10,11... | collective-permute-start | bytes 6291464 | tf_op jit(solution)/shard_map/ppermute | solution.py:365
  138.4 54.5 %collective-permute-start.21 = (bf16[1024,1024]{1,0:T(8,128)(2,1)}, bf16[1024,1024]{1,0:T(8,128)(2,1)S(1)}, u32[]{:S(2)}, u32[]{:S(2)}) collective-permute-start(bf16[1024,1024]{1,0:T(8,128)(2,1)} %get-tuple-element.174.hn_ref), channel_id=1, source_target_pairs={{0,1},{1,0},{2,3},{3,2},{4,5},{5,4},{6,7},{7,6},{8,9},{9,8},{10,11... | collective-permute-start | bytes 6291464 | tf_op jit(solution)/shard_map/ppermute | solution.py:365
  225.5 35.5 %collective-permute-start.22 = (bf16[512,1024]{1,0:T(8,128)(2,1)}, bf16[512,1024]{1,0:T(8,128)(2,1)S(1)}, u32[]{:S(2)}, u32[]{:S(2)}) collective-permute-start(bf16[512,1024]{1,0:T(8,128)(2,1)} %feed_forward_back.3), channel_id=1, source_target_pairs={{0,1},{1,0},{2,3},{3,2},{4,5},{5,4},{6,7},{7,6},{8,9},{9,8},{10,11... | collective-permute-start | bytes 3145736 | tf_op jit(solution)/shard_map/ppermute | solution.py:365
  272.8 32.5 %collective-permute-start.23 = (bf16[512,1024]{1,0:T(8,128)(2,1)}, bf16[512,1024]{1,0:T(8,128)(2,1)S(1)}, u32[]{:S(2)}, u32[]{:S(2)}) collective-permute-start(bf16[512,1024]{1,0:T(8,128)(2,1)} %feed_forward_back.4), channel_id=1, source_target_pairs={{0,1},{1,0},{2,3},{3,2},{4,5},{5,4},{6,7},{7,6},{8,9},{9,8},{10,11... | collective-permute-start | bytes 3145736 | tf_op jit(solution)/shard_map/ppermute | solution.py:365
  323.3 34.0 %collective-permute-start.24 = (bf16[2,2,2,2,64,512]{5,4,3,2,1,0:T(8,128)(2,1)}, bf16[2,2,2,2,64,512]{5,4,3,2,1,0:T(8,128)(2,1)S(1)}, u32[]{:S(2)}, u32[]{:S(2)}) collective-permute-start(bf16[2,2,2,2,64,512]{5,4,3,2,1,0:T(8,128)(2,1)} %bitcast.171), channel_id=1, source_target_pairs={{0,2},{2,0},{4,6},{6,4},{8,10},{10,8},{12,14},{14,12},{16,18},{18,... | collective-permute-start | bytes 3145736 | tf_op jit(solution)/shard_map/ppermute | solution.py:366
  323.3 75.3 %collective-permute-start.28 = (bf16[2,512,1024]{2,1,0:T(8,128)(2,1)S(1)}, bf16[2,512,1024]{2,1,0:T(8,128)(2,1)}, u32[]{:S(2)}, u32[]{:S(2)}) collective-permute-start(bf16[2,512,1024]{2,1,0:T(8,128)(2,1)S(1)} %copy-done.41), channel_id=1, source_target_pairs={{0,1},{1,0},{2,3},{3,2},{4,5},{5,4},{6,7},{7,6},{8,9},{9,8},{10,11... | collective-permute-start | bytes 6291464 | tf_op jit(solution)/shard_map/ppermute | solution.py:365
  367.1 13.4 %collective-permute-start.25 = (bf16[2,2,2,2,64,512]{5,4,3,2,1,0:T(8,128)(2,1)}, bf16[2,2,2,2,64,512]{5,4,3,2,1,0:T(8,128)(2,1)S(1)}, u32[]{:S(2)}, u32[]{:S(2)}) collective-permute-start(bf16[2,2,2,2,64,512]{5,4,3,2,1,0:T(8,128)(2,1)} %bitcast.169), channel_id=1, source_target_pairs={{0,2},{2,0},{4,6},{6,4},{8,10},{10,8},{12,14},{14,12},{16,18},{18,... | collective-permute-start | bytes 3145736 | tf_op jit(solution)/shard_map/ppermute | solution.py:366
  379.3 3.7 collective-permute-start.27
  379.8 3.8 collective-permute-start.26
  379.9 18.7 %collective-permute-start.32 = (bf16[2,2,2,64,512]{4,3,2,1,0:T(8,128)(2,1)S(1)}, bf16[2,2,2,64,512]{4,3,2,1,0:T(8,128)(2,1)S(1)}, u32[]{:S(2)}, u32[]{:S(2)}) collective-permute-start(bf16[2,2,2,64,512]{4,3,2,1,0:T(8,128)(2,1)S(1)} %copy-done.33), channel_id=1, source_target_pairs={{0,4},{2,6},{4,0},{6,2},{8,12},{10,14},{12,8},{14,10},{16,20},{18,... | collective-permute-start | bytes 1572872 | tf_op jit(solution)/shard_map/ppermute | solution.py:366
  388.1 17.2 %collective-permute-start.29 = (bf16[2,2,2,64,512]{4,3,2,1,0:T(8,128)(2,1)}, bf16[2,2,2,64,512]{4,3,2,1,0:T(8,128)(2,1)S(1)}, u32[]{:S(2)}, u32[]{:S(2)}) collective-permute-start(bf16[2,2,2,64,512]{4,3,2,1,0:T(8,128)(2,1)} %get-tuple-element.234), channel_id=1, source_target_pairs={{0,4},{2,6},{4,0},{6,2},{8,12},{10,14},{12,8},{14,10},{16,20},{18,... | collective-permute-start | bytes 1572872 | tf_op jit(solution)/shard_map/ppermute | solution.py:366
  388.8 16.6 %collective-permute-start.30 = (bf16[2,2,2,64,512]{4,3,2,1,0:T(8,128)(2,1)}, bf16[2,2,2,64,512]{4,3,2,1,0:T(8,128)(2,1)S(1)}, u32[]{:S(2)}, u32[]{:S(2)}) collective-permute-start(bf16[2,2,2,64,512]{4,3,2,1,0:T(8,128)(2,1)} %get-tuple-element.235), channel_id=1, source_target_pairs={{0,8},{2,10},{4,12},{6,14},{8,0},{10,2},{12,4},{14,6},{16,24},{18,... | collective-permute-start | bytes 1572872 | tf_op jit(solution)/shard_map/ppermute | solution.py:366
  388.8 16.6 %collective-permute-start.31 = (bf16[2,2,2,64,512]{4,3,2,1,0:T(8,128)(2,1)}, bf16[2,2,2,64,512]{4,3,2,1,0:T(8,128)(2,1)S(1)}, u32[]{:S(2)}, u32[]{:S(2)}) collective-permute-start(bf16[2,2,2,64,512]{4,3,2,1,0:T(8,128)(2,1)} %get-tuple-element.236), channel_id=1, source_target_pairs={{0,1},{1,0},{2,3},{3,2},{4,5},{5,4},{6,7},{7,6},{8,9},{9,8},{10,11... | collective-permute-start | bytes 1572872 | tf_op jit(solution)/shard_map/ppermute | solution.py:365
  410.8 41.0 %collective-permute-start.37 = (bf16[512,1024]{1,0:T(8,128)(2,1)}, bf16[512,1024]{1,0:T(8,128)(2,1)}, u32[]{:S(2)}, u32[]{:S(2)}) collective-permute-start(bf16[512,1024]{1,0:T(8,128)(2,1)} %qkv_back.2), channel_id=1, source_target_pairs={{0,1},{1,0},{2,3},{3,2},{4,5},{5,4},{6,7},{7,6},{8,9},{9,8},{10,11... | collective-permute-start | bytes 3145736 | tf_op jit(solution)/shard_map/ppermute | solution.py:365
  410.9 15.1 %collective-permute-start.33 = (bf16[2,2,64,512]{3,2,1,0:T(8,128)(2,1)}, bf16[2,2,64,512]{3,2,1,0:T(8,128)(2,1)S(1)}, u32[]{:S(2)}, u32[]{:S(2)}) collective-permute-start(bf16[2,2,64,512]{3,2,1,0:T(8,128)(2,1)} %get-tuple-element.248), channel_id=1, source_target_pairs={{0,8},{2,10},{4,12},{6,14},{8,0},{10,2},{12,4},{14,6},{16,24},{18,... | collective-permute-start | bytes 786440 | tf_op jit(solution)/shard_map/ppermute | solution.py:366
  411.4 14.6 %collective-permute-start.34 = (bf16[2,2,64,512]{3,2,1,0:T(8,128)(2,1)}, bf16[2,2,64,512]{3,2,1,0:T(8,128)(2,1)S(1)}, u32[]{:S(2)}, u32[]{:S(2)}) collective-permute-start(bf16[2,2,64,512]{3,2,1,0:T(8,128)(2,1)} %get-tuple-element.249), channel_id=1, source_target_pairs={{0,4},{2,6},{4,0},{6,2},{8,12},{10,14},{12,8},{14,10},{16,20},{18,... | collective-permute-start | bytes 786440 | tf_op jit(solution)/shard_map/ppermute | solution.py:366
  411.9 14.1 %collective-permute-start.35 = (bf16[2,2,64,512]{3,2,1,0:T(8,128)(2,1)}, bf16[2,2,64,512]{3,2,1,0:T(8,128)(2,1)S(1)}, u32[]{:S(2)}, u32[]{:S(2)}) collective-permute-start(bf16[2,2,64,512]{3,2,1,0:T(8,128)(2,1)} %get-tuple-element.250), channel_id=1, source_target_pairs={{0,16},{2,18},{4,20},{6,22},{8,24},{10,26},{12,28},{14,30},{16,0},... | collective-permute-start | bytes 786440 | tf_op jit(solution)/shard_map/ppermute | solution.py:366
  413.4 16.8 %collective-permute-start.36 = (bf16[2,2,64,512]{3,2,1,0:T(8,128)(2,1)}, bf16[2,2,64,512]{3,2,1,0:T(8,128)(2,1)S(1)}, u32[]{:S(2)}, u32[]{:S(2)}) collective-permute-start(bf16[2,2,64,512]{3,2,1,0:T(8,128)(2,1)} %get-tuple-element.251), channel_id=1, source_target_pairs={{0,8},{2,10},{4,12},{6,14},{8,0},{10,2},{12,4},{14,6},{16,24},{18,... | collective-permute-start | bytes 786440 | tf_op jit(solution)/shard_map/ppermute | solution.py:366
  434.4 8.0 %collective-permute-start.38 = (bf16[2,64,512]{2,1,0:T(8,128)(2,1)}, bf16[2,64,512]{2,1,0:T(8,128)(2,1)S(1)}, u32[]{:S(2)}, u32[]{:S(2)}) collective-permute-start(bf16[2,64,512]{2,1,0:T(8,128)(2,1)} %get-tuple-element.261), channel_id=1, source_target_pairs={{0,1},{1,0},{2,3},{3,2},{4,5},{5,4},{6,7},{7,6},{8,9},{9,8},{10,11... | collective-permute-start | bytes 393224 | tf_op jit(solution)/shard_map/ppermute | solution.py:365
  436.2 7.6 %collective-permute-start.39 = (bf16[2,64,512]{2,1,0:T(8,128)(2,1)}, bf16[2,64,512]{2,1,0:T(8,128)(2,1)S(1)}, u32[]{:S(2)}, u32[]{:S(2)}) collective-permute-start(bf16[2,64,512]{2,1,0:T(8,128)(2,1)} %get-tuple-element.262), channel_id=1, source_target_pairs={{0,16},{2,18},{4,20},{6,22},{8,24},{10,26},{12,28},{14,30},{16,0},... | collective-permute-start | bytes 393224 | tf_op jit(solution)/shard_map/ppermute | solution.py:366
  437.5 6.3 %collective-permute-start.40 = (bf16[2,64,512]{2,1,0:T(8,128)(2,1)}, bf16[2,64,512]{2,1,0:T(8,128)(2,1)S(1)}, u32[]{:S(2)}, u32[]{:S(2)}) collective-permute-start(bf16[2,64,512]{2,1,0:T(8,128)(2,1)} %get-tuple-element.263), channel_id=1, source_target_pairs={{0,4},{2,6},{4,0},{6,2},{8,12},{10,14},{12,8},{14,10},{16,20},{18,... | collective-permute-start | bytes 393224 | tf_op jit(solution)/shard_map/ppermute | solution.py:366
  438.1 5.7 %collective-permute-start.41 = (bf16[2,64,512]{2,1,0:T(8,128)(2,1)}, bf16[2,64,512]{2,1,0:T(8,128)(2,1)S(1)}, u32[]{:S(2)}, u32[]{:S(2)}) collective-permute-start(bf16[2,64,512]{2,1,0:T(8,128)(2,1)} %get-tuple-element.264), channel_id=1, source_target_pairs={{0,1},{1,0},{2,3},{3,2},{4,5},{5,4},{6,7},{7,6},{8,9},{9,8},{10,11... | collective-permute-start | bytes 393224 | tf_op jit(solution)/shard_map/ppermute | solution.py:365
  447.9 7.9 %collective-permute-start.42 = (bf16[64,512]{1,0:T(8,128)(2,1)}, bf16[64,512]{1,0:T(8,128)(2,1)S(1)}, u32[]{:S(2)}, u32[]{:S(2)}) collective-permute-start(bf16[64,512]{1,0:T(8,128)(2,1)} %get-tuple-element.269), channel_id=1, source_target_pairs={{0,16},{2,18},{4,20},{6,22},{8,24},{10,26},{12,28},{14,30},{16,0},... | collective-permute-start | bytes 196616 | tf_op jit(solution)/shard_map/ppermute | solution.py:366
  448.4 7.5 %collective-permute-start.43 = (bf16[64,512]{1,0:T(8,128)(2,1)}, bf16[64,512]{1,0:T(8,128)(2,1)S(1)}, u32[]{:S(2)}, u32[]{:S(2)}) collective-permute-start(bf16[64,512]{1,0:T(8,128)(2,1)} %get-tuple-element.270), channel_id=1, source_target_pairs={{0,1},{1,0},{2,3},{3,2},{4,5},{5,4},{6,7},{7,6},{8,9},{9,8},{10,11... | collective-permute-start | bytes 196616 | tf_op jit(solution)/shard_map/ppermute | solution.py:365
  449.7 6.2 %collective-permute-start.44 = (bf16[64,512]{1,0:T(8,128)(2,1)}, bf16[64,512]{1,0:T(8,128)(2,1)S(1)}, u32[]{:S(2)}, u32[]{:S(2)}) collective-permute-start(bf16[64,512]{1,0:T(8,128)(2,1)} %get-tuple-element.271), channel_id=1, source_target_pairs={{0,8},{2,10},{4,12},{6,14},{8,0},{10,2},{12,4},{14,6},{16,24},{18,... | collective-permute-start | bytes 196616 | tf_op jit(solution)/shard_map/ppermute | solution.py:366
  450.2 5.7 %collective-permute-start.45 = (bf16[64,512]{1,0:T(8,128)(2,1)}, bf16[64,512]{1,0:T(8,128)(2,1)S(1)}, u32[]{:S(2)}, u32[]{:S(2)}) collective-permute-start(bf16[64,512]{1,0:T(8,128)(2,1)} %get-tuple-element.272), channel_id=1, source_target_pairs={{0,16},{2,18},{4,20},{6,22},{8,24},{10,26},{12,28},{14,30},{16,0},... | collective-permute-start | bytes 196616 | tf_op jit(solution)/shard_map/ppermute | solution.py:366
  462.2 3.6 collective-permute-start.46
  (44 other events, 291.1 us)
Sparse Core Ops, SparseCore 0:
  70.2 101.6 all-gather.2
  261.1 131.8 reduce-scatter.1

commit v5 on v4

--- a/solution.py
+++ b/solution.py
@@ -788,7 +788,7 @@
         total = x_ref[...].astype(F32)
         for t in range(parts):
             total += dot_f32(a_ref[:, t * half : (t + 1) * half], w_ref[t], 1, 1)
-        hidden_ref[...] = total
+        hidden_ref[...] = total.astype(BF)
         hn_ref[...] = (total * rms_scale(total) * gain_ref[...]).astype(BF)
 
     tile = pl.BlockSpec((TILE, width), lambda r, ids: (r, 0))
@@ -798,7 +798,7 @@
         ids,
         (attended, w_out, x, gain),
         [tile, whole(w_out.shape), tile, whole((1, width))],
-        (shape((length, width), F32), shape((length, width), BF)),
+        (shape((length, width), BF), shape((length, width), BF)),
         [tile, tile],
         (length // TILE,),
     )
@@ -867,7 +867,7 @@
         keeps = pl.program_id(1) >= per
 
         rows = jnp.where(mine, own_ref[0], theirs_ref[0])
-        made = dot_f32(rows, w, 1, 1) + jnp.where(mine, hidden_ref[...], 0.0)
+        made = dot_f32(rows, w, 1, 1) + jnp.where(mine, hidden_ref[...].astype(F32), 0.0)
 
         @pl.when(keeps)
         def _():
@@ -1042,7 +1042,7 @@
         def _():
             got_scr[...] = tail_ref[...]
 
-        rows = hidden_ref[...]
+        rows = hidden_ref[...].astype(F32)
         scale = rms_scale(rows)
         normed = rows * scale
         d_normed = share_ref[...].astype(F32) + got_scr[...].astype(F32)

time: 478 us -> 478 us (level)
  no operation moved by 1% of the time
where the time goes in v5:
time: 478 us; the launch traced here: 473 us
  Pallas kernels  299 us (63%)
  waiting for transfers between devices  83 us (17%)
  starting transfers between devices  45.2 us (9%)
  local copies, waits for them, and re-layouts  21.4 us (4%)
  between operations  15 us (3%)
  other arithmetic  9.56 us (2%)
    pallas_call x26, Pallas kernels, call(): pl.pallas_call(body, name=name, out_shape=outs, grid_spec=pltpu.PrefetchS...  299 us
    ppermute x31, waiting for transfers between devices, swap(): lax.ppermute(value, 'fsdp', [(i, i ^ bit) for i in range(lax.axis_size('f...  51.4 us
    all_gather x1, waiting for transfers between devices, local_sequence(): packed = lax.all_gather(ff_mine, 'fsdp', axis=0, tiled=False)  28.8 us
    ppermute x31, starting transfers between devices, swap(): lax.ppermute(value, 'fsdp', [(i, i ^ bit) for i in range(lax.axis_size('f...  26.4 us
    ppermute x16, starting transfers between devices, swap(): return lax.ppermute(value, 'tensor', [(0, 1), (1, 0)])  18.6 us
    unnamed x89, local copies, waits for them, and re-layouts  11.1 us
  transfers between devices with their start and end apart: 49, of which 19 were waited for; matrix products, arithmetic and copies ran while one was open for 3% of the time, Pallas kernels for 56%

profile of v5, /device:TPU:0, one launch (start us, length us, event | category | flops | bytes accessed | tf_op | source)
XLA Modules:
  0.0 472.8 jit_solution(11819190970408018995)
XLA Ops:
  8.9 3.0 collective-permute-start.2
  13.6 2.7 collective-permute-start
  18.9 1.7 collective-permute-done
  24.3 2.6 collective-permute-start.6
  26.9 5.0 %collective-permute-done.6 = bf16[2,80,512]{2,1,0:T(8,128)(2,1)S(1)} collective-permute-done((bf16[2,80,512]{2,1,0:T(8,128)(2,1)S(1)}, bf16[2,80,512]{2,1,0:T(8,128)(2,1)S(1)}, u32[]{:S(2)}, u32[]{:S(2)}) %collective-permute-start.6) | collective-permute-done | bytes 163872 | tf_op jit(solution)/shard_map/ppermute | solution.py:366
  31.9 1.8 collective-permute-done.5
  37.5 2.9 collective-permute-start.10
  40.4 12.9 %collective-permute-done.10 = bf16[2,2,80,512]{3,2,1,0:T(8,128)(2,1)S(1)} collective-permute-done((bf16[2,2,80,512]{3,2,1,0:T(8,128)(2,1)S(1)}, bf16[2,2,80,512]{3,2,1,0:T(8,128)(2,1)S(1)}, u32[]{:S(2)}, u32[]{:S(2)}) %collective-permute-start.10) | collective-permute-done | bytes 327712 | tf_op jit(solution)/shard_map/ppermute | solution.py:366
  54.3 1.6 collective-permute-start.11
  57.6 12.2 %collective-permute-done.13 = bf16[2,2,2,80,512]{4,3,2,1,0:T(8,128)(2,1)} collective-permute-done((bf16[2,2,2,80,512]{4,3,2,1,0:T(8,128)(2,1)S(1)}, bf16[2,2,2,80,512]{4,3,2,1,0:T(8,128)(2,1)}, u32[]{:S(2)}, u32[]{:S(2)}) %collective-permute-start.13) | collective-permute-done | bytes 655392 | tf_op jit(solution)/shard_map/ppermute | solution.py:366
  74.2 2.5 collective-permute-done.17
  80.7 19.3 %qkv.1 = (bf16[3,1024,1024]{2,1,0:T(8,128)(2,1)}, bf16[16,64,1024]{2,1,0:T(8,128)(2,1)}, bf16[1024,1024]{1,0:T(8,128)(2,1)}, bf16[3,2,1024,512]{3,2,1,0:T(8,128)(2,1)}, bf16[2,1024,512]{2,1,0:T(8,128)(2,1)}) custom-call(s32[7]{0:T(128)} %concatenate.43.ids, bf16[2,512,1024]{2,1,0:T(8,128)(2,1)} %bitcast.135, f32[1,1024]{1,0:T(1,128)} %reshape_squeeze.6.gain_ref, ...), custom_call_target="tpu_custom_call" | custom-call | flops 1024 | bytes 1024 | tf_op jit(solution)/shard_map/qkv/pallas_call | solution.py:312
  100.0 29.7 %attend.1 = (bf16[1024,1024]{1,0:T(8,128)(2,1)}, bf16[1024,1024]{1,0:T(8,128)(2,1)}, bf16[16,1024,1024]{2,1,0:T(8,128)(2,1)}, f32[8,2,1024]{2,1,0:T(2,128)}) custom-call(s32[7]{0:T(128)} %concatenate.43.ids, bf16[3,1024,1024]{2,1,0:T(8,128)(2,1)} %get-tuple-element.167.q_ref.k_ref.v_ref, bf16[3,1024,1024]{2,1,0:T(8,128)(2,1)} %get-tuple-element.167.q_ref.k_ref.v_ref, ...), custom_call_target="tpu_custom_call" | custom-call | flops 1024 | bytes 1024 | tf_op jit(solution)/shard_map/attend/pallas_call | solution.py:312
  130.4 7.7 %out_project.1 = (bf16[1024,1024]{1,0:T(8,128)(2,1)}, bf16[1024,1024]{1,0:T(8,128)(2,1)}) custom-call(s32[7]{0:T(128)} %concatenate.43.ids, bf16[1024,1024]{1,0:T(8,128)(2,1)} %get-tuple-element.168.a_ref, bf16[2,1024,512]{2,1,0:T(8,128)(2,1)} %get-tuple-element.169.w_ref, bf16[1024,1024]{1,0:T(8,128)(2,1)} %get-tuple-element.170.x_ref, ...), custom_call_target="tpu_custom_call" | custom-call | flops 1024 | bytes 1024 | tf_op jit(solution)/shard_map/out_project/pallas_call | solution.py:312
  138.7 4.4 join_rows.1.g_ref
  143.1 28.8 %all-gather.3.cloned.1.call-done = bf16[3072,2048]{1,0:T(8,128)(2,1)} async-done(((bf16[192,2048]{1,0:T(8,128)(2,1)}), bf16[3072,2048]{1,0:T(8,128)(2,1)}) %all-gather.3.cloned.1.call-update) | async-done | bytes 12582928 | tf_op jit(solution)/shard_map/all_gather | solution.py:1202
  171.9 21.1 %feed_forward.2 = (bf16[3,1024,2048]{2,1,0:T(8,128)(2,1)}, bf16[2,16,64,1024]{3,2,1,0:T(8,128)(2,1)}) custom-call(s32[7]{0:T(128)} %concatenate.43.ids, bf16[1024,1024]{1,0:T(8,128)(2,1)} %get-tuple-element.174.hn_ref, bf16[2,1024,1024]{2,1,0:T(8,128)(2,1)} %join_rows.1.g_ref, bf16[16,192,2048]{2,1,0:T(8,128)(2,1)} %bitcast.107), custom_call_target="tpu_custom_call" | custom-call | flops 1024 | bytes 1024 | tf_op jit(solution)/shard_map/feed_forward/pallas_call | solution.py:312
  194.3 21.1 %feed_forward.3 = (bf16[3,1024,2048]{2,1,0:T(8,128)(2,1)}, bf16[2,16,64,1024]{3,2,1,0:T(8,128)(2,1)}) custom-call(s32[7]{0:T(128)} %concatenate.43.ids, bf16[1024,1024]{1,0:T(8,128)(2,1)} %copy-done.22, bf16[2,1024,1024]{2,1,0:T(8,128)(2,1)} %join_rows.1.g_ref, bf16[16,192,2048]{2,1,0:T(8,128)(2,1)} %bitcast.108), custom_call_target="tpu_custom_call" | custom-call | flops 1024 | bytes 1024 | tf_op jit(solution)/shard_map/feed_forward/pallas_call | solution.py:312
  215.4 10.0 %feed_forward_back.3 = bf16[512,1024]{1,0:T(8,128)(2,1)} custom-call(s32[7]{0:T(128)} %concatenate.43.ids, bf16[3,1024,2048]{2,1,0:T(8,128)(2,1)} %get-tuple-element.191.d_ref.theirs_ref, bf16[16,192,2048]{2,1,0:T(8,128)(2,1)} %bitcast.109), custom_call_target="tpu_custom_call" | custom-call | flops 1024 | bytes 1024 | tf_op jit(solution)/shard_map/feed_forward_back/pallas_call | solution.py:312
  227.0 33.9 %feed_forward_grads.1 = bf16[16,192,2048]{2,1,0:T(8,128)(2,1)} custom-call(s32[7]{0:T(128)} %concatenate.43.ids, bf16[2,16,64,1024]{3,2,1,0:T(8,128)(2,1)} %get-tuple-element.177.a_ref, bf16[2,16,64,1024]{3,2,1,0:T(8,128)(2,1)} %get-tuple-element.180.b_ref, bf16[3,1024,2048]{2,1,0:T(8,128)(2,1)} %get-tuple-element.190.own_ref.d_ref, ...), custom_call_target="tpu_custom_call" | custom-call | flops 1024 | bytes 1024 | tf_op jit(solution)/shard_map/feed_forward_grads/pallas_call | solution.py:312
  261.9 10.9 %feed_forward_back.4 = bf16[512,1024]{1,0:T(8,128)(2,1)} custom-call(s32[7]{0:T(128)} %concatenate.43.ids, bf16[3,1024,2048]{2,1,0:T(8,128)(2,1)} %get-tuple-element.191.d_ref.theirs_ref, bf16[16,192,2048]{2,1,0:T(8,128)(2,1)} %bitcast.110), custom_call_target="tpu_custom_call" | custom-call | flops 1024 | bytes 1024 | tf_op jit(solution)/shard_map/feed_forward_back/pallas_call | solution.py:312
  272.9 15.3 %feed_forward_back.5.share_ref = bf16[1024,1024]{1,0:T(8,128)(2,1)} custom-call(s32[7]{0:T(128)} %concatenate.43.ids, bf16[3,1024,2048]{2,1,0:T(8,128)(2,1)} %get-tuple-element.190.own_ref.d_ref, bf16[16,192,2048]{2,1,0:T(8,128)(2,1)} %bitcast.111), custom_call_target="tpu_custom_call" | custom-call | flops 1024 | bytes 1024 | tf_op jit(solution)/shard_map/feed_forward_back/pallas_call | solution.py:312
  288.3 16.7 %feed_forward_out.1 = (f32[2,512,1024]{2,1,0:T(8,128)}, bf16[2,512,1024]{2,1,0:T(8,128)(2,1)}) custom-call(s32[7]{0:T(128)} %concatenate.43.ids, bf16[3,1024,2048]{2,1,0:T(8,128)(2,1)} %get-tuple-element.190.own_ref.d_ref, bf16[3,1024,2048]{2,1,0:T(8,128)(2,1)} %get-tuple-element.191.d_ref.theirs_ref, bf16[16,192,2048]{2,1,0:T(8,128)(2,1)} %bitcast.112, ...), custom_call_target="tpu_custom_call" | custom-call | flops 1024 | bytes 1024 | tf_op jit(solution)/shard_map/feed_forward_out/pallas_call | solution.py:312
  305.9 10.6 %norm_and_project_back.1 = (bf16[1024,1024]{1,0:T(8,128)(2,1)}, bf16[16,64,1024]{2,1,0:T(8,128)(2,1)}, bf16[1024,1024]{1,0:T(8,128)(2,1)}) custom-call(s32[7]{0:T(128)} %concatenate.43.ids, bf16[1024,1024]{1,0:T(8,128)(2,1)} %feed_forward_back.5.share_ref, bf16[512,1024]{1,0:T(8,128)(2,1)} %copy-done.23, bf16[512,1024]{1,0:T(8,128)(2,1)} %copy-done.24, ...), custom_call_target="tpu_custom_call" | custom-call | flops 1024 | bytes 1024 | tf_op jit(solution)/shard_map/norm_and_project_back/pallas_call | solution.py:312
  316.5 6.2 %grad_out.1 = (bf16[2,8,64,512]{3,2,1,0:T(8,128)(2,1)}, bf16[2,8,64,512]{3,2,1,0:T(8,128)(2,1)}) custom-call(s32[7]{0:T(128)} %concatenate.43.ids, bf16[16,64,1024]{2,1,0:T(8,128)(2,1)} %get-tuple-element.201.refs_0_, bf16[1,1024,1024]{2,1,0:T(8,128)(2,1)} %bitcast.134), custom_call_target="tpu_custom_call" | custom-call | flops 1024 | bytes 1024 | tf_op jit(solution)/shard_map/grad_out/pallas_call | solution.py:312
  322.7 2.0 collective-permute-start.28
  324.7 31.9 %attend_back.1.refs_1_.d_ref = bf16[3,1024,1024]{2,1,0:T(8,128)(2,1)} custom-call(s32[7]{0:T(128)} %concatenate.43.ids, bf16[3,1024,1024]{2,1,0:T(8,128)(2,1)} %get-tuple-element.167.q_ref.k_ref.v_ref, bf16[3,1024,1024]{2,1,0:T(8,128)(2,1)} %get-tuple-element.167.q_ref.k_ref.v_ref, bf16[3,1024,1024]{2,1,0:T(8,128)(2,1)} %get-tuple-element.167.q_ref.k_ref.v_ref, ...), custom_call_target="tpu_custom_call" | custom-call | flops 1024 | bytes 1024 | tf_op jit(solution)/shard_map/attend_back/pallas_call | solution.py:312
  357.6 2.9 halve.6
  360.5 5.9 %grad_qkv.3 = (bf16[2,8,64,512]{3,2,1,0:T(8,128)(2,1)}, bf16[2,8,64,512]{3,2,1,0:T(8,128)(2,1)}) custom-call(s32[7]{0:T(128)} %concatenate.43.ids, bf16[16,64,1024]{2,1,0:T(8,128)(2,1)} %get-tuple-element.194.refs_0_, bf16[3,1024,1024]{2,1,0:T(8,128)(2,1)} %attend_back.1.refs_1_.d_ref), custom_call_target="tpu_custom_call" | custom-call | flops 1024 | bytes 1024 | tf_op jit(solution)/shard_map/grad_qkv/pallas_call | solution.py:312
  366.6 5.9 %grad_qkv.4 = (bf16[2,8,64,512]{3,2,1,0:T(8,128)(2,1)}, bf16[2,8,64,512]{3,2,1,0:T(8,128)(2,1)}) custom-call(s32[7]{0:T(128)} %concatenate.43.ids, bf16[16,64,1024]{2,1,0:T(8,128)(2,1)} %get-tuple-element.194.refs_0_, bf16[3,1024,1024]{2,1,0:T(8,128)(2,1)} %attend_back.1.refs_1_.d_ref), custom_call_target="tpu_custom_call" | custom-call | flops 1024 | bytes 1024 | tf_op jit(solution)/shard_map/grad_qkv/pallas_call | solution.py:312
  372.5 6.1 %grad_qkv.5 = (bf16[2,8,64,512]{3,2,1,0:T(8,128)(2,1)}, bf16[2,8,64,512]{3,2,1,0:T(8,128)(2,1)}) custom-call(s32[7]{0:T(128)} %concatenate.43.ids, bf16[16,64,1024]{2,1,0:T(8,128)(2,1)} %get-tuple-element.194.refs_0_, bf16[3,1024,1024]{2,1,0:T(8,128)(2,1)} %attend_back.1.refs_1_.d_ref), custom_call_target="tpu_custom_call" | custom-call | flops 1024 | bytes 1024 | tf_op jit(solution)/shard_map/grad_qkv/pallas_call | solution.py:312
  379.7 1.8 collective-permute-done.27.refs_5_.refs_7_.refs_9_.refs_11_.refs_13_
  383.8 3.5 halve.7
  388.4 9.3 %qkv_back.2 = bf16[512,1024]{1,0:T(8,128)(2,1)} custom-call(s32[7]{0:T(128)} %concatenate.43.ids, bf16[3,1024,1024]{2,1,0:T(8,128)(2,1)} %attend_back.1.refs_1_.d_ref, bf16[3,2,1024,512]{3,2,1,0:T(8,128)(2,1)} %get-tuple-element.238.w_ref, bf16[1024,1024]{1,0:T(8,128)(2,1)} %get-tuple-element.170.x_ref, bf16[1024,1024]{1,0:T(8,128)(2,1)} %get-tuple-element.239.dh_ref, ...), custom_call_target="tpu_custom_call" | custom-call | flops 1024 | bytes 1024 | tf_op jit(solution)/shard_map/qkv_back/pallas_call | solution.py:312
  397.7 6.8 %collective-permute-done.29.refs_2_ = bf16[2,2,2,64,512]{4,3,2,1,0:T(8,128)(2,1)S(1)} collective-permute-done((bf16[2,2,2,64,512]{4,3,2,1,0:T(8,128)(2,1)}, bf16[2,2,2,64,512]{4,3,2,1,0:T(8,128)(2,1)S(1)}, u32[]{:S(2)}, u32[]{:S(2)}) %collective-permute-start.29) | collective-permute-done | bytes 524320 | tf_op jit(solution)/shard_map/ppermute | solution.py:366
  406.3 3.5 halve.8
  411.0 2.4 collective-permute-start.35
  414.9 9.6 %qkv_back.3._ = f32[2,4096,128]{2,1,0:T(8,128)} custom-call(s32[7]{0:T(128)} %concatenate.43.ids, bf16[3,1024,1024]{2,1,0:T(8,128)(2,1)} %attend_back.1.refs_1_.d_ref, bf16[3,2,1024,512]{3,2,1,0:T(8,128)(2,1)} %get-tuple-element.238.w_ref, bf16[1024,1024]{1,0:T(8,128)(2,1)} %get-tuple-element.170.x_ref, bf16[1024,1024]{1,0:T(8,128)(2,1)} %get-tuple-element.239.dh_ref, ...), custom_call_target="tpu_custom_call" | custom-call | flops 1024 | bytes 1024 | tf_op jit(solution)/shard_map/qkv_back/pallas_call | solution.py:312
  425.1 4.1 collective-permute-done.36.refs_15_.refs_18_.refs_21_
  429.9 3.5 halve.9
  433.4 1.7 collective-permute-start.38
  435.1 1.6 collective-permute-start.39
  438.5 3.8 fusion
  443.9 2.8 halve.10
  450.9 3.8 place_rows.1
  456.3 3.0 halve.11
  459.3 1.9 multiply_reduce_fusion.1
  461.4 1.6 collective-permute-start.46
  (219 shorter events, 53.9 us)
Async XLA Ops:
  7.2 164.7 %all-gather.3.cloned.1.call-start = ((), (), s32[]{:S(2)}) async-start(), calls=%async_computation.2 | async-start | bytes 13369344 | tf_op jit(solution)/shard_map/all_gather | solution.py:1202
  8.9 10.0 %collective-permute-start.2 = (bf16[80,512]{1,0:T(8,128)(2,1)S(1)}, bf16[80,512]{1,0:T(8,128)(2,1)S(1)}, u32[]{:S(2)}, u32[]{:S(2)}) collective-permute-start(bf16[80,512]{1,0:T(8,128)(2,1)S(1)} %get-tuple-element.356), channel_id=1, source_target_pairs={{0,1},{1,0},{2,3},{3,2},{4,5},{5,4},{6,7},{7,6},{8,9},{9,8},{10,11... | collective-permute-start | bytes 245768 | tf_op jit(solution)/shard_map/ppermute | solution.py:365
  13.6 7.0 %collective-permute-start = (bf16[88,512]{1,0:T(8,128)(2,1)S(1)}, bf16[88,512]{1,0:T(8,128)(2,1)S(1)}, u32[]{:S(2)}, u32[]{:S(2)}) collective-permute-start(bf16[88,512]{1,0:T(8,128)(2,1)S(1)} %get-tuple-element.354), channel_id=1, source_target_pairs={{0,16},{2,18},{4,20},{6,22},{8,24},{10,26},{12,28},{14,30},{16,0},... | collective-permute-start | bytes 270344 | tf_op jit(solution)/shard_map/ppermute | solution.py:366
  17.0 4.7 collective-permute-start.1
  21.7 12.2 %collective-permute-start.3 = (bf16[256,1024]{1,0:T(8,128)(2,1)S(1)}, bf16[256,1024]{1,0:T(8,128)(2,1)S(1)}, u32[]{:S(2)}, u32[]{:S(2)}) collective-permute-start(bf16[256,1024]{1,0:T(8,128)(2,1)S(1)} %get-tuple-element.147), channel_id=1, source_target_pairs={{0,1},{1,0},{2,3},{3,2},{4,5},{5,4},{6,7},{7,6},{8,9},{9,8},{10,11... | collective-permute-start | bytes 1572872 | tf_op jit(solution)/shard_map/ppermute | solution.py:365
  22.3 9.7 %collective-permute-start.4 = (bf16[2,88,512]{2,1,0:T(8,128)(2,1)S(1)}, bf16[2,88,512]{2,1,0:T(8,128)(2,1)S(1)}, u32[]{:S(2)}, u32[]{:S(2)}) collective-permute-start(bf16[2,88,512]{2,1,0:T(8,128)(2,1)S(1)} %get-tuple-element.348), channel_id=1, source_target_pairs={{0,4},{2,6},{4,0},{6,2},{8,12},{10,14},{12,8},{14,10},{16,20},{18,... | collective-permute-start | bytes 540680 | tf_op jit(solution)/shard_map/ppermute | solution.py:366
  23.8 9.8 %collective-permute-start.5 = (bf16[2,96,512]{2,1,0:T(8,128)(2,1)S(1)}, bf16[2,96,512]{2,1,0:T(8,128)(2,1)S(1)}, u32[]{:S(2)}, u32[]{:S(2)}) collective-permute-start(bf16[2,96,512]{2,1,0:T(8,128)(2,1)S(1)} %get-tuple-element.343), channel_id=1, source_target_pairs={{0,16},{2,18},{4,20},{6,22},{8,24},{10,26},{12,28},{14,30},{16,0},... | collective-permute-start | bytes 589832 | tf_op jit(solution)/shard_map/ppermute | solution.py:366
  24.3 7.7 %collective-permute-start.6 = (bf16[2,80,512]{2,1,0:T(8,128)(2,1)S(1)}, bf16[2,80,512]{2,1,0:T(8,128)(2,1)S(1)}, u32[]{:S(2)}, u32[]{:S(2)}) collective-permute-start(bf16[2,80,512]{2,1,0:T(8,128)(2,1)S(1)} %get-tuple-element.350), channel_id=1, source_target_pairs={{0,8},{2,10},{4,12},{6,14},{8,0},{10,2},{12,4},{14,6},{16,24},{18,... | collective-permute-start | bytes 491528 | tf_op jit(solution)/shard_map/ppermute | solution.py:366
  34.0 19.3 %collective-permute-start.8 = (bf16[2,2,88,512]{3,2,1,0:T(8,128)(2,1)S(1)}, bf16[2,2,88,512]{3,2,1,0:T(8,128)(2,1)S(1)}, u32[]{:S(2)}, u32[]{:S(2)}) collective-permute-start(bf16[2,2,88,512]{3,2,1,0:T(8,128)(2,1)S(1)} %get-tuple-element.339), channel_id=1, source_target_pairs={{0,8},{2,10},{4,12},{6,14},{8,0},{10,2},{12,4},{14,6},{16,24},{18,... | collective-permute-start | bytes 1081352 | tf_op jit(solution)/shard_map/ppermute | solution.py:366
  35.4 17.9 %collective-permute-start.7 = (bf16[256,1024]{1,0:T(8,128)(2,1)S(1)}, bf16[256,1024]{1,0:T(8,128)(2,1)S(1)}, u32[]{:S(2)}, u32[]{:S(2)}) collective-permute-start(bf16[256,1024]{1,0:T(8,128)(2,1)S(1)} %get-tuple-element.151), channel_id=1, source_target_pairs={{0,1},{1,0},{2,3},{3,2},{4,5},{5,4},{6,7},{7,6},{8,9},{9,8},{10,11... | collective-permute-start | bytes 1572872 | tf_op jit(solution)/shard_map/ppermute | solution.py:365
  35.9 17.4 %collective-permute-start.9 = (bf16[2,2,96,512]{3,2,1,0:T(8,128)(2,1)S(1)}, bf16[2,2,96,512]{3,2,1,0:T(8,128)(2,1)S(1)}, u32[]{:S(2)}, u32[]{:S(2)}) collective-permute-start(bf16[2,2,96,512]{3,2,1,0:T(8,128)(2,1)S(1)} %get-tuple-element.337), channel_id=1, source_target_pairs={{0,4},{2,6},{4,0},{6,2},{8,12},{10,14},{12,8},{14,10},{16,20},{18,... | collective-permute-start | bytes 1179656 | tf_op jit(solution)/shard_map/ppermute | solution.py:366
  37.5 15.7 %collective-permute-start.10 = (bf16[2,2,80,512]{3,2,1,0:T(8,128)(2,1)S(1)}, bf16[2,2,80,512]{3,2,1,0:T(8,128)(2,1)S(1)}, u32[]{:S(2)}, u32[]{:S(2)}) collective-permute-start(bf16[2,2,80,512]{3,2,1,0:T(8,128)(2,1)S(1)} %get-tuple-element.341), channel_id=1, source_target_pairs={{0,16},{2,18},{4,20},{6,22},{8,24},{10,26},{12,28},{14,30},{16,0},... | collective-permute-start | bytes 983048 | tf_op jit(solution)/shard_map/ppermute | solution.py:366
  54.2 15.9 %collective-permute-start.12 = (bf16[2,2,2,96,512]{4,3,2,1,0:T(8,128)(2,1)S(1)}, bf16[2,2,2,96,512]{4,3,2,1,0:T(8,128)(2,1)S(1)}, u32[]{:S(2)}, u32[]{:S(2)}) collective-permute-start(bf16[2,2,2,96,512]{4,3,2,1,0:T(8,128)(2,1)S(1)} %pad_maximum_fusion.1), channel_id=1, source_target_pairs={{0,8},{2,10},{4,12},{6,14},{8,0},{10,2},{12,4},{14,6},{16,24},{18,... | collective-permute-start | bytes 2359304 | tf_op jit(solution)/shard_map/ppermute | solution.py:366
  54.3 15.6 %collective-permute-start.11 = (bf16[2,2,2,88,512]{4,3,2,1,0:T(8,128)(2,1)S(1)}, bf16[2,2,2,88,512]{4,3,2,1,0:T(8,128)(2,1)}, u32[]{:S(2)}, u32[]{:S(2)}) collective-permute-start(bf16[2,2,2,88,512]{4,3,2,1,0:T(8,128)(2,1)S(1)} %pad_maximum_fusion.2), channel_id=1, source_target_pairs={{0,1},{1,0},{2,3},{3,2},{4,5},{5,4},{6,7},{7,6},{8,9},{9,8},{10,11... | collective-permute-start | bytes 2162696 | tf_op jit(solution)/shard_map/ppermute | solution.py:365
  56.0 13.8 %collective-permute-start.13 = (bf16[2,2,2,80,512]{4,3,2,1,0:T(8,128)(2,1)S(1)}, bf16[2,2,2,80,512]{4,3,2,1,0:T(8,128)(2,1)}, u32[]{:S(2)}, u32[]{:S(2)}) collective-permute-start(bf16[2,2,2,80,512]{4,3,2,1,0:T(8,128)(2,1)S(1)} %pad_maximum_fusion.3), channel_id=1, source_target_pairs={{0,4},{2,6},{4,0},{6,2},{8,12},{10,14},{12,8},{14,10},{16,20},{18,... | collective-permute-start | bytes 1966088 | tf_op jit(solution)/shard_map/ppermute | solution.py:366
  70.1 359.1 %reduce-scatter.2.cloned.1.call-start = ((), (), s32[]{:S(2)}) async-start(), calls=%async_computation.1 | async-start | bytes 13369344 | tf_op jit(solution)/shard_map/reduce_scatter | solution.py:1231
  70.2 6.5 %collective-permute-start.16 = (bf16[2,2,2,96,512]{4,3,2,1,0:T(8,128)(2,1)S(1)}, bf16[2,2,2,96,512]{4,3,2,1,0:T(8,128)(2,1)}, u32[]{:S(2)}, u32[]{:S(2)}) collective-permute-start(bf16[2,2,2,96,512]{4,3,2,1,0:T(8,128)(2,1)S(1)} %collective-permute-done.12), channel_id=1, source_target_pairs={{0,2},{2,0},{4,6},{6,4},{8,10},{10,8},{12,14},{14,12},{16,18},{18,... | collective-permute-start | bytes 2359304 | tf_op jit(solution)/shard_map/ppermute | solution.py:366
  70.7 6.0 %collective-permute-start.15 = (bf16[2,2,2,88,512]{4,3,2,1,0:T(8,128)(2,1)}, bf16[2,2,2,88,512]{4,3,2,1,0:T(8,128)(2,1)}, u32[]{:S(2)}, u32[]{:S(2)}) collective-permute-start(bf16[2,2,2,88,512]{4,3,2,1,0:T(8,128)(2,1)} %collective-permute-done.11), channel_id=1, source_target_pairs={{0,2},{2,0},{4,6},{6,4},{8,10},{10,8},{12,14},{14,12},{16,18},{18,... | collective-permute-start | bytes 2162696 | tf_op jit(solution)/shard_map/ppermute | solution.py:366
  70.8 5.9 %collective-permute-start.17 = (bf16[2,2,2,80,512]{4,3,2,1,0:T(8,128)(2,1)}, bf16[2,2,2,80,512]{4,3,2,1,0:T(8,128)(2,1)}, u32[]{:S(2)}, u32[]{:S(2)}) collective-permute-start(bf16[2,2,2,80,512]{4,3,2,1,0:T(8,128)(2,1)} %collective-permute-done.13), channel_id=1, source_target_pairs={{0,2},{2,0},{4,6},{6,4},{8,10},{10,8},{12,14},{14,12},{16,18},{18,... | collective-permute-start | bytes 1966088 | tf_op jit(solution)/shard_map/ppermute | solution.py:366
  71.9 8.7 %collective-permute-start.19 = (bf16[2,2,2,80,512]{4,3,2,1,0:T(8,128)(2,1)S(1)}, bf16[2,2,2,80,512]{4,3,2,1,0:T(8,128)(2,1)}, u32[]{:S(2)}, u32[]{:S(2)}) collective-permute-start(bf16[2,2,2,80,512]{4,3,2,1,0:T(8,128)(2,1)S(1)} %pad_maximum_fusion.3), channel_id=1, source_target_pairs={{0,2},{2,0},{4,6},{6,4},{8,10},{10,8},{12,14},{14,12},{16,18},{18,... | collective-permute-start | bytes 1966088 | tf_op jit(solution)/shard_map/ppermute | solution.py:366
  72.6 8.1 %collective-permute-start.18 = (bf16[2,2,2,96,512]{4,3,2,1,0:T(8,128)(2,1)S(1)}, bf16[2,2,2,96,512]{4,3,2,1,0:T(8,128)(2,1)}, u32[]{:S(2)}, u32[]{:S(2)}) collective-permute-start(bf16[2,2,2,96,512]{4,3,2,1,0:T(8,128)(2,1)S(1)} %pad_maximum_fusion.1), channel_id=1, source_target_pairs={{0,2},{2,0},{4,6},{6,4},{8,10},{10,8},{12,14},{14,12},{16,18},{18,... | collective-permute-start | bytes 2359304 | tf_op jit(solution)/shard_map/ppermute | solution.py:366
  79.1 59.6 %collective-permute-start.20 = (bf16[2,512,1024]{2,1,0:T(8,128)(2,1)}, bf16[2,512,1024]{2,1,0:T(8,128)(2,1)}, u32[]{:S(2)}, u32[]{:S(2)}) collective-permute-start(bf16[2,512,1024]{2,1,0:T(8,128)(2,1)} %bitcast.145), channel_id=1, source_target_pairs={{0,1},{1,0},{2,3},{3,2},{4,5},{5,4},{6,7},{7,6},{8,9},{9,8},{10,11... | collective-permute-start | bytes 6291464 | tf_op jit(solution)/shard_map/ppermute | solution.py:365
  138.1 54.8 %collective-permute-start.21 = (bf16[1024,1024]{1,0:T(8,128)(2,1)}, bf16[1024,1024]{1,0:T(8,128)(2,1)S(1)}, u32[]{:S(2)}, u32[]{:S(2)}) collective-permute-start(bf16[1024,1024]{1,0:T(8,128)(2,1)} %get-tuple-element.174.hn_ref), channel_id=1, source_target_pairs={{0,1},{1,0},{2,3},{3,2},{4,5},{5,4},{6,7},{7,6},{8,9},{9,8},{10,11... | collective-permute-start | bytes 6291464 | tf_op jit(solution)/shard_map/ppermute | solution.py:365
  225.5 35.5 %collective-permute-start.22 = (bf16[512,1024]{1,0:T(8,128)(2,1)}, bf16[512,1024]{1,0:T(8,128)(2,1)S(1)}, u32[]{:S(2)}, u32[]{:S(2)}) collective-permute-start(bf16[512,1024]{1,0:T(8,128)(2,1)} %feed_forward_back.3), channel_id=1, source_target_pairs={{0,1},{1,0},{2,3},{3,2},{4,5},{5,4},{6,7},{7,6},{8,9},{9,8},{10,11... | collective-permute-start | bytes 3145736 | tf_op jit(solution)/shard_map/ppermute | solution.py:365
  272.8 32.2 %collective-permute-start.23 = (bf16[512,1024]{1,0:T(8,128)(2,1)}, bf16[512,1024]{1,0:T(8,128)(2,1)S(1)}, u32[]{:S(2)}, u32[]{:S(2)}) collective-permute-start(bf16[512,1024]{1,0:T(8,128)(2,1)} %feed_forward_back.4), channel_id=1, source_target_pairs={{0,1},{1,0},{2,3},{3,2},{4,5},{5,4},{6,7},{7,6},{8,9},{9,8},{10,11... | collective-permute-start | bytes 3145736 | tf_op jit(solution)/shard_map/ppermute | solution.py:365
  322.7 33.9 %collective-permute-start.24 = (bf16[2,2,2,2,64,512]{5,4,3,2,1,0:T(8,128)(2,1)}, bf16[2,2,2,2,64,512]{5,4,3,2,1,0:T(8,128)(2,1)S(1)}, u32[]{:S(2)}, u32[]{:S(2)}) collective-permute-start(bf16[2,2,2,2,64,512]{5,4,3,2,1,0:T(8,128)(2,1)} %bitcast.171), channel_id=1, source_target_pairs={{0,2},{2,0},{4,6},{6,4},{8,10},{10,8},{12,14},{14,12},{16,18},{18,... | collective-permute-start | bytes 3145736 | tf_op jit(solution)/shard_map/ppermute | solution.py:366
  322.7 75.0 %collective-permute-start.28 = (bf16[2,512,1024]{2,1,0:T(8,128)(2,1)S(1)}, bf16[2,512,1024]{2,1,0:T(8,128)(2,1)}, u32[]{:S(2)}, u32[]{:S(2)}) collective-permute-start(bf16[2,512,1024]{2,1,0:T(8,128)(2,1)S(1)} %copy-done.41), channel_id=1, source_target_pairs={{0,1},{1,0},{2,3},{3,2},{4,5},{5,4},{6,7},{7,6},{8,9},{9,8},{10,11... | collective-permute-start | bytes 6291464 | tf_op jit(solution)/shard_map/ppermute | solution.py:365
  366.4 13.3 %collective-permute-start.25 = (bf16[2,2,2,2,64,512]{5,4,3,2,1,0:T(8,128)(2,1)}, bf16[2,2,2,2,64,512]{5,4,3,2,1,0:T(8,128)(2,1)S(1)}, u32[]{:S(2)}, u32[]{:S(2)}) collective-permute-start(bf16[2,2,2,2,64,512]{5,4,3,2,1,0:T(8,128)(2,1)} %bitcast.169), channel_id=1, source_target_pairs={{0,2},{2,0},{4,6},{6,4},{8,10},{10,8},{12,14},{14,12},{16,18},{18,... | collective-permute-start | bytes 3145736 | tf_op jit(solution)/shard_map/ppermute | solution.py:366
  378.6 2.9 collective-permute-start.27
  379.0 3.8 collective-permute-start.26
  379.2 18.6 %collective-permute-start.32 = (bf16[2,2,2,64,512]{4,3,2,1,0:T(8,128)(2,1)S(1)}, bf16[2,2,2,64,512]{4,3,2,1,0:T(8,128)(2,1)S(1)}, u32[]{:S(2)}, u32[]{:S(2)}) collective-permute-start(bf16[2,2,2,64,512]{4,3,2,1,0:T(8,128)(2,1)S(1)} %copy-done.33), channel_id=1, source_target_pairs={{0,4},{2,6},{4,0},{6,2},{8,12},{10,14},{12,8},{14,10},{16,20},{18,... | collective-permute-start | bytes 1572872 | tf_op jit(solution)/shard_map/ppermute | solution.py:366
  387.3 17.2 %collective-permute-start.29 = (bf16[2,2,2,64,512]{4,3,2,1,0:T(8,128)(2,1)}, bf16[2,2,2,64,512]{4,3,2,1,0:T(8,128)(2,1)S(1)}, u32[]{:S(2)}, u32[]{:S(2)}) collective-permute-start(bf16[2,2,2,64,512]{4,3,2,1,0:T(8,128)(2,1)} %get-tuple-element.234), channel_id=1, source_target_pairs={{0,4},{2,6},{4,0},{6,2},{8,12},{10,14},{12,8},{14,10},{16,20},{18,... | collective-permute-start | bytes 1572872 | tf_op jit(solution)/shard_map/ppermute | solution.py:366
  387.9 16.7 %collective-permute-start.30 = (bf16[2,2,2,64,512]{4,3,2,1,0:T(8,128)(2,1)}, bf16[2,2,2,64,512]{4,3,2,1,0:T(8,128)(2,1)S(1)}, u32[]{:S(2)}, u32[]{:S(2)}) collective-permute-start(bf16[2,2,2,64,512]{4,3,2,1,0:T(8,128)(2,1)} %get-tuple-element.235), channel_id=1, source_target_pairs={{0,8},{2,10},{4,12},{6,14},{8,0},{10,2},{12,4},{14,6},{16,24},{18,... | collective-permute-start | bytes 1572872 | tf_op jit(solution)/shard_map/ppermute | solution.py:366
  387.9 16.7 %collective-permute-start.31 = (bf16[2,2,2,64,512]{4,3,2,1,0:T(8,128)(2,1)}, bf16[2,2,2,64,512]{4,3,2,1,0:T(8,128)(2,1)S(1)}, u32[]{:S(2)}, u32[]{:S(2)}) collective-permute-start(bf16[2,2,2,64,512]{4,3,2,1,0:T(8,128)(2,1)} %get-tuple-element.236), channel_id=1, source_target_pairs={{0,1},{1,0},{2,3},{3,2},{4,5},{5,4},{6,7},{7,6},{8,9},{9,8},{10,11... | collective-permute-start | bytes 1572872 | tf_op jit(solution)/shard_map/ppermute | solution.py:365
  409.8 41.1 %collective-permute-start.37 = (bf16[512,1024]{1,0:T(8,128)(2,1)}, bf16[512,1024]{1,0:T(8,128)(2,1)}, u32[]{:S(2)}, u32[]{:S(2)}) collective-permute-start(bf16[512,1024]{1,0:T(8,128)(2,1)} %qkv_back.2), channel_id=1, source_target_pairs={{0,1},{1,0},{2,3},{3,2},{4,5},{5,4},{6,7},{7,6},{8,9},{9,8},{10,11... | collective-permute-start | bytes 3145736 | tf_op jit(solution)/shard_map/ppermute | solution.py:365
  410.0 15.1 %collective-permute-start.33 = (bf16[2,2,64,512]{3,2,1,0:T(8,128)(2,1)}, bf16[2,2,64,512]{3,2,1,0:T(8,128)(2,1)S(1)}, u32[]{:S(2)}, u32[]{:S(2)}) collective-permute-start(bf16[2,2,64,512]{3,2,1,0:T(8,128)(2,1)} %get-tuple-element.248), channel_id=1, source_target_pairs={{0,8},{2,10},{4,12},{6,14},{8,0},{10,2},{12,4},{14,6},{16,24},{18,... | collective-permute-start | bytes 786440 | tf_op jit(solution)/shard_map/ppermute | solution.py:366
  410.4 14.7 %collective-permute-start.34 = (bf16[2,2,64,512]{3,2,1,0:T(8,128)(2,1)}, bf16[2,2,64,512]{3,2,1,0:T(8,128)(2,1)S(1)}, u32[]{:S(2)}, u32[]{:S(2)}) collective-permute-start(bf16[2,2,64,512]{3,2,1,0:T(8,128)(2,1)} %get-tuple-element.249), channel_id=1, source_target_pairs={{0,4},{2,6},{4,0},{6,2},{8,12},{10,14},{12,8},{14,10},{16,20},{18,... | collective-permute-start | bytes 786440 | tf_op jit(solution)/shard_map/ppermute | solution.py:366
  411.0 14.1 %collective-permute-start.35 = (bf16[2,2,64,512]{3,2,1,0:T(8,128)(2,1)}, bf16[2,2,64,512]{3,2,1,0:T(8,128)(2,1)S(1)}, u32[]{:S(2)}, u32[]{:S(2)}) collective-permute-start(bf16[2,2,64,512]{3,2,1,0:T(8,128)(2,1)} %get-tuple-element.250), channel_id=1, source_target_pairs={{0,16},{2,18},{4,20},{6,22},{8,24},{10,26},{12,28},{14,30},{16,0},... | collective-permute-start | bytes 786440 | tf_op jit(solution)/shard_map/ppermute | solution.py:366
  413.4 15.8 %collective-permute-start.36 = (bf16[2,2,64,512]{3,2,1,0:T(8,128)(2,1)}, bf16[2,2,64,512]{3,2,1,0:T(8,128)(2,1)S(1)}, u32[]{:S(2)}, u32[]{:S(2)}) collective-permute-start(bf16[2,2,64,512]{3,2,1,0:T(8,128)(2,1)} %get-tuple-element.251), channel_id=1, source_target_pairs={{0,8},{2,10},{4,12},{6,14},{8,0},{10,2},{12,4},{14,6},{16,24},{18,... | collective-permute-start | bytes 786440 | tf_op jit(solution)/shard_map/ppermute | solution.py:366
  433.4 9.0 %collective-permute-start.38 = (bf16[2,64,512]{2,1,0:T(8,128)(2,1)}, bf16[2,64,512]{2,1,0:T(8,128)(2,1)S(1)}, u32[]{:S(2)}, u32[]{:S(2)}) collective-permute-start(bf16[2,64,512]{2,1,0:T(8,128)(2,1)} %get-tuple-element.261), channel_id=1, source_target_pairs={{0,1},{1,0},{2,3},{3,2},{4,5},{5,4},{6,7},{7,6},{8,9},{9,8},{10,11... | collective-permute-start | bytes 393224 | tf_op jit(solution)/shard_map/ppermute | solution.py:365
  435.1 7.4 %collective-permute-start.39 = (bf16[2,64,512]{2,1,0:T(8,128)(2,1)}, bf16[2,64,512]{2,1,0:T(8,128)(2,1)S(1)}, u32[]{:S(2)}, u32[]{:S(2)}) collective-permute-start(bf16[2,64,512]{2,1,0:T(8,128)(2,1)} %get-tuple-element.262), channel_id=1, source_target_pairs={{0,16},{2,18},{4,20},{6,22},{8,24},{10,26},{12,28},{14,30},{16,0},... | collective-permute-start | bytes 393224 | tf_op jit(solution)/shard_map/ppermute | solution.py:366
  436.7 5.8 %collective-permute-start.40 = (bf16[2,64,512]{2,1,0:T(8,128)(2,1)}, bf16[2,64,512]{2,1,0:T(8,128)(2,1)S(1)}, u32[]{:S(2)}, u32[]{:S(2)}) collective-permute-start(bf16[2,64,512]{2,1,0:T(8,128)(2,1)} %get-tuple-element.263), channel_id=1, source_target_pairs={{0,4},{2,6},{4,0},{6,2},{8,12},{10,14},{12,8},{14,10},{16,20},{18,... | collective-permute-start | bytes 393224 | tf_op jit(solution)/shard_map/ppermute | solution.py:366
  437.1 5.4 %collective-permute-start.41 = (bf16[2,64,512]{2,1,0:T(8,128)(2,1)}, bf16[2,64,512]{2,1,0:T(8,128)(2,1)S(1)}, u32[]{:S(2)}, u32[]{:S(2)}) collective-permute-start(bf16[2,64,512]{2,1,0:T(8,128)(2,1)} %get-tuple-element.264), channel_id=1, source_target_pairs={{0,1},{1,0},{2,3},{3,2},{4,5},{5,4},{6,7},{7,6},{8,9},{9,8},{10,11... | collective-permute-start | bytes 393224 | tf_op jit(solution)/shard_map/ppermute | solution.py:365
  446.6 8.3 %collective-permute-start.42 = (bf16[64,512]{1,0:T(8,128)(2,1)}, bf16[64,512]{1,0:T(8,128)(2,1)S(1)}, u32[]{:S(2)}, u32[]{:S(2)}) collective-permute-start(bf16[64,512]{1,0:T(8,128)(2,1)} %get-tuple-element.269), channel_id=1, source_target_pairs={{0,16},{2,18},{4,20},{6,22},{8,24},{10,26},{12,28},{14,30},{16,0},... | collective-permute-start | bytes 196616 | tf_op jit(solution)/shard_map/ppermute | solution.py:366
  447.3 7.6 %collective-permute-start.43 = (bf16[64,512]{1,0:T(8,128)(2,1)}, bf16[64,512]{1,0:T(8,128)(2,1)S(1)}, u32[]{:S(2)}, u32[]{:S(2)}) collective-permute-start(bf16[64,512]{1,0:T(8,128)(2,1)} %get-tuple-element.270), channel_id=1, source_target_pairs={{0,1},{1,0},{2,3},{3,2},{4,5},{5,4},{6,7},{7,6},{8,9},{9,8},{10,11... | collective-permute-start | bytes 196616 | tf_op jit(solution)/shard_map/ppermute | solution.py:365
  448.7 6.3 %collective-permute-start.44 = (bf16[64,512]{1,0:T(8,128)(2,1)}, bf16[64,512]{1,0:T(8,128)(2,1)S(1)}, u32[]{:S(2)}, u32[]{:S(2)}) collective-permute-start(bf16[64,512]{1,0:T(8,128)(2,1)} %get-tuple-element.271), channel_id=1, source_target_pairs={{0,8},{2,10},{4,12},{6,14},{8,0},{10,2},{12,4},{14,6},{16,24},{18,... | collective-permute-start | bytes 196616 | tf_op jit(solution)/shard_map/ppermute | solution.py:366
  449.4 5.6 %collective-permute-start.45 = (bf16[64,512]{1,0:T(8,128)(2,1)}, bf16[64,512]{1,0:T(8,128)(2,1)S(1)}, u32[]{:S(2)}, u32[]{:S(2)}) collective-permute-start(bf16[64,512]{1,0:T(8,128)(2,1)} %get-tuple-element.272), channel_id=1, source_target_pairs={{0,16},{2,18},{4,20},{6,22},{8,24},{10,26},{12,28},{14,30},{16,0},... | collective-permute-start | bytes 196616 | tf_op jit(solution)/shard_map/ppermute | solution.py:366
  461.4 3.6 collective-permute-start.46
  (44 other events, 289.2 us)
Sparse Core Ops, SparseCore 0:
  70.2 101.6 all-gather.2
  261.1 132.0 reduce-scatter.1
